TPU v7x, 32 devices: a whole 2x2x4 slice. The times are simulated.
32 devices in a mesh: row: 4 (over z), col: 8 (over y, x, core).
Axes of the slice: x: 2, y: 2, z: 4, core: 2. Of those that a mesh axis runs over, the one named last changes fastest.
Arguments:
- amplitudes: bfloat16 [16, 16, 12, 4096], P('row', 'col'), may hold values from -6 to 6
- integrals: bfloat16 [16, 16, 47, 4096], P('row', 'col'), may hold values from -0.1875 to 0.1875
- pair_lists: int32 [4, 12, 2], replicated, may hold values from 0 to 46, as said below
- tile_counts: int32 [4], replicated, may hold values from 1 to 12, as said below
Outputs:
- symmetric: float32 [16, 16, 12, 4096], P('row', 'col')
Inputs may be any that keep to these rules, and one draw needn't show every extreme that they name: `pair_lists`: each grid row lists 12 distinct ordered pairs of different tiles. `tile_counts`: the largest count equals 12.
All inputs are finite; a program needn't handle non-finite values.
Results may differ from a plain program's by a relative error of at most 0.0029.
Values may be sent and summed in bfloat16 or wider, within the bound.
No kernel may reach another device: no remote copies, remote signals or barrier semaphores. Data moves between devices by JAX's collectives and lax.ppermute only.
A program may use at most 128 MiB of HBM per device.

v0:
```python
import functools

import jax
import jax.numpy as jnp
from jax import lax
from jax.experimental import pallas as pl
from jax.experimental.pallas import tpu as pltpu
from jax.sharding import PartitionSpec as P


TILE = 64
LANES = 128
CHUNKS = 3
VMEM = pl.BlockSpec(memory_space=pltpu.VMEM)
SMEM = pl.BlockSpec(memory_space=pltpu.SMEM)
ANY = pl.BlockSpec(memory_space=pl.ANY)
PARAMS = pltpu.CompilerParams(vmem_limit_bytes=48 * 1024 * 1024)


def rows_of(x):
    outer, pair, slots, square = x.shape
    x = jnp.transpose(x, (0, 2, 1, 3)).reshape(outer, slots, pair, square // LANES, LANES)
    return jnp.transpose(x, (0, 1, 3, 2, 4)).reshape(outer, slots, square // LANES * pair, LANES)


def tiles_of(x, pair):
    outer, slots, rows, lanes = x.shape
    x = x.reshape(outer, slots, rows // pair, pair, lanes)
    x = jnp.transpose(x, (0, 1, 3, 2, 4)).reshape(outer, slots, pair, rows // pair * lanes)
    return jnp.transpose(x, (0, 2, 1, 3))


def swap(x):
    count = x.shape[0]
    x = x.reshape(count // 8, 8, LANES)
    z = pltpu.roll(x, TILE, 2)
    after = pltpu.roll(z, 7, 1)
    before = pltpu.roll(z, 1, 1)
    odd = lax.broadcasted_iota(jnp.int32, x.shape, 1) % 2
    half = lax.broadcasted_iota(jnp.int32, x.shape, 2) // TILE
    out = jnp.where(odd == half, x, jnp.where(odd == 0, after, before))
    return out.reshape(count, LANES)


def pick_kernel(base, size, rows, list_ref, w_ref, *outs):
    my_row = lax.axis_index("row")
    depth = w_ref.shape[0]
    for shift in range(rows):
        row = lax.rem(my_row + shift, rows)
        out = outs[shift]

        def one(s, _, out=out, row=row):
            tile = list_ref[row, 1, base + s]
            x = w_ref[:, tile].reshape(depth * TILE, LANES).astype(jnp.float32)
            out[s] = swap(x).astype(jnp.bfloat16)
            return 0

        lax.fori_loop(0, size, one, 0)


def left_kernel(a_ref, out):
    depth, slots = a_ref.shape[:2]

    def one(s, _):
        x = a_ref[:, s].reshape(depth * TILE, LANES).astype(jnp.float32)
        out[s] = swap(x).astype(jnp.bfloat16)
        return 0

    lax.fori_loop(0, slots, one, 0)


def cycle_kernel(rows, cols, ratio, base, size, *refs):
    count_ref = refs[0]
    lefts = refs[1 : 1 + cols]
    rights = refs[1 + cols : 1 + cols + rows]
    outs = refs[1 + cols + rows : -4]
    held_left, held_right, total, sem = refs[-4:]
    my_row = lax.axis_index("row")
    my_col = lax.axis_index("col")
    copies = []
    for e, left in enumerate(lefts):
        copies.append(pltpu.make_async_copy(left.at[pl.ds(base, size)], held_left.at[my_col ^ e], sem.at[len(copies)]))
    for d, right in enumerate(rights):
        row = lax.rem(my_row - d + rows, rows)
        copies.append(pltpu.make_async_copy(right, held_right.at[row], sem.at[len(copies)]))
    for copy in copies:
        copy.start()
    for copy in copies:
        copy.wait()
    my_count = count_ref[my_row]
    half = total.shape[0] // ratio

    def one(hop, s, _):
        at = s
        s = s + hop * (size // 2)
        acc = None
        for row in range(rows):
            left = jnp.concatenate([held_left[row * ratio + p, s] for p in range(ratio)], axis=1)
            part = jnp.dot(left, held_right[row, s], preferred_element_type=jnp.float32)
            acc = part if acc is None else acc + part
        live = (base + s < my_count).astype(jnp.float32)
        total[...] = acc * live
        for step in range(ratio):
            part = lax.rem(lax.rem(my_col, ratio) + step, ratio)
            outs[2 * step + hop][at] = total[pl.ds(pl.multiple_of(part * half, half), half), :].astype(jnp.bfloat16)
        return 0

    for hop in range(2):
        lax.fori_loop(0, size // 2, functools.partial(one, hop), 0)


def final_kernel(ratio, sizes, list_ref, count_ref, *refs):
    chunks = len(sizes)
    owns = refs[: 2 * chunks * ratio]
    theirs = refs[2 * chunks * ratio : 4 * chunks * ratio]
    out_ref, held_own, held_their, sem = refs[-4:]
    my_row = lax.axis_index("row")
    my_col = lax.axis_index("col")
    slots = sum(sizes)
    core = lax.rem(my_col, ratio)
    partner = my_col // ratio
    copies = []
    for step in range(ratio):
        mine = lax.rem(core + step, ratio)
        other = lax.rem(core - step + ratio, ratio)
        base = 0
        for chunk, size in enumerate(sizes):
            for hop in range(2):
                at = (chunk * ratio + step) * 2 + hop
                where = pl.ds(base, size // 2)
                copies.append(pltpu.make_async_copy(owns[at], held_own.at[mine, where], sem.at[len(copies)]))
                copies.append(pltpu.make_async_copy(theirs[at], held_their.at[other, where], sem.at[len(copies)]))
                base += size // 2
    for copy in copies:
        copy.start()
    for copy in copies:
        copy.wait()
    my_count = count_ref[my_row]
    depth = out_ref.shape[0]

    def one(s, _):
        first = list_ref[my_row, 0, s]
        second = list_ref[my_row, 1, s]
        found = jnp.int32(-1)
        for t in range(slots):
            hit = (list_ref[partner, 0, t] == second) & (list_ref[partner, 1, t] == first)
            found = jnp.where(hit, t, found)
        live = s < my_count
        own = jnp.concatenate([held_own[p, s] for p in range(ratio)], axis=0).astype(jnp.float32)

        @pl.when(live & (found >= 0))
        def _():
            t = jnp.maximum(found, 0)
            mirror = jnp.concatenate([held_their[p, t].astype(jnp.float32).T for p in range(ratio)], axis=0)
            out_ref[:, s] = swap(own + mirror).reshape(depth, TILE, LANES)

        @pl.when(jnp.logical_not(live & (found >= 0)))
        def _():
            out_ref[:, s] = swap(own).reshape(depth, TILE, LANES)

        return 0

    lax.fori_loop(0, slots, one, 0)


def mirror_pairs(rows, cols, step, hop):
    ratio = cols // rows
    pairs = []
    for row in range(rows):
        for col in range(cols):
            part = (col % ratio + step) % ratio
            held = col ^ (hop * (cols // 2))
            pairs.append((row * cols + held, (col // ratio) * cols + row * ratio + part))
    return pairs


def on_device(amplitudes, integrals, pair_lists, tile_counts):
    rows = lax.axis_size("row")
    cols = lax.axis_size("col")
    ratio = cols // rows
    occ_row, occ_col, slots, square = amplitudes.shape
    assert occ_col * TILE == LANES and occ_row == ratio * occ_col
    sizes = [slots // CHUNKS] * CHUNKS
    tall = occ_row * TILE
    wide = occ_col * TILE
    lists = jnp.transpose(pair_lists, (0, 2, 1))
    bf16 = jnp.bfloat16

    table = rows_of(integrals)

    rights = []
    base = 0
    for size in sizes:
        picked = pl.pallas_call(
            functools.partial(pick_kernel, base, size, rows),
            out_shape=[jax.ShapeDtypeStruct((size, tall, wide), bf16)] * rows,
            in_specs=[SMEM, VMEM],
            out_specs=[VMEM] * rows,
            compiler_params=PARAMS,
            name="pick",
        )(lists, table)
        got = [picked[0]]
        for shift in range(1, rows):
            pairs = [(r, (r + shift) % rows) for r in range(rows)]
            got.append(lax.ppermute(picked[shift], "row", pairs))
        rights.append(got)
        base += size

    mine = pl.pallas_call(
        left_kernel,
        out_shape=jax.ShapeDtypeStruct((slots, tall, wide), bf16),
        in_specs=[VMEM],
        out_specs=VMEM,
        compiler_params=PARAMS,
        name="left",
    )(rows_of(amplitudes))
    lefts = [mine]
    for e in range(1, cols):
        if e % 2:
            lefts.append(lax.ppermute(lefts[e - 1], "col", [(c, c ^ 1) for c in range(cols)]))
        else:
            lefts.append(lax.ppermute(mine, "col", [(c, c ^ e) for c in range(cols)]))

    owns, theirs = [], []
    base = 0
    for chunk, size in enumerate(sizes):
        sent = pl.pallas_call(
            functools.partial(cycle_kernel, rows, cols, ratio, base, size),
            out_shape=[jax.ShapeDtypeStruct((size // 2, tall // ratio, wide), bf16)] * (2 * ratio),
            in_specs=[SMEM] + [ANY] * (cols + rows),
            out_specs=[VMEM] * (2 * ratio),
            scratch_shapes=[
                pltpu.VMEM((cols, size, tall, wide), bf16),
                pltpu.VMEM((rows, size, tall, wide), bf16),
                pltpu.VMEM((tall, wide), jnp.float32),
                pltpu.SemaphoreType.DMA((cols + rows,)),
            ],
            compiler_params=PARAMS,
            name="cycle",
        )(tile_counts, *lefts, *rights[chunk])
        owns += sent
        for step in range(ratio):
            for hop in range(2):
                block = sent[2 * step + hop]
                if hop:
                    block = lax.ppermute(block, "col", [(c, c ^ (cols // 2)) for c in range(cols)])
                theirs.append(lax.ppermute(block, ("row", "col"), mirror_pairs(rows, cols, step, hop)))
        base += size

    out = pl.pallas_call(
        functools.partial(final_kernel, ratio, sizes),
        out_shape=jax.ShapeDtypeStruct((occ_row, slots, square // LANES * occ_col, LANES), jnp.float32),
        in_specs=[SMEM, SMEM] + [ANY] * (4 * len(sizes) * ratio),
        out_specs=VMEM,
        scratch_shapes=[
            pltpu.VMEM((ratio, slots, tall // ratio, wide), bf16),
            pltpu.VMEM((ratio, slots, tall // ratio, wide), bf16),
            pltpu.SemaphoreType.DMA((4 * len(sizes) * ratio,)),
        ],
        compiler_params=PARAMS,
        name="final",
    )(lists, tile_counts, *owns, *theirs)
    return tiles_of(out, occ_col)


def solution(mesh):
    return jax.shard_map(
        on_device,
        mesh=mesh,
        in_specs=(P("row", "col", None, None), P("row", "col", None, None), P(), P()),
        out_specs=P("row", "col", None, None),
        check_vma=False,
    )
```

profile of v0, /device:TPU:3, one launch (start us, length us, event | category | flops | bytes accessed | tf_op | source)
XLA Modules:
  0.0 153.7 jit_solution(10661133396971502633)
XLA Ops:
  0.0 1.1 copy-done.1
  1.1 1.2 left.1.refs_1_
  2.4 1.5 collective-permute-start.3
  3.9 1.2 collective-permute-start.5
  5.0 1.9 %copy-done = bf16[4,2,47,4096]{3,1,2,0:T(2,128)(2,1)S(1)} copy-done((bf16[4,2,47,4096]{3,1,2,0:T(2,128)(2,1)S(1)}, bf16[4,2,47,4096]{3,1,2,0:T(2,128)(2,1)}, u32[]{:S(2)}) %copy-start) | copy-done | bytes 3080216
  6.9 0.7 copy-done.2
  7.6 2.2 %pick.3 = (bf16[4,256,128]{2,1,0:T(8,128)(2,1)S(1)}, bf16[4,256,128]{2,1,0:T(8,128)(2,1)S(1)}, bf16[4,256,128]{2,1,0:T(8,128)(2,1)S(1)}, bf16[4,256,128]{2,1,0:T(8,128)(2,1)S(1)}) custom-call(s32[4,2,12]{2,1,0:T(2,128)S(1)} %bitcast.26, bf16[4,47,64,128]{3,2,1,0:T(8,128)(2,1)S(1)} %bitcast.22), custom_call_target="tpu_custom_call" | custom-call | tf_op jit(solution)/shard_map/pick/pallas_call | solution.py:194
  9.8 1.3 collective-permute-start.7
  11.1 2.3 %collective-permute-start.8 = (bf16[4,256,128]{2,1,0:T(8,128)(2,1)S(1)}, bf16[4,256,128]{2,1,0:T(8,128)(2,1)S(1)}, u32[]{:S(2)}, u32[]{:S(2)}) collective-permute-start(bf16[4,256,128]{2,1,0:T(8,128)(2,1)S(1)} %get-tuple-element.31), channel_id=1, source_target_pairs={{0,16},{8,24},{16,0},{24,8},{1,17},{9,25},{17,1},{25,9},{2,18},{10... | collective-permute-start | bytes 786440 | tf_op jit(solution)/shard_map/ppermute | solution.py:205
  13.4 4.7 %collective-permute-done.7.refs_10_ = bf16[4,256,128]{2,1,0:T(8,128)(2,1)S(1)} collective-permute-done((bf16[4,256,128]{2,1,0:T(8,128)(2,1)S(1)}, bf16[4,256,128]{2,1,0:T(8,128)(2,1)S(1)}, u32[]{:S(2)}, u32[]{:S(2)}) %collective-permute-start.7) | collective-permute-done | bytes 262176 | tf_op jit(solution)/shard_map/ppermute | solution.py:205
  18.2 4.3 %collective-permute-start = (bf16[12,256,128]{2,1,0:T(8,128)(2,1)S(1)}, bf16[12,256,128]{2,1,0:T(8,128)(2,1)S(1)}, u32[]{:S(2)}, u32[]{:S(2)}) collective-permute-start(bf16[12,256,128]{2,1,0:T(8,128)(2,1)S(1)} %left.1.refs_1_), channel_id=1, source_target_pairs={{0,1},{1,0},{2,3},{3,2},{4,5},{5,4},{6,7},{7,6},{8,9},{9,8},{10,11... | collective-permute-start | bytes 2359304 | tf_op jit(solution)/shard_map/ppermute | solution.py:220
  22.4 1.0 collective-permute-start.2
  23.5 15.0 %collective-permute-start.4 = (bf16[12,256,128]{2,1,0:T(8,128)(2,1)S(1)}, bf16[12,256,128]{2,1,0:T(8,128)(2,1)S(1)}, u32[]{:S(2)}, u32[]{:S(2)}) collective-permute-start(bf16[12,256,128]{2,1,0:T(8,128)(2,1)S(1)} %collective-permute-done.3.refs_5_), channel_id=1, source_target_pairs={{0,1},{1,0},{2,3},{3,2},{4,5},{5,4},{6,7},{7,6},{8,9},{9,8},{10,11... | collective-permute-start | bytes 2359304 | tf_op jit(solution)/shard_map/ppermute | solution.py:220
  38.6 1.5 collective-permute-start.6
  40.1 3.3 %collective-permute-start.9 = (bf16[4,256,128]{2,1,0:T(8,128)(2,1)S(1)}, bf16[4,256,128]{2,1,0:T(8,128)(2,1)S(1)}, u32[]{:S(2)}, u32[]{:S(2)}) collective-permute-start(bf16[4,256,128]{2,1,0:T(8,128)(2,1)S(1)} %get-tuple-element.32), channel_id=1, source_target_pairs={{0,24},{8,0},{16,8},{24,16},{1,25},{9,1},{17,9},{25,17},{2,26},{10... | collective-permute-start | bytes 786440 | tf_op jit(solution)/shard_map/ppermute | solution.py:205
  43.5 2.2 %pick.4 = (bf16[4,256,128]{2,1,0:T(8,128)(2,1)S(1)}, bf16[4,256,128]{2,1,0:T(8,128)(2,1)S(1)}, bf16[4,256,128]{2,1,0:T(8,128)(2,1)S(1)}, bf16[4,256,128]{2,1,0:T(8,128)(2,1)S(1)}) custom-call(s32[4,2,12]{2,1,0:T(2,128)S(1)} %bitcast.27, bf16[4,47,64,128]{3,2,1,0:T(8,128)(2,1)S(1)} %bitcast.23), custom_call_target="tpu_custom_call" | custom-call | tf_op jit(solution)/shard_map/pick/pallas_call | solution.py:194
  45.7 3.4 %collective-permute-done.9.refs_12_ = bf16[4,256,128]{2,1,0:T(8,128)(2,1)S(1)} collective-permute-done((bf16[4,256,128]{2,1,0:T(8,128)(2,1)S(1)}, bf16[4,256,128]{2,1,0:T(8,128)(2,1)S(1)}, u32[]{:S(2)}, u32[]{:S(2)}) %collective-permute-start.9) | collective-permute-done | bytes 262176 | tf_op jit(solution)/shard_map/ppermute | solution.py:205
  49.2 2.2 %pick.5 = (bf16[4,256,128]{2,1,0:T(8,128)(2,1)S(1)}, bf16[4,256,128]{2,1,0:T(8,128)(2,1)S(1)}, bf16[4,256,128]{2,1,0:T(8,128)(2,1)S(1)}, bf16[4,256,128]{2,1,0:T(8,128)(2,1)S(1)}) custom-call(s32[4,2,12]{2,1,0:T(2,128)S(1)} %bitcast.28, bf16[4,47,64,128]{3,2,1,0:T(8,128)(2,1)S(1)} %bitcast.24), custom_call_target="tpu_custom_call" | custom-call | tf_op jit(solution)/shard_map/pick/pallas_call | solution.py:194
  51.5 7.3 %collective-permute-done.10.refs_10_ = bf16[4,256,128]{2,1,0:T(8,128)(2,1)S(1)} collective-permute-done((bf16[4,256,128]{2,1,0:T(8,128)(2,1)S(1)}, bf16[4,256,128]{2,1,0:T(8,128)(2,1)S(1)}, u32[]{:S(2)}, u32[]{:S(2)}) %collective-permute-start.10) | collective-permute-done | bytes 262176 | tf_op jit(solution)/shard_map/ppermute | solution.py:205
  58.8 1.2 collective-permute-start.12
  60.0 0.3 collective-permute-start.13
  60.3 2.3 %collective-permute-start.14 = (bf16[4,256,128]{2,1,0:T(8,128)(2,1)S(1)}, bf16[4,256,128]{2,1,0:T(8,128)(2,1)S(1)}, u32[]{:S(2)}, u32[]{:S(2)}) collective-permute-start(bf16[4,256,128]{2,1,0:T(8,128)(2,1)S(1)} %get-tuple-element.47), channel_id=1, source_target_pairs={{0,16},{8,24},{16,0},{24,8},{1,17},{9,25},{17,1},{25,9},{2,18},{10... | collective-permute-start | bytes 786440 | tf_op jit(solution)/shard_map/ppermute | solution.py:205
  62.7 1.2 collective-permute-start.15
  63.8 3.1 %cycle.3 = (bf16[2,128,128]{2,1,0:T(8,128)(2,1)S(1)}, bf16[2,128,128]{2,1,0:T(8,128)(2,1)S(1)}, bf16[2,128,128]{2,1,0:T(8,128)(2,1)S(1)}, bf16[2,128,128]{2,1,0:T(8,128)(2,1)S(1)}) custom-call(s32[4]{0:T(128)S(1)} %copy-done.4, bf16[12,256,128]{2,1,0:T(8,128)(2,1)S(1)} %left.1.refs_1_, bf16[12,256,128]{2,1,0:T(8,128)(2,1)S(1)} %collective-permute-done.refs_2_, ...), custom_call_target="tpu_custom_call" | custom-call | tf_op jit(solution)/shard_map/cycle/pallas_call | solution.py:227
  66.9 7.3 %collective-permute-done.11.refs_11_ = bf16[4,256,128]{2,1,0:T(8,128)(2,1)S(1)} collective-permute-done((bf16[4,256,128]{2,1,0:T(8,128)(2,1)S(1)}, bf16[4,256,128]{2,1,0:T(8,128)(2,1)S(1)}, u32[]{:S(2)}, u32[]{:S(2)}) %collective-permute-start.11) | collective-permute-done | bytes 262176 | tf_op jit(solution)/shard_map/ppermute | solution.py:205
  74.3 5.9 %collective-permute-start.16 = (bf16[2,128,128]{2,1,0:T(8,128)(2,1)S(1)}, bf16[2,128,128]{2,1,0:T(8,128)(2,1)S(1)}, u32[]{:S(2)}, u32[]{:S(2)}) collective-permute-start(bf16[2,128,128]{2,1,0:T(8,128)(2,1)S(1)} %get-tuple-element.33.refs_0_), channel_id=1, source_target_pairs={{0,0},{1,1},{2,8},{3,9},{4,16},{5,17},{6,24},{7,25},{8,2},{9,3},{1... | collective-permute-start | bytes 196616 | tf_op jit(solution)/shard_map/ppermute | solution.py:247
  80.2 4.6 %collective-permute-start.17 = (bf16[2,128,128]{2,1,0:T(8,128)(2,1)S(1)}, bf16[2,128,128]{2,1,0:T(8,128)(2,1)S(1)}, u32[]{:S(2)}, u32[]{:S(2)}) collective-permute-start(bf16[2,128,128]{2,1,0:T(8,128)(2,1)S(1)} %get-tuple-element.34.refs_1_), channel_id=1, source_target_pairs={{0,4},{1,5},{2,6},{3,7},{4,0},{5,1},{6,2},{7,3},{8,12},{9,13},{10,... | collective-permute-start | bytes 196616 | tf_op jit(solution)/shard_map/ppermute | solution.py:246
  84.8 9.2 %collective-permute-start.19 = (bf16[2,128,128]{2,1,0:T(8,128)(2,1)S(1)}, bf16[2,128,128]{2,1,0:T(8,128)(2,1)S(1)}, u32[]{:S(2)}, u32[]{:S(2)}) collective-permute-start(bf16[2,128,128]{2,1,0:T(8,128)(2,1)S(1)} %get-tuple-element.35.refs_2_), channel_id=1, source_target_pairs={{0,1},{1,0},{2,9},{3,8},{4,17},{5,16},{6,25},{7,24},{8,3},{9,2},{1... | collective-permute-start | bytes 196616 | tf_op jit(solution)/shard_map/ppermute | solution.py:247
  94.0 3.1 %cycle.4 = (bf16[2,128,128]{2,1,0:T(8,128)(2,1)S(1)}, bf16[2,128,128]{2,1,0:T(8,128)(2,1)S(1)}, bf16[2,128,128]{2,1,0:T(8,128)(2,1)S(1)}, bf16[2,128,128]{2,1,0:T(8,128)(2,1)S(1)}) custom-call(s32[4]{0:T(128)S(1)} %copy-done.4, bf16[12,256,128]{2,1,0:T(8,128)(2,1)S(1)} %left.1.refs_1_, bf16[12,256,128]{2,1,0:T(8,128)(2,1)S(1)} %collective-permute-done.refs_2_, ...), custom_call_target="tpu_custom_call" | custom-call | tf_op jit(solution)/shard_map/cycle/pallas_call | solution.py:227
  97.2 7.9 %collective-permute-start.22 = (bf16[2,128,128]{2,1,0:T(8,128)(2,1)S(1)}, bf16[2,128,128]{2,1,0:T(8,128)(2,1)S(1)}, u32[]{:S(2)}, u32[]{:S(2)}) collective-permute-start(bf16[2,128,128]{2,1,0:T(8,128)(2,1)S(1)} %get-tuple-element.41.refs_4_), channel_id=1, source_target_pairs={{0,0},{1,1},{2,8},{3,9},{4,16},{5,17},{6,24},{7,25},{8,2},{9,3},{1... | collective-permute-start | bytes 196616 | tf_op jit(solution)/shard_map/ppermute | solution.py:247
  105.1 4.1 %collective-permute-start.23 = (bf16[2,128,128]{2,1,0:T(8,128)(2,1)S(1)}, bf16[2,128,128]{2,1,0:T(8,128)(2,1)S(1)}, u32[]{:S(2)}, u32[]{:S(2)}) collective-permute-start(bf16[2,128,128]{2,1,0:T(8,128)(2,1)S(1)} %get-tuple-element.42.refs_5_), channel_id=1, source_target_pairs={{0,4},{1,5},{2,6},{3,7},{4,0},{5,1},{6,2},{7,3},{8,12},{9,13},{10,... | collective-permute-start | bytes 196616 | tf_op jit(solution)/shard_map/ppermute | solution.py:246
  109.2 0.8 collective-permute-start.26
  110.0 3.1 %cycle.5 = (bf16[2,128,128]{2,1,0:T(8,128)(2,1)S(1)}, bf16[2,128,128]{2,1,0:T(8,128)(2,1)S(1)}, bf16[2,128,128]{2,1,0:T(8,128)(2,1)S(1)}, bf16[2,128,128]{2,1,0:T(8,128)(2,1)S(1)}) custom-call(s32[4]{0:T(128)S(1)} %copy-done.4, bf16[12,256,128]{2,1,0:T(8,128)(2,1)S(1)} %left.1.refs_1_, bf16[12,256,128]{2,1,0:T(8,128)(2,1)S(1)} %collective-permute-done.refs_2_, ...), custom_call_target="tpu_custom_call" | custom-call | tf_op jit(solution)/shard_map/cycle/pallas_call | solution.py:227
  113.1 4.8 %collective-permute-start.28 = (bf16[2,128,128]{2,1,0:T(8,128)(2,1)S(1)}, bf16[2,128,128]{2,1,0:T(8,128)(2,1)S(1)}, u32[]{:S(2)}, u32[]{:S(2)}) collective-permute-start(bf16[2,128,128]{2,1,0:T(8,128)(2,1)S(1)} %get-tuple-element.49.refs_8_), channel_id=1, source_target_pairs={{0,0},{1,1},{2,8},{3,9},{4,16},{5,17},{6,24},{7,25},{8,2},{9,3},{1... | collective-permute-start | bytes 196616 | tf_op jit(solution)/shard_map/ppermute | solution.py:247
  117.9 2.6 %collective-permute-start.29 = (bf16[2,128,128]{2,1,0:T(8,128)(2,1)S(1)}, bf16[2,128,128]{2,1,0:T(8,128)(2,1)S(1)}, u32[]{:S(2)}, u32[]{:S(2)}) collective-permute-start(bf16[2,128,128]{2,1,0:T(8,128)(2,1)S(1)} %get-tuple-element.50.refs_9_), channel_id=1, source_target_pairs={{0,4},{1,5},{2,6},{3,7},{4,0},{5,1},{6,2},{7,3},{8,12},{9,13},{10,... | collective-permute-start | bytes 196616 | tf_op jit(solution)/shard_map/ppermute | solution.py:246
  120.5 2.3 %collective-permute-start.32 = (bf16[2,128,128]{2,1,0:T(8,128)(2,1)S(1)}, bf16[2,128,128]{2,1,0:T(8,128)(2,1)S(1)}, u32[]{:S(2)}, u32[]{:S(2)}) collective-permute-start(bf16[2,128,128]{2,1,0:T(8,128)(2,1)S(1)} %get-tuple-element.52.refs_11_), channel_id=1, source_target_pairs={{0,4},{1,5},{2,6},{3,7},{4,0},{5,1},{6,2},{7,3},{8,12},{9,13},{10,... | collective-permute-start | bytes 196616 | tf_op jit(solution)/shard_map/ppermute | solution.py:246
  122.8 1.2 collective-permute-start.18
  124.0 3.0 %collective-permute-start.21 = (bf16[2,128,128]{2,1,0:T(8,128)(2,1)S(1)}, bf16[2,128,128]{2,1,0:T(8,128)(2,1)S(1)}, u32[]{:S(2)}, u32[]{:S(2)}) collective-permute-start(bf16[2,128,128]{2,1,0:T(8,128)(2,1)S(1)} %collective-permute-done.20), channel_id=1, source_target_pairs={{4,1},{5,0},{6,9},{7,8},{0,17},{1,16},{2,25},{3,24},{12,3},{13,2},... | collective-permute-start | bytes 196616 | tf_op jit(solution)/shard_map/ppermute | solution.py:247
  127.0 2.2 %collective-permute-start.24 = (bf16[2,128,128]{2,1,0:T(8,128)(2,1)S(1)}, bf16[2,128,128]{2,1,0:T(8,128)(2,1)S(1)}, u32[]{:S(2)}, u32[]{:S(2)}) collective-permute-start(bf16[2,128,128]{2,1,0:T(8,128)(2,1)S(1)} %collective-permute-done.23), channel_id=1, source_target_pairs={{4,0},{5,1},{6,8},{7,9},{0,16},{1,17},{2,24},{3,25},{12,2},{13,3},... | collective-permute-start | bytes 196616 | tf_op jit(solution)/shard_map/ppermute | solution.py:247
  129.1 1.3 collective-permute-start.27
  130.5 0.6 collective-permute-start.30
  131.1 6.4 %collective-permute-done.18.refs_13_ = bf16[2,128,128]{2,1,0:T(8,128)(2,1)S(1)} collective-permute-done((bf16[2,128,128]{2,1,0:T(8,128)(2,1)S(1)}, bf16[2,128,128]{2,1,0:T(8,128)(2,1)S(1)}, u32[]{:S(2)}, u32[]{:S(2)}) %collective-permute-start.18) | collective-permute-done | bytes 65568 | tf_op jit(solution)/shard_map/ppermute | solution.py:247
  137.5 2.8 %collective-permute-done.21.refs_15_ = bf16[2,128,128]{2,1,0:T(8,128)(2,1)S(1)} collective-permute-done((bf16[2,128,128]{2,1,0:T(8,128)(2,1)S(1)}, bf16[2,128,128]{2,1,0:T(8,128)(2,1)S(1)}, u32[]{:S(2)}, u32[]{:S(2)}) %collective-permute-start.21) | collective-permute-done | bytes 65568 | tf_op jit(solution)/shard_map/ppermute | solution.py:247
  140.3 1.4 collective-permute-done.24.refs_17_
  141.7 1.4 collective-permute-done.27.refs_19_
  143.1 2.1 %collective-permute-done.30.refs_21_ = bf16[2,128,128]{2,1,0:T(8,128)(2,1)S(1)} collective-permute-done((bf16[2,128,128]{2,1,0:T(8,128)(2,1)S(1)}, bf16[2,128,128]{2,1,0:T(8,128)(2,1)S(1)}, u32[]{:S(2)}, u32[]{:S(2)}) %collective-permute-start.30) | collective-permute-done | bytes 65568 | tf_op jit(solution)/shard_map/ppermute | solution.py:247
  145.2 2.1 %collective-permute-done.33.refs_23_ = bf16[2,128,128]{2,1,0:T(8,128)(2,1)S(1)} collective-permute-done((bf16[2,128,128]{2,1,0:T(8,128)(2,1)S(1)}, bf16[2,128,128]{2,1,0:T(8,128)(2,1)S(1)}, u32[]{:S(2)}, u32[]{:S(2)}) %collective-permute-start.33) | collective-permute-done | bytes 65568 | tf_op jit(solution)/shard_map/ppermute | solution.py:247
  147.3 6.4 %final.1 = f32[4,12,64,128]{3,2,1,0:T(8,128)} custom-call(s32[4,2,12]{2,1,0:T(2,128)S(1)} %bitcast.29, s32[4]{0:T(128)S(1)} %copy-done.4, bf16[2,128,128]{2,1,0:T(8,128)(2,1)S(1)} %get-tuple-element.33.refs_0_, bf16[2,128,128]{2,1,0:T(8,128)(2,1)S(1)} %get-tuple-element.34.refs_1_, bf16[2,128,128]{2,1,0:T(8,128)(2,1)S(1)} %get-tuple-element.35.refs_2_, ...), custom_call_target="tpu_custom_call" | custom-call | tf_op jit(solution)/shard_map/final/pallas_call | solution.py:250
  (42 shorter events, 0.5 us)
Async XLA Ops:
  0.0 1.1 copy-start.1
  2.3 20.1 %collective-permute-start.1 = (bf16[12,256,128]{2,1,0:T(8,128)(2,1)S(1)}, bf16[12,256,128]{2,1,0:T(8,128)(2,1)S(1)}, u32[]{:S(2)}, u32[]{:S(2)}) collective-permute-start(bf16[12,256,128]{2,1,0:T(8,128)(2,1)S(1)} %left.1.refs_1_), channel_id=1, source_target_pairs={{0,2},{1,3},{2,0},{3,1},{4,6},{5,7},{6,4},{7,5},{8,10},{9,11},{10,... | collective-permute-start | bytes 2359304 | tf_op jit(solution)/shard_map/ppermute | solution.py:222
  2.4 21.1 %collective-permute-start.3 = (bf16[12,256,128]{2,1,0:T(8,128)(2,1)S(1)}, bf16[12,256,128]{2,1,0:T(8,128)(2,1)S(1)}, u32[]{:S(2)}, u32[]{:S(2)}) collective-permute-start(bf16[12,256,128]{2,1,0:T(8,128)(2,1)S(1)} %left.1.refs_1_), channel_id=1, source_target_pairs={{0,4},{1,5},{2,6},{3,7},{4,0},{5,1},{6,2},{7,3},{8,12},{9,13},{10,... | collective-permute-start | bytes 2359304 | tf_op jit(solution)/shard_map/ppermute | solution.py:222
  3.9 34.7 %collective-permute-start.5 = (bf16[12,256,128]{2,1,0:T(8,128)(2,1)S(1)}, bf16[12,256,128]{2,1,0:T(8,128)(2,1)S(1)}, u32[]{:S(2)}, u32[]{:S(2)}) collective-permute-start(bf16[12,256,128]{2,1,0:T(8,128)(2,1)S(1)} %left.1.refs_1_), channel_id=1, source_target_pairs={{0,6},{1,7},{2,4},{3,5},{4,2},{5,3},{6,0},{7,1},{8,14},{9,15},{10,... | collective-permute-start | bytes 2359304 | tf_op jit(solution)/shard_map/ppermute | solution.py:222
  5.0 1.9 %copy-start = (bf16[4,2,47,4096]{3,1,2,0:T(2,128)(2,1)S(1)}, bf16[4,2,47,4096]{3,1,2,0:T(2,128)(2,1)}, u32[]{:S(2)}) copy-start(bf16[4,2,47,4096]{3,1,2,0:T(2,128)(2,1)} %param.5) | copy-start | bytes 9240580
  6.9 0.7 copy-start.2
  9.8 8.4 %collective-permute-start.7 = (bf16[4,256,128]{2,1,0:T(8,128)(2,1)S(1)}, bf16[4,256,128]{2,1,0:T(8,128)(2,1)S(1)}, u32[]{:S(2)}, u32[]{:S(2)}) collective-permute-start(bf16[4,256,128]{2,1,0:T(8,128)(2,1)S(1)} %get-tuple-element.30), channel_id=1, source_target_pairs={{0,8},{8,16},{16,24},{24,0},{1,9},{9,17},{17,25},{25,1},{2,10},{10... | collective-permute-start | bytes 786440 | tf_op jit(solution)/shard_map/ppermute | solution.py:205
  11.1 29.0 %collective-permute-start.8 = (bf16[4,256,128]{2,1,0:T(8,128)(2,1)S(1)}, bf16[4,256,128]{2,1,0:T(8,128)(2,1)S(1)}, u32[]{:S(2)}, u32[]{:S(2)}) collective-permute-start(bf16[4,256,128]{2,1,0:T(8,128)(2,1)S(1)} %get-tuple-element.31), channel_id=1, source_target_pairs={{0,16},{8,24},{16,0},{24,8},{1,17},{9,25},{17,1},{25,9},{2,18},{10... | collective-permute-start | bytes 786440 | tf_op jit(solution)/shard_map/ppermute | solution.py:205
  18.2 40.6 %collective-permute-start = (bf16[12,256,128]{2,1,0:T(8,128)(2,1)S(1)}, bf16[12,256,128]{2,1,0:T(8,128)(2,1)S(1)}, u32[]{:S(2)}, u32[]{:S(2)}) collective-permute-start(bf16[12,256,128]{2,1,0:T(8,128)(2,1)S(1)} %left.1.refs_1_), channel_id=1, source_target_pairs={{0,1},{1,0},{2,3},{3,2},{4,5},{5,4},{6,7},{7,6},{8,9},{9,8},{10,11... | collective-permute-start | bytes 2359304 | tf_op jit(solution)/shard_map/ppermute | solution.py:220
  22.4 37.6 %collective-permute-start.2 = (bf16[12,256,128]{2,1,0:T(8,128)(2,1)S(1)}, bf16[12,256,128]{2,1,0:T(8,128)(2,1)S(1)}, u32[]{:S(2)}, u32[]{:S(2)}) collective-permute-start(bf16[12,256,128]{2,1,0:T(8,128)(2,1)S(1)} %collective-permute-done.1.refs_3_), channel_id=1, source_target_pairs={{0,1},{1,0},{2,3},{3,2},{4,5},{5,4},{6,7},{7,6},{8,9},{9,8},{10,11... | collective-permute-start | bytes 2359304 | tf_op jit(solution)/shard_map/ppermute | solution.py:220
  23.5 36.9 %collective-permute-start.4 = (bf16[12,256,128]{2,1,0:T(8,128)(2,1)S(1)}, bf16[12,256,128]{2,1,0:T(8,128)(2,1)S(1)}, u32[]{:S(2)}, u32[]{:S(2)}) collective-permute-start(bf16[12,256,128]{2,1,0:T(8,128)(2,1)S(1)} %collective-permute-done.3.refs_5_), channel_id=1, source_target_pairs={{0,1},{1,0},{2,3},{3,2},{4,5},{5,4},{6,7},{7,6},{8,9},{9,8},{10,11... | collective-permute-start | bytes 2359304 | tf_op jit(solution)/shard_map/ppermute | solution.py:220
  38.6 12.9 %copy-start.5 = (bf16[12,256,128]{2,1,0:T(8,128)(2,1)}, bf16[12,256,128]{2,1,0:T(8,128)(2,1)S(1)}, u32[]{:S(2)}) copy-start(bf16[12,256,128]{2,1,0:T(8,128)(2,1)S(1)} %collective-permute-done.5.refs_7_) | copy-start | bytes 2359300
  38.6 24.1 %collective-permute-start.6 = (bf16[12,256,128]{2,1,0:T(8,128)(2,1)S(1)}, bf16[12,256,128]{2,1,0:T(8,128)(2,1)S(1)}, u32[]{:S(2)}, u32[]{:S(2)}) collective-permute-start(bf16[12,256,128]{2,1,0:T(8,128)(2,1)S(1)} %collective-permute-done.5.refs_7_), channel_id=1, source_target_pairs={{0,1},{1,0},{2,3},{3,2},{4,5},{5,4},{6,7},{7,6},{8,9},{9,8},{10,11... | collective-permute-start | bytes 2359304 | tf_op jit(solution)/shard_map/ppermute | solution.py:220
  40.1 23.7 %copy-start.4 = (s32[4]{0:T(128)S(1)}, s32[4]{0:T(128)}, u32[]{:S(2)}) copy-start(s32[4]{0:T(128)} %count_ref.1) | copy-start | bytes 52
  40.1 8.9 %collective-permute-start.9 = (bf16[4,256,128]{2,1,0:T(8,128)(2,1)S(1)}, bf16[4,256,128]{2,1,0:T(8,128)(2,1)S(1)}, u32[]{:S(2)}, u32[]{:S(2)}) collective-permute-start(bf16[4,256,128]{2,1,0:T(8,128)(2,1)S(1)} %get-tuple-element.32), channel_id=1, source_target_pairs={{0,24},{8,0},{16,8},{24,16},{1,25},{9,1},{17,9},{25,17},{2,26},{10... | collective-permute-start | bytes 786440 | tf_op jit(solution)/shard_map/ppermute | solution.py:205
  49.1 9.8 %collective-permute-start.10 = (bf16[4,256,128]{2,1,0:T(8,128)(2,1)S(1)}, bf16[4,256,128]{2,1,0:T(8,128)(2,1)S(1)}, u32[]{:S(2)}, u32[]{:S(2)}) collective-permute-start(bf16[4,256,128]{2,1,0:T(8,128)(2,1)S(1)} %get-tuple-element.38), channel_id=1, source_target_pairs={{0,8},{8,16},{16,24},{24,0},{1,9},{9,17},{17,25},{25,1},{2,10},{10... | collective-permute-start | bytes 786440 | tf_op jit(solution)/shard_map/ppermute | solution.py:205
  58.8 15.5 %collective-permute-start.11 = (bf16[4,256,128]{2,1,0:T(8,128)(2,1)S(1)}, bf16[4,256,128]{2,1,0:T(8,128)(2,1)S(1)}, u32[]{:S(2)}, u32[]{:S(2)}) collective-permute-start(bf16[4,256,128]{2,1,0:T(8,128)(2,1)S(1)} %get-tuple-element.39), channel_id=1, source_target_pairs={{0,16},{8,24},{16,0},{24,8},{1,17},{9,25},{17,1},{25,9},{2,18},{10... | collective-permute-start | bytes 786440 | tf_op jit(solution)/shard_map/ppermute | solution.py:205
  58.8 21.4 %collective-permute-start.12 = (bf16[4,256,128]{2,1,0:T(8,128)(2,1)S(1)}, bf16[4,256,128]{2,1,0:T(8,128)(2,1)S(1)}, u32[]{:S(2)}, u32[]{:S(2)}) collective-permute-start(bf16[4,256,128]{2,1,0:T(8,128)(2,1)S(1)} %get-tuple-element.40), channel_id=1, source_target_pairs={{0,24},{8,0},{16,8},{24,16},{1,25},{9,1},{17,9},{25,17},{2,26},{10... | collective-permute-start | bytes 786440 | tf_op jit(solution)/shard_map/ppermute | solution.py:205
  60.0 24.8 %collective-permute-start.13 = (bf16[4,256,128]{2,1,0:T(8,128)(2,1)S(1)}, bf16[4,256,128]{2,1,0:T(8,128)(2,1)S(1)}, u32[]{:S(2)}, u32[]{:S(2)}) collective-permute-start(bf16[4,256,128]{2,1,0:T(8,128)(2,1)S(1)} %get-tuple-element.46), channel_id=1, source_target_pairs={{0,8},{8,16},{16,24},{24,0},{1,9},{9,17},{17,25},{25,1},{2,10},{10... | collective-permute-start | bytes 786440 | tf_op jit(solution)/shard_map/ppermute | solution.py:205
  60.3 36.7 %collective-permute-start.14 = (bf16[4,256,128]{2,1,0:T(8,128)(2,1)S(1)}, bf16[4,256,128]{2,1,0:T(8,128)(2,1)S(1)}, u32[]{:S(2)}, u32[]{:S(2)}) collective-permute-start(bf16[4,256,128]{2,1,0:T(8,128)(2,1)S(1)} %get-tuple-element.47), channel_id=1, source_target_pairs={{0,16},{8,24},{16,0},{24,8},{1,17},{9,25},{17,1},{25,9},{2,18},{10... | collective-permute-start | bytes 786440 | tf_op jit(solution)/shard_map/ppermute | solution.py:205
  62.7 1.2 copy-start.6
  62.7 34.5 %collective-permute-start.15 = (bf16[4,256,128]{2,1,0:T(8,128)(2,1)S(1)}, bf16[4,256,128]{2,1,0:T(8,128)(2,1)S(1)}, u32[]{:S(2)}, u32[]{:S(2)}) collective-permute-start(bf16[4,256,128]{2,1,0:T(8,128)(2,1)S(1)} %get-tuple-element.48), channel_id=1, source_target_pairs={{0,24},{8,0},{16,8},{24,16},{1,25},{9,1},{17,9},{25,17},{2,26},{10... | collective-permute-start | bytes 786440 | tf_op jit(solution)/shard_map/ppermute | solution.py:205
  74.3 30.8 %collective-permute-start.16 = (bf16[2,128,128]{2,1,0:T(8,128)(2,1)S(1)}, bf16[2,128,128]{2,1,0:T(8,128)(2,1)S(1)}, u32[]{:S(2)}, u32[]{:S(2)}) collective-permute-start(bf16[2,128,128]{2,1,0:T(8,128)(2,1)S(1)} %get-tuple-element.33.refs_0_), channel_id=1, source_target_pairs={{0,0},{1,1},{2,8},{3,9},{4,16},{5,17},{6,24},{7,25},{8,2},{9,3},{1... | collective-permute-start | bytes 196616 | tf_op jit(solution)/shard_map/ppermute | solution.py:247
  80.2 29.0 %collective-permute-start.17 = (bf16[2,128,128]{2,1,0:T(8,128)(2,1)S(1)}, bf16[2,128,128]{2,1,0:T(8,128)(2,1)S(1)}, u32[]{:S(2)}, u32[]{:S(2)}) collective-permute-start(bf16[2,128,128]{2,1,0:T(8,128)(2,1)S(1)} %get-tuple-element.34.refs_1_), channel_id=1, source_target_pairs={{0,4},{1,5},{2,6},{3,7},{4,0},{5,1},{6,2},{7,3},{8,12},{9,13},{10,... | collective-permute-start | bytes 196616 | tf_op jit(solution)/shard_map/ppermute | solution.py:246
  84.8 24.4 %collective-permute-start.19 = (bf16[2,128,128]{2,1,0:T(8,128)(2,1)S(1)}, bf16[2,128,128]{2,1,0:T(8,128)(2,1)S(1)}, u32[]{:S(2)}, u32[]{:S(2)}) collective-permute-start(bf16[2,128,128]{2,1,0:T(8,128)(2,1)S(1)} %get-tuple-element.35.refs_2_), channel_id=1, source_target_pairs={{0,1},{1,0},{2,9},{3,8},{4,17},{5,16},{6,25},{7,24},{8,3},{9,2},{1... | collective-permute-start | bytes 196616 | tf_op jit(solution)/shard_map/ppermute | solution.py:247
  97.1 16.0 %collective-permute-start.20 = (bf16[2,128,128]{2,1,0:T(8,128)(2,1)S(1)}, bf16[2,128,128]{2,1,0:T(8,128)(2,1)S(1)}, u32[]{:S(2)}, u32[]{:S(2)}) collective-permute-start(bf16[2,128,128]{2,1,0:T(8,128)(2,1)S(1)} %get-tuple-element.36.refs_3_), channel_id=1, source_target_pairs={{0,4},{1,5},{2,6},{3,7},{4,0},{5,1},{6,2},{7,3},{8,12},{9,13},{10,... | collective-permute-start | bytes 196616 | tf_op jit(solution)/shard_map/ppermute | solution.py:246
  97.2 20.7 %collective-permute-start.22 = (bf16[2,128,128]{2,1,0:T(8,128)(2,1)S(1)}, bf16[2,128,128]{2,1,0:T(8,128)(2,1)S(1)}, u32[]{:S(2)}, u32[]{:S(2)}) collective-permute-start(bf16[2,128,128]{2,1,0:T(8,128)(2,1)S(1)} %get-tuple-element.41.refs_4_), channel_id=1, source_target_pairs={{0,0},{1,1},{2,8},{3,9},{4,16},{5,17},{6,24},{7,25},{8,2},{9,3},{1... | collective-permute-start | bytes 196616 | tf_op jit(solution)/shard_map/ppermute | solution.py:247
  105.1 15.4 %collective-permute-start.23 = (bf16[2,128,128]{2,1,0:T(8,128)(2,1)S(1)}, bf16[2,128,128]{2,1,0:T(8,128)(2,1)S(1)}, u32[]{:S(2)}, u32[]{:S(2)}) collective-permute-start(bf16[2,128,128]{2,1,0:T(8,128)(2,1)S(1)} %get-tuple-element.42.refs_5_), channel_id=1, source_target_pairs={{0,4},{1,5},{2,6},{3,7},{4,0},{5,1},{6,2},{7,3},{8,12},{9,13},{10,... | collective-permute-start | bytes 196616 | tf_op jit(solution)/shard_map/ppermute | solution.py:246
  109.2 11.3 %collective-permute-start.25 = (bf16[2,128,128]{2,1,0:T(8,128)(2,1)S(1)}, bf16[2,128,128]{2,1,0:T(8,128)(2,1)S(1)}, u32[]{:S(2)}, u32[]{:S(2)}) collective-permute-start(bf16[2,128,128]{2,1,0:T(8,128)(2,1)S(1)} %get-tuple-element.43.refs_6_), channel_id=1, source_target_pairs={{0,1},{1,0},{2,9},{3,8},{4,17},{5,16},{6,25},{7,24},{8,3},{9,2},{1... | collective-permute-start | bytes 196616 | tf_op jit(solution)/shard_map/ppermute | solution.py:247
  109.2 13.6 %collective-permute-start.26 = (bf16[2,128,128]{2,1,0:T(8,128)(2,1)S(1)}, bf16[2,128,128]{2,1,0:T(8,128)(2,1)S(1)}, u32[]{:S(2)}, u32[]{:S(2)}) collective-permute-start(bf16[2,128,128]{2,1,0:T(8,128)(2,1)S(1)} %get-tuple-element.44.refs_7_), channel_id=1, source_target_pairs={{0,4},{1,5},{2,6},{3,7},{4,0},{5,1},{6,2},{7,3},{8,12},{9,13},{10,... | collective-permute-start | bytes 196616 | tf_op jit(solution)/shard_map/ppermute | solution.py:246
  110.0 37.3 %copy-start.3 = (s32[4,12,2]{1,2,0:T(2,128)S(1)}, s32[4,12,2]{1,2,0:T(2,128)}, u32[]{:S(2)}) copy-start(s32[4,12,2]{1,2,0:T(2,128)} %param.6) | copy-start | bytes 1156
  113.1 10.9 %collective-permute-start.28 = (bf16[2,128,128]{2,1,0:T(8,128)(2,1)S(1)}, bf16[2,128,128]{2,1,0:T(8,128)(2,1)S(1)}, u32[]{:S(2)}, u32[]{:S(2)}) collective-permute-start(bf16[2,128,128]{2,1,0:T(8,128)(2,1)S(1)} %get-tuple-element.49.refs_8_), channel_id=1, source_target_pairs={{0,0},{1,1},{2,8},{3,9},{4,16},{5,17},{6,24},{7,25},{8,2},{9,3},{1... | collective-permute-start | bytes 196616 | tf_op jit(solution)/shard_map/ppermute | solution.py:247
  117.9 9.1 %collective-permute-start.29 = (bf16[2,128,128]{2,1,0:T(8,128)(2,1)S(1)}, bf16[2,128,128]{2,1,0:T(8,128)(2,1)S(1)}, u32[]{:S(2)}, u32[]{:S(2)}) collective-permute-start(bf16[2,128,128]{2,1,0:T(8,128)(2,1)S(1)} %get-tuple-element.50.refs_9_), channel_id=1, source_target_pairs={{0,4},{1,5},{2,6},{3,7},{4,0},{5,1},{6,2},{7,3},{8,12},{9,13},{10,... | collective-permute-start | bytes 196616 | tf_op jit(solution)/shard_map/ppermute | solution.py:246
  120.4 8.7 %collective-permute-start.31 = (bf16[2,128,128]{2,1,0:T(8,128)(2,1)S(1)}, bf16[2,128,128]{2,1,0:T(8,128)(2,1)S(1)}, u32[]{:S(2)}, u32[]{:S(2)}) collective-permute-start(bf16[2,128,128]{2,1,0:T(8,128)(2,1)S(1)} %get-tuple-element.51.refs_10_), channel_id=1, source_target_pairs={{0,1},{1,0},{2,9},{3,8},{4,17},{5,16},{6,25},{7,24},{8,3},{9,2},{1... | collective-permute-start | bytes 196616 | tf_op jit(solution)/shard_map/ppermute | solution.py:247
  120.5 10.0 %collective-permute-start.32 = (bf16[2,128,128]{2,1,0:T(8,128)(2,1)S(1)}, bf16[2,128,128]{2,1,0:T(8,128)(2,1)S(1)}, u32[]{:S(2)}, u32[]{:S(2)}) collective-permute-start(bf16[2,128,128]{2,1,0:T(8,128)(2,1)S(1)} %get-tuple-element.52.refs_11_), channel_id=1, source_target_pairs={{0,4},{1,5},{2,6},{3,7},{4,0},{5,1},{6,2},{7,3},{8,12},{9,13},{10,... | collective-permute-start | bytes 196616 | tf_op jit(solution)/shard_map/ppermute | solution.py:246
  122.8 14.7 %collective-permute-start.18 = (bf16[2,128,128]{2,1,0:T(8,128)(2,1)S(1)}, bf16[2,128,128]{2,1,0:T(8,128)(2,1)S(1)}, u32[]{:S(2)}, u32[]{:S(2)}) collective-permute-start(bf16[2,128,128]{2,1,0:T(8,128)(2,1)S(1)} %collective-permute-done.17), channel_id=1, source_target_pairs={{4,0},{5,1},{6,8},{7,9},{0,16},{1,17},{2,24},{3,25},{12,2},{13,3},... | collective-permute-start | bytes 196616 | tf_op jit(solution)/shard_map/ppermute | solution.py:247
  124.0 16.3 %collective-permute-start.21 = (bf16[2,128,128]{2,1,0:T(8,128)(2,1)S(1)}, bf16[2,128,128]{2,1,0:T(8,128)(2,1)S(1)}, u32[]{:S(2)}, u32[]{:S(2)}) collective-permute-start(bf16[2,128,128]{2,1,0:T(8,128)(2,1)S(1)} %collective-permute-done.20), channel_id=1, source_target_pairs={{4,1},{5,0},{6,9},{7,8},{0,17},{1,16},{2,25},{3,24},{12,3},{13,2},... | collective-permute-start | bytes 196616 | tf_op jit(solution)/shard_map/ppermute | solution.py:247
  127.0 14.7 %collective-permute-start.24 = (bf16[2,128,128]{2,1,0:T(8,128)(2,1)S(1)}, bf16[2,128,128]{2,1,0:T(8,128)(2,1)S(1)}, u32[]{:S(2)}, u32[]{:S(2)}) collective-permute-start(bf16[2,128,128]{2,1,0:T(8,128)(2,1)S(1)} %collective-permute-done.23), channel_id=1, source_target_pairs={{4,0},{5,1},{6,8},{7,9},{0,16},{1,17},{2,24},{3,25},{12,2},{13,3},... | collective-permute-start | bytes 196616 | tf_op jit(solution)/shard_map/ppermute | solution.py:247
  129.1 13.9 %collective-permute-start.27 = (bf16[2,128,128]{2,1,0:T(8,128)(2,1)S(1)}, bf16[2,128,128]{2,1,0:T(8,128)(2,1)S(1)}, u32[]{:S(2)}, u32[]{:S(2)}) collective-permute-start(bf16[2,128,128]{2,1,0:T(8,128)(2,1)S(1)} %collective-permute-done.26), channel_id=1, source_target_pairs={{4,1},{5,0},{6,9},{7,8},{0,17},{1,16},{2,25},{3,24},{12,3},{13,2},... | collective-permute-start | bytes 196616 | tf_op jit(solution)/shard_map/ppermute | solution.py:247
  130.5 14.7 %collective-permute-start.30 = (bf16[2,128,128]{2,1,0:T(8,128)(2,1)S(1)}, bf16[2,128,128]{2,1,0:T(8,128)(2,1)S(1)}, u32[]{:S(2)}, u32[]{:S(2)}) collective-permute-start(bf16[2,128,128]{2,1,0:T(8,128)(2,1)S(1)} %collective-permute-done.29), channel_id=1, source_target_pairs={{4,0},{5,1},{6,8},{7,9},{0,16},{1,17},{2,24},{3,25},{12,2},{13,3},... | collective-permute-start | bytes 196616 | tf_op jit(solution)/shard_map/ppermute | solution.py:247
  137.5 9.8 %collective-permute-start.33 = (bf16[2,128,128]{2,1,0:T(8,128)(2,1)S(1)}, bf16[2,128,128]{2,1,0:T(8,128)(2,1)S(1)}, u32[]{:S(2)}, u32[]{:S(2)}) collective-permute-start(bf16[2,128,128]{2,1,0:T(8,128)(2,1)S(1)} %collective-permute-done.32), channel_id=1, source_target_pairs={{4,1},{5,0},{6,9},{7,8},{0,17},{1,16},{2,25},{3,24},{12,3},{13,2},... | collective-permute-start | bytes 196616 | tf_op jit(solution)/shard_map/ppermute | solution.py:247
where the time goes:
time: 154 us
  starting transfers between devices  87.3 us (57%)
  waiting for transfers between devices  39.1 us (25%)
  Pallas kernels  23.4 us (15%)
  local copies, waits for them, and re-layouts  3.7 us (2%)
    ppermute x12, starting transfers between devices, on_device(): lax.ppermute(block, ('row', 'col'), mirror_pairs(rows, cols, step, hop))  36.1 us
    ppermute x9, waiting for transfers between devices, on_device(): got.append(lax.ppermute(picked[shift], 'row', pairs))  22.8 us
    ppermute x4, starting transfers between devices, on_device(): lax.ppermute(lefts[e - 1], 'col', [(c, c ^ 1) for c in range(cols)])  21.9 us
    ppermute x12, waiting for transfers between devices, on_device(): lax.ppermute(block, ('row', 'col'), mirror_pairs(rows, cols, step, hop))  16.2 us
    ppermute x6, starting transfers between devices, on_device(): lax.ppermute(block, 'col', [(c, c ^ cols // 2) for c in range(cols)])  14.4 us
    ppermute x9, starting transfers between devices, on_device(): got.append(lax.ppermute(picked[shift], 'row', pairs))  12.2 us
    pallas_call x3, Pallas kernels, on_device(): pl.pallas_call(functools.partial(cycle_kernel, rows, cols, ratio, base, s...  9.22 us
    pallas_call x3, Pallas kernels, on_device(): pl.pallas_call(functools.partial(pick_kernel, base, size, rows), out_shap...  6.63 us
  transfers between devices with their start and end apart: 34, of which 11 were waited for; matrix products, arithmetic and copies ran while one was open for 0% of the time, Pallas kernels for 10%

commit v1 on v0

v1 whole, which is shorter than its diff:
```python
import functools

import jax
import jax.numpy as jnp
from jax import lax
from jax.experimental import pallas as pl
from jax.experimental.pallas import tpu as pltpu
from jax.sharding import PartitionSpec as P


TILE = 64
LANES = 128
SPLIT = (5, 5, 2)
VMEM = pl.BlockSpec(memory_space=pltpu.VMEM)
SMEM = pl.BlockSpec(memory_space=pltpu.SMEM)
HBM = pl.BlockSpec(memory_space=pltpu.HBM)
PARAMS = pltpu.CompilerParams(vmem_limit_bytes=16 * 1024 * 1024)


def rows_of(x):
    outer, pair, slots, square = x.shape
    x = jnp.transpose(x, (0, 2, 1, 3)).reshape(outer, slots, pair, square // LANES, LANES)
    return jnp.transpose(x, (0, 1, 3, 2, 4)).reshape(outer, slots, square // LANES * pair, LANES)


def tiles_of(x, pair):
    outer, slots, rows, lanes = x.shape
    x = x.reshape(outer, slots, rows // pair, pair, lanes)
    x = jnp.transpose(x, (0, 1, 3, 2, 4)).reshape(outer, slots, pair, rows // pair * lanes)
    return jnp.transpose(x, (0, 2, 1, 3))


def swap(x):
    count = x.shape[0]
    x = x.reshape(count // 8, 8, LANES)
    z = pltpu.roll(x, TILE, 2)
    after = pltpu.roll(z, 7, 1)
    before = pltpu.roll(z, 1, 1)
    odd = lax.broadcasted_iota(jnp.int32, x.shape, 1) % 2
    half = lax.broadcasted_iota(jnp.int32, x.shape, 2) // TILE
    out = jnp.where(odd == half, x, jnp.where(odd == 0, after, before))
    return out.reshape(count, LANES)


def pick_kernel(base, size, rows, list_ref, w_ref, *outs):
    my_row = lax.axis_index("row")
    depth = w_ref.shape[0]
    for shift in range(rows):
        row = lax.rem(my_row + shift, rows)
        out = outs[shift]

        def one(s, _, out=out, row=row):
            tile = list_ref[row, 1, base + s]
            x = w_ref[:, tile].reshape(depth * TILE, LANES).astype(jnp.float32)
            out[s] = swap(x).astype(jnp.bfloat16)
            return 0

        lax.fori_loop(0, size, one, 0)


def left_kernel(a_ref, out):
    depth, slots = a_ref.shape[:2]

    def one(s, _):
        x = a_ref[:, s].reshape(depth * TILE, LANES).astype(jnp.float32)
        out[s] = swap(x).astype(jnp.bfloat16)
        return 0

    lax.fori_loop(0, slots, one, 0)


def cycle_kernel(rows, cols, ratio, base, size, *refs):
    count_ref = refs[0]
    lefts = refs[1 : 1 + cols]
    rights = refs[1 + cols : 1 + cols + rows]
    outs = refs[1 + cols + rows : -2]
    held, total = refs[-2:]
    my_row = lax.axis_index("row")
    my_col = lax.axis_index("col")
    core = lax.rem(my_col, ratio)
    half = total.shape[0] // ratio
    for d, right in enumerate(rights):
        row = lax.rem(my_row - d + rows, rows)
        for p in range(ratio):
            held[row, p] = right[:, pl.ds(pl.multiple_of((p ^ core) * half, half), half), :]
    my_count = count_ref[my_row]

    def one(s, _):
        acc = None
        for chip in range(rows):
            row = (my_col // ratio) ^ chip
            left = jnp.concatenate([lefts[chip * ratio + p][base + s] for p in range(ratio)], axis=1)
            right = jnp.concatenate([held[row, p, s] for p in range(ratio)], axis=0)
            part = jnp.dot(left, right, preferred_element_type=jnp.float32)
            acc = part if acc is None else acc + part
        live = (base + s < my_count).astype(jnp.float32)
        total[...] = acc * live
        for step in range(ratio):
            part = core ^ step
            outs[step][s] = total[pl.ds(pl.multiple_of(part * half, half), half), :].astype(jnp.bfloat16)
        return 0

    lax.fori_loop(0, size, one, 0)


def collect(refs, held, sizes, ratio, core):
    base = 0
    for chunk, size in enumerate(sizes):
        for step in range(ratio):
            held[core ^ step, base : base + size] = refs[chunk * ratio + step][...]
        base += size


def summed(held_own, s, held_their, t, ratio):
    own = jnp.concatenate([held_own[p, s] for p in range(ratio)], axis=0).astype(jnp.float32)
    if t is None:
        return own
    return own + jnp.concatenate([held_their[p, t].astype(jnp.float32).T for p in range(ratio)], axis=0)


def final_kernel(ratio, sizes, list_ref, count_ref, *refs):
    slots = sum(sizes)
    early = slots - sizes[-1]
    owns = refs[: len(sizes) * ratio]
    theirs = refs[len(sizes) * ratio : -3]
    out_ref, held_own, held_their = refs[-3:]
    my_row = lax.axis_index("row")
    my_col = lax.axis_index("col")
    core = lax.rem(my_col, ratio)
    partner = my_col // ratio
    collect(owns, held_own, sizes, ratio, core)
    collect(theirs, held_their, sizes[:-1], ratio, core)
    my_count = count_ref[my_row]
    depth = out_ref.shape[0]

    def one(s, _):
        first = list_ref[my_row, 0, s]
        second = list_ref[my_row, 1, s]
        found = jnp.int32(-1)
        for t in range(early):
            hit = (list_ref[partner, 0, t] == second) & (list_ref[partner, 1, t] == first)
            found = jnp.where(hit, t, found)
        use = (s < my_count) & (found >= 0)

        @pl.when(use)
        def _():
            x = summed(held_own, s, held_their, jnp.maximum(found, 0), ratio)
            out_ref[:, s] = swap(x).reshape(depth, TILE, LANES)

        @pl.when(jnp.logical_not(use))
        def _():
            x = summed(held_own, s, None, None, ratio)
            out_ref[:, s] = swap(x).reshape(depth, TILE, LANES)

        return 0

    lax.fori_loop(0, slots, one, 0)


def patch_kernel(ratio, sizes, list_ref, count_ref, *refs):
    slots = sum(sizes)
    early = slots - sizes[-1]
    owns = refs[: len(sizes) * ratio]
    theirs = refs[len(sizes) * ratio : -6]
    _, out_ref, held_own, held_their, built, sem = refs[-6:]
    my_row = lax.axis_index("row")
    my_col = lax.axis_index("col")
    core = lax.rem(my_col, ratio)
    partner = my_col // ratio
    collect(owns, held_own, sizes, ratio, core)
    collect(theirs, held_their, sizes[-1:], ratio, core)
    my_count = count_ref[my_row]
    depth = out_ref.shape[0]
    uses, copies = [], []
    for t in range(sizes[-1]):
        first = list_ref[partner, 0, early + t]
        second = list_ref[partner, 1, early + t]
        found = jnp.int32(-1)
        for s in range(slots):
            hit = (list_ref[my_row, 0, s] == second) & (list_ref[my_row, 1, s] == first)
            found = jnp.where(hit, s, found)
        uses.append((found < my_count) & (found >= 0))
        s = jnp.maximum(found, 0)
        copies.append(pltpu.make_async_copy(built.at[t], out_ref.at[:, s], sem.at[t]))

        @pl.when(uses[-1])
        def _(s=s, t=t):
            built[t] = swap(summed(held_own, s, held_their, t, ratio)).reshape(depth, TILE, LANES)
            copies[t].start()

    for use, copy in zip(uses, copies):
        pl.when(use)(copy.wait)


def mirror_pairs(rows, cols, step, hop):
    ratio = cols // rows
    pairs = []
    for row in range(rows):
        for col in range(cols):
            part = (col % ratio + step) % ratio
            held = col ^ (hop * (cols // 2))
            pairs.append((row * cols + held, (col // ratio) * cols + row * ratio + part))
    return pairs


def on_device(amplitudes, integrals, pair_lists, tile_counts):
    rows = lax.axis_size("row")
    cols = lax.axis_size("col")
    ratio = cols // rows
    occ_row, occ_col, slots, square = amplitudes.shape
    assert occ_col * TILE == LANES and occ_row == ratio * occ_col
    assert ratio == 2 and cols % 2 == 0 and cols & (cols - 1) == 0
    sizes = SPLIT if sum(SPLIT) == slots else (slots - 1, 1)
    tall = occ_row * TILE
    wide = occ_col * TILE
    lists = jnp.transpose(pair_lists, (0, 2, 1))
    bf16 = jnp.bfloat16

    table = rows_of(integrals)

    rights = []
    base = 0
    for size in sizes:
        picked = pl.pallas_call(
            functools.partial(pick_kernel, base, size, rows),
            out_shape=[jax.ShapeDtypeStruct((size, tall, wide), bf16)] * rows,
            in_specs=[SMEM, VMEM],
            out_specs=[VMEM] * rows,
            compiler_params=PARAMS,
            name="pick",
        )(lists, table)
        got = [picked[0]]
        for shift in range(1, rows):
            pairs = [(r, (r + shift) % rows) for r in range(rows)]
            got.append(lax.ppermute(picked[shift], "row", pairs))
        rights.append(got)
        base += size

    mine = pl.pallas_call(
        left_kernel,
        out_shape=jax.ShapeDtypeStruct((slots, tall, wide), bf16),
        in_specs=[VMEM],
        out_specs=VMEM,
        compiler_params=PARAMS,
        name="left",
    )(rows_of(amplitudes))
    lefts = [mine]
    for e in range(1, cols):
        if e % 2:
            lefts.append(lax.ppermute(lefts[e - 1], "col", [(c, c ^ 1) for c in range(cols)]))
        else:
            lefts.append(lax.ppermute(mine, "col", [(c, c ^ e) for c in range(cols)]))

    owns, theirs = [], []
    base = 0
    for chunk, size in enumerate(sizes):
        sent = pl.pallas_call(
            functools.partial(cycle_kernel, rows, cols, ratio, base, size),
            out_shape=[jax.ShapeDtypeStruct((size, tall // ratio, wide), bf16)] * ratio,
            in_specs=[SMEM] + [VMEM] * (cols + rows),
            out_specs=[VMEM] * ratio,
            scratch_shapes=[
                pltpu.VMEM((rows, ratio, size, tall // ratio, wide), bf16),
                pltpu.VMEM((tall, wide), jnp.float32),
            ],
            compiler_params=PARAMS,
            name="cycle",
        )(tile_counts, *lefts, *rights[chunk])
        owns += sent
        for step in range(ratio):
            block = sent[step]
            hop = step % 2
            if hop:
                block = lax.ppermute(block, "col", [(c, c ^ (cols // 2)) for c in range(cols)])
            theirs.append(lax.ppermute(block, ("row", "col"), mirror_pairs(rows, cols, step, hop)))
        base += size

    out_shape = jax.ShapeDtypeStruct((occ_row, slots, square // LANES * occ_col, LANES), jnp.float32)
    block = (tall // ratio, wide)
    split = ratio * (len(sizes) - 1)
    out = pl.pallas_call(
        functools.partial(final_kernel, ratio, sizes),
        out_shape=out_shape,
        in_specs=[SMEM, SMEM] + [VMEM] * (len(owns) + split),
        out_specs=VMEM,
        scratch_shapes=[
            pltpu.VMEM((ratio, slots) + block, bf16),
            pltpu.VMEM((ratio, slots - sizes[-1]) + block, bf16),
        ],
        compiler_params=PARAMS,
        name="final",
    )(lists, tile_counts, *owns, *theirs[:split])
    out = pl.pallas_call(
        functools.partial(patch_kernel, ratio, sizes),
        out_shape=out_shape,
        in_specs=[SMEM, SMEM] + [VMEM] * (len(owns) + ratio) + [HBM],
        out_specs=HBM,
        scratch_shapes=[
            pltpu.VMEM((ratio, slots) + block, bf16),
            pltpu.VMEM((ratio, sizes[-1]) + block, bf16),
            pltpu.VMEM((sizes[-1], occ_row, TILE, LANES), jnp.float32),
            pltpu.SemaphoreType.DMA((sizes[-1],)),
        ],
        input_output_aliases={2 + len(owns) + ratio: 0},
        compiler_params=PARAMS,
        name="patch",
    )(lists, tile_counts, *owns, *theirs[split:], out)
    return tiles_of(out, occ_col)


def solution(mesh):
    return jax.shard_map(
        on_device,
        mesh=mesh,
        in_specs=(P("row", "col", None, None), P("row", "col", None, None), P(), P()),
        out_specs=P("row", "col", None, None),
        check_vma=False,
    )
```

time: 154 us -> 137 us (0.89)
  the two profiles are of different devices: /device:TPU:3 before, /device:TPU:29 now
where the time goes in v1:
time: 137 us; the launch traced here: 136 us
  waiting for transfers between devices  62.7 us (46%)
  starting transfers between devices  52.5 us (38%)
  Pallas kernels  18.1 us (13%)
  local copies, waits for them, and re-layouts  3.01 us (2%)
    ppermute x9, waiting for transfers between devices, on_device(): got.append(lax.ppermute(picked[shift], 'row', pairs))  42.2 us
    ppermute x4, starting transfers between devices, on_device(): lax.ppermute(lefts[e - 1], 'col', [(c, c ^ 1) for c in range(cols)])  21.3 us
    ppermute x6, starting transfers between devices, on_device(): lax.ppermute(block, ('row', 'col'), mirror_pairs(rows, cols, step, hop))  13 us
    ppermute x9, starting transfers between devices, on_device(): got.append(lax.ppermute(picked[shift], 'row', pairs))  10.3 us
    ppermute x3, waiting for transfers between devices, on_device(): lefts.append(lax.ppermute(mine, 'col', [(c, c ^ e) for c in range(cols)]))  9.5 us
    ppermute x6, waiting for transfers between devices, on_device(): lax.ppermute(block, ('row', 'col'), mirror_pairs(rows, cols, step, hop))  8.9 us
    pallas_call x3, Pallas kernels, on_device(): pl.pallas_call(functools.partial(pick_kernel, base, size, rows), out_shap...  6.63 us
    pallas_call x3, Pallas kernels, on_device(): pl.pallas_call(functools.partial(cycle_kernel, rows, cols, ratio, base, s...  5.71 us
  transfers between devices with their start and end apart: 25, of which 9 were waited for; matrix products, arithmetic and copies ran while one was open for 0% of the time, Pallas kernels for 12%

profile of v1, /device:TPU:29, one launch (start us, length us, event | category | flops | bytes accessed | tf_op | source)
XLA Modules:
  0.0 136.5 jit_solution(5052790763942039139)
XLA Ops:
  0.0 1.1 copy-done.1
  1.1 1.2 left.1.refs_1_
  2.3 1.3 collective-permute-start.1
  3.6 0.2 collective-permute-start.3
  3.8 1.2 collective-permute-start.5
  5.0 1.9 %copy-done = bf16[4,2,47,4096]{3,1,2,0:T(2,128)(2,1)S(1)} copy-done((bf16[4,2,47,4096]{3,1,2,0:T(2,128)(2,1)S(1)}, bf16[4,2,47,4096]{3,1,2,0:T(2,128)(2,1)}, u32[]{:S(2)}) %copy-start) | copy-done | bytes 3080216
  6.9 2.6 %pick.3 = (bf16[5,256,128]{2,1,0:T(8,128)(2,1)S(1)}, bf16[5,256,128]{2,1,0:T(8,128)(2,1)S(1)}, bf16[5,256,128]{2,1,0:T(8,128)(2,1)S(1)}, bf16[5,256,128]{2,1,0:T(8,128)(2,1)S(1)}) custom-call(s32[4,2,12]{2,1,0:T(2,128)S(1)} %bitcast.26, bf16[4,47,64,128]{3,2,1,0:T(8,128)(2,1)S(1)} %bitcast.22), custom_call_target="tpu_custom_call" | custom-call | tf_op jit(solution)/shard_map/pick/pallas_call | solution.py:224
  9.5 0.1 collective-permute-start.7
  9.6 1.7 %collective-permute-start = (bf16[12,256,128]{2,1,0:T(8,128)(2,1)S(1)}, bf16[12,256,128]{2,1,0:T(8,128)(2,1)S(1)}, u32[]{:S(2)}, u32[]{:S(2)}) collective-permute-start(bf16[12,256,128]{2,1,0:T(8,128)(2,1)S(1)} %left.1.refs_1_), channel_id=1, source_target_pairs={{0,1},{1,0},{2,3},{3,2},{4,5},{5,4},{6,7},{7,6},{8,9},{9,8},{10,11... | collective-permute-start | bytes 2359304 | tf_op jit(solution)/shard_map/ppermute | solution.py:250
  11.3 9.5 %collective-permute-done.1.refs_3_ = bf16[12,256,128]{2,1,0:T(8,128)(2,1)S(1)} collective-permute-done((bf16[12,256,128]{2,1,0:T(8,128)(2,1)S(1)}, bf16[12,256,128]{2,1,0:T(8,128)(2,1)S(1)}, u32[]{:S(2)}, u32[]{:S(2)}) %collective-permute-start.1) | collective-permute-done | bytes 786464 | tf_op jit(solution)/shard_map/ppermute | solution.py:252
  20.8 2.7 %collective-permute-start.2 = (bf16[12,256,128]{2,1,0:T(8,128)(2,1)S(1)}, bf16[12,256,128]{2,1,0:T(8,128)(2,1)S(1)}, u32[]{:S(2)}, u32[]{:S(2)}) collective-permute-start(bf16[12,256,128]{2,1,0:T(8,128)(2,1)S(1)} %collective-permute-done.1.refs_3_), channel_id=1, source_target_pairs={{0,1},{1,0},{2,3},{3,2},{4,5},{5,4},{6,7},{7,6},{8,9},{9,8},{10,11... | collective-permute-start | bytes 2359304 | tf_op jit(solution)/shard_map/ppermute | solution.py:250
  23.4 0.0 collective-permute-done.7.refs_10_
  23.5 0.1 collective-permute-start.8
  23.5 0.0 collective-permute-done.3.refs_5_
  23.5 16.9 %collective-permute-start.4 = (bf16[12,256,128]{2,1,0:T(8,128)(2,1)S(1)}, bf16[12,256,128]{2,1,0:T(8,128)(2,1)S(1)}, u32[]{:S(2)}, u32[]{:S(2)}) collective-permute-start(bf16[12,256,128]{2,1,0:T(8,128)(2,1)S(1)} %collective-permute-done.3.refs_5_), channel_id=1, source_target_pairs={{0,1},{1,0},{2,3},{3,2},{4,5},{5,4},{6,7},{7,6},{8,9},{9,8},{10,11... | collective-permute-start | bytes 2359304 | tf_op jit(solution)/shard_map/ppermute | solution.py:250
  40.4 0.0 collective-permute-done.5.refs_7_
  40.4 0.0 collective-permute-start.6
  40.4 0.6 collective-permute-done.8.refs_11_
  41.0 2.6 %pick.4 = (bf16[5,256,128]{2,1,0:T(8,128)(2,1)S(1)}, bf16[5,256,128]{2,1,0:T(8,128)(2,1)S(1)}, bf16[5,256,128]{2,1,0:T(8,128)(2,1)S(1)}, bf16[5,256,128]{2,1,0:T(8,128)(2,1)S(1)}) custom-call(s32[4,2,12]{2,1,0:T(2,128)S(1)} %bitcast.27, bf16[4,47,64,128]{3,2,1,0:T(8,128)(2,1)S(1)} %bitcast.23), custom_call_target="tpu_custom_call" | custom-call | tf_op jit(solution)/shard_map/pick/pallas_call | solution.py:224
  43.6 0.0 copy-start.3
  43.6 8.0 %collective-permute-done.9.refs_12_ = bf16[5,256,128]{2,1,0:T(8,128)(2,1)S(1)} collective-permute-done((bf16[5,256,128]{2,1,0:T(8,128)(2,1)S(1)}, bf16[5,256,128]{2,1,0:T(8,128)(2,1)S(1)}, u32[]{:S(2)}, u32[]{:S(2)}) %collective-permute-start.9) | collective-permute-done | bytes 327712 | tf_op jit(solution)/shard_map/ppermute | solution.py:235
  51.6 0.0 collective-permute-start.10
  51.6 0.0 collective-permute-done.refs_2_
  51.6 0.0 collective-permute-start.11
  51.6 1.5 %collective-permute-start.12 = (bf16[5,256,128]{2,1,0:T(8,128)(2,1)S(1)}, bf16[5,256,128]{2,1,0:T(8,128)(2,1)S(1)}, u32[]{:S(2)}, u32[]{:S(2)}) collective-permute-start(bf16[5,256,128]{2,1,0:T(8,128)(2,1)S(1)} %get-tuple-element.32), channel_id=1, source_target_pairs={{0,24},{8,0},{16,8},{24,16},{1,25},{9,1},{17,9},{25,17},{2,26},{10... | collective-permute-start | bytes 983048 | tf_op jit(solution)/shard_map/ppermute | solution.py:235
  53.1 1.4 %pick.5 = (bf16[2,256,128]{2,1,0:T(8,128)(2,1)S(1)}, bf16[2,256,128]{2,1,0:T(8,128)(2,1)S(1)}, bf16[2,256,128]{2,1,0:T(8,128)(2,1)S(1)}, bf16[2,256,128]{2,1,0:T(8,128)(2,1)S(1)}) custom-call(s32[4,2,12]{2,1,0:T(2,128)S(1)} %bitcast.28, bf16[4,47,64,128]{3,2,1,0:T(8,128)(2,1)S(1)} %bitcast.24), custom_call_target="tpu_custom_call" | custom-call | tf_op jit(solution)/shard_map/pick/pallas_call | solution.py:224
  54.5 2.1 %collective-permute-start.13 = (bf16[2,256,128]{2,1,0:T(8,128)(2,1)S(1)}, bf16[2,256,128]{2,1,0:T(8,128)(2,1)S(1)}, u32[]{:S(2)}, u32[]{:S(2)}) collective-permute-start(bf16[2,256,128]{2,1,0:T(8,128)(2,1)S(1)} %get-tuple-element.36), channel_id=1, source_target_pairs={{0,8},{8,16},{16,24},{24,0},{1,9},{9,17},{17,25},{25,1},{2,10},{10... | collective-permute-start | bytes 393224 | tf_op jit(solution)/shard_map/ppermute | solution.py:235
  56.6 2.2 %cycle.3 = (bf16[5,128,128]{2,1,0:T(8,128)(2,1)S(1)}, bf16[5,128,128]{2,1,0:T(8,128)(2,1)S(1)}) custom-call(s32[4]{0:T(128)S(1)} %copy-done.3, bf16[12,256,128]{2,1,0:T(8,128)(2,1)S(1)} %left.1.refs_1_, bf16[12,256,128]{2,1,0:T(8,128)(2,1)S(1)} %collective-permute-done.refs_2_, bf16[12,256,128]{2,1,0:T(8,128)(2,1)S(1)} %collective-permute-done.1.refs_3_, ...), custom_call_target="tpu_custom_call" | custom-call | tf_op jit(solution)/shard_map/cycle/pallas_call | solution.py:257
  58.9 0.3 collective-permute-start.20
  59.2 0.1 collective-permute-done.10.refs_10_
  59.3 20.2 %collective-permute-done.11.refs_11_ = bf16[5,256,128]{2,1,0:T(8,128)(2,1)S(1)} collective-permute-done((bf16[5,256,128]{2,1,0:T(8,128)(2,1)S(1)}, bf16[5,256,128]{2,1,0:T(8,128)(2,1)S(1)}, u32[]{:S(2)}, u32[]{:S(2)}) %collective-permute-start.11) | collective-permute-done | bytes 327712 | tf_op jit(solution)/shard_map/ppermute | solution.py:235
  79.5 2.2 %cycle.4 = (bf16[5,128,128]{2,1,0:T(8,128)(2,1)S(1)}, bf16[5,128,128]{2,1,0:T(8,128)(2,1)S(1)}) custom-call(s32[4]{0:T(128)S(1)} %copy-done.3, bf16[12,256,128]{2,1,0:T(8,128)(2,1)S(1)} %left.1.refs_1_, bf16[12,256,128]{2,1,0:T(8,128)(2,1)S(1)} %collective-permute-done.refs_2_, bf16[12,256,128]{2,1,0:T(8,128)(2,1)S(1)} %collective-permute-done.1.refs_3_, ...), custom_call_target="tpu_custom_call" | custom-call | tf_op jit(solution)/shard_map/cycle/pallas_call | solution.py:257
  81.7 0.3 collective-permute-start.23
  82.0 6.6 %collective-permute-start.14 = (bf16[2,256,128]{2,1,0:T(8,128)(2,1)S(1)}, bf16[2,256,128]{2,1,0:T(8,128)(2,1)S(1)}, u32[]{:S(2)}, u32[]{:S(2)}) collective-permute-start(bf16[2,256,128]{2,1,0:T(8,128)(2,1)S(1)} %get-tuple-element.37), channel_id=1, source_target_pairs={{0,16},{8,24},{16,0},{24,8},{1,17},{9,25},{17,1},{25,9},{2,18},{10... | collective-permute-start | bytes 393224 | tf_op jit(solution)/shard_map/ppermute | solution.py:235
  88.6 3.1 %collective-permute-start.19 = (bf16[5,128,128]{2,1,0:T(8,128)(2,1)S(1)}, bf16[5,128,128]{2,1,0:T(8,128)(2,1)S(1)}, u32[]{:S(2)}, u32[]{:S(2)}) collective-permute-start(bf16[5,128,128]{2,1,0:T(8,128)(2,1)S(1)} %get-tuple-element.27.refs_0_), channel_id=1, source_target_pairs={{0,0},{1,1},{2,8},{3,9},{4,16},{5,17},{6,24},{7,25},{8,2},{9,3},{1... | collective-permute-start | bytes 491528 | tf_op jit(solution)/shard_map/ppermute | solution.py:275
  91.7 13.3 %collective-permute-done.14.refs_11_ = bf16[2,256,128]{2,1,0:T(8,128)(2,1)S(1)} collective-permute-done((bf16[2,256,128]{2,1,0:T(8,128)(2,1)S(1)}, bf16[2,256,128]{2,1,0:T(8,128)(2,1)S(1)}, u32[]{:S(2)}, u32[]{:S(2)}) %collective-permute-start.14) | collective-permute-done | bytes 131104 | tf_op jit(solution)/shard_map/ppermute | solution.py:235
  105.0 1.9 %collective-permute-start.22 = (bf16[5,128,128]{2,1,0:T(8,128)(2,1)S(1)}, bf16[5,128,128]{2,1,0:T(8,128)(2,1)S(1)}, u32[]{:S(2)}, u32[]{:S(2)}) collective-permute-start(bf16[5,128,128]{2,1,0:T(8,128)(2,1)S(1)} %get-tuple-element.33.refs_2_), channel_id=1, source_target_pairs={{0,0},{1,1},{2,8},{3,9},{4,16},{5,17},{6,24},{7,25},{8,2},{9,3},{1... | collective-permute-start | bytes 491528 | tf_op jit(solution)/shard_map/ppermute | solution.py:275
  106.9 0.1 collective-permute-start.21
  107.0 0.1 collective-permute-start.24
  107.1 1.2 cycle.5
  108.3 4.7 %collective-permute-start.17 = (bf16[2,128,128]{2,1,0:T(8,128)(2,1)S(1)}, bf16[2,128,128]{2,1,0:T(8,128)(2,1)S(1)}, u32[]{:S(2)}, u32[]{:S(2)}) collective-permute-start(bf16[2,128,128]{2,1,0:T(8,128)(2,1)S(1)} %get-tuple-element.40.refs_5_), channel_id=1, source_target_pairs={{0,4},{1,5},{2,6},{3,7},{4,0},{5,1},{6,2},{7,3},{8,12},{9,13},{10,... | collective-permute-start | bytes 196616 | tf_op jit(solution)/shard_map/ppermute | solution.py:274
  113.0 2.1 %collective-permute-done.17 = bf16[2,128,128]{2,1,0:T(8,128)(2,1)S(1)} collective-permute-done((bf16[2,128,128]{2,1,0:T(8,128)(2,1)S(1)}, bf16[2,128,128]{2,1,0:T(8,128)(2,1)S(1)}, u32[]{:S(2)}, u32[]{:S(2)}) %collective-permute-start.17) | collective-permute-done | bytes 65568 | tf_op jit(solution)/shard_map/ppermute | solution.py:274
  115.1 2.6 %collective-permute-start.16 = (bf16[2,128,128]{2,1,0:T(8,128)(2,1)S(1)}, bf16[2,128,128]{2,1,0:T(8,128)(2,1)S(1)}, u32[]{:S(2)}, u32[]{:S(2)}) collective-permute-start(bf16[2,128,128]{2,1,0:T(8,128)(2,1)S(1)} %get-tuple-element.39.refs_4_), channel_id=1, source_target_pairs={{0,0},{1,1},{2,8},{3,9},{4,16},{5,17},{6,24},{7,25},{8,2},{9,3},{1... | collective-permute-start | bytes 196616 | tf_op jit(solution)/shard_map/ppermute | solution.py:275
  117.7 5.3 %collective-permute-start.18 = (bf16[2,128,128]{2,1,0:T(8,128)(2,1)S(1)}, bf16[2,128,128]{2,1,0:T(8,128)(2,1)S(1)}, u32[]{:S(2)}, u32[]{:S(2)}) collective-permute-start(bf16[2,128,128]{2,1,0:T(8,128)(2,1)S(1)} %collective-permute-done.17), channel_id=1, source_target_pairs={{4,1},{5,0},{6,9},{7,8},{0,17},{1,16},{2,25},{3,24},{12,3},{13,2},... | collective-permute-start | bytes 196616 | tf_op jit(solution)/shard_map/ppermute | solution.py:275
  123.0 4.0 %collective-permute-done.21.refs_7_ = bf16[5,128,128]{2,1,0:T(8,128)(2,1)S(1)} collective-permute-done((bf16[5,128,128]{2,1,0:T(8,128)(2,1)S(1)}, bf16[5,128,128]{2,1,0:T(8,128)(2,1)S(1)}, u32[]{:S(2)}, u32[]{:S(2)}) %collective-permute-start.21) | collective-permute-done | bytes 163872 | tf_op jit(solution)/shard_map/ppermute | solution.py:275
  127.0 4.9 %collective-permute-done.24.refs_9_ = bf16[5,128,128]{2,1,0:T(8,128)(2,1)S(1)} collective-permute-done((bf16[5,128,128]{2,1,0:T(8,128)(2,1)S(1)}, bf16[5,128,128]{2,1,0:T(8,128)(2,1)S(1)}, u32[]{:S(2)}, u32[]{:S(2)}) %collective-permute-start.24) | collective-permute-done | bytes 163872 | tf_op jit(solution)/shard_map/ppermute | solution.py:275
  131.9 3.8 %final.1.refs_8_ = f32[4,12,64,128]{3,2,1,0:T(8,128)} custom-call(s32[4,2,12]{2,1,0:T(2,128)S(1)} %bitcast.29, s32[4]{0:T(128)S(1)} %copy-done.3, bf16[5,128,128]{2,1,0:T(8,128)(2,1)S(1)} %get-tuple-element.27.refs_0_, bf16[5,128,128]{2,1,0:T(8,128)(2,1)S(1)} %get-tuple-element.28.refs_1_, bf16[5,128,128]{2,1,0:T(8,128)(2,1)S(1)} %get-tuple-element.33.refs_2_, ...), custom_call_target="tpu_custom_call" | custom-call | tf_op jit(solution)/shard_map/final/pallas_call | solution.py:281
  135.7 0.8 patch.1
  (19 shorter events, 0.0 us)
Async XLA Ops:
  0.0 1.1 copy-start.1
  1.1 3.9 %copy-start.2 = (s32[4,12,2]{1,2,0:T(2,128)S(1)}, s32[4,12,2]{1,2,0:T(2,128)}, u32[]{:S(2)}) copy-start(s32[4,12,2]{1,2,0:T(2,128)} %param.6) | copy-start | bytes 1156
  2.3 18.5 %collective-permute-start.1 = (bf16[12,256,128]{2,1,0:T(8,128)(2,1)S(1)}, bf16[12,256,128]{2,1,0:T(8,128)(2,1)S(1)}, u32[]{:S(2)}, u32[]{:S(2)}) collective-permute-start(bf16[12,256,128]{2,1,0:T(8,128)(2,1)S(1)} %left.1.refs_1_), channel_id=1, source_target_pairs={{0,2},{1,3},{2,0},{3,1},{4,6},{5,7},{6,4},{7,5},{8,10},{9,11},{10,... | collective-permute-start | bytes 2359304 | tf_op jit(solution)/shard_map/ppermute | solution.py:252
  3.6 19.9 %collective-permute-start.3 = (bf16[12,256,128]{2,1,0:T(8,128)(2,1)S(1)}, bf16[12,256,128]{2,1,0:T(8,128)(2,1)S(1)}, u32[]{:S(2)}, u32[]{:S(2)}) collective-permute-start(bf16[12,256,128]{2,1,0:T(8,128)(2,1)S(1)} %left.1.refs_1_), channel_id=1, source_target_pairs={{0,4},{1,5},{2,6},{3,7},{4,0},{5,1},{6,2},{7,3},{8,12},{9,13},{10,... | collective-permute-start | bytes 2359304 | tf_op jit(solution)/shard_map/ppermute | solution.py:252
  3.8 36.6 %collective-permute-start.5 = (bf16[12,256,128]{2,1,0:T(8,128)(2,1)S(1)}, bf16[12,256,128]{2,1,0:T(8,128)(2,1)S(1)}, u32[]{:S(2)}, u32[]{:S(2)}) collective-permute-start(bf16[12,256,128]{2,1,0:T(8,128)(2,1)S(1)} %left.1.refs_1_), channel_id=1, source_target_pairs={{0,6},{1,7},{2,4},{3,5},{4,2},{5,3},{6,0},{7,1},{8,14},{9,15},{10,... | collective-permute-start | bytes 2359304 | tf_op jit(solution)/shard_map/ppermute | solution.py:252
  5.0 1.9 %copy-start = (bf16[4,2,47,4096]{3,1,2,0:T(2,128)(2,1)S(1)}, bf16[4,2,47,4096]{3,1,2,0:T(2,128)(2,1)}, u32[]{:S(2)}) copy-start(bf16[4,2,47,4096]{3,1,2,0:T(2,128)(2,1)} %param.5) | copy-start | bytes 9240580
  9.5 14.0 %collective-permute-start.7 = (bf16[5,256,128]{2,1,0:T(8,128)(2,1)S(1)}, bf16[5,256,128]{2,1,0:T(8,128)(2,1)S(1)}, u32[]{:S(2)}, u32[]{:S(2)}) collective-permute-start(bf16[5,256,128]{2,1,0:T(8,128)(2,1)S(1)} %get-tuple-element.24), channel_id=1, source_target_pairs={{0,8},{8,16},{16,24},{24,0},{1,9},{9,17},{17,25},{25,1},{2,10},{10... | collective-permute-start | bytes 983048 | tf_op jit(solution)/shard_map/ppermute | solution.py:235
  9.6 42.0 %collective-permute-start = (bf16[12,256,128]{2,1,0:T(8,128)(2,1)S(1)}, bf16[12,256,128]{2,1,0:T(8,128)(2,1)S(1)}, u32[]{:S(2)}, u32[]{:S(2)}) collective-permute-start(bf16[12,256,128]{2,1,0:T(8,128)(2,1)S(1)} %left.1.refs_1_), channel_id=1, source_target_pairs={{0,1},{1,0},{2,3},{3,2},{4,5},{5,4},{6,7},{7,6},{8,9},{9,8},{10,11... | collective-permute-start | bytes 2359304 | tf_op jit(solution)/shard_map/ppermute | solution.py:250
  20.8 30.8 %collective-permute-start.2 = (bf16[12,256,128]{2,1,0:T(8,128)(2,1)S(1)}, bf16[12,256,128]{2,1,0:T(8,128)(2,1)S(1)}, u32[]{:S(2)}, u32[]{:S(2)}) collective-permute-start(bf16[12,256,128]{2,1,0:T(8,128)(2,1)S(1)} %collective-permute-done.1.refs_3_), channel_id=1, source_target_pairs={{0,1},{1,0},{2,3},{3,2},{4,5},{5,4},{6,7},{7,6},{8,9},{9,8},{10,11... | collective-permute-start | bytes 2359304 | tf_op jit(solution)/shard_map/ppermute | solution.py:250
  23.5 17.5 %collective-permute-start.8 = (bf16[5,256,128]{2,1,0:T(8,128)(2,1)S(1)}, bf16[5,256,128]{2,1,0:T(8,128)(2,1)S(1)}, u32[]{:S(2)}, u32[]{:S(2)}) collective-permute-start(bf16[5,256,128]{2,1,0:T(8,128)(2,1)S(1)} %get-tuple-element.25), channel_id=1, source_target_pairs={{0,16},{8,24},{16,0},{24,8},{1,17},{9,25},{17,1},{25,9},{2,18},{10... | collective-permute-start | bytes 983048 | tf_op jit(solution)/shard_map/ppermute | solution.py:235
  23.5 31.0 %collective-permute-start.4 = (bf16[12,256,128]{2,1,0:T(8,128)(2,1)S(1)}, bf16[12,256,128]{2,1,0:T(8,128)(2,1)S(1)}, u32[]{:S(2)}, u32[]{:S(2)}) collective-permute-start(bf16[12,256,128]{2,1,0:T(8,128)(2,1)S(1)} %collective-permute-done.3.refs_5_), channel_id=1, source_target_pairs={{0,1},{1,0},{2,3},{3,2},{4,5},{5,4},{6,7},{7,6},{8,9},{9,8},{10,11... | collective-permute-start | bytes 2359304 | tf_op jit(solution)/shard_map/ppermute | solution.py:250
  40.4 16.2 %collective-permute-start.6 = (bf16[12,256,128]{2,1,0:T(8,128)(2,1)S(1)}, bf16[12,256,128]{2,1,0:T(8,128)(2,1)S(1)}, u32[]{:S(2)}, u32[]{:S(2)}) collective-permute-start(bf16[12,256,128]{2,1,0:T(8,128)(2,1)S(1)} %collective-permute-done.5.refs_7_), channel_id=1, source_target_pairs={{0,1},{1,0},{2,3},{3,2},{4,5},{5,4},{6,7},{7,6},{8,9},{9,8},{10,11... | collective-permute-start | bytes 2359304 | tf_op jit(solution)/shard_map/ppermute | solution.py:250
  40.9 10.6 %collective-permute-start.9 = (bf16[5,256,128]{2,1,0:T(8,128)(2,1)S(1)}, bf16[5,256,128]{2,1,0:T(8,128)(2,1)S(1)}, u32[]{:S(2)}, u32[]{:S(2)}) collective-permute-start(bf16[5,256,128]{2,1,0:T(8,128)(2,1)S(1)} %get-tuple-element.26), channel_id=1, source_target_pairs={{0,24},{8,0},{16,8},{24,16},{1,25},{9,1},{17,9},{25,17},{2,26},{10... | collective-permute-start | bytes 983048 | tf_op jit(solution)/shard_map/ppermute | solution.py:235
  43.6 13.1 %copy-start.3 = (s32[4]{0:T(128)S(1)}, s32[4]{0:T(128)}, u32[]{:S(2)}) copy-start(s32[4]{0:T(128)} %count_ref.3) | copy-start | bytes 52
  51.6 7.7 %collective-permute-start.10 = (bf16[5,256,128]{2,1,0:T(8,128)(2,1)S(1)}, bf16[5,256,128]{2,1,0:T(8,128)(2,1)S(1)}, u32[]{:S(2)}, u32[]{:S(2)}) collective-permute-start(bf16[5,256,128]{2,1,0:T(8,128)(2,1)S(1)} %get-tuple-element.30), channel_id=1, source_target_pairs={{0,8},{8,16},{16,24},{24,0},{1,9},{9,17},{17,25},{25,1},{2,10},{10... | collective-permute-start | bytes 983048 | tf_op jit(solution)/shard_map/ppermute | solution.py:235
  51.6 27.9 %collective-permute-start.11 = (bf16[5,256,128]{2,1,0:T(8,128)(2,1)S(1)}, bf16[5,256,128]{2,1,0:T(8,128)(2,1)S(1)}, u32[]{:S(2)}, u32[]{:S(2)}) collective-permute-start(bf16[5,256,128]{2,1,0:T(8,128)(2,1)S(1)} %get-tuple-element.31), channel_id=1, source_target_pairs={{0,16},{8,24},{16,0},{24,8},{1,17},{9,25},{17,1},{25,9},{2,18},{10... | collective-permute-start | bytes 983048 | tf_op jit(solution)/shard_map/ppermute | solution.py:235
  51.6 27.9 %collective-permute-start.12 = (bf16[5,256,128]{2,1,0:T(8,128)(2,1)S(1)}, bf16[5,256,128]{2,1,0:T(8,128)(2,1)S(1)}, u32[]{:S(2)}, u32[]{:S(2)}) collective-permute-start(bf16[5,256,128]{2,1,0:T(8,128)(2,1)S(1)} %get-tuple-element.32), channel_id=1, source_target_pairs={{0,24},{8,0},{16,8},{24,16},{1,25},{9,1},{17,9},{25,17},{2,26},{10... | collective-permute-start | bytes 983048 | tf_op jit(solution)/shard_map/ppermute | solution.py:235
  54.5 34.0 %collective-permute-start.13 = (bf16[2,256,128]{2,1,0:T(8,128)(2,1)S(1)}, bf16[2,256,128]{2,1,0:T(8,128)(2,1)S(1)}, u32[]{:S(2)}, u32[]{:S(2)}) collective-permute-start(bf16[2,256,128]{2,1,0:T(8,128)(2,1)S(1)} %get-tuple-element.36), channel_id=1, source_target_pairs={{0,8},{8,16},{16,24},{24,0},{1,9},{9,17},{17,25},{25,1},{2,10},{10... | collective-permute-start | bytes 393224 | tf_op jit(solution)/shard_map/ppermute | solution.py:235
  58.9 48.0 %collective-permute-start.20 = (bf16[5,128,128]{2,1,0:T(8,128)(2,1)S(1)}, bf16[5,128,128]{2,1,0:T(8,128)(2,1)S(1)}, u32[]{:S(2)}, u32[]{:S(2)}) collective-permute-start(bf16[5,128,128]{2,1,0:T(8,128)(2,1)S(1)} %get-tuple-element.28.refs_1_), channel_id=1, source_target_pairs={{0,4},{1,5},{2,6},{3,7},{4,0},{5,1},{6,2},{7,3},{8,12},{9,13},{10,... | collective-permute-start | bytes 491528 | tf_op jit(solution)/shard_map/ppermute | solution.py:274
  81.7 25.3 %collective-permute-start.23 = (bf16[5,128,128]{2,1,0:T(8,128)(2,1)S(1)}, bf16[5,128,128]{2,1,0:T(8,128)(2,1)S(1)}, u32[]{:S(2)}, u32[]{:S(2)}) collective-permute-start(bf16[5,128,128]{2,1,0:T(8,128)(2,1)S(1)} %get-tuple-element.34.refs_3_), channel_id=1, source_target_pairs={{0,4},{1,5},{2,6},{3,7},{4,0},{5,1},{6,2},{7,3},{8,12},{9,13},{10,... | collective-permute-start | bytes 491528 | tf_op jit(solution)/shard_map/ppermute | solution.py:274
  82.0 23.0 %collective-permute-start.14 = (bf16[2,256,128]{2,1,0:T(8,128)(2,1)S(1)}, bf16[2,256,128]{2,1,0:T(8,128)(2,1)S(1)}, u32[]{:S(2)}, u32[]{:S(2)}) collective-permute-start(bf16[2,256,128]{2,1,0:T(8,128)(2,1)S(1)} %get-tuple-element.37), channel_id=1, source_target_pairs={{0,16},{8,24},{16,0},{24,8},{1,17},{9,25},{17,1},{25,9},{2,18},{10... | collective-permute-start | bytes 393224 | tf_op jit(solution)/shard_map/ppermute | solution.py:235
  88.6 18.5 %collective-permute-start.15 = (bf16[2,256,128]{2,1,0:T(8,128)(2,1)S(1)}, bf16[2,256,128]{2,1,0:T(8,128)(2,1)S(1)}, u32[]{:S(2)}, u32[]{:S(2)}) collective-permute-start(bf16[2,256,128]{2,1,0:T(8,128)(2,1)S(1)} %get-tuple-element.38), channel_id=1, source_target_pairs={{0,24},{8,0},{16,8},{24,16},{1,25},{9,1},{17,9},{25,17},{2,26},{10... | collective-permute-start | bytes 393224 | tf_op jit(solution)/shard_map/ppermute | solution.py:235
  88.6 29.1 %collective-permute-start.19 = (bf16[5,128,128]{2,1,0:T(8,128)(2,1)S(1)}, bf16[5,128,128]{2,1,0:T(8,128)(2,1)S(1)}, u32[]{:S(2)}, u32[]{:S(2)}) collective-permute-start(bf16[5,128,128]{2,1,0:T(8,128)(2,1)S(1)} %get-tuple-element.27.refs_0_), channel_id=1, source_target_pairs={{0,0},{1,1},{2,8},{3,9},{4,16},{5,17},{6,24},{7,25},{8,2},{9,3},{1... | collective-permute-start | bytes 491528 | tf_op jit(solution)/shard_map/ppermute | solution.py:275
  105.0 18.0 %collective-permute-start.22 = (bf16[5,128,128]{2,1,0:T(8,128)(2,1)S(1)}, bf16[5,128,128]{2,1,0:T(8,128)(2,1)S(1)}, u32[]{:S(2)}, u32[]{:S(2)}) collective-permute-start(bf16[5,128,128]{2,1,0:T(8,128)(2,1)S(1)} %get-tuple-element.33.refs_2_), channel_id=1, source_target_pairs={{0,0},{1,1},{2,8},{3,9},{4,16},{5,17},{6,24},{7,25},{8,2},{9,3},{1... | collective-permute-start | bytes 491528 | tf_op jit(solution)/shard_map/ppermute | solution.py:275
  106.9 20.0 %collective-permute-start.21 = (bf16[5,128,128]{2,1,0:T(8,128)(2,1)S(1)}, bf16[5,128,128]{2,1,0:T(8,128)(2,1)S(1)}, u32[]{:S(2)}, u32[]{:S(2)}) collective-permute-start(bf16[5,128,128]{2,1,0:T(8,128)(2,1)S(1)} %collective-permute-done.20), channel_id=1, source_target_pairs={{4,1},{5,0},{6,9},{7,8},{0,17},{1,16},{2,25},{3,24},{12,3},{13,2},... | collective-permute-start | bytes 491528 | tf_op jit(solution)/shard_map/ppermute | solution.py:275
  107.0 24.9 %collective-permute-start.24 = (bf16[5,128,128]{2,1,0:T(8,128)(2,1)S(1)}, bf16[5,128,128]{2,1,0:T(8,128)(2,1)S(1)}, u32[]{:S(2)}, u32[]{:S(2)}) collective-permute-start(bf16[5,128,128]{2,1,0:T(8,128)(2,1)S(1)} %collective-permute-done.23), channel_id=1, source_target_pairs={{4,1},{5,0},{6,9},{7,8},{0,17},{1,16},{2,25},{3,24},{12,3},{13,2},... | collective-permute-start | bytes 491528 | tf_op jit(solution)/shard_map/ppermute | solution.py:275
  108.3 6.8 %collective-permute-start.17 = (bf16[2,128,128]{2,1,0:T(8,128)(2,1)S(1)}, bf16[2,128,128]{2,1,0:T(8,128)(2,1)S(1)}, u32[]{:S(2)}, u32[]{:S(2)}) collective-permute-start(bf16[2,128,128]{2,1,0:T(8,128)(2,1)S(1)} %get-tuple-element.40.refs_5_), channel_id=1, source_target_pairs={{0,4},{1,5},{2,6},{3,7},{4,0},{5,1},{6,2},{7,3},{8,12},{9,13},{10,... | collective-permute-start | bytes 196616 | tf_op jit(solution)/shard_map/ppermute | solution.py:274
  115.1 20.6 %collective-permute-start.16 = (bf16[2,128,128]{2,1,0:T(8,128)(2,1)S(1)}, bf16[2,128,128]{2,1,0:T(8,128)(2,1)S(1)}, u32[]{:S(2)}, u32[]{:S(2)}) collective-permute-start(bf16[2,128,128]{2,1,0:T(8,128)(2,1)S(1)} %get-tuple-element.39.refs_4_), channel_id=1, source_target_pairs={{0,0},{1,1},{2,8},{3,9},{4,16},{5,17},{6,24},{7,25},{8,2},{9,3},{1... | collective-permute-start | bytes 196616 | tf_op jit(solution)/shard_map/ppermute | solution.py:275
  117.7 18.0 %collective-permute-start.18 = (bf16[2,128,128]{2,1,0:T(8,128)(2,1)S(1)}, bf16[2,128,128]{2,1,0:T(8,128)(2,1)S(1)}, u32[]{:S(2)}, u32[]{:S(2)}) collective-permute-start(bf16[2,128,128]{2,1,0:T(8,128)(2,1)S(1)} %collective-permute-done.17), channel_id=1, source_target_pairs={{4,1},{5,0},{6,9},{7,8},{0,17},{1,16},{2,25},{3,24},{12,3},{13,2},... | collective-permute-start | bytes 196616 | tf_op jit(solution)/shard_map/ppermute | solution.py:275

commit v2 on v1

--- a/solution.py
+++ b/solution.py
@@ -11,6 +11,7 @@
 TILE = 64
 LANES = 128
 SPLIT = (5, 5, 2)
+HOPPED = (True, True, False)
 VMEM = pl.BlockSpec(memory_space=pltpu.VMEM)
 SMEM = pl.BlockSpec(memory_space=pltpu.SMEM)
 HBM = pl.BlockSpec(memory_space=pltpu.HBM)
@@ -58,18 +59,21 @@
         lax.fori_loop(0, size, one, 0)
 
 
-def left_kernel(a_ref, out):
-    depth, slots = a_ref.shape[:2]
-
-    def one(s, _):
-        x = a_ref[:, s].reshape(depth * TILE, LANES).astype(jnp.float32)
-        out[s] = swap(x).astype(jnp.bfloat16)
-        return 0
-
-    lax.fori_loop(0, slots, one, 0)
-
-
-def cycle_kernel(rows, cols, ratio, base, size, *refs):
+def left_kernel(a_ref, *outs):
+    depth = a_ref.shape[0]
+    base = 0
+    for out in outs:
+
+        def one(s, _, out=out, base=base):
+            x = a_ref[:, base + s].reshape(depth * TILE, LANES).astype(jnp.float32)
+            out[s] = swap(x).astype(jnp.bfloat16)
+            return 0
+
+        lax.fori_loop(0, out.shape[0], one, 0)
+        base += out.shape[0]
+
+
+def cycle_kernel(rows, cols, ratio, base, skip, size, *refs):
     count_ref = refs[0]
     lefts = refs[1 : 1 + cols]
     rights = refs[1 + cols : 1 + cols + rows]
@@ -89,7 +93,7 @@
         acc = None
         for chip in range(rows):
             row = (my_col // ratio) ^ chip
-            left = jnp.concatenate([lefts[chip * ratio + p][base + s] for p in range(ratio)], axis=1)
+            left = jnp.concatenate([lefts[chip * ratio + p][skip + s] for p in range(ratio)], axis=1)
             right = jnp.concatenate([held[row, p, s] for p in range(ratio)], axis=0)
             part = jnp.dot(left, right, preferred_element_type=jnp.float32)
             acc = part if acc is None else acc + part
@@ -120,7 +124,7 @@
 
 def final_kernel(ratio, sizes, list_ref, count_ref, *refs):
     slots = sum(sizes)
-    early = slots - sizes[-1]
+    early = sizes[0]
     owns = refs[: len(sizes) * ratio]
     theirs = refs[len(sizes) * ratio : -3]
     out_ref, held_own, held_their = refs[-3:]
@@ -129,7 +133,7 @@
     core = lax.rem(my_col, ratio)
     partner = my_col // ratio
     collect(owns, held_own, sizes, ratio, core)
-    collect(theirs, held_their, sizes[:-1], ratio, core)
+    collect(theirs, held_their, sizes[:1], ratio, core)
     my_count = count_ref[my_row]
     depth = out_ref.shape[0]
 
@@ -159,7 +163,7 @@
 
 def patch_kernel(ratio, sizes, list_ref, count_ref, *refs):
     slots = sum(sizes)
-    early = slots - sizes[-1]
+    early = sizes[0]
     owns = refs[: len(sizes) * ratio]
     theirs = refs[len(sizes) * ratio : -6]
     _, out_ref, held_own, held_their, built, sem = refs[-6:]
@@ -168,11 +172,11 @@
     core = lax.rem(my_col, ratio)
     partner = my_col // ratio
     collect(owns, held_own, sizes, ratio, core)
-    collect(theirs, held_their, sizes[-1:], ratio, core)
+    collect(theirs, held_their, sizes[1:], ratio, core)
     my_count = count_ref[my_row]
     depth = out_ref.shape[0]
     uses, copies = [], []
-    for t in range(sizes[-1]):
+    for t in range(slots - early):
         first = list_ref[partner, 0, early + t]
         second = list_ref[partner, 1, early + t]
         found = jnp.int32(-1)
@@ -236,26 +240,29 @@
         rights.append(got)
         base += size
 
+    parts = (sizes[0], slots - sizes[0])
     mine = pl.pallas_call(
         left_kernel,
-        out_shape=jax.ShapeDtypeStruct((slots, tall, wide), bf16),
+        out_shape=[jax.ShapeDtypeStruct((n, tall, wide), bf16) for n in parts],
         in_specs=[VMEM],
-        out_specs=VMEM,
+        out_specs=[VMEM] * 2,
         compiler_params=PARAMS,
         name="left",
     )(rows_of(amplitudes))
-    lefts = [mine]
-    for e in range(1, cols):
-        if e % 2:
-            lefts.append(lax.ppermute(lefts[e - 1], "col", [(c, c ^ 1) for c in range(cols)]))
-        else:
-            lefts.append(lax.ppermute(mine, "col", [(c, c ^ e) for c in range(cols)]))
+    lefts = []
+    for part in range(2):
+        got = [mine[part]]
+        for e in range(1, cols):
+            source = got[e - 1] if e % 2 else got[0]
+            step = 1 if e % 2 else e
+            got.append(lax.ppermute(source, "col", [(c, c ^ step) for c in range(cols)]))
+        lefts.append(got)
 
     owns, theirs = [], []
     base = 0
     for chunk, size in enumerate(sizes):
         sent = pl.pallas_call(
-            functools.partial(cycle_kernel, rows, cols, ratio, base, size),
+            functools.partial(cycle_kernel, rows, cols, ratio, base, base if chunk == 0 else base - sizes[0], size),
             out_shape=[jax.ShapeDtypeStruct((size, tall // ratio, wide), bf16)] * ratio,
             in_specs=[SMEM] + [VMEM] * (cols + rows),
             out_specs=[VMEM] * ratio,
@@ -265,11 +272,11 @@
             ],
             compiler_params=PARAMS,
             name="cycle",
-        )(tile_counts, *lefts, *rights[chunk])
+        )(tile_counts, *lefts[min(chunk, 1)], *rights[chunk])
         owns += sent
         for step in range(ratio):
             block = sent[step]
-            hop = step % 2
+            hop = step % 2 if HOPPED[chunk] else 0
             if hop:
                 block = lax.ppermute(block, "col", [(c, c ^ (cols // 2)) for c in range(cols)])
             theirs.append(lax.ppermute(block, ("row", "col"), mirror_pairs(rows, cols, step, hop)))
@@ -277,7 +284,8 @@
 
     out_shape = jax.ShapeDtypeStruct((occ_row, slots, square // LANES * occ_col, LANES), jnp.float32)
     block = (tall // ratio, wide)
-    split = ratio * (len(sizes) - 1)
+    split = ratio
+    late = slots - sizes[0]
     out = pl.pallas_call(
         functools.partial(final_kernel, ratio, sizes),
         out_shape=out_shape,
@@ -285,7 +293,7 @@
         out_specs=VMEM,
         scratch_shapes=[
             pltpu.VMEM((ratio, slots) + block, bf16),
-            pltpu.VMEM((ratio, slots - sizes[-1]) + block, bf16),
+            pltpu.VMEM((ratio, sizes[0]) + block, bf16),
         ],
         compiler_params=PARAMS,
         name="final",
@@ -293,15 +301,15 @@
     out = pl.pallas_call(
         functools.partial(patch_kernel, ratio, sizes),
         out_shape=out_shape,
-        in_specs=[SMEM, SMEM] + [VMEM] * (len(owns) + ratio) + [HBM],
+        in_specs=[SMEM, SMEM] + [VMEM] * (len(owns) + len(theirs) - split) + [HBM],
         out_specs=HBM,
         scratch_shapes=[
             pltpu.VMEM((ratio, slots) + block, bf16),
-            pltpu.VMEM((ratio, sizes[-1]) + block, bf16),
-            pltpu.VMEM((sizes[-1], occ_row, TILE, LANES), jnp.float32),
-            pltpu.SemaphoreType.DMA((sizes[-1],)),
+            pltpu.VMEM((ratio, late) + block, bf16),
+            pltpu.VMEM((late, occ_row, TILE, LANES), jnp.float32),
+            pltpu.SemaphoreType.DMA((late,)),
         ],
-        input_output_aliases={2 + len(owns) + ratio: 0},
+        input_output_aliases={2 + len(owns) + len(theirs) - split: 0},
         compiler_params=PARAMS,
         name="patch",
     )(lists, tile_counts, *owns, *theirs[split:], out)

time: 137 us -> 129 us (0.942)
  the two profiles are of different devices: /device:TPU:29 before, /device:TPU:3 now
where the time goes in v2:
time: 129 us; the launch traced here: 128 us
  starting transfers between devices  59.7 us (46%)
  waiting for transfers between devices  45.2 us (35%)
  Pallas kernels  19.4 us (15%)
  local copies, waits for them, and re-layouts  3.7 us (3%)
    ppermute x9, waiting for transfers between devices, on_device(): got.append(lax.ppermute(picked[shift], 'row', pairs))  44.9 us
    ppermute x6, starting transfers between devices, on_device(): lax.ppermute(block, ('row', 'col'), mirror_pairs(rows, cols, step, hop))  32.6 us
    ppermute x14, starting transfers between devices, on_device(): lax.ppermute(source, 'col', [(c, c ^ step) for c in range(cols)])  13.3 us
    ppermute x9, starting transfers between devices, on_device(): got.append(lax.ppermute(picked[shift], 'row', pairs))  12.2 us
    pallas_call x3, Pallas kernels, on_device(): pl.pallas_call(functools.partial(pick_kernel, base, size, rows), out_shap...  6.63 us
    pallas_call x3, Pallas kernels, on_device(): pl.pallas_call(functools.partial(cycle_kernel, rows, cols, ratio, base, b...  5.71 us
    unnamed x8, local copies, waits for them, and re-layouts  3.7 us
    pallas_call x1, Pallas kernels, on_device(): pl.pallas_call(functools.partial(final_kernel, ratio, sizes), out_shape=o...  3.25 us
  transfers between devices with their start and end apart: 31, of which 6 were waited for; matrix products, arithmetic and copies ran while one was open for 0% of the time, Pallas kernels for 12%

profile of v2, /device:TPU:3, one launch (start us, length us, event | category | flops | bytes accessed | tf_op | source)
XLA Modules:
  0.0 128.1 jit_solution(15271390535370147566)
XLA Ops:
  0.0 1.1 copy-done.1
  1.1 1.2 left.1
  2.3 0.7 collective-permute-start
  3.0 0.0 collective-permute-start.1
  3.0 1.5 %collective-permute-start.3 = (bf16[5,256,128]{2,1,0:T(8,128)(2,1)S(1)}, bf16[5,256,128]{2,1,0:T(8,128)(2,1)S(1)}, u32[]{:S(2)}, u32[]{:S(2)}) collective-permute-start(bf16[5,256,128]{2,1,0:T(8,128)(2,1)S(1)} %get-tuple-element.25.refs_1_), channel_id=1, source_target_pairs={{0,4},{1,5},{2,6},{3,7},{4,0},{5,1},{6,2},{7,3},{8,12},{9,13},{10,... | collective-permute-start | bytes 983048 | tf_op jit(solution)/shard_map/ppermute | solution.py:258
  4.5 1.2 collective-permute-start.5
  5.7 1.9 %copy-done = bf16[4,2,47,4096]{3,1,2,0:T(2,128)(2,1)S(1)} copy-done((bf16[4,2,47,4096]{3,1,2,0:T(2,128)(2,1)S(1)}, bf16[4,2,47,4096]{3,1,2,0:T(2,128)(2,1)}, u32[]{:S(2)}) %copy-start) | copy-done | bytes 3080216
  7.6 0.7 copy-done.2
  8.2 2.6 %pick.3 = (bf16[5,256,128]{2,1,0:T(8,128)(2,1)S(1)}, bf16[5,256,128]{2,1,0:T(8,128)(2,1)S(1)}, bf16[5,256,128]{2,1,0:T(8,128)(2,1)S(1)}, bf16[5,256,128]{2,1,0:T(8,128)(2,1)S(1)}) custom-call(s32[4,2,12]{2,1,0:T(2,128)S(1)} %bitcast.26, bf16[4,47,64,128]{3,2,1,0:T(8,128)(2,1)S(1)} %bitcast.22), custom_call_target="tpu_custom_call" | custom-call | tf_op jit(solution)/shard_map/pick/pallas_call | solution.py:228
  10.9 1.3 %collective-permute-start.7 = (bf16[5,256,128]{2,1,0:T(8,128)(2,1)S(1)}, bf16[5,256,128]{2,1,0:T(8,128)(2,1)S(1)}, u32[]{:S(2)}, u32[]{:S(2)}) collective-permute-start(bf16[5,256,128]{2,1,0:T(8,128)(2,1)S(1)} %get-tuple-element.27), channel_id=1, source_target_pairs={{0,8},{8,16},{16,24},{24,0},{1,9},{9,17},{17,25},{25,1},{2,10},{10... | collective-permute-start | bytes 983048 | tf_op jit(solution)/shard_map/ppermute | solution.py:239
  12.2 2.3 %collective-permute-start.8 = (bf16[5,256,128]{2,1,0:T(8,128)(2,1)S(1)}, bf16[5,256,128]{2,1,0:T(8,128)(2,1)S(1)}, u32[]{:S(2)}, u32[]{:S(2)}) collective-permute-start(bf16[5,256,128]{2,1,0:T(8,128)(2,1)S(1)} %get-tuple-element.28), channel_id=1, source_target_pairs={{0,16},{8,24},{16,0},{24,8},{1,17},{9,25},{17,1},{25,9},{2,18},{10... | collective-permute-start | bytes 983048 | tf_op jit(solution)/shard_map/ppermute | solution.py:239
  14.5 1.1 collective-permute-start.9
  15.6 3.7 %collective-permute-start.11 = (bf16[7,256,128]{2,1,0:T(8,128)(2,1)S(1)}, bf16[7,256,128]{2,1,0:T(8,128)(2,1)S(1)}, u32[]{:S(2)}, u32[]{:S(2)}) collective-permute-start(bf16[7,256,128]{2,1,0:T(8,128)(2,1)S(1)} %get-tuple-element.32.refs_1_), channel_id=1, source_target_pairs={{0,2},{1,3},{2,0},{3,1},{4,6},{5,7},{6,4},{7,5},{8,10},{9,11},{10,... | collective-permute-start | bytes 1376264 | tf_op jit(solution)/shard_map/ppermute | solution.py:258
  19.3 2.6 %pick.4 = (bf16[5,256,128]{2,1,0:T(8,128)(2,1)S(1)}, bf16[5,256,128]{2,1,0:T(8,128)(2,1)S(1)}, bf16[5,256,128]{2,1,0:T(8,128)(2,1)S(1)}, bf16[5,256,128]{2,1,0:T(8,128)(2,1)S(1)}) custom-call(s32[4,2,12]{2,1,0:T(2,128)S(1)} %bitcast.27, bf16[4,47,64,128]{3,2,1,0:T(8,128)(2,1)S(1)} %bitcast.23), custom_call_target="tpu_custom_call" | custom-call | tf_op jit(solution)/shard_map/pick/pallas_call | solution.py:228
  22.0 0.0 copy-start.3
  22.0 0.1 collective-permute-start.17
  22.1 1.8 %collective-permute-start.18 = (bf16[5,256,128]{2,1,0:T(8,128)(2,1)S(1)}, bf16[5,256,128]{2,1,0:T(8,128)(2,1)S(1)}, u32[]{:S(2)}, u32[]{:S(2)}) collective-permute-start(bf16[5,256,128]{2,1,0:T(8,128)(2,1)S(1)} %get-tuple-element.35), channel_id=1, source_target_pairs={{0,16},{8,24},{16,0},{24,8},{1,17},{9,25},{17,1},{25,9},{2,18},{10... | collective-permute-start | bytes 983048 | tf_op jit(solution)/shard_map/ppermute | solution.py:239
  23.8 13.8 %collective-permute-done.8.refs_11_ = bf16[5,256,128]{2,1,0:T(8,128)(2,1)S(1)} collective-permute-done((bf16[5,256,128]{2,1,0:T(8,128)(2,1)S(1)}, bf16[5,256,128]{2,1,0:T(8,128)(2,1)S(1)}, u32[]{:S(2)}, u32[]{:S(2)}) %collective-permute-start.8) | collective-permute-done | bytes 327712 | tf_op jit(solution)/shard_map/ppermute | solution.py:239
  37.7 1.2 collective-permute-start.13
  38.9 3.5 %collective-permute-done.17.refs_10_ = bf16[5,256,128]{2,1,0:T(8,128)(2,1)S(1)} collective-permute-done((bf16[5,256,128]{2,1,0:T(8,128)(2,1)S(1)}, bf16[5,256,128]{2,1,0:T(8,128)(2,1)S(1)}, u32[]{:S(2)}, u32[]{:S(2)}) %collective-permute-start.17) | collective-permute-done | bytes 327712 | tf_op jit(solution)/shard_map/ppermute | solution.py:239
  42.4 3.1 %collective-permute-start.2 = (bf16[5,256,128]{2,1,0:T(8,128)(2,1)S(1)}, bf16[5,256,128]{2,1,0:T(8,128)(2,1)S(1)}, u32[]{:S(2)}, u32[]{:S(2)}) collective-permute-start(bf16[5,256,128]{2,1,0:T(8,128)(2,1)S(1)} %collective-permute-done.1.refs_3_), channel_id=1, source_target_pairs={{0,1},{1,0},{2,3},{3,2},{4,5},{5,4},{6,7},{7,6},{8,9},{9,8},{10,11... | collective-permute-start | bytes 983048 | tf_op jit(solution)/shard_map/ppermute | solution.py:258
  45.5 19.1 %collective-permute-done.18.refs_11_ = bf16[5,256,128]{2,1,0:T(8,128)(2,1)S(1)} collective-permute-done((bf16[5,256,128]{2,1,0:T(8,128)(2,1)S(1)}, bf16[5,256,128]{2,1,0:T(8,128)(2,1)S(1)}, u32[]{:S(2)}, u32[]{:S(2)}) %collective-permute-start.18) | collective-permute-done | bytes 327712 | tf_op jit(solution)/shard_map/ppermute | solution.py:239
  64.6 0.5 collective-permute-start.4
  65.1 0.0 collective-permute-start.6
  65.1 0.5 collective-permute-start.10
  65.6 0.1 collective-permute-start.12
  65.7 0.4 collective-permute-start.14
  66.1 0.2 collective-permute-done.4.refs_6_
  66.3 0.4 collective-permute-start.16
  66.7 0.1 collective-permute-done.6.refs_8_
  66.8 1.3 %collective-permute-start.19 = (bf16[5,256,128]{2,1,0:T(8,128)(2,1)S(1)}, bf16[5,256,128]{2,1,0:T(8,128)(2,1)S(1)}, u32[]{:S(2)}, u32[]{:S(2)}) collective-permute-start(bf16[5,256,128]{2,1,0:T(8,128)(2,1)S(1)} %get-tuple-element.36), channel_id=1, source_target_pairs={{0,24},{8,0},{16,8},{24,16},{1,25},{9,1},{17,9},{25,17},{2,26},{10... | collective-permute-start | bytes 983048 | tf_op jit(solution)/shard_map/ppermute | solution.py:239
  68.1 1.4 %pick.5 = (bf16[2,256,128]{2,1,0:T(8,128)(2,1)S(1)}, bf16[2,256,128]{2,1,0:T(8,128)(2,1)S(1)}, bf16[2,256,128]{2,1,0:T(8,128)(2,1)S(1)}, bf16[2,256,128]{2,1,0:T(8,128)(2,1)S(1)}) custom-call(s32[4,2,12]{2,1,0:T(2,128)S(1)} %bitcast.28, bf16[4,47,64,128]{3,2,1,0:T(8,128)(2,1)S(1)} %bitcast.24), custom_call_target="tpu_custom_call" | custom-call | tf_op jit(solution)/shard_map/pick/pallas_call | solution.py:228
  69.6 2.2 %cycle.3 = (bf16[5,128,128]{2,1,0:T(8,128)(2,1)S(1)}, bf16[5,128,128]{2,1,0:T(8,128)(2,1)S(1)}) custom-call(s32[4]{0:T(128)S(1)} %copy-done.3, bf16[5,256,128]{2,1,0:T(8,128)(2,1)S(1)} %get-tuple-element.25.refs_1_, bf16[5,256,128]{2,1,0:T(8,128)(2,1)S(1)} %collective-permute-done.refs_2_, bf16[5,256,128]{2,1,0:T(8,128)(2,1)S(1)} %collective-permute-done.1.refs_3_, ...), custom_call_target="tpu_custom_call" | custom-call | tf_op jit(solution)/shard_map/cycle/pallas_call | solution.py:264
  71.8 8.4 %collective-permute-done.19.refs_12_ = bf16[5,256,128]{2,1,0:T(8,128)(2,1)S(1)} collective-permute-done((bf16[5,256,128]{2,1,0:T(8,128)(2,1)S(1)}, bf16[5,256,128]{2,1,0:T(8,128)(2,1)S(1)}, u32[]{:S(2)}, u32[]{:S(2)}) %collective-permute-start.19) | collective-permute-done | bytes 327712 | tf_op jit(solution)/shard_map/ppermute | solution.py:239
  80.2 1.2 collective-permute-start.20
  81.4 1.2 collective-permute-start.29
  82.7 2.2 %cycle.4 = (bf16[5,128,128]{2,1,0:T(8,128)(2,1)S(1)}, bf16[5,128,128]{2,1,0:T(8,128)(2,1)S(1)}) custom-call(s32[4]{0:T(128)S(1)} %copy-done.3, bf16[7,256,128]{2,1,0:T(8,128)(2,1)S(1)} %get-tuple-element.32.refs_1_, bf16[7,256,128]{2,1,0:T(8,128)(2,1)S(1)} %collective-permute-done.10.refs_2_, bf16[7,256,128]{2,1,0:T(8,128)(2,1)S(1)} %collective-permute-done.11.refs_3_, ...), custom_call_target="tpu_custom_call" | custom-call | tf_op jit(solution)/shard_map/cycle/pallas_call | solution.py:264
  84.9 0.3 collective-permute-start.24
  85.2 4.2 %collective-permute-start.28 = (bf16[5,128,128]{2,1,0:T(8,128)(2,1)S(1)}, bf16[5,128,128]{2,1,0:T(8,128)(2,1)S(1)}, u32[]{:S(2)}, u32[]{:S(2)}) collective-permute-start(bf16[5,128,128]{2,1,0:T(8,128)(2,1)S(1)} %get-tuple-element.30.refs_0_), channel_id=1, source_target_pairs={{0,0},{1,1},{2,8},{3,9},{4,16},{5,17},{6,24},{7,25},{8,2},{9,3},{1... | collective-permute-start | bytes 491528 | tf_op jit(solution)/shard_map/ppermute | solution.py:282
  89.4 3.1 %collective-permute-start.22 = (bf16[2,256,128]{2,1,0:T(8,128)(2,1)S(1)}, bf16[2,256,128]{2,1,0:T(8,128)(2,1)S(1)}, u32[]{:S(2)}, u32[]{:S(2)}) collective-permute-start(bf16[2,256,128]{2,1,0:T(8,128)(2,1)S(1)} %get-tuple-element.42), channel_id=1, source_target_pairs={{0,24},{8,0},{16,8},{24,16},{1,25},{9,1},{17,9},{25,17},{2,26},{10... | collective-permute-start | bytes 393224 | tf_op jit(solution)/shard_map/ppermute | solution.py:239
  92.6 1.7 %collective-permute-start.30 = (bf16[5,128,128]{2,1,0:T(8,128)(2,1)S(1)}, bf16[5,128,128]{2,1,0:T(8,128)(2,1)S(1)}, u32[]{:S(2)}, u32[]{:S(2)}) collective-permute-start(bf16[5,128,128]{2,1,0:T(8,128)(2,1)S(1)} %collective-permute-done.29), channel_id=1, source_target_pairs={{4,1},{5,0},{6,9},{7,8},{0,17},{1,16},{2,25},{3,24},{12,3},{13,2},... | collective-permute-start | bytes 491528 | tf_op jit(solution)/shard_map/ppermute | solution.py:282
  94.2 2.4 %collective-permute-start.23 = (bf16[5,128,128]{2,1,0:T(8,128)(2,1)S(1)}, bf16[5,128,128]{2,1,0:T(8,128)(2,1)S(1)}, u32[]{:S(2)}, u32[]{:S(2)}) collective-permute-start(bf16[5,128,128]{2,1,0:T(8,128)(2,1)S(1)} %get-tuple-element.37.refs_2_), channel_id=1, source_target_pairs={{0,0},{1,1},{2,8},{3,9},{4,16},{5,17},{6,24},{7,25},{8,2},{9,3},{1... | collective-permute-start | bytes 491528 | tf_op jit(solution)/shard_map/ppermute | solution.py:282
  96.7 5.6 %collective-permute-start.25 = (bf16[5,128,128]{2,1,0:T(8,128)(2,1)S(1)}, bf16[5,128,128]{2,1,0:T(8,128)(2,1)S(1)}, u32[]{:S(2)}, u32[]{:S(2)}) collective-permute-start(bf16[5,128,128]{2,1,0:T(8,128)(2,1)S(1)} %collective-permute-done.24), channel_id=1, source_target_pairs={{4,1},{5,0},{6,9},{7,8},{0,17},{1,16},{2,25},{3,24},{12,3},{13,2},... | collective-permute-start | bytes 491528 | tf_op jit(solution)/shard_map/ppermute | solution.py:282
  102.3 1.2 cycle.5
  103.5 13.9 %collective-permute-start.26 = (bf16[2,128,128]{2,1,0:T(8,128)(2,1)S(1)}, bf16[2,128,128]{2,1,0:T(8,128)(2,1)S(1)}, u32[]{:S(2)}, u32[]{:S(2)}) collective-permute-start(bf16[2,128,128]{2,1,0:T(8,128)(2,1)S(1)} %get-tuple-element.43.refs_4_), channel_id=1, source_target_pairs={{0,0},{1,1},{2,8},{3,9},{4,16},{5,17},{6,24},{7,25},{8,2},{9,3},{1... | collective-permute-start | bytes 196616 | tf_op jit(solution)/shard_map/ppermute | solution.py:282
  117.4 4.8 %collective-permute-start.27 = (bf16[2,128,128]{2,1,0:T(8,128)(2,1)S(1)}, bf16[2,128,128]{2,1,0:T(8,128)(2,1)S(1)}, u32[]{:S(2)}, u32[]{:S(2)}) collective-permute-start(bf16[2,128,128]{2,1,0:T(8,128)(2,1)S(1)} %get-tuple-element.44.refs_5_), channel_id=1, source_target_pairs={{0,1},{1,0},{2,9},{3,8},{4,17},{5,16},{6,25},{7,24},{8,3},{9,2},{1... | collective-permute-start | bytes 196616 | tf_op jit(solution)/shard_map/ppermute | solution.py:282
  122.2 3.3 %final.1.refs_10_ = f32[4,12,64,128]{3,2,1,0:T(8,128)} custom-call(s32[4,2,12]{2,1,0:T(2,128)S(1)} %bitcast.29, s32[4]{0:T(128)S(1)} %copy-done.3, bf16[5,128,128]{2,1,0:T(8,128)(2,1)S(1)} %get-tuple-element.30.refs_0_, bf16[5,128,128]{2,1,0:T(8,128)(2,1)S(1)} %get-tuple-element.31.refs_1_, bf16[5,128,128]{2,1,0:T(8,128)(2,1)S(1)} %get-tuple-element.37.refs_2_, ...), custom_call_target="tpu_custom_call" | custom-call | tf_op jit(solution)/shard_map/final/pallas_call | solution.py:289
  125.5 2.6 %patch.1 = f32[4,12,64,128]{3,2,1,0:T(8,128)} custom-call(s32[4,2,12]{2,1,0:T(2,128)S(1)} %bitcast.30, s32[4]{0:T(128)S(1)} %copy-done.3, bf16[5,128,128]{2,1,0:T(8,128)(2,1)S(1)} %get-tuple-element.30.refs_0_, bf16[5,128,128]{2,1,0:T(8,128)(2,1)S(1)} %get-tuple-element.31.refs_1_, ...), custom_call_target="tpu_custom_call", output_to_operand_aliasing={{}: (12, {})} | custom-call | tf_op jit(solution)/shard_map/patch/pallas_call | solution.py:301
  (31 shorter events, 0.1 us)
Async XLA Ops:
  0.0 1.1 copy-start.1
  2.3 9.9 %collective-permute-start = (bf16[5,256,128]{2,1,0:T(8,128)(2,1)S(1)}, bf16[5,256,128]{2,1,0:T(8,128)(2,1)S(1)}, u32[]{:S(2)}, u32[]{:S(2)}) collective-permute-start(bf16[5,256,128]{2,1,0:T(8,128)(2,1)S(1)} %get-tuple-element.25.refs_1_), channel_id=1, source_target_pairs={{0,1},{1,0},{2,3},{3,2},{4,5},{5,4},{6,7},{7,6},{8,9},{9,8},{10,11... | collective-permute-start | bytes 983048 | tf_op jit(solution)/shard_map/ppermute | solution.py:258
  3.0 11.5 %collective-permute-start.1 = (bf16[5,256,128]{2,1,0:T(8,128)(2,1)S(1)}, bf16[5,256,128]{2,1,0:T(8,128)(2,1)S(1)}, u32[]{:S(2)}, u32[]{:S(2)}) collective-permute-start(bf16[5,256,128]{2,1,0:T(8,128)(2,1)S(1)} %get-tuple-element.25.refs_1_), channel_id=1, source_target_pairs={{0,2},{1,3},{2,0},{3,1},{4,6},{5,7},{6,4},{7,5},{8,10},{9,11},{10,... | collective-permute-start | bytes 983048 | tf_op jit(solution)/shard_map/ppermute | solution.py:258
  3.0 12.6 %collective-permute-start.3 = (bf16[5,256,128]{2,1,0:T(8,128)(2,1)S(1)}, bf16[5,256,128]{2,1,0:T(8,128)(2,1)S(1)}, u32[]{:S(2)}, u32[]{:S(2)}) collective-permute-start(bf16[5,256,128]{2,1,0:T(8,128)(2,1)S(1)} %get-tuple-element.25.refs_1_), channel_id=1, source_target_pairs={{0,4},{1,5},{2,6},{3,7},{4,0},{5,1},{6,2},{7,3},{8,12},{9,13},{10,... | collective-permute-start | bytes 983048 | tf_op jit(solution)/shard_map/ppermute | solution.py:258
  4.5 17.4 %collective-permute-start.5 = (bf16[5,256,128]{2,1,0:T(8,128)(2,1)S(1)}, bf16[5,256,128]{2,1,0:T(8,128)(2,1)S(1)}, u32[]{:S(2)}, u32[]{:S(2)}) collective-permute-start(bf16[5,256,128]{2,1,0:T(8,128)(2,1)S(1)} %get-tuple-element.25.refs_1_), channel_id=1, source_target_pairs={{0,6},{1,7},{2,4},{3,5},{4,2},{5,3},{6,0},{7,1},{8,14},{9,15},{10,... | collective-permute-start | bytes 983048 | tf_op jit(solution)/shard_map/ppermute | solution.py:258
  5.7 1.9 %copy-start = (bf16[4,2,47,4096]{3,1,2,0:T(2,128)(2,1)S(1)}, bf16[4,2,47,4096]{3,1,2,0:T(2,128)(2,1)}, u32[]{:S(2)}) copy-start(bf16[4,2,47,4096]{3,1,2,0:T(2,128)(2,1)} %param.5) | copy-start | bytes 9240580
  7.6 0.7 copy-start.2
  10.9 11.2 %collective-permute-start.7 = (bf16[5,256,128]{2,1,0:T(8,128)(2,1)S(1)}, bf16[5,256,128]{2,1,0:T(8,128)(2,1)S(1)}, u32[]{:S(2)}, u32[]{:S(2)}) collective-permute-start(bf16[5,256,128]{2,1,0:T(8,128)(2,1)S(1)} %get-tuple-element.27), channel_id=1, source_target_pairs={{0,8},{8,16},{16,24},{24,0},{1,9},{9,17},{17,25},{25,1},{2,10},{10... | collective-permute-start | bytes 983048 | tf_op jit(solution)/shard_map/ppermute | solution.py:239
  12.2 25.4 %collective-permute-start.8 = (bf16[5,256,128]{2,1,0:T(8,128)(2,1)S(1)}, bf16[5,256,128]{2,1,0:T(8,128)(2,1)S(1)}, u32[]{:S(2)}, u32[]{:S(2)}) collective-permute-start(bf16[5,256,128]{2,1,0:T(8,128)(2,1)S(1)} %get-tuple-element.28), channel_id=1, source_target_pairs={{0,16},{8,24},{16,0},{24,8},{1,17},{9,25},{17,1},{25,9},{2,18},{10... | collective-permute-start | bytes 983048 | tf_op jit(solution)/shard_map/ppermute | solution.py:239
  14.5 24.4 %collective-permute-start.9 = (bf16[5,256,128]{2,1,0:T(8,128)(2,1)S(1)}, bf16[5,256,128]{2,1,0:T(8,128)(2,1)S(1)}, u32[]{:S(2)}, u32[]{:S(2)}) collective-permute-start(bf16[5,256,128]{2,1,0:T(8,128)(2,1)S(1)} %get-tuple-element.29), channel_id=1, source_target_pairs={{0,24},{8,0},{16,8},{24,16},{1,25},{9,1},{17,9},{25,17},{2,26},{10... | collective-permute-start | bytes 983048 | tf_op jit(solution)/shard_map/ppermute | solution.py:239
  15.6 49.5 %collective-permute-start.11 = (bf16[7,256,128]{2,1,0:T(8,128)(2,1)S(1)}, bf16[7,256,128]{2,1,0:T(8,128)(2,1)S(1)}, u32[]{:S(2)}, u32[]{:S(2)}) collective-permute-start(bf16[7,256,128]{2,1,0:T(8,128)(2,1)S(1)} %get-tuple-element.32.refs_1_), channel_id=1, source_target_pairs={{0,2},{1,3},{2,0},{3,1},{4,6},{5,7},{6,4},{7,5},{8,10},{9,11},{10,... | collective-permute-start | bytes 1376264 | tf_op jit(solution)/shard_map/ppermute | solution.py:258
  22.0 47.6 %copy-start.3 = (s32[4]{0:T(128)S(1)}, s32[4]{0:T(128)}, u32[]{:S(2)}) copy-start(s32[4]{0:T(128)} %count_ref.3) | copy-start | bytes 52
  22.0 20.4 %collective-permute-start.17 = (bf16[5,256,128]{2,1,0:T(8,128)(2,1)S(1)}, bf16[5,256,128]{2,1,0:T(8,128)(2,1)S(1)}, u32[]{:S(2)}, u32[]{:S(2)}) collective-permute-start(bf16[5,256,128]{2,1,0:T(8,128)(2,1)S(1)} %get-tuple-element.34), channel_id=1, source_target_pairs={{0,8},{8,16},{16,24},{24,0},{1,9},{9,17},{17,25},{25,1},{2,10},{10... | collective-permute-start | bytes 983048 | tf_op jit(solution)/shard_map/ppermute | solution.py:239
  22.1 42.5 %collective-permute-start.18 = (bf16[5,256,128]{2,1,0:T(8,128)(2,1)S(1)}, bf16[5,256,128]{2,1,0:T(8,128)(2,1)S(1)}, u32[]{:S(2)}, u32[]{:S(2)}) collective-permute-start(bf16[5,256,128]{2,1,0:T(8,128)(2,1)S(1)} %get-tuple-element.35), channel_id=1, source_target_pairs={{0,16},{8,24},{16,0},{24,8},{1,17},{9,25},{17,1},{25,9},{2,18},{10... | collective-permute-start | bytes 983048 | tf_op jit(solution)/shard_map/ppermute | solution.py:239
  37.7 27.4 %collective-permute-start.13 = (bf16[7,256,128]{2,1,0:T(8,128)(2,1)S(1)}, bf16[7,256,128]{2,1,0:T(8,128)(2,1)S(1)}, u32[]{:S(2)}, u32[]{:S(2)}) collective-permute-start(bf16[7,256,128]{2,1,0:T(8,128)(2,1)S(1)} %get-tuple-element.32.refs_1_), channel_id=1, source_target_pairs={{0,4},{1,5},{2,6},{3,7},{4,0},{5,1},{6,2},{7,3},{8,12},{9,13},{10,... | collective-permute-start | bytes 1376264 | tf_op jit(solution)/shard_map/ppermute | solution.py:258
  38.9 26.7 %collective-permute-start.15 = (bf16[7,256,128]{2,1,0:T(8,128)(2,1)S(1)}, bf16[7,256,128]{2,1,0:T(8,128)(2,1)S(1)}, u32[]{:S(2)}, u32[]{:S(2)}) collective-permute-start(bf16[7,256,128]{2,1,0:T(8,128)(2,1)S(1)} %get-tuple-element.32.refs_1_), channel_id=1, source_target_pairs={{0,6},{1,7},{2,4},{3,5},{4,2},{5,3},{6,0},{7,1},{8,14},{9,15},{10,... | collective-permute-start | bytes 1376264 | tf_op jit(solution)/shard_map/ppermute | solution.py:258
  42.4 23.3 %collective-permute-start.2 = (bf16[5,256,128]{2,1,0:T(8,128)(2,1)S(1)}, bf16[5,256,128]{2,1,0:T(8,128)(2,1)S(1)}, u32[]{:S(2)}, u32[]{:S(2)}) collective-permute-start(bf16[5,256,128]{2,1,0:T(8,128)(2,1)S(1)} %collective-permute-done.1.refs_3_), channel_id=1, source_target_pairs={{0,1},{1,0},{2,3},{3,2},{4,5},{5,4},{6,7},{7,6},{8,9},{9,8},{10,11... | collective-permute-start | bytes 983048 | tf_op jit(solution)/shard_map/ppermute | solution.py:258
  64.6 1.8 %collective-permute-start.4 = (bf16[5,256,128]{2,1,0:T(8,128)(2,1)S(1)}, bf16[5,256,128]{2,1,0:T(8,128)(2,1)S(1)}, u32[]{:S(2)}, u32[]{:S(2)}) collective-permute-start(bf16[5,256,128]{2,1,0:T(8,128)(2,1)S(1)} %collective-permute-done.3.refs_5_), channel_id=1, source_target_pairs={{0,1},{1,0},{2,3},{3,2},{4,5},{5,4},{6,7},{7,6},{8,9},{9,8},{10,11... | collective-permute-start | bytes 983048 | tf_op jit(solution)/shard_map/ppermute | solution.py:258
  65.1 1.7 %collective-permute-start.6 = (bf16[5,256,128]{2,1,0:T(8,128)(2,1)S(1)}, bf16[5,256,128]{2,1,0:T(8,128)(2,1)S(1)}, u32[]{:S(2)}, u32[]{:S(2)}) collective-permute-start(bf16[5,256,128]{2,1,0:T(8,128)(2,1)S(1)} %collective-permute-done.5.refs_7_), channel_id=1, source_target_pairs={{0,1},{1,0},{2,3},{3,2},{4,5},{5,4},{6,7},{7,6},{8,9},{9,8},{10,11... | collective-permute-start | bytes 983048 | tf_op jit(solution)/shard_map/ppermute | solution.py:258
  65.1 16.3 %collective-permute-start.10 = (bf16[7,256,128]{2,1,0:T(8,128)(2,1)S(1)}, bf16[7,256,128]{2,1,0:T(8,128)(2,1)S(1)}, u32[]{:S(2)}, u32[]{:S(2)}) collective-permute-start(bf16[7,256,128]{2,1,0:T(8,128)(2,1)S(1)} %get-tuple-element.32.refs_1_), channel_id=1, source_target_pairs={{0,1},{1,0},{2,3},{3,2},{4,5},{5,4},{6,7},{7,6},{8,9},{9,8},{10,11... | collective-permute-start | bytes 1376264 | tf_op jit(solution)/shard_map/ppermute | solution.py:258
  65.6 17.0 %collective-permute-start.12 = (bf16[7,256,128]{2,1,0:T(8,128)(2,1)S(1)}, bf16[7,256,128]{2,1,0:T(8,128)(2,1)S(1)}, u32[]{:S(2)}, u32[]{:S(2)}) collective-permute-start(bf16[7,256,128]{2,1,0:T(8,128)(2,1)S(1)} %collective-permute-done.11.refs_3_), channel_id=1, source_target_pairs={{0,1},{1,0},{2,3},{3,2},{4,5},{5,4},{6,7},{7,6},{8,9},{9,8},{10,11... | collective-permute-start | bytes 1376264 | tf_op jit(solution)/shard_map/ppermute | solution.py:258
  65.7 17.0 %collective-permute-start.14 = (bf16[7,256,128]{2,1,0:T(8,128)(2,1)S(1)}, bf16[7,256,128]{2,1,0:T(8,128)(2,1)S(1)}, u32[]{:S(2)}, u32[]{:S(2)}) collective-permute-start(bf16[7,256,128]{2,1,0:T(8,128)(2,1)S(1)} %collective-permute-done.13.refs_5_), channel_id=1, source_target_pairs={{0,1},{1,0},{2,3},{3,2},{4,5},{5,4},{6,7},{7,6},{8,9},{9,8},{10,11... | collective-permute-start | bytes 1376264 | tf_op jit(solution)/shard_map/ppermute | solution.py:258
  66.3 16.3 %collective-permute-start.16 = (bf16[7,256,128]{2,1,0:T(8,128)(2,1)S(1)}, bf16[7,256,128]{2,1,0:T(8,128)(2,1)S(1)}, u32[]{:S(2)}, u32[]{:S(2)}) collective-permute-start(bf16[7,256,128]{2,1,0:T(8,128)(2,1)S(1)} %collective-permute-done.15.refs_7_), channel_id=1, source_target_pairs={{0,1},{1,0},{2,3},{3,2},{4,5},{5,4},{6,7},{7,6},{8,9},{9,8},{10,11... | collective-permute-start | bytes 1376264 | tf_op jit(solution)/shard_map/ppermute | solution.py:258
  66.8 13.4 %collective-permute-start.19 = (bf16[5,256,128]{2,1,0:T(8,128)(2,1)S(1)}, bf16[5,256,128]{2,1,0:T(8,128)(2,1)S(1)}, u32[]{:S(2)}, u32[]{:S(2)}) collective-permute-start(bf16[5,256,128]{2,1,0:T(8,128)(2,1)S(1)} %get-tuple-element.36), channel_id=1, source_target_pairs={{0,24},{8,0},{16,8},{24,16},{1,25},{9,1},{17,9},{25,17},{2,26},{10... | collective-permute-start | bytes 983048 | tf_op jit(solution)/shard_map/ppermute | solution.py:239
  80.2 9.2 %collective-permute-start.20 = (bf16[2,256,128]{2,1,0:T(8,128)(2,1)S(1)}, bf16[2,256,128]{2,1,0:T(8,128)(2,1)S(1)}, u32[]{:S(2)}, u32[]{:S(2)}) collective-permute-start(bf16[2,256,128]{2,1,0:T(8,128)(2,1)S(1)} %get-tuple-element.40), channel_id=1, source_target_pairs={{0,8},{8,16},{16,24},{24,0},{1,9},{9,17},{17,25},{25,1},{2,10},{10... | collective-permute-start | bytes 393224 | tf_op jit(solution)/shard_map/ppermute | solution.py:239
  81.4 11.2 %collective-permute-start.29 = (bf16[5,128,128]{2,1,0:T(8,128)(2,1)S(1)}, bf16[5,128,128]{2,1,0:T(8,128)(2,1)S(1)}, u32[]{:S(2)}, u32[]{:S(2)}) collective-permute-start(bf16[5,128,128]{2,1,0:T(8,128)(2,1)S(1)} %get-tuple-element.31.refs_1_), channel_id=1, source_target_pairs={{0,4},{1,5},{2,6},{3,7},{4,0},{5,1},{6,2},{7,3},{8,12},{9,13},{10,... | collective-permute-start | bytes 491528 | tf_op jit(solution)/shard_map/ppermute | solution.py:281
  84.9 11.8 %collective-permute-start.24 = (bf16[5,128,128]{2,1,0:T(8,128)(2,1)S(1)}, bf16[5,128,128]{2,1,0:T(8,128)(2,1)S(1)}, u32[]{:S(2)}, u32[]{:S(2)}) collective-permute-start(bf16[5,128,128]{2,1,0:T(8,128)(2,1)S(1)} %get-tuple-element.38.refs_3_), channel_id=1, source_target_pairs={{0,4},{1,5},{2,6},{3,7},{4,0},{5,1},{6,2},{7,3},{8,12},{9,13},{10,... | collective-permute-start | bytes 491528 | tf_op jit(solution)/shard_map/ppermute | solution.py:281
  85.2 9.0 %collective-permute-start.21 = (bf16[2,256,128]{2,1,0:T(8,128)(2,1)S(1)}, bf16[2,256,128]{2,1,0:T(8,128)(2,1)S(1)}, u32[]{:S(2)}, u32[]{:S(2)}) collective-permute-start(bf16[2,256,128]{2,1,0:T(8,128)(2,1)S(1)} %get-tuple-element.41), channel_id=1, source_target_pairs={{0,16},{8,24},{16,0},{24,8},{1,17},{9,25},{17,1},{25,9},{2,18},{10... | collective-permute-start | bytes 393224 | tf_op jit(solution)/shard_map/ppermute | solution.py:239
  85.2 32.2 %collective-permute-start.28 = (bf16[5,128,128]{2,1,0:T(8,128)(2,1)S(1)}, bf16[5,128,128]{2,1,0:T(8,128)(2,1)S(1)}, u32[]{:S(2)}, u32[]{:S(2)}) collective-permute-start(bf16[5,128,128]{2,1,0:T(8,128)(2,1)S(1)} %get-tuple-element.30.refs_0_), channel_id=1, source_target_pairs={{0,0},{1,1},{2,8},{3,9},{4,16},{5,17},{6,24},{7,25},{8,2},{9,3},{1... | collective-permute-start | bytes 491528 | tf_op jit(solution)/shard_map/ppermute | solution.py:282
  89.4 12.9 %collective-permute-start.22 = (bf16[2,256,128]{2,1,0:T(8,128)(2,1)S(1)}, bf16[2,256,128]{2,1,0:T(8,128)(2,1)S(1)}, u32[]{:S(2)}, u32[]{:S(2)}) collective-permute-start(bf16[2,256,128]{2,1,0:T(8,128)(2,1)S(1)} %get-tuple-element.42), channel_id=1, source_target_pairs={{0,24},{8,0},{16,8},{24,16},{1,25},{9,1},{17,9},{25,17},{2,26},{10... | collective-permute-start | bytes 393224 | tf_op jit(solution)/shard_map/ppermute | solution.py:239
  92.6 29.7 %collective-permute-start.30 = (bf16[5,128,128]{2,1,0:T(8,128)(2,1)S(1)}, bf16[5,128,128]{2,1,0:T(8,128)(2,1)S(1)}, u32[]{:S(2)}, u32[]{:S(2)}) collective-permute-start(bf16[5,128,128]{2,1,0:T(8,128)(2,1)S(1)} %collective-permute-done.29), channel_id=1, source_target_pairs={{4,1},{5,0},{6,9},{7,8},{0,17},{1,16},{2,25},{3,24},{12,3},{13,2},... | collective-permute-start | bytes 491528 | tf_op jit(solution)/shard_map/ppermute | solution.py:282
  94.2 31.3 %collective-permute-start.23 = (bf16[5,128,128]{2,1,0:T(8,128)(2,1)S(1)}, bf16[5,128,128]{2,1,0:T(8,128)(2,1)S(1)}, u32[]{:S(2)}, u32[]{:S(2)}) collective-permute-start(bf16[5,128,128]{2,1,0:T(8,128)(2,1)S(1)} %get-tuple-element.37.refs_2_), channel_id=1, source_target_pairs={{0,0},{1,1},{2,8},{3,9},{4,16},{5,17},{6,24},{7,25},{8,2},{9,3},{1... | collective-permute-start | bytes 491528 | tf_op jit(solution)/shard_map/ppermute | solution.py:282
  96.7 28.8 %collective-permute-start.25 = (bf16[5,128,128]{2,1,0:T(8,128)(2,1)S(1)}, bf16[5,128,128]{2,1,0:T(8,128)(2,1)S(1)}, u32[]{:S(2)}, u32[]{:S(2)}) collective-permute-start(bf16[5,128,128]{2,1,0:T(8,128)(2,1)S(1)} %collective-permute-done.24), channel_id=1, source_target_pairs={{4,1},{5,0},{6,9},{7,8},{0,17},{1,16},{2,25},{3,24},{12,3},{13,2},... | collective-permute-start | bytes 491528 | tf_op jit(solution)/shard_map/ppermute | solution.py:282
  103.5 22.0 %collective-permute-start.26 = (bf16[2,128,128]{2,1,0:T(8,128)(2,1)S(1)}, bf16[2,128,128]{2,1,0:T(8,128)(2,1)S(1)}, u32[]{:S(2)}, u32[]{:S(2)}) collective-permute-start(bf16[2,128,128]{2,1,0:T(8,128)(2,1)S(1)} %get-tuple-element.43.refs_4_), channel_id=1, source_target_pairs={{0,0},{1,1},{2,8},{3,9},{4,16},{5,17},{6,24},{7,25},{8,2},{9,3},{1... | collective-permute-start | bytes 196616 | tf_op jit(solution)/shard_map/ppermute | solution.py:282
  117.4 8.1 %collective-permute-start.27 = (bf16[2,128,128]{2,1,0:T(8,128)(2,1)S(1)}, bf16[2,128,128]{2,1,0:T(8,128)(2,1)S(1)}, u32[]{:S(2)}, u32[]{:S(2)}) collective-permute-start(bf16[2,128,128]{2,1,0:T(8,128)(2,1)S(1)} %get-tuple-element.44.refs_5_), channel_id=1, source_target_pairs={{0,1},{1,0},{2,9},{3,8},{4,17},{5,16},{6,25},{7,24},{8,3},{9,2},{1... | collective-permute-start | bytes 196616 | tf_op jit(solution)/shard_map/ppermute | solution.py:282

commit v3 on v2

--- a/solution.py
+++ b/solution.py
@@ -11,7 +11,7 @@
 TILE = 64
 LANES = 128
 SPLIT = (5, 5, 2)
-HOPPED = (True, True, False)
+HOPPED = (True, True, True)
 VMEM = pl.BlockSpec(memory_space=pltpu.VMEM)
 SMEM = pl.BlockSpec(memory_space=pltpu.SMEM)
 HBM = pl.BlockSpec(memory_space=pltpu.HBM)
@@ -34,12 +34,10 @@
 def swap(x):
     count = x.shape[0]
     x = x.reshape(count // 8, 8, LANES)
-    z = pltpu.roll(x, TILE, 2)
-    after = pltpu.roll(z, 7, 1)
-    before = pltpu.roll(z, 1, 1)
     odd = lax.broadcasted_iota(jnp.int32, x.shape, 1) % 2
     half = lax.broadcasted_iota(jnp.int32, x.shape, 2) // TILE
-    out = jnp.where(odd == half, x, jnp.where(odd == 0, after, before))
+    other = jnp.where(odd == 0, pltpu.roll(x, 7, 1), pltpu.roll(x, 1, 1))
+    out = jnp.where(odd == half, x, pltpu.roll(other, TILE, 2))
     return out.reshape(count, LANES)
 
 
@@ -56,7 +54,7 @@
             out[s] = swap(x).astype(jnp.bfloat16)
             return 0
 
-        lax.fori_loop(0, size, one, 0)
+        lax.fori_loop(0, size, one, 0, unroll=True)
 
 
 def left_kernel(a_ref, *outs):
@@ -69,7 +67,7 @@
             out[s] = swap(x).astype(jnp.bfloat16)
             return 0
 
-        lax.fori_loop(0, out.shape[0], one, 0)
+        lax.fori_loop(0, out.shape[0], one, 0, unroll=True)
         base += out.shape[0]
 
 

time: 129 us -> 128 us (level)
  the two profiles are of different devices: /device:TPU:3 before, /device:TPU:23 now
where the time goes in v3:
time: 128 us; the launch traced here: 127 us
  waiting for transfers between devices  61.5 us (48%)
  starting transfers between devices  46.6 us (36%)
  Pallas kernels  15.5 us (12%)
  local copies, waits for them, and re-layouts  3.7 us (3%)
    ppermute x9, waiting for transfers between devices, on_device(): got.append(lax.ppermute(picked[shift], 'row', pairs))  41.4 us
    ppermute x6, starting transfers between devices, on_device(): lax.ppermute(block, ('row', 'col'), mirror_pairs(rows, cols, step, hop))  23 us
    ppermute x14, waiting for transfers between devices, on_device(): lax.ppermute(source, 'col', [(c, c ^ step) for c in range(cols)])  14 us
    ppermute x14, starting transfers between devices, on_device(): lax.ppermute(source, 'col', [(c, c ^ step) for c in range(cols)])  10 us
    ppermute x9, starting transfers between devices, on_device(): got.append(lax.ppermute(picked[shift], 'row', pairs))  8.82 us
    ppermute x6, waiting for transfers between devices, on_device(): lax.ppermute(block, ('row', 'col'), mirror_pairs(rows, cols, step, hop))  6.08 us
    pallas_call x3, Pallas kernels, on_device(): pl.pallas_call(functools.partial(cycle_kernel, rows, cols, ratio, base, b...  5.71 us
    ppermute x3, starting transfers between devices, on_device(): lax.ppermute(block, 'col', [(c, c ^ cols // 2) for c in range(cols)])  4.75 us
  transfers between devices with their start and end apart: 32, of which 9 were waited for; matrix products, arithmetic and copies ran while one was open for 0% of the time, Pallas kernels for 10%

profile of v3, /device:TPU:23, one launch (start us, length us, event | category | flops | bytes accessed | tf_op | source)
XLA Modules:
  0.0 127.4 jit_solution(3633889357220337607)
XLA Ops:
  0.0 1.1 copy-done.1
  1.1 0.4 left.1
  1.5 0.7 collective-permute-start
  2.3 0.3 collective-permute-start.1
  2.5 0.2 collective-permute-start.3
  2.7 2.2 %collective-permute-start.5 = (bf16[5,256,128]{2,1,0:T(8,128)(2,1)S(1)}, bf16[5,256,128]{2,1,0:T(8,128)(2,1)S(1)}, u32[]{:S(2)}, u32[]{:S(2)}) collective-permute-start(bf16[5,256,128]{2,1,0:T(8,128)(2,1)S(1)} %get-tuple-element.25.refs_1_), channel_id=1, source_target_pairs={{0,6},{1,7},{2,4},{3,5},{4,2},{5,3},{6,0},{7,1},{8,14},{9,15},{10,... | collective-permute-start | bytes 983048 | tf_op jit(solution)/shard_map/ppermute | solution.py:256
  4.9 1.9 %copy-done = bf16[4,2,47,4096]{3,1,2,0:T(2,128)(2,1)S(1)} copy-done((bf16[4,2,47,4096]{3,1,2,0:T(2,128)(2,1)S(1)}, bf16[4,2,47,4096]{3,1,2,0:T(2,128)(2,1)}, u32[]{:S(2)}) %copy-start) | copy-done | bytes 3080216
  6.8 0.7 copy-done.2
  7.5 1.2 pick.3
  8.7 1.3 %collective-permute-start.7 = (bf16[5,256,128]{2,1,0:T(8,128)(2,1)S(1)}, bf16[5,256,128]{2,1,0:T(8,128)(2,1)S(1)}, u32[]{:S(2)}, u32[]{:S(2)}) collective-permute-start(bf16[5,256,128]{2,1,0:T(8,128)(2,1)S(1)} %get-tuple-element.27), channel_id=1, source_target_pairs={{0,8},{8,16},{16,24},{24,0},{1,9},{9,17},{17,25},{25,1},{2,10},{10... | collective-permute-start | bytes 983048 | tf_op jit(solution)/shard_map/ppermute | solution.py:237
  10.1 1.2 pick.4
  11.3 0.1 collective-permute-start.8
  11.5 1.1 collective-permute-start.9
  12.6 0.3 collective-permute-start.17
  13.0 5.5 %collective-permute-done.5.refs_7_ = bf16[5,256,128]{2,1,0:T(8,128)(2,1)S(1)} collective-permute-done((bf16[5,256,128]{2,1,0:T(8,128)(2,1)S(1)}, bf16[5,256,128]{2,1,0:T(8,128)(2,1)S(1)}, u32[]{:S(2)}, u32[]{:S(2)}) %collective-permute-start.5) | collective-permute-done | bytes 327712 | tf_op jit(solution)/shard_map/ppermute | solution.py:256
  18.5 2.4 %collective-permute-start.19 = (bf16[5,256,128]{2,1,0:T(8,128)(2,1)S(1)}, bf16[5,256,128]{2,1,0:T(8,128)(2,1)S(1)}, u32[]{:S(2)}, u32[]{:S(2)}) collective-permute-start(bf16[5,256,128]{2,1,0:T(8,128)(2,1)S(1)} %get-tuple-element.36), channel_id=1, source_target_pairs={{0,24},{8,0},{16,8},{24,16},{1,25},{9,1},{17,9},{25,17},{2,26},{10... | collective-permute-start | bytes 983048 | tf_op jit(solution)/shard_map/ppermute | solution.py:237
  20.9 11.1 %collective-permute-done.8.refs_11_ = bf16[5,256,128]{2,1,0:T(8,128)(2,1)S(1)} collective-permute-done((bf16[5,256,128]{2,1,0:T(8,128)(2,1)S(1)}, bf16[5,256,128]{2,1,0:T(8,128)(2,1)S(1)}, u32[]{:S(2)}, u32[]{:S(2)}) %collective-permute-start.8) | collective-permute-done | bytes 327712 | tf_op jit(solution)/shard_map/ppermute | solution.py:237
  32.1 0.3 collective-permute-start.11
  32.3 20.1 %collective-permute-done.9.refs_12_ = bf16[5,256,128]{2,1,0:T(8,128)(2,1)S(1)} collective-permute-done((bf16[5,256,128]{2,1,0:T(8,128)(2,1)S(1)}, bf16[5,256,128]{2,1,0:T(8,128)(2,1)S(1)}, u32[]{:S(2)}, u32[]{:S(2)}) %collective-permute-start.9) | collective-permute-done | bytes 327712 | tf_op jit(solution)/shard_map/ppermute | solution.py:237
  52.4 0.2 collective-permute-start.13
  52.7 6.6 %collective-permute-done.17.refs_10_ = bf16[5,256,128]{2,1,0:T(8,128)(2,1)S(1)} collective-permute-done((bf16[5,256,128]{2,1,0:T(8,128)(2,1)S(1)}, bf16[5,256,128]{2,1,0:T(8,128)(2,1)S(1)}, u32[]{:S(2)}, u32[]{:S(2)}) %collective-permute-start.17) | collective-permute-done | bytes 327712 | tf_op jit(solution)/shard_map/ppermute | solution.py:237
  59.3 0.2 collective-permute-start.15
  59.5 3.4 %collective-permute-start.2 = (bf16[5,256,128]{2,1,0:T(8,128)(2,1)S(1)}, bf16[5,256,128]{2,1,0:T(8,128)(2,1)S(1)}, u32[]{:S(2)}, u32[]{:S(2)}) collective-permute-start(bf16[5,256,128]{2,1,0:T(8,128)(2,1)S(1)} %collective-permute-done.1.refs_3_), channel_id=1, source_target_pairs={{0,1},{1,0},{2,3},{3,2},{4,5},{5,4},{6,7},{7,6},{8,9},{9,8},{10,11... | collective-permute-start | bytes 983048 | tf_op jit(solution)/shard_map/ppermute | solution.py:256
  62.9 3.5 %collective-permute-done.19.refs_12_ = bf16[5,256,128]{2,1,0:T(8,128)(2,1)S(1)} collective-permute-done((bf16[5,256,128]{2,1,0:T(8,128)(2,1)S(1)}, bf16[5,256,128]{2,1,0:T(8,128)(2,1)S(1)}, u32[]{:S(2)}, u32[]{:S(2)}) %collective-permute-start.19) | collective-permute-done | bytes 327712 | tf_op jit(solution)/shard_map/ppermute | solution.py:237
  66.5 0.5 collective-permute-start.4
  67.0 6.8 %collective-permute-done.13.refs_5_ = bf16[7,256,128]{2,1,0:T(8,128)(2,1)S(1)} collective-permute-done((bf16[7,256,128]{2,1,0:T(8,128)(2,1)S(1)}, bf16[7,256,128]{2,1,0:T(8,128)(2,1)S(1)}, u32[]{:S(2)}, u32[]{:S(2)}) %collective-permute-start.13) | collective-permute-done | bytes 458784 | tf_op jit(solution)/shard_map/ppermute | solution.py:256
  73.7 1.4 %collective-permute-start.12 = (bf16[7,256,128]{2,1,0:T(8,128)(2,1)S(1)}, bf16[7,256,128]{2,1,0:T(8,128)(2,1)S(1)}, u32[]{:S(2)}, u32[]{:S(2)}) collective-permute-start(bf16[7,256,128]{2,1,0:T(8,128)(2,1)S(1)} %collective-permute-done.11.refs_3_), channel_id=1, source_target_pairs={{0,1},{1,0},{2,3},{3,2},{4,5},{5,4},{6,7},{7,6},{8,9},{9,8},{10,11... | collective-permute-start | bytes 1376264 | tf_op jit(solution)/shard_map/ppermute | solution.py:256
  75.2 0.5 collective-permute-start.16
  75.7 0.1 collective-permute-start.6
  75.8 0.9 pick.5
  76.7 1.7 %collective-permute-done.6.refs_8_ = bf16[5,256,128]{2,1,0:T(8,128)(2,1)S(1)} collective-permute-done((bf16[5,256,128]{2,1,0:T(8,128)(2,1)S(1)}, bf16[5,256,128]{2,1,0:T(8,128)(2,1)S(1)}, u32[]{:S(2)}, u32[]{:S(2)}) %collective-permute-start.6) | collective-permute-done | bytes 327712 | tf_op jit(solution)/shard_map/ppermute | solution.py:256
  78.4 2.2 %cycle.3 = (bf16[5,128,128]{2,1,0:T(8,128)(2,1)S(1)}, bf16[5,128,128]{2,1,0:T(8,128)(2,1)S(1)}) custom-call(s32[4]{0:T(128)S(1)} %copy-done.3, bf16[5,256,128]{2,1,0:T(8,128)(2,1)S(1)} %get-tuple-element.25.refs_1_, bf16[5,256,128]{2,1,0:T(8,128)(2,1)S(1)} %collective-permute-done.refs_2_, bf16[5,256,128]{2,1,0:T(8,128)(2,1)S(1)} %collective-permute-done.1.refs_3_, ...), custom_call_target="tpu_custom_call" | custom-call | tf_op jit(solution)/shard_map/cycle/pallas_call | solution.py:262
  80.7 0.3 collective-permute-start.30
  81.0 2.2 %cycle.4 = (bf16[5,128,128]{2,1,0:T(8,128)(2,1)S(1)}, bf16[5,128,128]{2,1,0:T(8,128)(2,1)S(1)}) custom-call(s32[4]{0:T(128)S(1)} %copy-done.3, bf16[7,256,128]{2,1,0:T(8,128)(2,1)S(1)} %get-tuple-element.32.refs_1_, bf16[7,256,128]{2,1,0:T(8,128)(2,1)S(1)} %collective-permute-done.10.refs_2_, bf16[7,256,128]{2,1,0:T(8,128)(2,1)S(1)} %collective-permute-done.11.refs_3_, ...), custom_call_target="tpu_custom_call" | custom-call | tf_op jit(solution)/shard_map/cycle/pallas_call | solution.py:262
  83.2 1.3 %collective-permute-start.24 = (bf16[5,128,128]{2,1,0:T(8,128)(2,1)S(1)}, bf16[5,128,128]{2,1,0:T(8,128)(2,1)S(1)}, u32[]{:S(2)}, u32[]{:S(2)}) collective-permute-start(bf16[5,128,128]{2,1,0:T(8,128)(2,1)S(1)} %get-tuple-element.38.refs_3_), channel_id=1, source_target_pairs={{0,4},{1,5},{2,6},{3,7},{4,0},{5,1},{6,2},{7,3},{8,12},{9,13},{10,... | collective-permute-start | bytes 491528 | tf_op jit(solution)/shard_map/ppermute | solution.py:279
  84.5 3.4 %collective-permute-start.21 = (bf16[2,256,128]{2,1,0:T(8,128)(2,1)S(1)}, bf16[2,256,128]{2,1,0:T(8,128)(2,1)S(1)}, u32[]{:S(2)}, u32[]{:S(2)}) collective-permute-start(bf16[2,256,128]{2,1,0:T(8,128)(2,1)S(1)} %get-tuple-element.41), channel_id=1, source_target_pairs={{0,16},{8,24},{16,0},{24,8},{1,17},{9,25},{17,1},{25,9},{2,18},{10... | collective-permute-start | bytes 393224 | tf_op jit(solution)/shard_map/ppermute | solution.py:237
  87.9 3.3 %collective-permute-start.29 = (bf16[5,128,128]{2,1,0:T(8,128)(2,1)S(1)}, bf16[5,128,128]{2,1,0:T(8,128)(2,1)S(1)}, u32[]{:S(2)}, u32[]{:S(2)}) collective-permute-start(bf16[5,128,128]{2,1,0:T(8,128)(2,1)S(1)} %get-tuple-element.30.refs_0_), channel_id=1, source_target_pairs={{0,0},{1,1},{2,8},{3,9},{4,16},{5,17},{6,24},{7,25},{8,2},{9,3},{1... | collective-permute-start | bytes 491528 | tf_op jit(solution)/shard_map/ppermute | solution.py:280
  91.3 2.4 %collective-permute-start.31 = (bf16[5,128,128]{2,1,0:T(8,128)(2,1)S(1)}, bf16[5,128,128]{2,1,0:T(8,128)(2,1)S(1)}, u32[]{:S(2)}, u32[]{:S(2)}) collective-permute-start(bf16[5,128,128]{2,1,0:T(8,128)(2,1)S(1)} %collective-permute-done.30), channel_id=1, source_target_pairs={{4,1},{5,0},{6,9},{7,8},{0,17},{1,16},{2,25},{3,24},{12,3},{13,2},... | collective-permute-start | bytes 491528 | tf_op jit(solution)/shard_map/ppermute | solution.py:280
  93.7 8.3 %collective-permute-start.23 = (bf16[5,128,128]{2,1,0:T(8,128)(2,1)S(1)}, bf16[5,128,128]{2,1,0:T(8,128)(2,1)S(1)}, u32[]{:S(2)}, u32[]{:S(2)}) collective-permute-start(bf16[5,128,128]{2,1,0:T(8,128)(2,1)S(1)} %get-tuple-element.37.refs_2_), channel_id=1, source_target_pairs={{0,0},{1,1},{2,8},{3,9},{4,16},{5,17},{6,24},{7,25},{8,2},{9,3},{1... | collective-permute-start | bytes 491528 | tf_op jit(solution)/shard_map/ppermute | solution.py:280
  102.0 3.9 %collective-permute-start.25 = (bf16[5,128,128]{2,1,0:T(8,128)(2,1)S(1)}, bf16[5,128,128]{2,1,0:T(8,128)(2,1)S(1)}, u32[]{:S(2)}, u32[]{:S(2)}) collective-permute-start(bf16[5,128,128]{2,1,0:T(8,128)(2,1)S(1)} %collective-permute-done.24), channel_id=1, source_target_pairs={{4,1},{5,0},{6,9},{7,8},{0,17},{1,16},{2,25},{3,24},{12,3},{13,2},... | collective-permute-start | bytes 491528 | tf_op jit(solution)/shard_map/ppermute | solution.py:280
  105.9 1.2 cycle.5
  107.1 3.2 %collective-permute-start.27 = (bf16[2,128,128]{2,1,0:T(8,128)(2,1)S(1)}, bf16[2,128,128]{2,1,0:T(8,128)(2,1)S(1)}, u32[]{:S(2)}, u32[]{:S(2)}) collective-permute-start(bf16[2,128,128]{2,1,0:T(8,128)(2,1)S(1)} %get-tuple-element.44.refs_5_), channel_id=1, source_target_pairs={{0,4},{1,5},{2,6},{3,7},{4,0},{5,1},{6,2},{7,3},{8,12},{9,13},{10,... | collective-permute-start | bytes 196616 | tf_op jit(solution)/shard_map/ppermute | solution.py:279
  110.3 3.2 %collective-permute-done.29.refs_6_ = bf16[5,128,128]{2,1,0:T(8,128)(2,1)S(1)} collective-permute-done((bf16[5,128,128]{2,1,0:T(8,128)(2,1)S(1)}, bf16[5,128,128]{2,1,0:T(8,128)(2,1)S(1)}, u32[]{:S(2)}, u32[]{:S(2)}) %collective-permute-start.29) | collective-permute-done | bytes 163872 | tf_op jit(solution)/shard_map/ppermute | solution.py:280
  113.5 5.0 %collective-permute-start.26 = (bf16[2,128,128]{2,1,0:T(8,128)(2,1)S(1)}, bf16[2,128,128]{2,1,0:T(8,128)(2,1)S(1)}, u32[]{:S(2)}, u32[]{:S(2)}) collective-permute-start(bf16[2,128,128]{2,1,0:T(8,128)(2,1)S(1)} %get-tuple-element.43.refs_4_), channel_id=1, source_target_pairs={{0,0},{1,1},{2,8},{3,9},{4,16},{5,17},{6,24},{7,25},{8,2},{9,3},{1... | collective-permute-start | bytes 196616 | tf_op jit(solution)/shard_map/ppermute | solution.py:280
  118.5 0.1 collective-permute-start.28
  118.6 3.3 %final.1.refs_10_ = f32[4,12,64,128]{3,2,1,0:T(8,128)} custom-call(s32[4,2,12]{2,1,0:T(2,128)S(1)} %bitcast.29, s32[4]{0:T(128)S(1)} %copy-done.3, bf16[5,128,128]{2,1,0:T(8,128)(2,1)S(1)} %get-tuple-element.30.refs_0_, bf16[5,128,128]{2,1,0:T(8,128)(2,1)S(1)} %get-tuple-element.31.refs_1_, bf16[5,128,128]{2,1,0:T(8,128)(2,1)S(1)} %get-tuple-element.37.refs_2_, ...), custom_call_target="tpu_custom_call" | custom-call | tf_op jit(solution)/shard_map/final/pallas_call | solution.py:287
  121.9 2.9 %collective-permute-done.28.refs_9_ = bf16[2,128,128]{2,1,0:T(8,128)(2,1)S(1)} collective-permute-done((bf16[2,128,128]{2,1,0:T(8,128)(2,1)S(1)}, bf16[2,128,128]{2,1,0:T(8,128)(2,1)S(1)}, u32[]{:S(2)}, u32[]{:S(2)}) %collective-permute-start.28) | collective-permute-done | bytes 65568 | tf_op jit(solution)/shard_map/ppermute | solution.py:280
  124.8 2.6 %patch.1 = f32[4,12,64,128]{3,2,1,0:T(8,128)} custom-call(s32[4,2,12]{2,1,0:T(2,128)S(1)} %bitcast.30, s32[4]{0:T(128)S(1)} %copy-done.3, bf16[5,128,128]{2,1,0:T(8,128)(2,1)S(1)} %get-tuple-element.30.refs_0_, bf16[5,128,128]{2,1,0:T(8,128)(2,1)S(1)} %get-tuple-element.31.refs_1_, ...), custom_call_target="tpu_custom_call", output_to_operand_aliasing={{}: (12, {})} | custom-call | tf_op jit(solution)/shard_map/patch/pallas_call | solution.py:299
  (33 shorter events, 0.2 us)
Async XLA Ops:
  0.0 1.1 copy-start.1
  1.5 9.8 %collective-permute-start = (bf16[5,256,128]{2,1,0:T(8,128)(2,1)S(1)}, bf16[5,256,128]{2,1,0:T(8,128)(2,1)S(1)}, u32[]{:S(2)}, u32[]{:S(2)}) collective-permute-start(bf16[5,256,128]{2,1,0:T(8,128)(2,1)S(1)} %get-tuple-element.25.refs_1_), channel_id=1, source_target_pairs={{0,1},{1,0},{2,3},{3,2},{4,5},{5,4},{6,7},{7,6},{8,9},{9,8},{10,11... | collective-permute-start | bytes 983048 | tf_op jit(solution)/shard_map/ppermute | solution.py:256
  2.3 9.2 %collective-permute-start.1 = (bf16[5,256,128]{2,1,0:T(8,128)(2,1)S(1)}, bf16[5,256,128]{2,1,0:T(8,128)(2,1)S(1)}, u32[]{:S(2)}, u32[]{:S(2)}) collective-permute-start(bf16[5,256,128]{2,1,0:T(8,128)(2,1)S(1)} %get-tuple-element.25.refs_1_), channel_id=1, source_target_pairs={{0,2},{1,3},{2,0},{3,1},{4,6},{5,7},{6,4},{7,5},{8,10},{9,11},{10,... | collective-permute-start | bytes 983048 | tf_op jit(solution)/shard_map/ppermute | solution.py:256
  2.5 10.1 %collective-permute-start.3 = (bf16[5,256,128]{2,1,0:T(8,128)(2,1)S(1)}, bf16[5,256,128]{2,1,0:T(8,128)(2,1)S(1)}, u32[]{:S(2)}, u32[]{:S(2)}) collective-permute-start(bf16[5,256,128]{2,1,0:T(8,128)(2,1)S(1)} %get-tuple-element.25.refs_1_), channel_id=1, source_target_pairs={{0,4},{1,5},{2,6},{3,7},{4,0},{5,1},{6,2},{7,3},{8,12},{9,13},{10,... | collective-permute-start | bytes 983048 | tf_op jit(solution)/shard_map/ppermute | solution.py:256
  2.7 15.7 %collective-permute-start.5 = (bf16[5,256,128]{2,1,0:T(8,128)(2,1)S(1)}, bf16[5,256,128]{2,1,0:T(8,128)(2,1)S(1)}, u32[]{:S(2)}, u32[]{:S(2)}) collective-permute-start(bf16[5,256,128]{2,1,0:T(8,128)(2,1)S(1)} %get-tuple-element.25.refs_1_), channel_id=1, source_target_pairs={{0,6},{1,7},{2,4},{3,5},{4,2},{5,3},{6,0},{7,1},{8,14},{9,15},{10,... | collective-permute-start | bytes 983048 | tf_op jit(solution)/shard_map/ppermute | solution.py:256
  4.9 1.9 %copy-start = (bf16[4,2,47,4096]{3,1,2,0:T(2,128)(2,1)S(1)}, bf16[4,2,47,4096]{3,1,2,0:T(2,128)(2,1)}, u32[]{:S(2)}) copy-start(bf16[4,2,47,4096]{3,1,2,0:T(2,128)(2,1)} %param.5) | copy-start | bytes 9240580
  6.8 0.7 copy-start.2
  8.7 9.8 %collective-permute-start.7 = (bf16[5,256,128]{2,1,0:T(8,128)(2,1)S(1)}, bf16[5,256,128]{2,1,0:T(8,128)(2,1)S(1)}, u32[]{:S(2)}, u32[]{:S(2)}) collective-permute-start(bf16[5,256,128]{2,1,0:T(8,128)(2,1)S(1)} %get-tuple-element.27), channel_id=1, source_target_pairs={{0,8},{8,16},{16,24},{24,0},{1,9},{9,17},{17,25},{25,1},{2,10},{10... | collective-permute-start | bytes 983048 | tf_op jit(solution)/shard_map/ppermute | solution.py:237
  11.3 67.1 %copy-start.3 = (s32[4]{0:T(128)S(1)}, s32[4]{0:T(128)}, u32[]{:S(2)}) copy-start(s32[4]{0:T(128)} %count_ref.3) | copy-start | bytes 52
  11.3 20.7 %collective-permute-start.8 = (bf16[5,256,128]{2,1,0:T(8,128)(2,1)S(1)}, bf16[5,256,128]{2,1,0:T(8,128)(2,1)S(1)}, u32[]{:S(2)}, u32[]{:S(2)}) collective-permute-start(bf16[5,256,128]{2,1,0:T(8,128)(2,1)S(1)} %get-tuple-element.28), channel_id=1, source_target_pairs={{0,16},{8,24},{16,0},{24,8},{1,17},{9,25},{17,1},{25,9},{2,18},{10... | collective-permute-start | bytes 983048 | tf_op jit(solution)/shard_map/ppermute | solution.py:237
  11.5 41.0 %collective-permute-start.9 = (bf16[5,256,128]{2,1,0:T(8,128)(2,1)S(1)}, bf16[5,256,128]{2,1,0:T(8,128)(2,1)S(1)}, u32[]{:S(2)}, u32[]{:S(2)}) collective-permute-start(bf16[5,256,128]{2,1,0:T(8,128)(2,1)S(1)} %get-tuple-element.29), channel_id=1, source_target_pairs={{0,24},{8,0},{16,8},{24,16},{1,25},{9,1},{17,9},{25,17},{2,26},{10... | collective-permute-start | bytes 983048 | tf_op jit(solution)/shard_map/ppermute | solution.py:237
  12.6 46.7 %collective-permute-start.17 = (bf16[5,256,128]{2,1,0:T(8,128)(2,1)S(1)}, bf16[5,256,128]{2,1,0:T(8,128)(2,1)S(1)}, u32[]{:S(2)}, u32[]{:S(2)}) collective-permute-start(bf16[5,256,128]{2,1,0:T(8,128)(2,1)S(1)} %get-tuple-element.34), channel_id=1, source_target_pairs={{0,8},{8,16},{16,24},{24,0},{1,9},{9,17},{17,25},{25,1},{2,10},{10... | collective-permute-start | bytes 983048 | tf_op jit(solution)/shard_map/ppermute | solution.py:237
  18.5 41.0 %collective-permute-start.18 = (bf16[5,256,128]{2,1,0:T(8,128)(2,1)S(1)}, bf16[5,256,128]{2,1,0:T(8,128)(2,1)S(1)}, u32[]{:S(2)}, u32[]{:S(2)}) collective-permute-start(bf16[5,256,128]{2,1,0:T(8,128)(2,1)S(1)} %get-tuple-element.35), channel_id=1, source_target_pairs={{0,16},{8,24},{16,0},{24,8},{1,17},{9,25},{17,1},{25,9},{2,18},{10... | collective-permute-start | bytes 983048 | tf_op jit(solution)/shard_map/ppermute | solution.py:237
  18.5 47.9 %collective-permute-start.19 = (bf16[5,256,128]{2,1,0:T(8,128)(2,1)S(1)}, bf16[5,256,128]{2,1,0:T(8,128)(2,1)S(1)}, u32[]{:S(2)}, u32[]{:S(2)}) collective-permute-start(bf16[5,256,128]{2,1,0:T(8,128)(2,1)S(1)} %get-tuple-element.36), channel_id=1, source_target_pairs={{0,24},{8,0},{16,8},{24,16},{1,25},{9,1},{17,9},{25,17},{2,26},{10... | collective-permute-start | bytes 983048 | tf_op jit(solution)/shard_map/ppermute | solution.py:237
  32.1 34.9 %collective-permute-start.11 = (bf16[7,256,128]{2,1,0:T(8,128)(2,1)S(1)}, bf16[7,256,128]{2,1,0:T(8,128)(2,1)S(1)}, u32[]{:S(2)}, u32[]{:S(2)}) collective-permute-start(bf16[7,256,128]{2,1,0:T(8,128)(2,1)S(1)} %get-tuple-element.32.refs_1_), channel_id=1, source_target_pairs={{0,2},{1,3},{2,0},{3,1},{4,6},{5,7},{6,4},{7,5},{8,10},{9,11},{10,... | collective-permute-start | bytes 1376264 | tf_op jit(solution)/shard_map/ppermute | solution.py:256
  52.4 21.3 %collective-permute-start.13 = (bf16[7,256,128]{2,1,0:T(8,128)(2,1)S(1)}, bf16[7,256,128]{2,1,0:T(8,128)(2,1)S(1)}, u32[]{:S(2)}, u32[]{:S(2)}) collective-permute-start(bf16[7,256,128]{2,1,0:T(8,128)(2,1)S(1)} %get-tuple-element.32.refs_1_), channel_id=1, source_target_pairs={{0,4},{1,5},{2,6},{3,7},{4,0},{5,1},{6,2},{7,3},{8,12},{9,13},{10,... | collective-permute-start | bytes 1376264 | tf_op jit(solution)/shard_map/ppermute | solution.py:256
  59.3 15.9 %collective-permute-start.15 = (bf16[7,256,128]{2,1,0:T(8,128)(2,1)S(1)}, bf16[7,256,128]{2,1,0:T(8,128)(2,1)S(1)}, u32[]{:S(2)}, u32[]{:S(2)}) collective-permute-start(bf16[7,256,128]{2,1,0:T(8,128)(2,1)S(1)} %get-tuple-element.32.refs_1_), channel_id=1, source_target_pairs={{0,6},{1,7},{2,4},{3,5},{4,2},{5,3},{6,0},{7,1},{8,14},{9,15},{10,... | collective-permute-start | bytes 1376264 | tf_op jit(solution)/shard_map/ppermute | solution.py:256
  59.5 15.7 %collective-permute-start.2 = (bf16[5,256,128]{2,1,0:T(8,128)(2,1)S(1)}, bf16[5,256,128]{2,1,0:T(8,128)(2,1)S(1)}, u32[]{:S(2)}, u32[]{:S(2)}) collective-permute-start(bf16[5,256,128]{2,1,0:T(8,128)(2,1)S(1)} %collective-permute-done.1.refs_3_), channel_id=1, source_target_pairs={{0,1},{1,0},{2,3},{3,2},{4,5},{5,4},{6,7},{7,6},{8,9},{9,8},{10,11... | collective-permute-start | bytes 983048 | tf_op jit(solution)/shard_map/ppermute | solution.py:256
  66.5 9.2 %collective-permute-start.4 = (bf16[5,256,128]{2,1,0:T(8,128)(2,1)S(1)}, bf16[5,256,128]{2,1,0:T(8,128)(2,1)S(1)}, u32[]{:S(2)}, u32[]{:S(2)}) collective-permute-start(bf16[5,256,128]{2,1,0:T(8,128)(2,1)S(1)} %collective-permute-done.3.refs_5_), channel_id=1, source_target_pairs={{0,1},{1,0},{2,3},{3,2},{4,5},{5,4},{6,7},{7,6},{8,9},{9,8},{10,11... | collective-permute-start | bytes 983048 | tf_op jit(solution)/shard_map/ppermute | solution.py:256
  67.0 13.7 %collective-permute-start.10 = (bf16[7,256,128]{2,1,0:T(8,128)(2,1)S(1)}, bf16[7,256,128]{2,1,0:T(8,128)(2,1)S(1)}, u32[]{:S(2)}, u32[]{:S(2)}) collective-permute-start(bf16[7,256,128]{2,1,0:T(8,128)(2,1)S(1)} %get-tuple-element.32.refs_1_), channel_id=1, source_target_pairs={{0,1},{1,0},{2,3},{3,2},{4,5},{5,4},{6,7},{7,6},{8,9},{9,8},{10,11... | collective-permute-start | bytes 1376264 | tf_op jit(solution)/shard_map/ppermute | solution.py:256
  73.7 7.2 %collective-permute-start.12 = (bf16[7,256,128]{2,1,0:T(8,128)(2,1)S(1)}, bf16[7,256,128]{2,1,0:T(8,128)(2,1)S(1)}, u32[]{:S(2)}, u32[]{:S(2)}) collective-permute-start(bf16[7,256,128]{2,1,0:T(8,128)(2,1)S(1)} %collective-permute-done.11.refs_3_), channel_id=1, source_target_pairs={{0,1},{1,0},{2,3},{3,2},{4,5},{5,4},{6,7},{7,6},{8,9},{9,8},{10,11... | collective-permute-start | bytes 1376264 | tf_op jit(solution)/shard_map/ppermute | solution.py:256
  75.2 5.8 %collective-permute-start.14 = (bf16[7,256,128]{2,1,0:T(8,128)(2,1)S(1)}, bf16[7,256,128]{2,1,0:T(8,128)(2,1)S(1)}, u32[]{:S(2)}, u32[]{:S(2)}) collective-permute-start(bf16[7,256,128]{2,1,0:T(8,128)(2,1)S(1)} %collective-permute-done.13.refs_5_), channel_id=1, source_target_pairs={{0,1},{1,0},{2,3},{3,2},{4,5},{5,4},{6,7},{7,6},{8,9},{9,8},{10,11... | collective-permute-start | bytes 1376264 | tf_op jit(solution)/shard_map/ppermute | solution.py:256
  75.2 5.8 %collective-permute-start.16 = (bf16[7,256,128]{2,1,0:T(8,128)(2,1)S(1)}, bf16[7,256,128]{2,1,0:T(8,128)(2,1)S(1)}, u32[]{:S(2)}, u32[]{:S(2)}) collective-permute-start(bf16[7,256,128]{2,1,0:T(8,128)(2,1)S(1)} %collective-permute-done.15.refs_7_), channel_id=1, source_target_pairs={{0,1},{1,0},{2,3},{3,2},{4,5},{5,4},{6,7},{7,6},{8,9},{9,8},{10,11... | collective-permute-start | bytes 1376264 | tf_op jit(solution)/shard_map/ppermute | solution.py:256
  75.7 2.7 %collective-permute-start.6 = (bf16[5,256,128]{2,1,0:T(8,128)(2,1)S(1)}, bf16[5,256,128]{2,1,0:T(8,128)(2,1)S(1)}, u32[]{:S(2)}, u32[]{:S(2)}) collective-permute-start(bf16[5,256,128]{2,1,0:T(8,128)(2,1)S(1)} %collective-permute-done.5.refs_7_), channel_id=1, source_target_pairs={{0,1},{1,0},{2,3},{3,2},{4,5},{5,4},{6,7},{7,6},{8,9},{9,8},{10,11... | collective-permute-start | bytes 983048 | tf_op jit(solution)/shard_map/ppermute | solution.py:256
  78.4 9.5 %collective-permute-start.20 = (bf16[2,256,128]{2,1,0:T(8,128)(2,1)S(1)}, bf16[2,256,128]{2,1,0:T(8,128)(2,1)S(1)}, u32[]{:S(2)}, u32[]{:S(2)}) collective-permute-start(bf16[2,256,128]{2,1,0:T(8,128)(2,1)S(1)} %get-tuple-element.40), channel_id=1, source_target_pairs={{0,8},{8,16},{16,24},{24,0},{1,9},{9,17},{17,25},{25,1},{2,10},{10... | collective-permute-start | bytes 393224 | tf_op jit(solution)/shard_map/ppermute | solution.py:237
  80.7 10.6 %collective-permute-start.30 = (bf16[5,128,128]{2,1,0:T(8,128)(2,1)S(1)}, bf16[5,128,128]{2,1,0:T(8,128)(2,1)S(1)}, u32[]{:S(2)}, u32[]{:S(2)}) collective-permute-start(bf16[5,128,128]{2,1,0:T(8,128)(2,1)S(1)} %get-tuple-element.31.refs_1_), channel_id=1, source_target_pairs={{0,4},{1,5},{2,6},{3,7},{4,0},{5,1},{6,2},{7,3},{8,12},{9,13},{10,... | collective-permute-start | bytes 491528 | tf_op jit(solution)/shard_map/ppermute | solution.py:279
  83.2 18.8 %collective-permute-start.24 = (bf16[5,128,128]{2,1,0:T(8,128)(2,1)S(1)}, bf16[5,128,128]{2,1,0:T(8,128)(2,1)S(1)}, u32[]{:S(2)}, u32[]{:S(2)}) collective-permute-start(bf16[5,128,128]{2,1,0:T(8,128)(2,1)S(1)} %get-tuple-element.38.refs_3_), channel_id=1, source_target_pairs={{0,4},{1,5},{2,6},{3,7},{4,0},{5,1},{6,2},{7,3},{8,12},{9,13},{10,... | collective-permute-start | bytes 491528 | tf_op jit(solution)/shard_map/ppermute | solution.py:279
  84.5 9.2 %collective-permute-start.21 = (bf16[2,256,128]{2,1,0:T(8,128)(2,1)S(1)}, bf16[2,256,128]{2,1,0:T(8,128)(2,1)S(1)}, u32[]{:S(2)}, u32[]{:S(2)}) collective-permute-start(bf16[2,256,128]{2,1,0:T(8,128)(2,1)S(1)} %get-tuple-element.41), channel_id=1, source_target_pairs={{0,16},{8,24},{16,0},{24,8},{1,17},{9,25},{17,1},{25,9},{2,18},{10... | collective-permute-start | bytes 393224 | tf_op jit(solution)/shard_map/ppermute | solution.py:237
  87.9 18.0 %collective-permute-start.22 = (bf16[2,256,128]{2,1,0:T(8,128)(2,1)S(1)}, bf16[2,256,128]{2,1,0:T(8,128)(2,1)S(1)}, u32[]{:S(2)}, u32[]{:S(2)}) collective-permute-start(bf16[2,256,128]{2,1,0:T(8,128)(2,1)S(1)} %get-tuple-element.42), channel_id=1, source_target_pairs={{0,24},{8,0},{16,8},{24,16},{1,25},{9,1},{17,9},{25,17},{2,26},{10... | collective-permute-start | bytes 393224 | tf_op jit(solution)/shard_map/ppermute | solution.py:237
  87.9 25.6 %collective-permute-start.29 = (bf16[5,128,128]{2,1,0:T(8,128)(2,1)S(1)}, bf16[5,128,128]{2,1,0:T(8,128)(2,1)S(1)}, u32[]{:S(2)}, u32[]{:S(2)}) collective-permute-start(bf16[5,128,128]{2,1,0:T(8,128)(2,1)S(1)} %get-tuple-element.30.refs_0_), channel_id=1, source_target_pairs={{0,0},{1,1},{2,8},{3,9},{4,16},{5,17},{6,24},{7,25},{8,2},{9,3},{1... | collective-permute-start | bytes 491528 | tf_op jit(solution)/shard_map/ppermute | solution.py:280
  91.3 27.3 %collective-permute-start.31 = (bf16[5,128,128]{2,1,0:T(8,128)(2,1)S(1)}, bf16[5,128,128]{2,1,0:T(8,128)(2,1)S(1)}, u32[]{:S(2)}, u32[]{:S(2)}) collective-permute-start(bf16[5,128,128]{2,1,0:T(8,128)(2,1)S(1)} %collective-permute-done.30), channel_id=1, source_target_pairs={{4,1},{5,0},{6,9},{7,8},{0,17},{1,16},{2,25},{3,24},{12,3},{13,2},... | collective-permute-start | bytes 491528 | tf_op jit(solution)/shard_map/ppermute | solution.py:280
  93.7 31.1 %collective-permute-start.23 = (bf16[5,128,128]{2,1,0:T(8,128)(2,1)S(1)}, bf16[5,128,128]{2,1,0:T(8,128)(2,1)S(1)}, u32[]{:S(2)}, u32[]{:S(2)}) collective-permute-start(bf16[5,128,128]{2,1,0:T(8,128)(2,1)S(1)} %get-tuple-element.37.refs_2_), channel_id=1, source_target_pairs={{0,0},{1,1},{2,8},{3,9},{4,16},{5,17},{6,24},{7,25},{8,2},{9,3},{1... | collective-permute-start | bytes 491528 | tf_op jit(solution)/shard_map/ppermute | solution.py:280
  102.0 22.8 %collective-permute-start.25 = (bf16[5,128,128]{2,1,0:T(8,128)(2,1)S(1)}, bf16[5,128,128]{2,1,0:T(8,128)(2,1)S(1)}, u32[]{:S(2)}, u32[]{:S(2)}) collective-permute-start(bf16[5,128,128]{2,1,0:T(8,128)(2,1)S(1)} %collective-permute-done.24), channel_id=1, source_target_pairs={{4,1},{5,0},{6,9},{7,8},{0,17},{1,16},{2,25},{3,24},{12,3},{13,2},... | collective-permute-start | bytes 491528 | tf_op jit(solution)/shard_map/ppermute | solution.py:280
  107.1 11.4 %collective-permute-start.27 = (bf16[2,128,128]{2,1,0:T(8,128)(2,1)S(1)}, bf16[2,128,128]{2,1,0:T(8,128)(2,1)S(1)}, u32[]{:S(2)}, u32[]{:S(2)}) collective-permute-start(bf16[2,128,128]{2,1,0:T(8,128)(2,1)S(1)} %get-tuple-element.44.refs_5_), channel_id=1, source_target_pairs={{0,4},{1,5},{2,6},{3,7},{4,0},{5,1},{6,2},{7,3},{8,12},{9,13},{10,... | collective-permute-start | bytes 196616 | tf_op jit(solution)/shard_map/ppermute | solution.py:279
  113.5 8.4 %collective-permute-start.26 = (bf16[2,128,128]{2,1,0:T(8,128)(2,1)S(1)}, bf16[2,128,128]{2,1,0:T(8,128)(2,1)S(1)}, u32[]{:S(2)}, u32[]{:S(2)}) collective-permute-start(bf16[2,128,128]{2,1,0:T(8,128)(2,1)S(1)} %get-tuple-element.43.refs_4_), channel_id=1, source_target_pairs={{0,0},{1,1},{2,8},{3,9},{4,16},{5,17},{6,24},{7,25},{8,2},{9,3},{1... | collective-permute-start | bytes 196616 | tf_op jit(solution)/shard_map/ppermute | solution.py:280
  118.5 6.3 %collective-permute-start.28 = (bf16[2,128,128]{2,1,0:T(8,128)(2,1)S(1)}, bf16[2,128,128]{2,1,0:T(8,128)(2,1)S(1)}, u32[]{:S(2)}, u32[]{:S(2)}) collective-permute-start(bf16[2,128,128]{2,1,0:T(8,128)(2,1)S(1)} %collective-permute-done.27), channel_id=1, source_target_pairs={{4,1},{5,0},{6,9},{7,8},{0,17},{1,16},{2,25},{3,24},{12,3},{13,2},... | collective-permute-start | bytes 196616 | tf_op jit(solution)/shard_map/ppermute | solution.py:280

commit v4 on v3

--- a/solution.py
+++ b/solution.py
@@ -10,8 +10,8 @@
 
 TILE = 64
 LANES = 128
-SPLIT = (5, 5, 2)
-HOPPED = (True, True, True)
+SPLIT = (6, 4, 2)
+HOPS = ((1, 3), (0, 2), (0, 2))
 VMEM = pl.BlockSpec(memory_space=pltpu.VMEM)
 SMEM = pl.BlockSpec(memory_space=pltpu.SMEM)
 HBM = pl.BlockSpec(memory_space=pltpu.HBM)
@@ -45,7 +45,7 @@
     my_row = lax.axis_index("row")
     depth = w_ref.shape[0]
     for shift in range(rows):
-        row = lax.rem(my_row + shift, rows)
+        row = my_row ^ shift
         out = outs[shift]
 
         def one(s, _, out=out, row=row):
@@ -82,7 +82,7 @@
     core = lax.rem(my_col, ratio)
     half = total.shape[0] // ratio
     for d, right in enumerate(rights):
-        row = lax.rem(my_row - d + rows, rows)
+        row = my_row ^ d
         for p in range(ratio):
             held[row, p] = right[:, pl.ds(pl.multiple_of((p ^ core) * half, half), half), :]
     my_count = count_ref[my_row]
@@ -200,7 +200,7 @@
     for row in range(rows):
         for col in range(cols):
             part = (col % ratio + step) % ratio
-            held = col ^ (hop * (cols // 2))
+            held = col ^ hop
             pairs.append((row * cols + held, (col // ratio) * cols + row * ratio + part))
     return pairs
 
@@ -211,7 +211,7 @@
     ratio = cols // rows
     occ_row, occ_col, slots, square = amplitudes.shape
     assert occ_col * TILE == LANES and occ_row == ratio * occ_col
-    assert ratio == 2 and cols % 2 == 0 and cols & (cols - 1) == 0
+    assert ratio == 2 and rows & (rows - 1) == 0
     sizes = SPLIT if sum(SPLIT) == slots else (slots - 1, 1)
     tall = occ_row * TILE
     wide = occ_col * TILE
@@ -233,7 +233,7 @@
         )(lists, table)
         got = [picked[0]]
         for shift in range(1, rows):
-            pairs = [(r, (r + shift) % rows) for r in range(rows)]
+            pairs = [(r, r ^ shift) for r in range(rows)]
             got.append(lax.ppermute(picked[shift], "row", pairs))
         rights.append(got)
         base += size
@@ -274,9 +274,10 @@
         owns += sent
         for step in range(ratio):
             block = sent[step]
-            hop = step % 2 if HOPPED[chunk] else 0
+            way = HOPS[chunk][step]
+            hop = (way & 1) * ratio + (way >> 1) * (cols // 2)
             if hop:
-                block = lax.ppermute(block, "col", [(c, c ^ (cols // 2)) for c in range(cols)])
+                block = lax.ppermute(block, "col", [(c, c ^ hop) for c in range(cols)])
             theirs.append(lax.ppermute(block, ("row", "col"), mirror_pairs(rows, cols, step, hop)))
         base += size
 

time: 128 us -> 119 us (0.930)
  the two profiles are of different devices: /device:TPU:23 before, /device:TPU:3 now
where the time goes in v4:
time: 119 us; the launch traced here: 118 us
  starting transfers between devices  69.5 us (58%)
  waiting for transfers between devices  30 us (25%)
  Pallas kernels  15.2 us (13%)
  local copies, waits for them, and re-layouts  3.7 us (3%)
    ppermute x9, starting transfers between devices, on_device(): got.append(lax.ppermute(picked[shift], 'row', pairs))  29.6 us
    ppermute x9, waiting for transfers between devices, on_device(): got.append(lax.ppermute(picked[shift], 'row', pairs))  23.7 us
    ppermute x6, starting transfers between devices, on_device(): lax.ppermute(block, ('row', 'col'), mirror_pairs(rows, cols, step, hop))  22.9 us
    ppermute x14, starting transfers between devices, on_device(): lax.ppermute(source, 'col', [(c, c ^ step) for c in range(cols)])  11.7 us
    ppermute x6, waiting for transfers between devices, on_device(): lax.ppermute(block, ('row', 'col'), mirror_pairs(rows, cols, step, hop))  6.25 us
    pallas_call x3, Pallas kernels, on_device(): pl.pallas_call(functools.partial(cycle_kernel, rows, cols, ratio, base, b...  5.7 us
    ppermute x4, starting transfers between devices, on_device(): block = lax.ppermute(block, 'col', [(c, c ^ hop) for c in range(cols)])  5.25 us
    unnamed x12, local copies, waits for them, and re-layouts  3.7 us
  transfers between devices with their start and end apart: 33, of which 5 were waited for; matrix products, arithmetic and copies ran while one was open for 0% of the time, Pallas kernels for 10%

profile of v4, /device:TPU:3, one launch (start us, length us, event | category | flops | bytes accessed | tf_op | source)
XLA Modules:
  0.0 118.5 jit_solution(3854582415115242998)
XLA Ops:
  0.0 1.1 copy-done.2
  1.1 0.4 left.1
  1.5 0.1 collective-permute-start.11
  1.6 1.5 %collective-permute-start.13 = (bf16[6,256,128]{2,1,0:T(8,128)(2,1)S(1)}, bf16[6,256,128]{2,1,0:T(8,128)(2,1)S(1)}, u32[]{:S(2)}, u32[]{:S(2)}) collective-permute-start(bf16[6,256,128]{2,1,0:T(8,128)(2,1)S(1)} %get-tuple-element.32.refs_1_), channel_id=1, source_target_pairs={{0,4},{1,5},{2,6},{3,7},{4,0},{5,1},{6,2},{7,3},{8,12},{9,13},{10,... | collective-permute-start | bytes 1179656 | tf_op jit(solution)/shard_map/ppermute | solution.py:256
  3.1 1.2 collective-permute-start.15
  4.2 1.9 %copy-done = bf16[4,2,47,4096]{3,1,2,0:T(2,128)(2,1)S(1)} copy-done((bf16[4,2,47,4096]{3,1,2,0:T(2,128)(2,1)S(1)}, bf16[4,2,47,4096]{3,1,2,0:T(2,128)(2,1)}, u32[]{:S(2)}) %copy-start) | copy-done | bytes 3080216
  6.1 0.7 copy-done.3
  6.8 1.1 pick.4
  7.9 1.4 %collective-permute-start.17 = (bf16[4,256,128]{2,1,0:T(8,128)(2,1)S(1)}, bf16[4,256,128]{2,1,0:T(8,128)(2,1)S(1)}, u32[]{:S(2)}, u32[]{:S(2)}) collective-permute-start(bf16[4,256,128]{2,1,0:T(8,128)(2,1)S(1)} %get-tuple-element.34), channel_id=1, source_target_pairs={{0,8},{8,0},{16,24},{24,16},{1,9},{9,1},{17,25},{25,17},{2,10},{10... | collective-permute-start | bytes 786440 | tf_op jit(solution)/shard_map/ppermute | solution.py:237
  9.3 2.3 %collective-permute-start.18 = (bf16[4,256,128]{2,1,0:T(8,128)(2,1)S(1)}, bf16[4,256,128]{2,1,0:T(8,128)(2,1)S(1)}, u32[]{:S(2)}, u32[]{:S(2)}) collective-permute-start(bf16[4,256,128]{2,1,0:T(8,128)(2,1)S(1)} %get-tuple-element.35), channel_id=1, source_target_pairs={{0,16},{8,24},{16,0},{24,8},{1,17},{9,25},{17,1},{25,9},{2,18},{10... | collective-permute-start | bytes 786440 | tf_op jit(solution)/shard_map/ppermute | solution.py:237
  11.6 1.4 %pick.3 = (bf16[6,256,128]{2,1,0:T(8,128)(2,1)S(1)}, bf16[6,256,128]{2,1,0:T(8,128)(2,1)S(1)}, bf16[6,256,128]{2,1,0:T(8,128)(2,1)S(1)}, bf16[6,256,128]{2,1,0:T(8,128)(2,1)S(1)}) custom-call(s32[4,2,12]{2,1,0:T(2,128)S(1)} %bitcast.27, bf16[4,47,64,128]{3,2,1,0:T(8,128)(2,1)S(1)} %bitcast.23), custom_call_target="tpu_custom_call" | custom-call | tf_op jit(solution)/shard_map/pick/pallas_call | solution.py:226
  13.0 6.2 %collective-permute-done.17.refs_10_ = bf16[4,256,128]{2,1,0:T(8,128)(2,1)S(1)} collective-permute-done((bf16[4,256,128]{2,1,0:T(8,128)(2,1)S(1)}, bf16[4,256,128]{2,1,0:T(8,128)(2,1)S(1)}, u32[]{:S(2)}, u32[]{:S(2)}) %collective-permute-start.17) | collective-permute-done | bytes 262176 | tf_op jit(solution)/shard_map/ppermute | solution.py:237
  19.2 4.0 %collective-permute-start.8 = (bf16[6,256,128]{2,1,0:T(8,128)(2,1)S(1)}, bf16[6,256,128]{2,1,0:T(8,128)(2,1)S(1)}, u32[]{:S(2)}, u32[]{:S(2)}) collective-permute-start(bf16[6,256,128]{2,1,0:T(8,128)(2,1)S(1)} %get-tuple-element.28), channel_id=1, source_target_pairs={{0,16},{8,24},{16,0},{24,8},{1,17},{9,25},{17,1},{25,9},{2,18},{10... | collective-permute-start | bytes 1179656 | tf_op jit(solution)/shard_map/ppermute | solution.py:237
  23.2 0.3 collective-permute-start.1
  23.4 1.2 %collective-permute-start.3 = (bf16[6,256,128]{2,1,0:T(8,128)(2,1)S(1)}, bf16[6,256,128]{2,1,0:T(8,128)(2,1)S(1)}, u32[]{:S(2)}, u32[]{:S(2)}) collective-permute-start(bf16[6,256,128]{2,1,0:T(8,128)(2,1)S(1)} %get-tuple-element.25.refs_1_), channel_id=1, source_target_pairs={{0,4},{1,5},{2,6},{3,7},{4,0},{5,1},{6,2},{7,3},{8,12},{9,13},{10,... | collective-permute-start | bytes 1179656 | tf_op jit(solution)/shard_map/ppermute | solution.py:256
  24.7 1.2 collective-permute-start.5
  25.8 10.3 %collective-permute-done.7.refs_10_ = bf16[6,256,128]{2,1,0:T(8,128)(2,1)S(1)} collective-permute-done((bf16[6,256,128]{2,1,0:T(8,128)(2,1)S(1)}, bf16[6,256,128]{2,1,0:T(8,128)(2,1)S(1)}, u32[]{:S(2)}, u32[]{:S(2)}) %collective-permute-start.7) | collective-permute-done | bytes 393248 | tf_op jit(solution)/shard_map/ppermute | solution.py:237
  36.1 4.6 %collective-permute-start.9 = (bf16[6,256,128]{2,1,0:T(8,128)(2,1)S(1)}, bf16[6,256,128]{2,1,0:T(8,128)(2,1)S(1)}, u32[]{:S(2)}, u32[]{:S(2)}) collective-permute-start(bf16[6,256,128]{2,1,0:T(8,128)(2,1)S(1)} %get-tuple-element.29), channel_id=1, source_target_pairs={{0,24},{8,16},{16,8},{24,0},{1,25},{9,17},{17,9},{25,1},{2,26},{10... | collective-permute-start | bytes 1179656 | tf_op jit(solution)/shard_map/ppermute | solution.py:237
  40.7 1.4 %collective-permute-start = (bf16[6,256,128]{2,1,0:T(8,128)(2,1)S(1)}, bf16[6,256,128]{2,1,0:T(8,128)(2,1)S(1)}, u32[]{:S(2)}, u32[]{:S(2)}) collective-permute-start(bf16[6,256,128]{2,1,0:T(8,128)(2,1)S(1)} %get-tuple-element.25.refs_1_), channel_id=1, source_target_pairs={{0,1},{1,0},{2,3},{3,2},{4,5},{5,4},{6,7},{7,6},{8,9},{9,8},{10,11... | collective-permute-start | bytes 1179656 | tf_op jit(solution)/shard_map/ppermute | solution.py:256
  42.1 0.1 collective-permute-start.2
  42.2 0.5 collective-permute-start.4
  42.6 1.4 %collective-permute-start.6 = (bf16[6,256,128]{2,1,0:T(8,128)(2,1)S(1)}, bf16[6,256,128]{2,1,0:T(8,128)(2,1)S(1)}, u32[]{:S(2)}, u32[]{:S(2)}) collective-permute-start(bf16[6,256,128]{2,1,0:T(8,128)(2,1)S(1)} %collective-permute-done.5.refs_7_), channel_id=1, source_target_pairs={{0,1},{1,0},{2,3},{3,2},{4,5},{5,4},{6,7},{7,6},{8,9},{9,8},{10,11... | collective-permute-start | bytes 1179656 | tf_op jit(solution)/shard_map/ppermute | solution.py:256
  44.1 4.6 %collective-permute-done.9.refs_12_ = bf16[6,256,128]{2,1,0:T(8,128)(2,1)S(1)} collective-permute-done((bf16[6,256,128]{2,1,0:T(8,128)(2,1)S(1)}, bf16[6,256,128]{2,1,0:T(8,128)(2,1)S(1)}, u32[]{:S(2)}, u32[]{:S(2)}) %collective-permute-start.9) | collective-permute-done | bytes 393248 | tf_op jit(solution)/shard_map/ppermute | solution.py:237
  48.6 2.3 %collective-permute-start.10 = (bf16[6,256,128]{2,1,0:T(8,128)(2,1)S(1)}, bf16[6,256,128]{2,1,0:T(8,128)(2,1)S(1)}, u32[]{:S(2)}, u32[]{:S(2)}) collective-permute-start(bf16[6,256,128]{2,1,0:T(8,128)(2,1)S(1)} %get-tuple-element.32.refs_1_), channel_id=1, source_target_pairs={{0,1},{1,0},{2,3},{3,2},{4,5},{5,4},{6,7},{7,6},{8,9},{9,8},{10,11... | collective-permute-start | bytes 1179656 | tf_op jit(solution)/shard_map/ppermute | solution.py:256
  50.9 3.3 %collective-permute-start.19 = (bf16[4,256,128]{2,1,0:T(8,128)(2,1)S(1)}, bf16[4,256,128]{2,1,0:T(8,128)(2,1)S(1)}, u32[]{:S(2)}, u32[]{:S(2)}) collective-permute-start(bf16[4,256,128]{2,1,0:T(8,128)(2,1)S(1)} %get-tuple-element.36), channel_id=1, source_target_pairs={{0,24},{8,16},{16,8},{24,0},{1,25},{9,17},{17,9},{25,1},{2,26},{10... | collective-permute-start | bytes 786440 | tf_op jit(solution)/shard_map/ppermute | solution.py:237
  54.3 0.7 collective-permute-start.14
  55.0 0.1 collective-permute-start.16
  55.1 2.6 %cycle.3 = (bf16[6,128,128]{2,1,0:T(8,128)(2,1)S(1)}, bf16[6,128,128]{2,1,0:T(8,128)(2,1)S(1)}) custom-call(s32[4]{0:T(128)S(1)} %copy-done.5, bf16[6,256,128]{2,1,0:T(8,128)(2,1)S(1)} %get-tuple-element.25.refs_1_, bf16[6,256,128]{2,1,0:T(8,128)(2,1)S(1)} %collective-permute-done.refs_2_, bf16[6,256,128]{2,1,0:T(8,128)(2,1)S(1)} %collective-permute-done.1.refs_3_, ...), custom_call_target="tpu_custom_call" | custom-call | tf_op jit(solution)/shard_map/cycle/pallas_call | solution.py:262
  57.6 2.6 %collective-permute-done.19.refs_12_ = bf16[4,256,128]{2,1,0:T(8,128)(2,1)S(1)} collective-permute-done((bf16[4,256,128]{2,1,0:T(8,128)(2,1)S(1)}, bf16[4,256,128]{2,1,0:T(8,128)(2,1)S(1)}, u32[]{:S(2)}, u32[]{:S(2)}) %collective-permute-start.19) | collective-permute-done | bytes 262176 | tf_op jit(solution)/shard_map/ppermute | solution.py:237
  60.3 0.4 collective-permute-start.29
  60.7 2.0 %collective-permute-start.31 = (bf16[6,128,128]{2,1,0:T(8,128)(2,1)S(1)}, bf16[6,128,128]{2,1,0:T(8,128)(2,1)S(1)}, u32[]{:S(2)}, u32[]{:S(2)}) collective-permute-start(bf16[6,128,128]{2,1,0:T(8,128)(2,1)S(1)} %get-tuple-element.31.refs_1_), channel_id=1, source_target_pairs={{0,6},{1,7},{2,4},{3,5},{4,2},{5,3},{6,0},{7,1},{8,14},{9,15},{10,... | collective-permute-start | bytes 589832 | tf_op jit(solution)/shard_map/ppermute | solution.py:280
  62.7 0.9 pick.5
  63.6 11.9 %collective-permute-start.20 = (bf16[2,256,128]{2,1,0:T(8,128)(2,1)S(1)}, bf16[2,256,128]{2,1,0:T(8,128)(2,1)S(1)}, u32[]{:S(2)}, u32[]{:S(2)}) collective-permute-start(bf16[2,256,128]{2,1,0:T(8,128)(2,1)S(1)} %get-tuple-element.40), channel_id=1, source_target_pairs={{0,8},{8,0},{16,24},{24,16},{1,9},{9,1},{17,25},{25,17},{2,10},{10... | collective-permute-start | bytes 393224 | tf_op jit(solution)/shard_map/ppermute | solution.py:237
  75.4 0.9 collective-permute-start.21
  76.3 1.3 %collective-permute-start.22 = (bf16[2,256,128]{2,1,0:T(8,128)(2,1)S(1)}, bf16[2,256,128]{2,1,0:T(8,128)(2,1)S(1)}, u32[]{:S(2)}, u32[]{:S(2)}) collective-permute-start(bf16[2,256,128]{2,1,0:T(8,128)(2,1)S(1)} %get-tuple-element.42), channel_id=1, source_target_pairs={{0,24},{8,16},{16,8},{24,0},{1,25},{9,17},{17,9},{25,1},{2,26},{10... | collective-permute-start | bytes 393224 | tf_op jit(solution)/shard_map/ppermute | solution.py:237
  77.6 1.9 %cycle.4 = (bf16[4,128,128]{2,1,0:T(8,128)(2,1)S(1)}, bf16[4,128,128]{2,1,0:T(8,128)(2,1)S(1)}) custom-call(s32[4]{0:T(128)S(1)} %copy-done.5, bf16[6,256,128]{2,1,0:T(8,128)(2,1)S(1)} %get-tuple-element.32.refs_1_, bf16[6,256,128]{2,1,0:T(8,128)(2,1)S(1)} %collective-permute-done.10.refs_2_, bf16[6,256,128]{2,1,0:T(8,128)(2,1)S(1)} %collective-permute-done.11.refs_3_, ...), custom_call_target="tpu_custom_call" | custom-call | tf_op jit(solution)/shard_map/cycle/pallas_call | solution.py:262
  79.5 0.3 collective-permute-start.30
  79.8 2.2 %collective-permute-start.24 = (bf16[4,128,128]{2,1,0:T(8,128)(2,1)S(1)}, bf16[4,128,128]{2,1,0:T(8,128)(2,1)S(1)}, u32[]{:S(2)}, u32[]{:S(2)}) collective-permute-start(bf16[4,128,128]{2,1,0:T(8,128)(2,1)S(1)} %get-tuple-element.38.refs_3_), channel_id=1, source_target_pairs={{0,4},{1,5},{2,6},{3,7},{4,0},{5,1},{6,2},{7,3},{8,12},{9,13},{10,... | collective-permute-start | bytes 393224 | tf_op jit(solution)/shard_map/ppermute | solution.py:280
  82.0 4.4 %collective-permute-start.32 = (bf16[6,128,128]{2,1,0:T(8,128)(2,1)S(1)}, bf16[6,128,128]{2,1,0:T(8,128)(2,1)S(1)}, u32[]{:S(2)}, u32[]{:S(2)}) collective-permute-start(bf16[6,128,128]{2,1,0:T(8,128)(2,1)S(1)} %collective-permute-done.31), channel_id=1, source_target_pairs={{6,1},{7,0},{4,9},{5,8},{2,17},{3,16},{0,25},{1,24},{14,3},{15,2},... | collective-permute-start | bytes 589832 | tf_op jit(solution)/shard_map/ppermute | solution.py:281
  86.4 1.2 %cycle.5 = (bf16[2,128,128]{2,1,0:T(8,128)(2,1)S(1)}, bf16[2,128,128]{2,1,0:T(8,128)(2,1)S(1)}) custom-call(s32[4]{0:T(128)S(1)} %copy-done.5, bf16[6,256,128]{2,1,0:T(8,128)(2,1)S(1)} %get-tuple-element.32.refs_1_, bf16[6,256,128]{2,1,0:T(8,128)(2,1)S(1)} %collective-permute-done.10.refs_2_, bf16[6,256,128]{2,1,0:T(8,128)(2,1)S(1)} %collective-permute-done.11.refs_3_, ...), custom_call_target="tpu_custom_call" | custom-call | tf_op jit(solution)/shard_map/cycle/pallas_call | solution.py:262
  87.7 0.6 collective-permute-start.27
  88.3 8.4 %collective-permute-start.23 = (bf16[4,128,128]{2,1,0:T(8,128)(2,1)S(1)}, bf16[4,128,128]{2,1,0:T(8,128)(2,1)S(1)}, u32[]{:S(2)}, u32[]{:S(2)}) collective-permute-start(bf16[4,128,128]{2,1,0:T(8,128)(2,1)S(1)} %get-tuple-element.37.refs_2_), channel_id=1, source_target_pairs={{0,0},{1,1},{2,8},{3,9},{4,16},{5,17},{6,24},{7,25},{8,2},{9,3},{1... | collective-permute-start | bytes 393224 | tf_op jit(solution)/shard_map/ppermute | solution.py:281
  96.7 5.2 %collective-permute-start.25 = (bf16[4,128,128]{2,1,0:T(8,128)(2,1)S(1)}, bf16[4,128,128]{2,1,0:T(8,128)(2,1)S(1)}, u32[]{:S(2)}, u32[]{:S(2)}) collective-permute-start(bf16[4,128,128]{2,1,0:T(8,128)(2,1)S(1)} %collective-permute-done.24), channel_id=1, source_target_pairs={{4,1},{5,0},{6,9},{7,8},{0,17},{1,16},{2,25},{3,24},{12,3},{13,2},... | collective-permute-start | bytes 393224 | tf_op jit(solution)/shard_map/ppermute | solution.py:281
  101.9 3.7 %collective-permute-start.26 = (bf16[2,128,128]{2,1,0:T(8,128)(2,1)S(1)}, bf16[2,128,128]{2,1,0:T(8,128)(2,1)S(1)}, u32[]{:S(2)}, u32[]{:S(2)}) collective-permute-start(bf16[2,128,128]{2,1,0:T(8,128)(2,1)S(1)} %get-tuple-element.43.refs_4_), channel_id=1, source_target_pairs={{0,0},{1,1},{2,8},{3,9},{4,16},{5,17},{6,24},{7,25},{8,2},{9,3},{1... | collective-permute-start | bytes 196616 | tf_op jit(solution)/shard_map/ppermute | solution.py:281
  105.7 0.8 collective-permute-start.28
  106.5 3.4 %final.1.refs_10_ = f32[4,12,64,128]{3,2,1,0:T(8,128)} custom-call(s32[4,2,12]{2,1,0:T(2,128)S(1)} %bitcast.29, s32[4]{0:T(128)S(1)} %copy-done.5, bf16[6,128,128]{2,1,0:T(8,128)(2,1)S(1)} %get-tuple-element.30.refs_0_, bf16[6,128,128]{2,1,0:T(8,128)(2,1)S(1)} %get-tuple-element.31.refs_1_, bf16[4,128,128]{2,1,0:T(8,128)(2,1)S(1)} %get-tuple-element.37.refs_2_, ...), custom_call_target="tpu_custom_call" | custom-call | tf_op jit(solution)/shard_map/final/pallas_call | solution.py:288
  109.9 6.2 %collective-permute-done.28.refs_9_ = bf16[2,128,128]{2,1,0:T(8,128)(2,1)S(1)} collective-permute-done((bf16[2,128,128]{2,1,0:T(8,128)(2,1)S(1)}, bf16[2,128,128]{2,1,0:T(8,128)(2,1)S(1)}, u32[]{:S(2)}, u32[]{:S(2)}) %collective-permute-start.28) | collective-permute-done | bytes 65568 | tf_op jit(solution)/shard_map/ppermute | solution.py:281
  116.1 2.4 %patch.1 = f32[4,12,64,128]{3,2,1,0:T(8,128)} custom-call(s32[4,2,12]{2,1,0:T(2,128)S(1)} %bitcast.30, s32[4]{0:T(128)S(1)} %copy-done.5, bf16[6,128,128]{2,1,0:T(8,128)(2,1)S(1)} %get-tuple-element.30.refs_0_, bf16[6,128,128]{2,1,0:T(8,128)(2,1)S(1)} %get-tuple-element.31.refs_1_, ...), custom_call_target="tpu_custom_call", output_to_operand_aliasing={{}: (12, {})} | custom-call | tf_op jit(solution)/shard_map/patch/pallas_call | solution.py:300
  (39 shorter events, 0.1 us)
Async XLA Ops:
  0.0 1.1 copy-start.2
  1.5 21.6 %collective-permute-start.11 = (bf16[6,256,128]{2,1,0:T(8,128)(2,1)S(1)}, bf16[6,256,128]{2,1,0:T(8,128)(2,1)S(1)}, u32[]{:S(2)}, u32[]{:S(2)}) collective-permute-start(bf16[6,256,128]{2,1,0:T(8,128)(2,1)S(1)} %get-tuple-element.32.refs_1_), channel_id=1, source_target_pairs={{0,2},{1,3},{2,0},{3,1},{4,6},{5,7},{6,4},{7,5},{8,10},{9,11},{10,... | collective-permute-start | bytes 1179656 | tf_op jit(solution)/shard_map/ppermute | solution.py:256
  1.6 21.8 %collective-permute-start.13 = (bf16[6,256,128]{2,1,0:T(8,128)(2,1)S(1)}, bf16[6,256,128]{2,1,0:T(8,128)(2,1)S(1)}, u32[]{:S(2)}, u32[]{:S(2)}) collective-permute-start(bf16[6,256,128]{2,1,0:T(8,128)(2,1)S(1)} %get-tuple-element.32.refs_1_), channel_id=1, source_target_pairs={{0,4},{1,5},{2,6},{3,7},{4,0},{5,1},{6,2},{7,3},{8,12},{9,13},{10,... | collective-permute-start | bytes 1179656 | tf_op jit(solution)/shard_map/ppermute | solution.py:256
  3.1 21.6 %collective-permute-start.15 = (bf16[6,256,128]{2,1,0:T(8,128)(2,1)S(1)}, bf16[6,256,128]{2,1,0:T(8,128)(2,1)S(1)}, u32[]{:S(2)}, u32[]{:S(2)}) collective-permute-start(bf16[6,256,128]{2,1,0:T(8,128)(2,1)S(1)} %get-tuple-element.32.refs_1_), channel_id=1, source_target_pairs={{0,6},{1,7},{2,4},{3,5},{4,2},{5,3},{6,0},{7,1},{8,14},{9,15},{10,... | collective-permute-start | bytes 1179656 | tf_op jit(solution)/shard_map/ppermute | solution.py:256
  4.2 1.9 %copy-start = (bf16[4,2,47,4096]{3,1,2,0:T(2,128)(2,1)S(1)}, bf16[4,2,47,4096]{3,1,2,0:T(2,128)(2,1)}, u32[]{:S(2)}) copy-start(bf16[4,2,47,4096]{3,1,2,0:T(2,128)(2,1)} %param.5) | copy-start | bytes 9240580
  6.1 0.7 copy-start.3
  7.9 47.1 %copy-start.5 = (s32[4]{0:T(128)S(1)}, s32[4]{0:T(128)}, u32[]{:S(2)}) copy-start(s32[4]{0:T(128)} %count_ref.3) | copy-start | bytes 52
  7.9 11.2 %collective-permute-start.17 = (bf16[4,256,128]{2,1,0:T(8,128)(2,1)S(1)}, bf16[4,256,128]{2,1,0:T(8,128)(2,1)S(1)}, u32[]{:S(2)}, u32[]{:S(2)}) collective-permute-start(bf16[4,256,128]{2,1,0:T(8,128)(2,1)S(1)} %get-tuple-element.34), channel_id=1, source_target_pairs={{0,8},{8,0},{16,24},{24,16},{1,9},{9,1},{17,25},{25,17},{2,10},{10... | collective-permute-start | bytes 786440 | tf_op jit(solution)/shard_map/ppermute | solution.py:237
  9.3 9.9 %collective-permute-start.18 = (bf16[4,256,128]{2,1,0:T(8,128)(2,1)S(1)}, bf16[4,256,128]{2,1,0:T(8,128)(2,1)S(1)}, u32[]{:S(2)}, u32[]{:S(2)}) collective-permute-start(bf16[4,256,128]{2,1,0:T(8,128)(2,1)S(1)} %get-tuple-element.35), channel_id=1, source_target_pairs={{0,16},{8,24},{16,0},{24,8},{1,17},{9,25},{17,1},{25,9},{2,18},{10... | collective-permute-start | bytes 786440 | tf_op jit(solution)/shard_map/ppermute | solution.py:237
  19.2 16.9 %collective-permute-start.7 = (bf16[6,256,128]{2,1,0:T(8,128)(2,1)S(1)}, bf16[6,256,128]{2,1,0:T(8,128)(2,1)S(1)}, u32[]{:S(2)}, u32[]{:S(2)}) collective-permute-start(bf16[6,256,128]{2,1,0:T(8,128)(2,1)S(1)} %get-tuple-element.27), channel_id=1, source_target_pairs={{0,8},{8,0},{16,24},{24,16},{1,9},{9,1},{17,25},{25,17},{2,10},{10... | collective-permute-start | bytes 1179656 | tf_op jit(solution)/shard_map/ppermute | solution.py:237
  19.2 21.6 %collective-permute-start.8 = (bf16[6,256,128]{2,1,0:T(8,128)(2,1)S(1)}, bf16[6,256,128]{2,1,0:T(8,128)(2,1)S(1)}, u32[]{:S(2)}, u32[]{:S(2)}) collective-permute-start(bf16[6,256,128]{2,1,0:T(8,128)(2,1)S(1)} %get-tuple-element.28), channel_id=1, source_target_pairs={{0,16},{8,24},{16,0},{24,8},{1,17},{9,25},{17,1},{25,9},{2,18},{10... | collective-permute-start | bytes 1179656 | tf_op jit(solution)/shard_map/ppermute | solution.py:237
  23.2 19.0 %collective-permute-start.1 = (bf16[6,256,128]{2,1,0:T(8,128)(2,1)S(1)}, bf16[6,256,128]{2,1,0:T(8,128)(2,1)S(1)}, u32[]{:S(2)}, u32[]{:S(2)}) collective-permute-start(bf16[6,256,128]{2,1,0:T(8,128)(2,1)S(1)} %get-tuple-element.25.refs_1_), channel_id=1, source_target_pairs={{0,2},{1,3},{2,0},{3,1},{4,6},{5,7},{6,4},{7,5},{8,10},{9,11},{10,... | collective-permute-start | bytes 1179656 | tf_op jit(solution)/shard_map/ppermute | solution.py:256
  23.4 18.8 %collective-permute-start.3 = (bf16[6,256,128]{2,1,0:T(8,128)(2,1)S(1)}, bf16[6,256,128]{2,1,0:T(8,128)(2,1)S(1)}, u32[]{:S(2)}, u32[]{:S(2)}) collective-permute-start(bf16[6,256,128]{2,1,0:T(8,128)(2,1)S(1)} %get-tuple-element.25.refs_1_), channel_id=1, source_target_pairs={{0,4},{1,5},{2,6},{3,7},{4,0},{5,1},{6,2},{7,3},{8,12},{9,13},{10,... | collective-permute-start | bytes 1179656 | tf_op jit(solution)/shard_map/ppermute | solution.py:256
  24.7 18.0 %collective-permute-start.5 = (bf16[6,256,128]{2,1,0:T(8,128)(2,1)S(1)}, bf16[6,256,128]{2,1,0:T(8,128)(2,1)S(1)}, u32[]{:S(2)}, u32[]{:S(2)}) collective-permute-start(bf16[6,256,128]{2,1,0:T(8,128)(2,1)S(1)} %get-tuple-element.25.refs_1_), channel_id=1, source_target_pairs={{0,6},{1,7},{2,4},{3,5},{4,2},{5,3},{6,0},{7,1},{8,14},{9,15},{10,... | collective-permute-start | bytes 1179656 | tf_op jit(solution)/shard_map/ppermute | solution.py:256
  36.1 12.5 %collective-permute-start.9 = (bf16[6,256,128]{2,1,0:T(8,128)(2,1)S(1)}, bf16[6,256,128]{2,1,0:T(8,128)(2,1)S(1)}, u32[]{:S(2)}, u32[]{:S(2)}) collective-permute-start(bf16[6,256,128]{2,1,0:T(8,128)(2,1)S(1)} %get-tuple-element.29), channel_id=1, source_target_pairs={{0,24},{8,16},{16,8},{24,0},{1,25},{9,17},{17,9},{25,1},{2,26},{10... | collective-permute-start | bytes 1179656 | tf_op jit(solution)/shard_map/ppermute | solution.py:237
  40.7 10.2 %collective-permute-start = (bf16[6,256,128]{2,1,0:T(8,128)(2,1)S(1)}, bf16[6,256,128]{2,1,0:T(8,128)(2,1)S(1)}, u32[]{:S(2)}, u32[]{:S(2)}) collective-permute-start(bf16[6,256,128]{2,1,0:T(8,128)(2,1)S(1)} %get-tuple-element.25.refs_1_), channel_id=1, source_target_pairs={{0,1},{1,0},{2,3},{3,2},{4,5},{5,4},{6,7},{7,6},{8,9},{9,8},{10,11... | collective-permute-start | bytes 1179656 | tf_op jit(solution)/shard_map/ppermute | solution.py:256
  42.1 8.8 %collective-permute-start.2 = (bf16[6,256,128]{2,1,0:T(8,128)(2,1)S(1)}, bf16[6,256,128]{2,1,0:T(8,128)(2,1)S(1)}, u32[]{:S(2)}, u32[]{:S(2)}) collective-permute-start(bf16[6,256,128]{2,1,0:T(8,128)(2,1)S(1)} %collective-permute-done.1.refs_3_), channel_id=1, source_target_pairs={{0,1},{1,0},{2,3},{3,2},{4,5},{5,4},{6,7},{7,6},{8,9},{9,8},{10,11... | collective-permute-start | bytes 1179656 | tf_op jit(solution)/shard_map/ppermute | solution.py:256
  42.2 12.1 %collective-permute-start.4 = (bf16[6,256,128]{2,1,0:T(8,128)(2,1)S(1)}, bf16[6,256,128]{2,1,0:T(8,128)(2,1)S(1)}, u32[]{:S(2)}, u32[]{:S(2)}) collective-permute-start(bf16[6,256,128]{2,1,0:T(8,128)(2,1)S(1)} %collective-permute-done.3.refs_5_), channel_id=1, source_target_pairs={{0,1},{1,0},{2,3},{3,2},{4,5},{5,4},{6,7},{7,6},{8,9},{9,8},{10,11... | collective-permute-start | bytes 1179656 | tf_op jit(solution)/shard_map/ppermute | solution.py:256
  42.6 12.3 %collective-permute-start.6 = (bf16[6,256,128]{2,1,0:T(8,128)(2,1)S(1)}, bf16[6,256,128]{2,1,0:T(8,128)(2,1)S(1)}, u32[]{:S(2)}, u32[]{:S(2)}) collective-permute-start(bf16[6,256,128]{2,1,0:T(8,128)(2,1)S(1)} %collective-permute-done.5.refs_7_), channel_id=1, source_target_pairs={{0,1},{1,0},{2,3},{3,2},{4,5},{5,4},{6,7},{7,6},{8,9},{9,8},{10,11... | collective-permute-start | bytes 1179656 | tf_op jit(solution)/shard_map/ppermute | solution.py:256
  48.6 12.0 %collective-permute-start.10 = (bf16[6,256,128]{2,1,0:T(8,128)(2,1)S(1)}, bf16[6,256,128]{2,1,0:T(8,128)(2,1)S(1)}, u32[]{:S(2)}, u32[]{:S(2)}) collective-permute-start(bf16[6,256,128]{2,1,0:T(8,128)(2,1)S(1)} %get-tuple-element.32.refs_1_), channel_id=1, source_target_pairs={{0,1},{1,0},{2,3},{3,2},{4,5},{5,4},{6,7},{7,6},{8,9},{9,8},{10,11... | collective-permute-start | bytes 1179656 | tf_op jit(solution)/shard_map/ppermute | solution.py:256
  50.9 12.7 %collective-permute-start.12 = (bf16[6,256,128]{2,1,0:T(8,128)(2,1)S(1)}, bf16[6,256,128]{2,1,0:T(8,128)(2,1)S(1)}, u32[]{:S(2)}, u32[]{:S(2)}) collective-permute-start(bf16[6,256,128]{2,1,0:T(8,128)(2,1)S(1)} %collective-permute-done.11.refs_3_), channel_id=1, source_target_pairs={{0,1},{1,0},{2,3},{3,2},{4,5},{5,4},{6,7},{7,6},{8,9},{9,8},{10,11... | collective-permute-start | bytes 1179656 | tf_op jit(solution)/shard_map/ppermute | solution.py:256
  50.9 9.3 %collective-permute-start.19 = (bf16[4,256,128]{2,1,0:T(8,128)(2,1)S(1)}, bf16[4,256,128]{2,1,0:T(8,128)(2,1)S(1)}, u32[]{:S(2)}, u32[]{:S(2)}) collective-permute-start(bf16[4,256,128]{2,1,0:T(8,128)(2,1)S(1)} %get-tuple-element.36), channel_id=1, source_target_pairs={{0,24},{8,16},{16,8},{24,0},{1,25},{9,17},{17,9},{25,1},{2,26},{10... | collective-permute-start | bytes 786440 | tf_op jit(solution)/shard_map/ppermute | solution.py:237
  54.3 21.2 %collective-permute-start.14 = (bf16[6,256,128]{2,1,0:T(8,128)(2,1)S(1)}, bf16[6,256,128]{2,1,0:T(8,128)(2,1)S(1)}, u32[]{:S(2)}, u32[]{:S(2)}) collective-permute-start(bf16[6,256,128]{2,1,0:T(8,128)(2,1)S(1)} %collective-permute-done.13.refs_5_), channel_id=1, source_target_pairs={{0,1},{1,0},{2,3},{3,2},{4,5},{5,4},{6,7},{7,6},{8,9},{9,8},{10,11... | collective-permute-start | bytes 1179656 | tf_op jit(solution)/shard_map/ppermute | solution.py:256
  55.0 21.4 %collective-permute-start.16 = (bf16[6,256,128]{2,1,0:T(8,128)(2,1)S(1)}, bf16[6,256,128]{2,1,0:T(8,128)(2,1)S(1)}, u32[]{:S(2)}, u32[]{:S(2)}) collective-permute-start(bf16[6,256,128]{2,1,0:T(8,128)(2,1)S(1)} %collective-permute-done.15.refs_7_), channel_id=1, source_target_pairs={{0,1},{1,0},{2,3},{3,2},{4,5},{5,4},{6,7},{7,6},{8,9},{9,8},{10,11... | collective-permute-start | bytes 1179656 | tf_op jit(solution)/shard_map/ppermute | solution.py:256
  55.1 7.6 %copy-start.1 = (bf16[4,2,47,4096]{3,1,2,0:T(2,128)(2,1)S(1)}, bf16[4,2,47,4096]{3,1,2,0:T(2,128)(2,1)}, u32[]{:S(2)}) copy-start(bf16[4,2,47,4096]{3,1,2,0:T(2,128)(2,1)} %param.5) | copy-start | bytes 9240580
  55.1 7.6 %copy-start.4 = (s32[4,12,2]{1,2,0:T(2,128)S(1)}, s32[4,12,2]{1,2,0:T(2,128)}, u32[]{:S(2)}) copy-start(s32[4,12,2]{1,2,0:T(2,128)} %param.6) | copy-start | bytes 1156
  60.3 19.3 %collective-permute-start.29 = (bf16[6,128,128]{2,1,0:T(8,128)(2,1)S(1)}, bf16[6,128,128]{2,1,0:T(8,128)(2,1)S(1)}, u32[]{:S(2)}, u32[]{:S(2)}) collective-permute-start(bf16[6,128,128]{2,1,0:T(8,128)(2,1)S(1)} %get-tuple-element.30.refs_0_), channel_id=1, source_target_pairs={{0,2},{1,3},{2,0},{3,1},{4,6},{5,7},{6,4},{7,5},{8,10},{9,11},{10,... | collective-permute-start | bytes 589832 | tf_op jit(solution)/shard_map/ppermute | solution.py:280
  60.7 21.3 %collective-permute-start.31 = (bf16[6,128,128]{2,1,0:T(8,128)(2,1)S(1)}, bf16[6,128,128]{2,1,0:T(8,128)(2,1)S(1)}, u32[]{:S(2)}, u32[]{:S(2)}) collective-permute-start(bf16[6,128,128]{2,1,0:T(8,128)(2,1)S(1)} %get-tuple-element.31.refs_1_), channel_id=1, source_target_pairs={{0,6},{1,7},{2,4},{3,5},{4,2},{5,3},{6,0},{7,1},{8,14},{9,15},{10,... | collective-permute-start | bytes 589832 | tf_op jit(solution)/shard_map/ppermute | solution.py:280
  63.6 16.2 %collective-permute-start.20 = (bf16[2,256,128]{2,1,0:T(8,128)(2,1)S(1)}, bf16[2,256,128]{2,1,0:T(8,128)(2,1)S(1)}, u32[]{:S(2)}, u32[]{:S(2)}) collective-permute-start(bf16[2,256,128]{2,1,0:T(8,128)(2,1)S(1)} %get-tuple-element.40), channel_id=1, source_target_pairs={{0,8},{8,0},{16,24},{24,16},{1,9},{9,1},{17,25},{25,17},{2,10},{10... | collective-permute-start | bytes 393224 | tf_op jit(solution)/shard_map/ppermute | solution.py:237
  75.4 11.0 %collective-permute-start.21 = (bf16[2,256,128]{2,1,0:T(8,128)(2,1)S(1)}, bf16[2,256,128]{2,1,0:T(8,128)(2,1)S(1)}, u32[]{:S(2)}, u32[]{:S(2)}) collective-permute-start(bf16[2,256,128]{2,1,0:T(8,128)(2,1)S(1)} %get-tuple-element.41), channel_id=1, source_target_pairs={{0,16},{8,24},{16,0},{24,8},{1,17},{9,25},{17,1},{25,9},{2,18},{10... | collective-permute-start | bytes 393224 | tf_op jit(solution)/shard_map/ppermute | solution.py:237
  76.3 10.1 %collective-permute-start.22 = (bf16[2,256,128]{2,1,0:T(8,128)(2,1)S(1)}, bf16[2,256,128]{2,1,0:T(8,128)(2,1)S(1)}, u32[]{:S(2)}, u32[]{:S(2)}) collective-permute-start(bf16[2,256,128]{2,1,0:T(8,128)(2,1)S(1)} %get-tuple-element.42), channel_id=1, source_target_pairs={{0,24},{8,16},{16,8},{24,0},{1,25},{9,17},{17,9},{25,1},{2,26},{10... | collective-permute-start | bytes 393224 | tf_op jit(solution)/shard_map/ppermute | solution.py:237
  79.5 26.1 %collective-permute-start.30 = (bf16[6,128,128]{2,1,0:T(8,128)(2,1)S(1)}, bf16[6,128,128]{2,1,0:T(8,128)(2,1)S(1)}, u32[]{:S(2)}, u32[]{:S(2)}) collective-permute-start(bf16[6,128,128]{2,1,0:T(8,128)(2,1)S(1)} %collective-permute-done.29), channel_id=1, source_target_pairs={{2,0},{3,1},{0,8},{1,9},{6,16},{7,17},{4,24},{5,25},{10,2},{11,3},... | collective-permute-start | bytes 589832 | tf_op jit(solution)/shard_map/ppermute | solution.py:281
  79.8 16.9 %collective-permute-start.24 = (bf16[4,128,128]{2,1,0:T(8,128)(2,1)S(1)}, bf16[4,128,128]{2,1,0:T(8,128)(2,1)S(1)}, u32[]{:S(2)}, u32[]{:S(2)}) collective-permute-start(bf16[4,128,128]{2,1,0:T(8,128)(2,1)S(1)} %get-tuple-element.38.refs_3_), channel_id=1, source_target_pairs={{0,4},{1,5},{2,6},{3,7},{4,0},{5,1},{6,2},{7,3},{8,12},{9,13},{10,... | collective-permute-start | bytes 393224 | tf_op jit(solution)/shard_map/ppermute | solution.py:280
  82.0 24.5 %collective-permute-start.32 = (bf16[6,128,128]{2,1,0:T(8,128)(2,1)S(1)}, bf16[6,128,128]{2,1,0:T(8,128)(2,1)S(1)}, u32[]{:S(2)}, u32[]{:S(2)}) collective-permute-start(bf16[6,128,128]{2,1,0:T(8,128)(2,1)S(1)} %collective-permute-done.31), channel_id=1, source_target_pairs={{6,1},{7,0},{4,9},{5,8},{2,17},{3,16},{0,25},{1,24},{14,3},{15,2},... | collective-permute-start | bytes 589832 | tf_op jit(solution)/shard_map/ppermute | solution.py:281
  87.7 14.2 %collective-permute-start.27 = (bf16[2,128,128]{2,1,0:T(8,128)(2,1)S(1)}, bf16[2,128,128]{2,1,0:T(8,128)(2,1)S(1)}, u32[]{:S(2)}, u32[]{:S(2)}) collective-permute-start(bf16[2,128,128]{2,1,0:T(8,128)(2,1)S(1)} %get-tuple-element.44.refs_5_), channel_id=1, source_target_pairs={{0,4},{1,5},{2,6},{3,7},{4,0},{5,1},{6,2},{7,3},{8,12},{9,13},{10,... | collective-permute-start | bytes 196616 | tf_op jit(solution)/shard_map/ppermute | solution.py:280
  88.3 27.8 %collective-permute-start.23 = (bf16[4,128,128]{2,1,0:T(8,128)(2,1)S(1)}, bf16[4,128,128]{2,1,0:T(8,128)(2,1)S(1)}, u32[]{:S(2)}, u32[]{:S(2)}) collective-permute-start(bf16[4,128,128]{2,1,0:T(8,128)(2,1)S(1)} %get-tuple-element.37.refs_2_), channel_id=1, source_target_pairs={{0,0},{1,1},{2,8},{3,9},{4,16},{5,17},{6,24},{7,25},{8,2},{9,3},{1... | collective-permute-start | bytes 393224 | tf_op jit(solution)/shard_map/ppermute | solution.py:281
  96.7 19.4 %collective-permute-start.25 = (bf16[4,128,128]{2,1,0:T(8,128)(2,1)S(1)}, bf16[4,128,128]{2,1,0:T(8,128)(2,1)S(1)}, u32[]{:S(2)}, u32[]{:S(2)}) collective-permute-start(bf16[4,128,128]{2,1,0:T(8,128)(2,1)S(1)} %collective-permute-done.24), channel_id=1, source_target_pairs={{4,1},{5,0},{6,9},{7,8},{0,17},{1,16},{2,25},{3,24},{12,3},{13,2},... | collective-permute-start | bytes 393224 | tf_op jit(solution)/shard_map/ppermute | solution.py:281
  101.9 8.0 %collective-permute-start.26 = (bf16[2,128,128]{2,1,0:T(8,128)(2,1)S(1)}, bf16[2,128,128]{2,1,0:T(8,128)(2,1)S(1)}, u32[]{:S(2)}, u32[]{:S(2)}) collective-permute-start(bf16[2,128,128]{2,1,0:T(8,128)(2,1)S(1)} %get-tuple-element.43.refs_4_), channel_id=1, source_target_pairs={{0,0},{1,1},{2,8},{3,9},{4,16},{5,17},{6,24},{7,25},{8,2},{9,3},{1... | collective-permute-start | bytes 196616 | tf_op jit(solution)/shard_map/ppermute | solution.py:281
  105.7 10.4 %collective-permute-start.28 = (bf16[2,128,128]{2,1,0:T(8,128)(2,1)S(1)}, bf16[2,128,128]{2,1,0:T(8,128)(2,1)S(1)}, u32[]{:S(2)}, u32[]{:S(2)}) collective-permute-start(bf16[2,128,128]{2,1,0:T(8,128)(2,1)S(1)} %collective-permute-done.27), channel_id=1, source_target_pairs={{4,1},{5,0},{6,9},{7,8},{0,17},{1,16},{2,25},{3,24},{12,3},{13,2},... | collective-permute-start | bytes 196616 | tf_op jit(solution)/shard_map/ppermute | solution.py:281

commit v5 on v4

--- a/solution.py
+++ b/solution.py
@@ -41,12 +41,11 @@
     return out.reshape(count, LANES)
 
 
-def pick_kernel(base, size, rows, list_ref, w_ref, *outs):
+def pick_kernel(base, size, shifts, list_ref, w_ref, *outs):
     my_row = lax.axis_index("row")
     depth = w_ref.shape[0]
-    for shift in range(rows):
+    for shift, out in zip(shifts, outs):
         row = my_row ^ shift
-        out = outs[shift]
 
         def one(s, _, out=out, row=row):
             tile = list_ref[row, 1, base + s]
@@ -80,7 +79,7 @@
     my_row = lax.axis_index("row")
     my_col = lax.axis_index("col")
     core = lax.rem(my_col, ratio)
-    half = total.shape[0] // ratio
+    half = total.shape[1] // ratio
     for d, right in enumerate(rights):
         row = my_row ^ d
         for p in range(ratio):
@@ -96,13 +95,13 @@
             part = jnp.dot(left, right, preferred_element_type=jnp.float32)
             acc = part if acc is None else acc + part
         live = (base + s < my_count).astype(jnp.float32)
-        total[...] = acc * live
+        total[s] = acc * live
         for step in range(ratio):
             part = core ^ step
-            outs[step][s] = total[pl.ds(pl.multiple_of(part * half, half), half), :].astype(jnp.bfloat16)
+            outs[step][s] = total[s, pl.ds(pl.multiple_of(part * half, half), half), :].astype(jnp.bfloat16)
         return 0
 
-    lax.fori_loop(0, size, one, 0)
+    lax.fori_loop(0, size, one, 0, unroll=True)
 
 
 def collect(refs, held, sizes, ratio, core):
@@ -125,7 +124,7 @@
     early = sizes[0]
     owns = refs[: len(sizes) * ratio]
     theirs = refs[len(sizes) * ratio : -3]
-    out_ref, held_own, held_their = refs[-3:]
+    out_ref, table_ref, held_own, held_their = refs[-4:]
     my_row = lax.axis_index("row")
     my_col = lax.axis_index("col")
     core = lax.rem(my_col, ratio)
@@ -135,18 +134,27 @@
     my_count = count_ref[my_row]
     depth = out_ref.shape[0]
 
+    for t in range(slots):
+        table_ref[0, t] = -1
+
     def one(s, _):
         first = list_ref[my_row, 0, s]
         second = list_ref[my_row, 1, s]
         found = jnp.int32(-1)
-        for t in range(early):
+        for t in range(slots):
             hit = (list_ref[partner, 0, t] == second) & (list_ref[partner, 1, t] == first)
             found = jnp.where(hit, t, found)
         use = (s < my_count) & (found >= 0)
 
         @pl.when(use)
         def _():
-            x = summed(held_own, s, held_their, jnp.maximum(found, 0), ratio)
+            table_ref[0, found] = s
+
+        use = use & (found < early)
+
+        @pl.when(use)
+        def _():
+            x = summed(held_own, s, held_their, jnp.where(use, found, 0), ratio)
             out_ref[:, s] = swap(x).reshape(depth, TILE, LANES)
 
         @pl.when(jnp.logical_not(use))
@@ -159,29 +167,20 @@
     lax.fori_loop(0, slots, one, 0)
 
 
-def patch_kernel(ratio, sizes, list_ref, count_ref, *refs):
+def patch_kernel(ratio, sizes, table_ref, *refs):
     slots = sum(sizes)
     early = sizes[0]
     owns = refs[: len(sizes) * ratio]
     theirs = refs[len(sizes) * ratio : -6]
     _, out_ref, held_own, held_their, built, sem = refs[-6:]
-    my_row = lax.axis_index("row")
-    my_col = lax.axis_index("col")
-    core = lax.rem(my_col, ratio)
-    partner = my_col // ratio
+    core = lax.rem(lax.axis_index("col"), ratio)
     collect(owns, held_own, sizes, ratio, core)
     collect(theirs, held_their, sizes[1:], ratio, core)
-    my_count = count_ref[my_row]
     depth = out_ref.shape[0]
     uses, copies = [], []
     for t in range(slots - early):
-        first = list_ref[partner, 0, early + t]
-        second = list_ref[partner, 1, early + t]
-        found = jnp.int32(-1)
-        for s in range(slots):
-            hit = (list_ref[my_row, 0, s] == second) & (list_ref[my_row, 1, s] == first)
-            found = jnp.where(hit, s, found)
-        uses.append((found < my_count) & (found >= 0))
+        found = table_ref[0, early + t]
+        uses.append(found >= 0)
         s = jnp.maximum(found, 0)
         copies.append(pltpu.make_async_copy(built.at[t], out_ref.at[:, s], sem.at[t]))
 
@@ -218,19 +217,23 @@
     lists = jnp.transpose(pair_lists, (0, 2, 1))
     bf16 = jnp.bfloat16
 
-    table = rows_of(integrals)
+    tiles = rows_of(integrals)
 
     rights = []
     base = 0
-    for size in sizes:
-        picked = pl.pallas_call(
-            functools.partial(pick_kernel, base, size, rows),
-            out_shape=[jax.ShapeDtypeStruct((size, tall, wide), bf16)] * rows,
-            in_specs=[SMEM, VMEM],
-            out_specs=[VMEM] * rows,
-            compiler_params=PARAMS,
-            name="pick",
-        )(lists, table)
+    for chunk, size in enumerate(sizes):
+        picked = {}
+        far = rows - 1
+        for shifts in ((far,), range(far)) if chunk == 0 else (range(rows),):
+            new = pl.pallas_call(
+                functools.partial(pick_kernel, base, size, tuple(shifts)),
+                out_shape=[jax.ShapeDtypeStruct((size, tall, wide), bf16)] * len(shifts),
+                in_specs=[SMEM, VMEM],
+                out_specs=[VMEM] * len(shifts),
+                compiler_params=PARAMS,
+                name="pick",
+            )(lists, tiles)
+            picked.update(zip(shifts, new))
         got = [picked[0]]
         for shift in range(1, rows):
             pairs = [(r, r ^ shift) for r in range(rows)]
@@ -266,7 +269,7 @@
             out_specs=[VMEM] * ratio,
             scratch_shapes=[
                 pltpu.VMEM((rows, ratio, size, tall // ratio, wide), bf16),
-                pltpu.VMEM((tall, wide), jnp.float32),
+                pltpu.VMEM((size, tall, wide), jnp.float32),
             ],
             compiler_params=PARAMS,
             name="cycle",
@@ -285,11 +288,11 @@
     block = (tall // ratio, wide)
     split = ratio
     late = slots - sizes[0]
-    out = pl.pallas_call(
+    out, table = pl.pallas_call(
         functools.partial(final_kernel, ratio, sizes),
-        out_shape=out_shape,
+        out_shape=[out_shape, jax.ShapeDtypeStruct((1, slots), jnp.int32)],
         in_specs=[SMEM, SMEM] + [VMEM] * (len(owns) + split),
-        out_specs=VMEM,
+        out_specs=[VMEM, SMEM],
         scratch_shapes=[
             pltpu.VMEM((ratio, slots) + block, bf16),
             pltpu.VMEM((ratio, sizes[0]) + block, bf16),
@@ -300,7 +303,7 @@
     out = pl.pallas_call(
         functools.partial(patch_kernel, ratio, sizes),
         out_shape=out_shape,
-        in_specs=[SMEM, SMEM] + [VMEM] * (len(owns) + len(theirs) - split) + [HBM],
+        in_specs=[SMEM] + [VMEM] * (len(owns) + len(theirs) - split) + [HBM],
         out_specs=HBM,
         scratch_shapes=[
             pltpu.VMEM((ratio, slots) + block, bf16),
@@ -308,10 +311,10 @@
             pltpu.VMEM((late, occ_row, TILE, LANES), jnp.float32),
             pltpu.SemaphoreType.DMA((late,)),
         ],
-        input_output_aliases={2 + len(owns) + len(theirs) - split: 0},
+        input_output_aliases={1 + len(owns) + len(theirs) - split: 0},
         compiler_params=PARAMS,
         name="patch",
-    )(lists, tile_counts, *owns, *theirs[split:], out)
+    )(table, *owns, *theirs[split:], out)
     return tiles_of(out, occ_col)
 
 

time: 119 us -> 118 us (level)
    pallas_call x3, Pallas kernels: 5.7 us -> 4.17 us  [on_device(): pl.pallas_call(functools.partial(cycle_kernel, rows, cols, ratio, base, b...]
    pallas_call x4 -> x5, Pallas kernels: 6.73 us -> 7.56 us  [the longest x4 4.02 us: on_device(): pl.pallas_call(functools.partial(pick_kernel, base, size, tuple(shifts)),...]
    unnamed x12 -> x10, local copies, waits for them, and re-layouts: 3.7 us -> 3.7 us
where the time goes in v5:
time: 118 us
  starting transfers between devices  70 us (59%)
  waiting for transfers between devices  29.9 us (25%)
  Pallas kernels  14.3 us (12%)
  local copies, waits for them, and re-layouts  3.7 us (3%)
    ppermute x9, starting transfers between devices, on_device(): got.append(lax.ppermute(picked[shift], 'row', pairs))  29.6 us
    ppermute x6, starting transfers between devices, on_device(): lax.ppermute(block, ('row', 'col'), mirror_pairs(rows, cols, step, hop))  23.9 us
    ppermute x9, waiting for transfers between devices, on_device(): got.append(lax.ppermute(picked[shift], 'row', pairs))  23.9 us
    ppermute x14, starting transfers between devices, on_device(): lax.ppermute(source, 'col', [(c, c ^ step) for c in range(cols)])  11.7 us
    ppermute x6, waiting for transfers between devices, on_device(): lax.ppermute(block, ('row', 'col'), mirror_pairs(rows, cols, step, hop))  6.02 us
    ppermute x4, starting transfers between devices, on_device(): block = lax.ppermute(block, 'col', [(c, c ^ hop) for c in range(cols)])  4.67 us
    pallas_call x3, Pallas kernels, on_device(): pl.pallas_call(functools.partial(cycle_kernel, rows, cols, ratio, base, b...  4.17 us
    pallas_call x4, Pallas kernels, on_device(): pl.pallas_call(functools.partial(pick_kernel, base, size, tuple(shifts)),...  4.02 us
  transfers between devices with their start and end apart: 33, of which 5 were waited for; matrix products, arithmetic and copies ran while one was open for 0% of the time, Pallas kernels for 10%

profile of v5, /device:TPU:3, one launch (start us, length us, event | category | flops | bytes accessed | tf_op | source)
XLA Modules:
  0.0 118.0 jit_solution(11174201579694658795)
XLA Ops:
  0.0 1.1 copy-done.2
  1.1 0.4 left.1
  1.5 0.1 collective-permute-start.11
  1.6 1.5 %collective-permute-start.13 = (bf16[6,256,128]{2,1,0:T(8,128)(2,1)S(1)}, bf16[6,256,128]{2,1,0:T(8,128)(2,1)S(1)}, u32[]{:S(2)}, u32[]{:S(2)}) collective-permute-start(bf16[6,256,128]{2,1,0:T(8,128)(2,1)S(1)} %get-tuple-element.32.refs_1_), channel_id=1, source_target_pairs={{0,4},{1,5},{2,6},{3,7},{4,0},{5,1},{6,2},{7,3},{8,12},{9,13},{10,... | collective-permute-start | bytes 1179656 | tf_op jit(solution)/shard_map/ppermute | solution.py:259
  3.1 1.2 collective-permute-start.15
  4.2 1.9 %copy-done = bf16[4,2,47,4096]{3,1,2,0:T(2,128)(2,1)S(1)} copy-done((bf16[4,2,47,4096]{3,1,2,0:T(2,128)(2,1)S(1)}, bf16[4,2,47,4096]{3,1,2,0:T(2,128)(2,1)}, u32[]{:S(2)}) %copy-start) | copy-done | bytes 3080216
  6.1 0.7 copy-done.3
  6.8 1.1 pick.6
  7.9 1.4 %collective-permute-start.17 = (bf16[4,256,128]{2,1,0:T(8,128)(2,1)S(1)}, bf16[4,256,128]{2,1,0:T(8,128)(2,1)S(1)}, u32[]{:S(2)}, u32[]{:S(2)}) collective-permute-start(bf16[4,256,128]{2,1,0:T(8,128)(2,1)S(1)} %get-tuple-element.34), channel_id=1, source_target_pairs={{0,8},{8,0},{16,24},{24,16},{1,9},{9,1},{17,25},{25,17},{2,10},{10... | collective-permute-start | bytes 786440 | tf_op jit(solution)/shard_map/ppermute | solution.py:240
  9.3 2.3 %collective-permute-start.18 = (bf16[4,256,128]{2,1,0:T(8,128)(2,1)S(1)}, bf16[4,256,128]{2,1,0:T(8,128)(2,1)S(1)}, u32[]{:S(2)}, u32[]{:S(2)}) collective-permute-start(bf16[4,256,128]{2,1,0:T(8,128)(2,1)S(1)} %get-tuple-element.35), channel_id=1, source_target_pairs={{0,16},{8,24},{16,0},{24,8},{1,17},{9,25},{17,1},{25,9},{2,18},{10... | collective-permute-start | bytes 786440 | tf_op jit(solution)/shard_map/ppermute | solution.py:240
  11.6 1.2 %pick.4 = (bf16[6,256,128]{2,1,0:T(8,128)(2,1)S(1)}, bf16[6,256,128]{2,1,0:T(8,128)(2,1)S(1)}, bf16[6,256,128]{2,1,0:T(8,128)(2,1)S(1)}) custom-call(s32[4,2,12]{2,1,0:T(2,128)S(1)} %bitcast.28, bf16[4,47,64,128]{3,2,1,0:T(8,128)(2,1)S(1)} %bitcast.23), custom_call_target="tpu_custom_call" | custom-call | tf_op jit(solution)/shard_map/pick/pallas_call | solution.py:228
  12.8 6.4 %collective-permute-done.17.refs_10_ = bf16[4,256,128]{2,1,0:T(8,128)(2,1)S(1)} collective-permute-done((bf16[4,256,128]{2,1,0:T(8,128)(2,1)S(1)}, bf16[4,256,128]{2,1,0:T(8,128)(2,1)S(1)}, u32[]{:S(2)}, u32[]{:S(2)}) %collective-permute-start.17) | collective-permute-done | bytes 262176 | tf_op jit(solution)/shard_map/ppermute | solution.py:240
  19.2 4.0 %collective-permute-start.8 = (bf16[6,256,128]{2,1,0:T(8,128)(2,1)S(1)}, bf16[6,256,128]{2,1,0:T(8,128)(2,1)S(1)}, u32[]{:S(2)}, u32[]{:S(2)}) collective-permute-start(bf16[6,256,128]{2,1,0:T(8,128)(2,1)S(1)} %get-tuple-element.29), channel_id=1, source_target_pairs={{0,16},{8,24},{16,0},{24,8},{1,17},{9,25},{17,1},{25,9},{2,18},{10... | collective-permute-start | bytes 1179656 | tf_op jit(solution)/shard_map/ppermute | solution.py:240
  23.1 0.3 collective-permute-start.1
  23.4 1.2 %collective-permute-start.3 = (bf16[6,256,128]{2,1,0:T(8,128)(2,1)S(1)}, bf16[6,256,128]{2,1,0:T(8,128)(2,1)S(1)}, u32[]{:S(2)}, u32[]{:S(2)}) collective-permute-start(bf16[6,256,128]{2,1,0:T(8,128)(2,1)S(1)} %get-tuple-element.26.refs_1_), channel_id=1, source_target_pairs={{0,4},{1,5},{2,6},{3,7},{4,0},{5,1},{6,2},{7,3},{8,12},{9,13},{10,... | collective-permute-start | bytes 1179656 | tf_op jit(solution)/shard_map/ppermute | solution.py:259
  24.6 1.2 collective-permute-start.5
  25.8 0.8 pick.5
  26.6 9.5 %collective-permute-done.7.refs_10_ = bf16[6,256,128]{2,1,0:T(8,128)(2,1)S(1)} collective-permute-done((bf16[6,256,128]{2,1,0:T(8,128)(2,1)S(1)}, bf16[6,256,128]{2,1,0:T(8,128)(2,1)S(1)}, u32[]{:S(2)}, u32[]{:S(2)}) %collective-permute-start.7) | collective-permute-done | bytes 393248 | tf_op jit(solution)/shard_map/ppermute | solution.py:240
  36.1 4.6 %collective-permute-start.9 = (bf16[6,256,128]{2,1,0:T(8,128)(2,1)S(1)}, bf16[6,256,128]{2,1,0:T(8,128)(2,1)S(1)}, u32[]{:S(2)}, u32[]{:S(2)}) collective-permute-start(bf16[6,256,128]{2,1,0:T(8,128)(2,1)S(1)} %pick.5), channel_id=1, source_target_pairs={{0,24},{8,16},{16,8},{24,0},{1,25},{9,17},{17,9},{25,1},{2,26},{10... | collective-permute-start | bytes 1179656 | tf_op jit(solution)/shard_map/ppermute | solution.py:240
  40.7 1.4 %collective-permute-start = (bf16[6,256,128]{2,1,0:T(8,128)(2,1)S(1)}, bf16[6,256,128]{2,1,0:T(8,128)(2,1)S(1)}, u32[]{:S(2)}, u32[]{:S(2)}) collective-permute-start(bf16[6,256,128]{2,1,0:T(8,128)(2,1)S(1)} %get-tuple-element.26.refs_1_), channel_id=1, source_target_pairs={{0,1},{1,0},{2,3},{3,2},{4,5},{5,4},{6,7},{7,6},{8,9},{9,8},{10,11... | collective-permute-start | bytes 1179656 | tf_op jit(solution)/shard_map/ppermute | solution.py:259
  42.2 0.5 collective-permute-start.4
  42.6 1.4 %collective-permute-start.6 = (bf16[6,256,128]{2,1,0:T(8,128)(2,1)S(1)}, bf16[6,256,128]{2,1,0:T(8,128)(2,1)S(1)}, u32[]{:S(2)}, u32[]{:S(2)}) collective-permute-start(bf16[6,256,128]{2,1,0:T(8,128)(2,1)S(1)} %collective-permute-done.5.refs_7_), channel_id=1, source_target_pairs={{0,1},{1,0},{2,3},{3,2},{4,5},{5,4},{6,7},{7,6},{8,9},{9,8},{10,11... | collective-permute-start | bytes 1179656 | tf_op jit(solution)/shard_map/ppermute | solution.py:259
  44.1 4.6 %collective-permute-done.9.refs_12_ = bf16[6,256,128]{2,1,0:T(8,128)(2,1)S(1)} collective-permute-done((bf16[6,256,128]{2,1,0:T(8,128)(2,1)S(1)}, bf16[6,256,128]{2,1,0:T(8,128)(2,1)S(1)}, u32[]{:S(2)}, u32[]{:S(2)}) %collective-permute-start.9) | collective-permute-done | bytes 393248 | tf_op jit(solution)/shard_map/ppermute | solution.py:240
  48.6 2.3 %collective-permute-start.10 = (bf16[6,256,128]{2,1,0:T(8,128)(2,1)S(1)}, bf16[6,256,128]{2,1,0:T(8,128)(2,1)S(1)}, u32[]{:S(2)}, u32[]{:S(2)}) collective-permute-start(bf16[6,256,128]{2,1,0:T(8,128)(2,1)S(1)} %get-tuple-element.32.refs_1_), channel_id=1, source_target_pairs={{0,1},{1,0},{2,3},{3,2},{4,5},{5,4},{6,7},{7,6},{8,9},{9,8},{10,11... | collective-permute-start | bytes 1179656 | tf_op jit(solution)/shard_map/ppermute | solution.py:259
  50.9 3.3 %collective-permute-start.19 = (bf16[4,256,128]{2,1,0:T(8,128)(2,1)S(1)}, bf16[4,256,128]{2,1,0:T(8,128)(2,1)S(1)}, u32[]{:S(2)}, u32[]{:S(2)}) collective-permute-start(bf16[4,256,128]{2,1,0:T(8,128)(2,1)S(1)} %get-tuple-element.36), channel_id=1, source_target_pairs={{0,24},{8,16},{16,8},{24,0},{1,25},{9,17},{17,9},{25,1},{2,26},{10... | collective-permute-start | bytes 786440 | tf_op jit(solution)/shard_map/ppermute | solution.py:240
  54.2 0.7 collective-permute-start.14
  55.0 0.1 collective-permute-start.16
  55.0 1.7 %cycle.3 = (bf16[6,128,128]{2,1,0:T(8,128)(2,1)S(1)}, bf16[6,128,128]{2,1,0:T(8,128)(2,1)S(1)}) custom-call(s32[4]{0:T(128)S(1)} %copy-done.4, bf16[6,256,128]{2,1,0:T(8,128)(2,1)S(1)} %get-tuple-element.26.refs_1_, bf16[6,256,128]{2,1,0:T(8,128)(2,1)S(1)} %collective-permute-done.refs_2_, bf16[6,256,128]{2,1,0:T(8,128)(2,1)S(1)} %collective-permute-done.1.refs_3_, ...), custom_call_target="tpu_custom_call" | custom-call | tf_op jit(solution)/shard_map/cycle/pallas_call | solution.py:265
  56.8 3.5 %collective-permute-done.19.refs_12_ = bf16[4,256,128]{2,1,0:T(8,128)(2,1)S(1)} collective-permute-done((bf16[4,256,128]{2,1,0:T(8,128)(2,1)S(1)}, bf16[4,256,128]{2,1,0:T(8,128)(2,1)S(1)}, u32[]{:S(2)}, u32[]{:S(2)}) %collective-permute-start.19) | collective-permute-done | bytes 262176 | tf_op jit(solution)/shard_map/ppermute | solution.py:240
  60.2 0.4 collective-permute-start.23
  60.7 2.0 %collective-permute-start.25 = (bf16[6,128,128]{2,1,0:T(8,128)(2,1)S(1)}, bf16[6,128,128]{2,1,0:T(8,128)(2,1)S(1)}, u32[]{:S(2)}, u32[]{:S(2)}) collective-permute-start(bf16[6,128,128]{2,1,0:T(8,128)(2,1)S(1)} %get-tuple-element.31.refs_1_), channel_id=1, source_target_pairs={{0,6},{1,7},{2,4},{3,5},{4,2},{5,3},{6,0},{7,1},{8,14},{9,15},{10,... | collective-permute-start | bytes 589832 | tf_op jit(solution)/shard_map/ppermute | solution.py:283
  62.7 0.9 pick.7
  63.6 11.9 %collective-permute-start.20 = (bf16[2,256,128]{2,1,0:T(8,128)(2,1)S(1)}, bf16[2,256,128]{2,1,0:T(8,128)(2,1)S(1)}, u32[]{:S(2)}, u32[]{:S(2)}) collective-permute-start(bf16[2,256,128]{2,1,0:T(8,128)(2,1)S(1)} %get-tuple-element.40), channel_id=1, source_target_pairs={{0,8},{8,0},{16,24},{24,16},{1,9},{9,1},{17,25},{25,17},{2,10},{10... | collective-permute-start | bytes 393224 | tf_op jit(solution)/shard_map/ppermute | solution.py:240
  75.4 0.9 collective-permute-start.21
  76.3 1.3 %collective-permute-start.22 = (bf16[2,256,128]{2,1,0:T(8,128)(2,1)S(1)}, bf16[2,256,128]{2,1,0:T(8,128)(2,1)S(1)}, u32[]{:S(2)}, u32[]{:S(2)}) collective-permute-start(bf16[2,256,128]{2,1,0:T(8,128)(2,1)S(1)} %get-tuple-element.42), channel_id=1, source_target_pairs={{0,24},{8,16},{16,8},{24,0},{1,25},{9,17},{17,9},{25,1},{2,26},{10... | collective-permute-start | bytes 393224 | tf_op jit(solution)/shard_map/ppermute | solution.py:240
  77.6 1.4 %cycle.4 = (bf16[4,128,128]{2,1,0:T(8,128)(2,1)S(1)}, bf16[4,128,128]{2,1,0:T(8,128)(2,1)S(1)}) custom-call(s32[4]{0:T(128)S(1)} %copy-done.4, bf16[6,256,128]{2,1,0:T(8,128)(2,1)S(1)} %get-tuple-element.32.refs_1_, bf16[6,256,128]{2,1,0:T(8,128)(2,1)S(1)} %collective-permute-done.10.refs_2_, bf16[6,256,128]{2,1,0:T(8,128)(2,1)S(1)} %collective-permute-done.11.refs_3_, ...), custom_call_target="tpu_custom_call" | custom-call | tf_op jit(solution)/shard_map/cycle/pallas_call | solution.py:265
  79.0 0.3 collective-permute-start.24
  79.3 2.2 %collective-permute-start.28 = (bf16[4,128,128]{2,1,0:T(8,128)(2,1)S(1)}, bf16[4,128,128]{2,1,0:T(8,128)(2,1)S(1)}, u32[]{:S(2)}, u32[]{:S(2)}) collective-permute-start(bf16[4,128,128]{2,1,0:T(8,128)(2,1)S(1)} %get-tuple-element.38.refs_3_), channel_id=1, source_target_pairs={{0,4},{1,5},{2,6},{3,7},{4,0},{5,1},{6,2},{7,3},{8,12},{9,13},{10,... | collective-permute-start | bytes 393224 | tf_op jit(solution)/shard_map/ppermute | solution.py:283
  81.5 6.1 %collective-permute-start.26 = (bf16[6,128,128]{2,1,0:T(8,128)(2,1)S(1)}, bf16[6,128,128]{2,1,0:T(8,128)(2,1)S(1)}, u32[]{:S(2)}, u32[]{:S(2)}) collective-permute-start(bf16[6,128,128]{2,1,0:T(8,128)(2,1)S(1)} %collective-permute-done.25), channel_id=1, source_target_pairs={{6,1},{7,0},{4,9},{5,8},{2,17},{3,16},{0,25},{1,24},{14,3},{15,2},... | collective-permute-start | bytes 589832 | tf_op jit(solution)/shard_map/ppermute | solution.py:284
  87.6 1.0 cycle.5
  88.6 0.1 collective-permute-start.31
  88.7 7.8 %collective-permute-start.27 = (bf16[4,128,128]{2,1,0:T(8,128)(2,1)S(1)}, bf16[4,128,128]{2,1,0:T(8,128)(2,1)S(1)}, u32[]{:S(2)}, u32[]{:S(2)}) collective-permute-start(bf16[4,128,128]{2,1,0:T(8,128)(2,1)S(1)} %get-tuple-element.37.refs_2_), channel_id=1, source_target_pairs={{0,0},{1,1},{2,8},{3,9},{4,16},{5,17},{6,24},{7,25},{8,2},{9,3},{1... | collective-permute-start | bytes 393224 | tf_op jit(solution)/shard_map/ppermute | solution.py:284
  96.5 5.2 %collective-permute-start.29 = (bf16[4,128,128]{2,1,0:T(8,128)(2,1)S(1)}, bf16[4,128,128]{2,1,0:T(8,128)(2,1)S(1)}, u32[]{:S(2)}, u32[]{:S(2)}) collective-permute-start(bf16[4,128,128]{2,1,0:T(8,128)(2,1)S(1)} %collective-permute-done.28), channel_id=1, source_target_pairs={{4,1},{5,0},{6,9},{7,8},{0,17},{1,16},{2,25},{3,24},{12,3},{13,2},... | collective-permute-start | bytes 393224 | tf_op jit(solution)/shard_map/ppermute | solution.py:284
  101.7 3.8 %collective-permute-start.30 = (bf16[2,128,128]{2,1,0:T(8,128)(2,1)S(1)}, bf16[2,128,128]{2,1,0:T(8,128)(2,1)S(1)}, u32[]{:S(2)}, u32[]{:S(2)}) collective-permute-start(bf16[2,128,128]{2,1,0:T(8,128)(2,1)S(1)} %get-tuple-element.43.refs_4_), channel_id=1, source_target_pairs={{0,0},{1,1},{2,8},{3,9},{4,16},{5,17},{6,24},{7,25},{8,2},{9,3},{1... | collective-permute-start | bytes 196616 | tf_op jit(solution)/shard_map/ppermute | solution.py:284
  105.5 0.8 collective-permute-start.32
  106.3 3.5 %final.1 = (f32[4,12,64,128]{3,2,1,0:T(8,128)}, s32[1,12]{1,0:T(1,128)S(1)}) custom-call(s32[4,2,12]{2,1,0:T(2,128)S(1)} %bitcast.31, s32[4]{0:T(128)S(1)} %copy-done.4, bf16[6,128,128]{2,1,0:T(8,128)(2,1)S(1)} %get-tuple-element.30.refs_0_, bf16[6,128,128]{2,1,0:T(8,128)(2,1)S(1)} %get-tuple-element.31.refs_1_, ...), custom_call_target="tpu_custom_call" | custom-call | tf_op jit(solution)/shard_map/final/pallas_call | solution.py:291
  109.9 6.0 %collective-permute-done.32.refs_9_ = bf16[2,128,128]{2,1,0:T(8,128)(2,1)S(1)} collective-permute-done((bf16[2,128,128]{2,1,0:T(8,128)(2,1)S(1)}, bf16[2,128,128]{2,1,0:T(8,128)(2,1)S(1)}, u32[]{:S(2)}, u32[]{:S(2)}) %collective-permute-start.32) | collective-permute-done | bytes 65568 | tf_op jit(solution)/shard_map/ppermute | solution.py:284
  115.9 2.1 %patch.1 = f32[4,12,64,128]{3,2,1,0:T(8,128)} custom-call(s32[1,12]{1,0:T(1,128)S(1)} %get-tuple-element.45.table_ref, bf16[6,128,128]{2,1,0:T(8,128)(2,1)S(1)} %get-tuple-element.30.refs_0_, bf16[6,128,128]{2,1,0:T(8,128)(2,1)S(1)} %get-tuple-element.31.refs_1_, ...), custom_call_target="tpu_custom_call", output_to_operand_aliasing={{}: (11, {})} | custom-call | tf_op jit(solution)/shard_map/patch/pallas_call | solution.py:303
  (38 shorter events, 0.1 us)
Async XLA Ops:
  0.0 1.1 copy-start.2
  1.5 21.6 %collective-permute-start.11 = (bf16[6,256,128]{2,1,0:T(8,128)(2,1)S(1)}, bf16[6,256,128]{2,1,0:T(8,128)(2,1)S(1)}, u32[]{:S(2)}, u32[]{:S(2)}) collective-permute-start(bf16[6,256,128]{2,1,0:T(8,128)(2,1)S(1)} %get-tuple-element.32.refs_1_), channel_id=1, source_target_pairs={{0,2},{1,3},{2,0},{3,1},{4,6},{5,7},{6,4},{7,5},{8,10},{9,11},{10,... | collective-permute-start | bytes 1179656 | tf_op jit(solution)/shard_map/ppermute | solution.py:259
  1.6 21.8 %collective-permute-start.13 = (bf16[6,256,128]{2,1,0:T(8,128)(2,1)S(1)}, bf16[6,256,128]{2,1,0:T(8,128)(2,1)S(1)}, u32[]{:S(2)}, u32[]{:S(2)}) collective-permute-start(bf16[6,256,128]{2,1,0:T(8,128)(2,1)S(1)} %get-tuple-element.32.refs_1_), channel_id=1, source_target_pairs={{0,4},{1,5},{2,6},{3,7},{4,0},{5,1},{6,2},{7,3},{8,12},{9,13},{10,... | collective-permute-start | bytes 1179656 | tf_op jit(solution)/shard_map/ppermute | solution.py:259
  3.1 21.6 %collective-permute-start.15 = (bf16[6,256,128]{2,1,0:T(8,128)(2,1)S(1)}, bf16[6,256,128]{2,1,0:T(8,128)(2,1)S(1)}, u32[]{:S(2)}, u32[]{:S(2)}) collective-permute-start(bf16[6,256,128]{2,1,0:T(8,128)(2,1)S(1)} %get-tuple-element.32.refs_1_), channel_id=1, source_target_pairs={{0,6},{1,7},{2,4},{3,5},{4,2},{5,3},{6,0},{7,1},{8,14},{9,15},{10,... | collective-permute-start | bytes 1179656 | tf_op jit(solution)/shard_map/ppermute | solution.py:259
  4.2 1.9 %copy-start = (bf16[4,2,47,4096]{3,1,2,0:T(2,128)(2,1)S(1)}, bf16[4,2,47,4096]{3,1,2,0:T(2,128)(2,1)}, u32[]{:S(2)}) copy-start(bf16[4,2,47,4096]{3,1,2,0:T(2,128)(2,1)} %param.5) | copy-start | bytes 9240580
  6.1 0.7 copy-start.3
  7.9 11.2 %collective-permute-start.17 = (bf16[4,256,128]{2,1,0:T(8,128)(2,1)S(1)}, bf16[4,256,128]{2,1,0:T(8,128)(2,1)S(1)}, u32[]{:S(2)}, u32[]{:S(2)}) collective-permute-start(bf16[4,256,128]{2,1,0:T(8,128)(2,1)S(1)} %get-tuple-element.34), channel_id=1, source_target_pairs={{0,8},{8,0},{16,24},{24,16},{1,9},{9,1},{17,25},{25,17},{2,10},{10... | collective-permute-start | bytes 786440 | tf_op jit(solution)/shard_map/ppermute | solution.py:240
  9.3 9.9 %collective-permute-start.18 = (bf16[4,256,128]{2,1,0:T(8,128)(2,1)S(1)}, bf16[4,256,128]{2,1,0:T(8,128)(2,1)S(1)}, u32[]{:S(2)}, u32[]{:S(2)}) collective-permute-start(bf16[4,256,128]{2,1,0:T(8,128)(2,1)S(1)} %get-tuple-element.35), channel_id=1, source_target_pairs={{0,16},{8,24},{16,0},{24,8},{1,17},{9,25},{17,1},{25,9},{2,18},{10... | collective-permute-start | bytes 786440 | tf_op jit(solution)/shard_map/ppermute | solution.py:240
  19.2 16.9 %collective-permute-start.7 = (bf16[6,256,128]{2,1,0:T(8,128)(2,1)S(1)}, bf16[6,256,128]{2,1,0:T(8,128)(2,1)S(1)}, u32[]{:S(2)}, u32[]{:S(2)}) collective-permute-start(bf16[6,256,128]{2,1,0:T(8,128)(2,1)S(1)} %get-tuple-element.28), channel_id=1, source_target_pairs={{0,8},{8,0},{16,24},{24,16},{1,9},{9,1},{17,25},{25,17},{2,10},{10... | collective-permute-start | bytes 1179656 | tf_op jit(solution)/shard_map/ppermute | solution.py:240
  19.2 21.6 %collective-permute-start.8 = (bf16[6,256,128]{2,1,0:T(8,128)(2,1)S(1)}, bf16[6,256,128]{2,1,0:T(8,128)(2,1)S(1)}, u32[]{:S(2)}, u32[]{:S(2)}) collective-permute-start(bf16[6,256,128]{2,1,0:T(8,128)(2,1)S(1)} %get-tuple-element.29), channel_id=1, source_target_pairs={{0,16},{8,24},{16,0},{24,8},{1,17},{9,25},{17,1},{25,9},{2,18},{10... | collective-permute-start | bytes 1179656 | tf_op jit(solution)/shard_map/ppermute | solution.py:240
  23.1 31.9 %copy-start.4 = (s32[4]{0:T(128)S(1)}, s32[4]{0:T(128)}, u32[]{:S(2)}) copy-start(s32[4]{0:T(128)} %count_ref.1) | copy-start | bytes 52
  23.1 19.0 %collective-permute-start.1 = (bf16[6,256,128]{2,1,0:T(8,128)(2,1)S(1)}, bf16[6,256,128]{2,1,0:T(8,128)(2,1)S(1)}, u32[]{:S(2)}, u32[]{:S(2)}) collective-permute-start(bf16[6,256,128]{2,1,0:T(8,128)(2,1)S(1)} %get-tuple-element.26.refs_1_), channel_id=1, source_target_pairs={{0,2},{1,3},{2,0},{3,1},{4,6},{5,7},{6,4},{7,5},{8,10},{9,11},{10,... | collective-permute-start | bytes 1179656 | tf_op jit(solution)/shard_map/ppermute | solution.py:259
  23.4 18.8 %collective-permute-start.3 = (bf16[6,256,128]{2,1,0:T(8,128)(2,1)S(1)}, bf16[6,256,128]{2,1,0:T(8,128)(2,1)S(1)}, u32[]{:S(2)}, u32[]{:S(2)}) collective-permute-start(bf16[6,256,128]{2,1,0:T(8,128)(2,1)S(1)} %get-tuple-element.26.refs_1_), channel_id=1, source_target_pairs={{0,4},{1,5},{2,6},{3,7},{4,0},{5,1},{6,2},{7,3},{8,12},{9,13},{10,... | collective-permute-start | bytes 1179656 | tf_op jit(solution)/shard_map/ppermute | solution.py:259
  24.6 18.0 %collective-permute-start.5 = (bf16[6,256,128]{2,1,0:T(8,128)(2,1)S(1)}, bf16[6,256,128]{2,1,0:T(8,128)(2,1)S(1)}, u32[]{:S(2)}, u32[]{:S(2)}) collective-permute-start(bf16[6,256,128]{2,1,0:T(8,128)(2,1)S(1)} %get-tuple-element.26.refs_1_), channel_id=1, source_target_pairs={{0,6},{1,7},{2,4},{3,5},{4,2},{5,3},{6,0},{7,1},{8,14},{9,15},{10,... | collective-permute-start | bytes 1179656 | tf_op jit(solution)/shard_map/ppermute | solution.py:259
  36.1 12.5 %collective-permute-start.9 = (bf16[6,256,128]{2,1,0:T(8,128)(2,1)S(1)}, bf16[6,256,128]{2,1,0:T(8,128)(2,1)S(1)}, u32[]{:S(2)}, u32[]{:S(2)}) collective-permute-start(bf16[6,256,128]{2,1,0:T(8,128)(2,1)S(1)} %pick.5), channel_id=1, source_target_pairs={{0,24},{8,16},{16,8},{24,0},{1,25},{9,17},{17,9},{25,1},{2,26},{10... | collective-permute-start | bytes 1179656 | tf_op jit(solution)/shard_map/ppermute | solution.py:240
  40.7 10.2 %collective-permute-start = (bf16[6,256,128]{2,1,0:T(8,128)(2,1)S(1)}, bf16[6,256,128]{2,1,0:T(8,128)(2,1)S(1)}, u32[]{:S(2)}, u32[]{:S(2)}) collective-permute-start(bf16[6,256,128]{2,1,0:T(8,128)(2,1)S(1)} %get-tuple-element.26.refs_1_), channel_id=1, source_target_pairs={{0,1},{1,0},{2,3},{3,2},{4,5},{5,4},{6,7},{7,6},{8,9},{9,8},{10,11... | collective-permute-start | bytes 1179656 | tf_op jit(solution)/shard_map/ppermute | solution.py:259
  42.1 8.8 %collective-permute-start.2 = (bf16[6,256,128]{2,1,0:T(8,128)(2,1)S(1)}, bf16[6,256,128]{2,1,0:T(8,128)(2,1)S(1)}, u32[]{:S(2)}, u32[]{:S(2)}) collective-permute-start(bf16[6,256,128]{2,1,0:T(8,128)(2,1)S(1)} %collective-permute-done.1.refs_3_), channel_id=1, source_target_pairs={{0,1},{1,0},{2,3},{3,2},{4,5},{5,4},{6,7},{7,6},{8,9},{9,8},{10,11... | collective-permute-start | bytes 1179656 | tf_op jit(solution)/shard_map/ppermute | solution.py:259
  42.2 12.1 %collective-permute-start.4 = (bf16[6,256,128]{2,1,0:T(8,128)(2,1)S(1)}, bf16[6,256,128]{2,1,0:T(8,128)(2,1)S(1)}, u32[]{:S(2)}, u32[]{:S(2)}) collective-permute-start(bf16[6,256,128]{2,1,0:T(8,128)(2,1)S(1)} %collective-permute-done.3.refs_5_), channel_id=1, source_target_pairs={{0,1},{1,0},{2,3},{3,2},{4,5},{5,4},{6,7},{7,6},{8,9},{9,8},{10,11... | collective-permute-start | bytes 1179656 | tf_op jit(solution)/shard_map/ppermute | solution.py:259
  42.6 12.3 %collective-permute-start.6 = (bf16[6,256,128]{2,1,0:T(8,128)(2,1)S(1)}, bf16[6,256,128]{2,1,0:T(8,128)(2,1)S(1)}, u32[]{:S(2)}, u32[]{:S(2)}) collective-permute-start(bf16[6,256,128]{2,1,0:T(8,128)(2,1)S(1)} %collective-permute-done.5.refs_7_), channel_id=1, source_target_pairs={{0,1},{1,0},{2,3},{3,2},{4,5},{5,4},{6,7},{7,6},{8,9},{9,8},{10,11... | collective-permute-start | bytes 1179656 | tf_op jit(solution)/shard_map/ppermute | solution.py:259
  48.6 12.0 %collective-permute-start.10 = (bf16[6,256,128]{2,1,0:T(8,128)(2,1)S(1)}, bf16[6,256,128]{2,1,0:T(8,128)(2,1)S(1)}, u32[]{:S(2)}, u32[]{:S(2)}) collective-permute-start(bf16[6,256,128]{2,1,0:T(8,128)(2,1)S(1)} %get-tuple-element.32.refs_1_), channel_id=1, source_target_pairs={{0,1},{1,0},{2,3},{3,2},{4,5},{5,4},{6,7},{7,6},{8,9},{9,8},{10,11... | collective-permute-start | bytes 1179656 | tf_op jit(solution)/shard_map/ppermute | solution.py:259
  50.9 12.7 %collective-permute-start.12 = (bf16[6,256,128]{2,1,0:T(8,128)(2,1)S(1)}, bf16[6,256,128]{2,1,0:T(8,128)(2,1)S(1)}, u32[]{:S(2)}, u32[]{:S(2)}) collective-permute-start(bf16[6,256,128]{2,1,0:T(8,128)(2,1)S(1)} %collective-permute-done.11.refs_3_), channel_id=1, source_target_pairs={{0,1},{1,0},{2,3},{3,2},{4,5},{5,4},{6,7},{7,6},{8,9},{9,8},{10,11... | collective-permute-start | bytes 1179656 | tf_op jit(solution)/shard_map/ppermute | solution.py:259
  50.9 9.3 %collective-permute-start.19 = (bf16[4,256,128]{2,1,0:T(8,128)(2,1)S(1)}, bf16[4,256,128]{2,1,0:T(8,128)(2,1)S(1)}, u32[]{:S(2)}, u32[]{:S(2)}) collective-permute-start(bf16[4,256,128]{2,1,0:T(8,128)(2,1)S(1)} %get-tuple-element.36), channel_id=1, source_target_pairs={{0,24},{8,16},{16,8},{24,0},{1,25},{9,17},{17,9},{25,1},{2,26},{10... | collective-permute-start | bytes 786440 | tf_op jit(solution)/shard_map/ppermute | solution.py:240
  54.2 21.2 %collective-permute-start.14 = (bf16[6,256,128]{2,1,0:T(8,128)(2,1)S(1)}, bf16[6,256,128]{2,1,0:T(8,128)(2,1)S(1)}, u32[]{:S(2)}, u32[]{:S(2)}) collective-permute-start(bf16[6,256,128]{2,1,0:T(8,128)(2,1)S(1)} %collective-permute-done.13.refs_5_), channel_id=1, source_target_pairs={{0,1},{1,0},{2,3},{3,2},{4,5},{5,4},{6,7},{7,6},{8,9},{9,8},{10,11... | collective-permute-start | bytes 1179656 | tf_op jit(solution)/shard_map/ppermute | solution.py:259
  55.0 21.4 %collective-permute-start.16 = (bf16[6,256,128]{2,1,0:T(8,128)(2,1)S(1)}, bf16[6,256,128]{2,1,0:T(8,128)(2,1)S(1)}, u32[]{:S(2)}, u32[]{:S(2)}) collective-permute-start(bf16[6,256,128]{2,1,0:T(8,128)(2,1)S(1)} %collective-permute-done.15.refs_7_), channel_id=1, source_target_pairs={{0,1},{1,0},{2,3},{3,2},{4,5},{5,4},{6,7},{7,6},{8,9},{9,8},{10,11... | collective-permute-start | bytes 1179656 | tf_op jit(solution)/shard_map/ppermute | solution.py:259
  55.0 7.6 %copy-start.1 = (bf16[4,2,47,4096]{3,1,2,0:T(2,128)(2,1)S(1)}, bf16[4,2,47,4096]{3,1,2,0:T(2,128)(2,1)}, u32[]{:S(2)}) copy-start(bf16[4,2,47,4096]{3,1,2,0:T(2,128)(2,1)} %param.5) | copy-start | bytes 9240580
  60.2 18.8 %collective-permute-start.23 = (bf16[6,128,128]{2,1,0:T(8,128)(2,1)S(1)}, bf16[6,128,128]{2,1,0:T(8,128)(2,1)S(1)}, u32[]{:S(2)}, u32[]{:S(2)}) collective-permute-start(bf16[6,128,128]{2,1,0:T(8,128)(2,1)S(1)} %get-tuple-element.30.refs_0_), channel_id=1, source_target_pairs={{0,2},{1,3},{2,0},{3,1},{4,6},{5,7},{6,4},{7,5},{8,10},{9,11},{10,... | collective-permute-start | bytes 589832 | tf_op jit(solution)/shard_map/ppermute | solution.py:283
  60.7 20.8 %collective-permute-start.25 = (bf16[6,128,128]{2,1,0:T(8,128)(2,1)S(1)}, bf16[6,128,128]{2,1,0:T(8,128)(2,1)S(1)}, u32[]{:S(2)}, u32[]{:S(2)}) collective-permute-start(bf16[6,128,128]{2,1,0:T(8,128)(2,1)S(1)} %get-tuple-element.31.refs_1_), channel_id=1, source_target_pairs={{0,6},{1,7},{2,4},{3,5},{4,2},{5,3},{6,0},{7,1},{8,14},{9,15},{10,... | collective-permute-start | bytes 589832 | tf_op jit(solution)/shard_map/ppermute | solution.py:283
  63.6 15.7 %collective-permute-start.20 = (bf16[2,256,128]{2,1,0:T(8,128)(2,1)S(1)}, bf16[2,256,128]{2,1,0:T(8,128)(2,1)S(1)}, u32[]{:S(2)}, u32[]{:S(2)}) collective-permute-start(bf16[2,256,128]{2,1,0:T(8,128)(2,1)S(1)} %get-tuple-element.40), channel_id=1, source_target_pairs={{0,8},{8,0},{16,24},{24,16},{1,9},{9,1},{17,25},{25,17},{2,10},{10... | collective-permute-start | bytes 393224 | tf_op jit(solution)/shard_map/ppermute | solution.py:240
  75.4 12.1 %collective-permute-start.21 = (bf16[2,256,128]{2,1,0:T(8,128)(2,1)S(1)}, bf16[2,256,128]{2,1,0:T(8,128)(2,1)S(1)}, u32[]{:S(2)}, u32[]{:S(2)}) collective-permute-start(bf16[2,256,128]{2,1,0:T(8,128)(2,1)S(1)} %get-tuple-element.41), channel_id=1, source_target_pairs={{0,16},{8,24},{16,0},{24,8},{1,17},{9,25},{17,1},{25,9},{2,18},{10... | collective-permute-start | bytes 393224 | tf_op jit(solution)/shard_map/ppermute | solution.py:240
  76.3 11.2 %collective-permute-start.22 = (bf16[2,256,128]{2,1,0:T(8,128)(2,1)S(1)}, bf16[2,256,128]{2,1,0:T(8,128)(2,1)S(1)}, u32[]{:S(2)}, u32[]{:S(2)}) collective-permute-start(bf16[2,256,128]{2,1,0:T(8,128)(2,1)S(1)} %get-tuple-element.42), channel_id=1, source_target_pairs={{0,24},{8,16},{16,8},{24,0},{1,25},{9,17},{17,9},{25,1},{2,26},{10... | collective-permute-start | bytes 393224 | tf_op jit(solution)/shard_map/ppermute | solution.py:240
  79.0 26.4 %collective-permute-start.24 = (bf16[6,128,128]{2,1,0:T(8,128)(2,1)S(1)}, bf16[6,128,128]{2,1,0:T(8,128)(2,1)S(1)}, u32[]{:S(2)}, u32[]{:S(2)}) collective-permute-start(bf16[6,128,128]{2,1,0:T(8,128)(2,1)S(1)} %collective-permute-done.23), channel_id=1, source_target_pairs={{2,0},{3,1},{0,8},{1,9},{6,16},{7,17},{4,24},{5,25},{10,2},{11,3},... | collective-permute-start | bytes 589832 | tf_op jit(solution)/shard_map/ppermute | solution.py:284
  79.3 17.2 %collective-permute-start.28 = (bf16[4,128,128]{2,1,0:T(8,128)(2,1)S(1)}, bf16[4,128,128]{2,1,0:T(8,128)(2,1)S(1)}, u32[]{:S(2)}, u32[]{:S(2)}) collective-permute-start(bf16[4,128,128]{2,1,0:T(8,128)(2,1)S(1)} %get-tuple-element.38.refs_3_), channel_id=1, source_target_pairs={{0,4},{1,5},{2,6},{3,7},{4,0},{5,1},{6,2},{7,3},{8,12},{9,13},{10,... | collective-permute-start | bytes 393224 | tf_op jit(solution)/shard_map/ppermute | solution.py:283
  81.5 24.8 %collective-permute-start.26 = (bf16[6,128,128]{2,1,0:T(8,128)(2,1)S(1)}, bf16[6,128,128]{2,1,0:T(8,128)(2,1)S(1)}, u32[]{:S(2)}, u32[]{:S(2)}) collective-permute-start(bf16[6,128,128]{2,1,0:T(8,128)(2,1)S(1)} %collective-permute-done.25), channel_id=1, source_target_pairs={{6,1},{7,0},{4,9},{5,8},{2,17},{3,16},{0,25},{1,24},{14,3},{15,2},... | collective-permute-start | bytes 589832 | tf_op jit(solution)/shard_map/ppermute | solution.py:284
  88.6 13.1 %collective-permute-start.31 = (bf16[2,128,128]{2,1,0:T(8,128)(2,1)S(1)}, bf16[2,128,128]{2,1,0:T(8,128)(2,1)S(1)}, u32[]{:S(2)}, u32[]{:S(2)}) collective-permute-start(bf16[2,128,128]{2,1,0:T(8,128)(2,1)S(1)} %get-tuple-element.44.refs_5_), channel_id=1, source_target_pairs={{0,4},{1,5},{2,6},{3,7},{4,0},{5,1},{6,2},{7,3},{8,12},{9,13},{10,... | collective-permute-start | bytes 196616 | tf_op jit(solution)/shard_map/ppermute | solution.py:283
  88.7 27.2 %collective-permute-start.27 = (bf16[4,128,128]{2,1,0:T(8,128)(2,1)S(1)}, bf16[4,128,128]{2,1,0:T(8,128)(2,1)S(1)}, u32[]{:S(2)}, u32[]{:S(2)}) collective-permute-start(bf16[4,128,128]{2,1,0:T(8,128)(2,1)S(1)} %get-tuple-element.37.refs_2_), channel_id=1, source_target_pairs={{0,0},{1,1},{2,8},{3,9},{4,16},{5,17},{6,24},{7,25},{8,2},{9,3},{1... | collective-permute-start | bytes 393224 | tf_op jit(solution)/shard_map/ppermute | solution.py:284
  96.5 19.4 %collective-permute-start.29 = (bf16[4,128,128]{2,1,0:T(8,128)(2,1)S(1)}, bf16[4,128,128]{2,1,0:T(8,128)(2,1)S(1)}, u32[]{:S(2)}, u32[]{:S(2)}) collective-permute-start(bf16[4,128,128]{2,1,0:T(8,128)(2,1)S(1)} %collective-permute-done.28), channel_id=1, source_target_pairs={{4,1},{5,0},{6,9},{7,8},{0,17},{1,16},{2,25},{3,24},{12,3},{13,2},... | collective-permute-start | bytes 393224 | tf_op jit(solution)/shard_map/ppermute | solution.py:284
  101.7 8.2 %collective-permute-start.30 = (bf16[2,128,128]{2,1,0:T(8,128)(2,1)S(1)}, bf16[2,128,128]{2,1,0:T(8,128)(2,1)S(1)}, u32[]{:S(2)}, u32[]{:S(2)}) collective-permute-start(bf16[2,128,128]{2,1,0:T(8,128)(2,1)S(1)} %get-tuple-element.43.refs_4_), channel_id=1, source_target_pairs={{0,0},{1,1},{2,8},{3,9},{4,16},{5,17},{6,24},{7,25},{8,2},{9,3},{1... | collective-permute-start | bytes 196616 | tf_op jit(solution)/shard_map/ppermute | solution.py:284
  105.5 10.4 %collective-permute-start.32 = (bf16[2,128,128]{2,1,0:T(8,128)(2,1)S(1)}, bf16[2,128,128]{2,1,0:T(8,128)(2,1)S(1)}, u32[]{:S(2)}, u32[]{:S(2)}) collective-permute-start(bf16[2,128,128]{2,1,0:T(8,128)(2,1)S(1)} %collective-permute-done.31), channel_id=1, source_target_pairs={{4,1},{5,0},{6,9},{7,8},{0,17},{1,16},{2,25},{3,24},{12,3},{13,2},... | collective-permute-start | bytes 196616 | tf_op jit(solution)/shard_map/ppermute | solution.py:284

commit v6 on v5

--- a/solution.py
+++ b/solution.py
@@ -167,18 +167,17 @@
     lax.fori_loop(0, slots, one, 0)
 
 
-def patch_kernel(ratio, sizes, table_ref, *refs):
-    slots = sum(sizes)
-    early = sizes[0]
+def patch_kernel(ratio, sizes, chunk, table_ref, *refs):
+    early = sum(sizes[:chunk])
     owns = refs[: len(sizes) * ratio]
     theirs = refs[len(sizes) * ratio : -6]
     _, out_ref, held_own, held_their, built, sem = refs[-6:]
     core = lax.rem(lax.axis_index("col"), ratio)
     collect(owns, held_own, sizes, ratio, core)
-    collect(theirs, held_their, sizes[1:], ratio, core)
+    collect(theirs, held_their, sizes[chunk : chunk + 1], ratio, core)
     depth = out_ref.shape[0]
     uses, copies = [], []
-    for t in range(slots - early):
+    for t in range(sizes[chunk]):
         found = table_ref[0, early + t]
         uses.append(found >= 0)
         s = jnp.maximum(found, 0)
@@ -287,7 +286,6 @@
     out_shape = jax.ShapeDtypeStruct((occ_row, slots, square // LANES * occ_col, LANES), jnp.float32)
     block = (tall // ratio, wide)
     split = ratio
-    late = slots - sizes[0]
     out, table = pl.pallas_call(
         functools.partial(final_kernel, ratio, sizes),
         out_shape=[out_shape, jax.ShapeDtypeStruct((1, slots), jnp.int32)],
@@ -300,21 +298,23 @@
         compiler_params=PARAMS,
         name="final",
     )(lists, tile_counts, *owns, *theirs[:split])
-    out = pl.pallas_call(
-        functools.partial(patch_kernel, ratio, sizes),
-        out_shape=out_shape,
-        in_specs=[SMEM] + [VMEM] * (len(owns) + len(theirs) - split) + [HBM],
-        out_specs=HBM,
-        scratch_shapes=[
-            pltpu.VMEM((ratio, slots) + block, bf16),
-            pltpu.VMEM((ratio, late) + block, bf16),
-            pltpu.VMEM((late, occ_row, TILE, LANES), jnp.float32),
-            pltpu.SemaphoreType.DMA((late,)),
-        ],
-        input_output_aliases={1 + len(owns) + len(theirs) - split: 0},
-        compiler_params=PARAMS,
-        name="patch",
-    )(table, *owns, *theirs[split:], out)
+    for chunk in range(1, len(sizes)):
+        late = sizes[chunk]
+        out = pl.pallas_call(
+            functools.partial(patch_kernel, ratio, sizes, chunk),
+            out_shape=out_shape,
+            in_specs=[SMEM] + [VMEM] * (len(owns) + ratio) + [HBM],
+            out_specs=HBM,
+            scratch_shapes=[
+                pltpu.VMEM((ratio, slots) + block, bf16),
+                pltpu.VMEM((ratio, late) + block, bf16),
+                pltpu.VMEM((late, occ_row, TILE, LANES), jnp.float32),
+                pltpu.SemaphoreType.DMA((late,)),
+            ],
+            input_output_aliases={1 + len(owns) + ratio: 0},
+            compiler_params=PARAMS,
+            name="patch",
+        )(table, *owns, *theirs[ratio * chunk : ratio * (chunk + 1)], out)
     return tiles_of(out, occ_col)
 
 

time: 118 us -> 117 us (level)
  waiting for transfers between devices: 29.9 us -> 21.7 us
  starting transfers between devices: 70 us -> 75.6 us
  Pallas kernels: 14.3 us -> 15.5 us
    ppermute x14, starting transfers between devices: 11.7 us -> 23.3 us  [on_device(): lax.ppermute(source, 'col', [(c, c ^ step) for c in range(cols)])]
    ppermute x9, waiting for transfers between devices: 23.9 us -> 16.6 us  [on_device(): got.append(lax.ppermute(picked[shift], 'row', pairs))]
    ppermute x9, starting transfers between devices: 29.6 us -> 24.1 us  [on_device(): got.append(lax.ppermute(picked[shift], 'row', pairs))]
    ppermute x6, waiting for transfers between devices: 6.02 us -> 2.71 us  [on_device(): lax.ppermute(block, ('row', 'col'), mirror_pairs(rows, cols, step, hop))]
    ppermute x6, starting transfers between devices: 23.9 us -> 21 us  [on_device(): lax.ppermute(block, ('row', 'col'), mirror_pairs(rows, cols, step, hop))]
    ppermute x4, starting transfers between devices: 4.67 us -> 7.1 us  [on_device(): block = lax.ppermute(block, 'col', [(c, c ^ hop) for c in range(cols)])]
    ppermute x4, waiting for transfers between devices: 0.01 us -> 1.83 us  [on_device(): block = lax.ppermute(block, 'col', [(c, c ^ hop) for c in range(cols)])]
    pallas_call x1 -> x2, Pallas kernels: 2.15 us -> 3.41 us  [on_device(): pl.pallas_call(functools.partial(patch_kernel, ratio, sizes, chunk), out_...]
  transfers between devices with their start and end apart: 33 -> 33, of which waited for: 5 -> 8; matrix products, arithmetic and copies ran while one was open for 0% -> 0% of each run, Pallas kernels for 10% -> 12%
where the time goes in v6:
time: 117 us
  starting transfers between devices  75.6 us (65%)
  waiting for transfers between devices  21.7 us (19%)
  Pallas kernels  15.5 us (13%)
  local copies, waits for them, and re-layouts  3.7 us (3%)
    ppermute x9, starting transfers between devices, on_device(): got.append(lax.ppermute(picked[shift], 'row', pairs))  24.1 us
    ppermute x14, starting transfers between devices, on_device(): lax.ppermute(source, 'col', [(c, c ^ step) for c in range(cols)])  23.3 us
    ppermute x6, starting transfers between devices, on_device(): lax.ppermute(block, ('row', 'col'), mirror_pairs(rows, cols, step, hop))  21 us
    ppermute x9, waiting for transfers between devices, on_device(): got.append(lax.ppermute(picked[shift], 'row', pairs))  16.6 us
    ppermute x4, starting transfers between devices, on_device(): block = lax.ppermute(block, 'col', [(c, c ^ hop) for c in range(cols)])  7.1 us
    pallas_call x3, Pallas kernels, on_device(): pl.pallas_call(functools.partial(cycle_kernel, rows, cols, ratio, base, b...  4.17 us
    pallas_call x4, Pallas kernels, on_device(): pl.pallas_call(functools.partial(pick_kernel, base, size, tuple(shifts)),...  4.02 us
    unnamed x10, local copies, waits for them, and re-layouts  3.7 us
  transfers between devices with their start and end apart: 33, of which 8 were waited for; matrix products, arithmetic and copies ran while one was open for 0% of the time, Pallas kernels for 12%

profile of v6, /device:TPU:3, one launch (start us, length us, event | category | flops | bytes accessed | tf_op | source)
XLA Modules:
  0.0 116.6 jit_solution(1173684308901867298)
XLA Ops:
  0.0 1.1 copy-done.2
  1.1 0.4 left.1
  1.6 1.5 %collective-permute-start.13 = (bf16[6,256,128]{2,1,0:T(8,128)(2,1)S(1)}, bf16[6,256,128]{2,1,0:T(8,128)(2,1)S(1)}, u32[]{:S(2)}, u32[]{:S(2)}) collective-permute-start(bf16[6,256,128]{2,1,0:T(8,128)(2,1)S(1)} %get-tuple-element.32.refs_1_), channel_id=1, source_target_pairs={{0,4},{1,5},{2,6},{3,7},{4,0},{5,1},{6,2},{7,3},{8,12},{9,13},{10,... | collective-permute-start | bytes 1179656 | tf_op jit(solution)/shard_map/ppermute | solution.py:258
  3.1 1.9 %copy-done = bf16[4,2,47,4096]{3,1,2,0:T(2,128)(2,1)S(1)} copy-done((bf16[4,2,47,4096]{3,1,2,0:T(2,128)(2,1)S(1)}, bf16[4,2,47,4096]{3,1,2,0:T(2,128)(2,1)}, u32[]{:S(2)}) %copy-start) | copy-done | bytes 3080216
  5.0 0.7 copy-done.3
  5.6 1.1 pick.6
  6.8 1.4 %collective-permute-start.17 = (bf16[4,256,128]{2,1,0:T(8,128)(2,1)S(1)}, bf16[4,256,128]{2,1,0:T(8,128)(2,1)S(1)}, u32[]{:S(2)}, u32[]{:S(2)}) collective-permute-start(bf16[4,256,128]{2,1,0:T(8,128)(2,1)S(1)} %get-tuple-element.34), channel_id=1, source_target_pairs={{0,8},{8,0},{16,24},{24,16},{1,9},{9,1},{17,25},{25,17},{2,10},{10... | collective-permute-start | bytes 786440 | tf_op jit(solution)/shard_map/ppermute | solution.py:239
  8.1 1.2 collective-permute-start.15
  9.3 2.3 %collective-permute-start.18 = (bf16[4,256,128]{2,1,0:T(8,128)(2,1)S(1)}, bf16[4,256,128]{2,1,0:T(8,128)(2,1)S(1)}, u32[]{:S(2)}, u32[]{:S(2)}) collective-permute-start(bf16[4,256,128]{2,1,0:T(8,128)(2,1)S(1)} %get-tuple-element.35), channel_id=1, source_target_pairs={{0,16},{8,24},{16,0},{24,8},{1,17},{9,25},{17,1},{25,9},{2,18},{10... | collective-permute-start | bytes 786440 | tf_op jit(solution)/shard_map/ppermute | solution.py:239
  11.6 1.2 %pick.4 = (bf16[6,256,128]{2,1,0:T(8,128)(2,1)S(1)}, bf16[6,256,128]{2,1,0:T(8,128)(2,1)S(1)}, bf16[6,256,128]{2,1,0:T(8,128)(2,1)S(1)}) custom-call(s32[4,2,12]{2,1,0:T(2,128)S(1)} %bitcast.28, bf16[4,47,64,128]{3,2,1,0:T(8,128)(2,1)S(1)} %bitcast.23), custom_call_target="tpu_custom_call" | custom-call | tf_op jit(solution)/shard_map/pick/pallas_call | solution.py:227
  12.8 3.8 %collective-permute-done.17.refs_10_ = bf16[4,256,128]{2,1,0:T(8,128)(2,1)S(1)} collective-permute-done((bf16[4,256,128]{2,1,0:T(8,128)(2,1)S(1)}, bf16[4,256,128]{2,1,0:T(8,128)(2,1)S(1)}, u32[]{:S(2)}, u32[]{:S(2)}) %collective-permute-start.17) | collective-permute-done | bytes 262176 | tf_op jit(solution)/shard_map/ppermute | solution.py:239
  16.5 1.7 %collective-permute-done.18.refs_11_ = bf16[4,256,128]{2,1,0:T(8,128)(2,1)S(1)} collective-permute-done((bf16[4,256,128]{2,1,0:T(8,128)(2,1)S(1)}, bf16[4,256,128]{2,1,0:T(8,128)(2,1)S(1)}, u32[]{:S(2)}, u32[]{:S(2)}) %collective-permute-start.18) | collective-permute-done | bytes 262176 | tf_op jit(solution)/shard_map/ppermute | solution.py:239
  18.2 3.1 %collective-permute-start.8 = (bf16[6,256,128]{2,1,0:T(8,128)(2,1)S(1)}, bf16[6,256,128]{2,1,0:T(8,128)(2,1)S(1)}, u32[]{:S(2)}, u32[]{:S(2)}) collective-permute-start(bf16[6,256,128]{2,1,0:T(8,128)(2,1)S(1)} %get-tuple-element.29), channel_id=1, source_target_pairs={{0,16},{8,24},{16,0},{24,8},{1,17},{9,25},{17,1},{25,9},{2,18},{10... | collective-permute-start | bytes 1179656 | tf_op jit(solution)/shard_map/ppermute | solution.py:239
  21.3 1.5 %collective-permute-start.1 = (bf16[6,256,128]{2,1,0:T(8,128)(2,1)S(1)}, bf16[6,256,128]{2,1,0:T(8,128)(2,1)S(1)}, u32[]{:S(2)}, u32[]{:S(2)}) collective-permute-start(bf16[6,256,128]{2,1,0:T(8,128)(2,1)S(1)} %get-tuple-element.26.refs_1_), channel_id=1, source_target_pairs={{0,2},{1,3},{2,0},{3,1},{4,6},{5,7},{6,4},{7,5},{8,10},{9,11},{10,... | collective-permute-start | bytes 1179656 | tf_op jit(solution)/shard_map/ppermute | solution.py:258
  22.8 1.3 %collective-permute-start.5 = (bf16[6,256,128]{2,1,0:T(8,128)(2,1)S(1)}, bf16[6,256,128]{2,1,0:T(8,128)(2,1)S(1)}, u32[]{:S(2)}, u32[]{:S(2)}) collective-permute-start(bf16[6,256,128]{2,1,0:T(8,128)(2,1)S(1)} %get-tuple-element.26.refs_1_), channel_id=1, source_target_pairs={{0,6},{1,7},{2,4},{3,5},{4,2},{5,3},{6,0},{7,1},{8,14},{9,15},{10,... | collective-permute-start | bytes 1179656 | tf_op jit(solution)/shard_map/ppermute | solution.py:258
  24.1 0.8 pick.5
  24.9 7.2 %collective-permute-done.7.refs_10_ = bf16[6,256,128]{2,1,0:T(8,128)(2,1)S(1)} collective-permute-done((bf16[6,256,128]{2,1,0:T(8,128)(2,1)S(1)}, bf16[6,256,128]{2,1,0:T(8,128)(2,1)S(1)}, u32[]{:S(2)}, u32[]{:S(2)}) %collective-permute-start.7) | collective-permute-done | bytes 393248 | tf_op jit(solution)/shard_map/ppermute | solution.py:239
  32.1 5.1 %collective-permute-start.9 = (bf16[6,256,128]{2,1,0:T(8,128)(2,1)S(1)}, bf16[6,256,128]{2,1,0:T(8,128)(2,1)S(1)}, u32[]{:S(2)}, u32[]{:S(2)}) collective-permute-start(bf16[6,256,128]{2,1,0:T(8,128)(2,1)S(1)} %pick.5), channel_id=1, source_target_pairs={{0,24},{8,16},{16,8},{24,0},{1,25},{9,17},{17,9},{25,1},{2,26},{10... | collective-permute-start | bytes 1179656 | tf_op jit(solution)/shard_map/ppermute | solution.py:239
  37.2 15.8 %collective-permute-start = (bf16[6,256,128]{2,1,0:T(8,128)(2,1)S(1)}, bf16[6,256,128]{2,1,0:T(8,128)(2,1)S(1)}, u32[]{:S(2)}, u32[]{:S(2)}) collective-permute-start(bf16[6,256,128]{2,1,0:T(8,128)(2,1)S(1)} %get-tuple-element.26.refs_1_), channel_id=1, source_target_pairs={{0,1},{1,0},{2,3},{3,2},{4,5},{5,4},{6,7},{7,6},{8,9},{9,8},{10,11... | collective-permute-start | bytes 1179656 | tf_op jit(solution)/shard_map/ppermute | solution.py:258
  53.0 0.5 collective-permute-start.4
  53.6 0.4 collective-permute-start.10
  54.0 0.3 collective-permute-done.refs_2_
  54.3 0.4 collective-permute-start.12
  54.7 0.2 collective-permute-done.2.refs_4_
  54.9 3.0 %collective-permute-start.19 = (bf16[4,256,128]{2,1,0:T(8,128)(2,1)S(1)}, bf16[4,256,128]{2,1,0:T(8,128)(2,1)S(1)}, u32[]{:S(2)}, u32[]{:S(2)}) collective-permute-start(bf16[4,256,128]{2,1,0:T(8,128)(2,1)S(1)} %get-tuple-element.36), channel_id=1, source_target_pairs={{0,24},{8,16},{16,8},{24,0},{1,25},{9,17},{17,9},{25,1},{2,26},{10... | collective-permute-start | bytes 786440 | tf_op jit(solution)/shard_map/ppermute | solution.py:239
  57.9 0.7 collective-permute-start.14
  58.6 1.7 %cycle.3 = (bf16[6,128,128]{2,1,0:T(8,128)(2,1)S(1)}, bf16[6,128,128]{2,1,0:T(8,128)(2,1)S(1)}) custom-call(s32[4]{0:T(128)S(1)} %copy-done.4, bf16[6,256,128]{2,1,0:T(8,128)(2,1)S(1)} %get-tuple-element.26.refs_1_, bf16[6,256,128]{2,1,0:T(8,128)(2,1)S(1)} %collective-permute-done.refs_2_, bf16[6,256,128]{2,1,0:T(8,128)(2,1)S(1)} %collective-permute-done.1.refs_3_, ...), custom_call_target="tpu_custom_call" | custom-call | tf_op jit(solution)/shard_map/cycle/pallas_call | solution.py:264
  60.3 3.9 %collective-permute-done.19.refs_12_ = bf16[4,256,128]{2,1,0:T(8,128)(2,1)S(1)} collective-permute-done((bf16[4,256,128]{2,1,0:T(8,128)(2,1)S(1)}, bf16[4,256,128]{2,1,0:T(8,128)(2,1)S(1)}, u32[]{:S(2)}, u32[]{:S(2)}) %collective-permute-start.19) | collective-permute-done | bytes 262176 | tf_op jit(solution)/shard_map/ppermute | solution.py:239
  64.3 0.9 pick.7
  65.2 3.1 %collective-permute-start.25 = (bf16[6,128,128]{2,1,0:T(8,128)(2,1)S(1)}, bf16[6,128,128]{2,1,0:T(8,128)(2,1)S(1)}, u32[]{:S(2)}, u32[]{:S(2)}) collective-permute-start(bf16[6,128,128]{2,1,0:T(8,128)(2,1)S(1)} %get-tuple-element.31.refs_1_), channel_id=1, source_target_pairs={{0,6},{1,7},{2,4},{3,5},{4,2},{5,3},{6,0},{7,1},{8,14},{9,15},{10,... | collective-permute-start | bytes 589832 | tf_op jit(solution)/shard_map/ppermute | solution.py:282
  68.3 6.6 %collective-permute-start.20 = (bf16[2,256,128]{2,1,0:T(8,128)(2,1)S(1)}, bf16[2,256,128]{2,1,0:T(8,128)(2,1)S(1)}, u32[]{:S(2)}, u32[]{:S(2)}) collective-permute-start(bf16[2,256,128]{2,1,0:T(8,128)(2,1)S(1)} %get-tuple-element.40), channel_id=1, source_target_pairs={{0,8},{8,0},{16,24},{24,16},{1,9},{9,1},{17,25},{25,17},{2,10},{10... | collective-permute-start | bytes 393224 | tf_op jit(solution)/shard_map/ppermute | solution.py:239
  74.9 1.5 %collective-permute-start.21 = (bf16[2,256,128]{2,1,0:T(8,128)(2,1)S(1)}, bf16[2,256,128]{2,1,0:T(8,128)(2,1)S(1)}, u32[]{:S(2)}, u32[]{:S(2)}) collective-permute-start(bf16[2,256,128]{2,1,0:T(8,128)(2,1)S(1)} %get-tuple-element.41), channel_id=1, source_target_pairs={{0,16},{8,24},{16,0},{24,8},{1,17},{9,25},{17,1},{25,9},{2,18},{10... | collective-permute-start | bytes 393224 | tf_op jit(solution)/shard_map/ppermute | solution.py:239
  76.4 1.2 %collective-permute-start.22 = (bf16[2,256,128]{2,1,0:T(8,128)(2,1)S(1)}, bf16[2,256,128]{2,1,0:T(8,128)(2,1)S(1)}, u32[]{:S(2)}, u32[]{:S(2)}) collective-permute-start(bf16[2,256,128]{2,1,0:T(8,128)(2,1)S(1)} %get-tuple-element.42), channel_id=1, source_target_pairs={{0,24},{8,16},{16,8},{24,0},{1,25},{9,17},{17,9},{25,1},{2,26},{10... | collective-permute-start | bytes 393224 | tf_op jit(solution)/shard_map/ppermute | solution.py:239
  77.6 1.4 %cycle.4 = (bf16[4,128,128]{2,1,0:T(8,128)(2,1)S(1)}, bf16[4,128,128]{2,1,0:T(8,128)(2,1)S(1)}) custom-call(s32[4]{0:T(128)S(1)} %copy-done.4, bf16[6,256,128]{2,1,0:T(8,128)(2,1)S(1)} %get-tuple-element.32.refs_1_, bf16[6,256,128]{2,1,0:T(8,128)(2,1)S(1)} %collective-permute-done.10.refs_2_, bf16[6,256,128]{2,1,0:T(8,128)(2,1)S(1)} %collective-permute-done.11.refs_3_, ...), custom_call_target="tpu_custom_call" | custom-call | tf_op jit(solution)/shard_map/cycle/pallas_call | solution.py:264
  79.0 0.1 collective-permute-start.31
  79.1 0.8 collective-permute-start.24
  79.8 6.1 %collective-permute-start.26 = (bf16[6,128,128]{2,1,0:T(8,128)(2,1)S(1)}, bf16[6,128,128]{2,1,0:T(8,128)(2,1)S(1)}, u32[]{:S(2)}, u32[]{:S(2)}) collective-permute-start(bf16[6,128,128]{2,1,0:T(8,128)(2,1)S(1)} %collective-permute-done.25), channel_id=1, source_target_pairs={{6,1},{7,0},{4,9},{5,8},{2,17},{3,16},{0,25},{1,24},{14,3},{15,2},... | collective-permute-start | bytes 589832 | tf_op jit(solution)/shard_map/ppermute | solution.py:283
  85.9 2.9 %collective-permute-start.30 = (bf16[4,128,128]{2,1,0:T(8,128)(2,1)S(1)}, bf16[4,128,128]{2,1,0:T(8,128)(2,1)S(1)}, u32[]{:S(2)}, u32[]{:S(2)}) collective-permute-start(bf16[4,128,128]{2,1,0:T(8,128)(2,1)S(1)} %get-tuple-element.37.refs_2_), channel_id=1, source_target_pairs={{0,0},{1,1},{2,8},{3,9},{4,16},{5,17},{6,24},{7,25},{8,2},{9,3},{1... | collective-permute-start | bytes 393224 | tf_op jit(solution)/shard_map/ppermute | solution.py:283
  88.8 1.0 cycle.5
  89.8 6.1 %collective-permute-start.32 = (bf16[4,128,128]{2,1,0:T(8,128)(2,1)S(1)}, bf16[4,128,128]{2,1,0:T(8,128)(2,1)S(1)}, u32[]{:S(2)}, u32[]{:S(2)}) collective-permute-start(bf16[4,128,128]{2,1,0:T(8,128)(2,1)S(1)} %collective-permute-done.31), channel_id=1, source_target_pairs={{4,1},{5,0},{6,9},{7,8},{0,17},{1,16},{2,25},{3,24},{12,3},{13,2},... | collective-permute-start | bytes 393224 | tf_op jit(solution)/shard_map/ppermute | solution.py:283
  95.9 3.9 %collective-permute-start.28 = (bf16[2,128,128]{2,1,0:T(8,128)(2,1)S(1)}, bf16[2,128,128]{2,1,0:T(8,128)(2,1)S(1)}, u32[]{:S(2)}, u32[]{:S(2)}) collective-permute-start(bf16[2,128,128]{2,1,0:T(8,128)(2,1)S(1)} %get-tuple-element.44.refs_5_), channel_id=1, source_target_pairs={{0,4},{1,5},{2,6},{3,7},{4,0},{5,1},{6,2},{7,3},{8,12},{9,13},{10,... | collective-permute-start | bytes 196616 | tf_op jit(solution)/shard_map/ppermute | solution.py:282
  99.8 1.8 %collective-permute-done.28 = bf16[2,128,128]{2,1,0:T(8,128)(2,1)S(1)} collective-permute-done((bf16[2,128,128]{2,1,0:T(8,128)(2,1)S(1)}, bf16[2,128,128]{2,1,0:T(8,128)(2,1)S(1)}, u32[]{:S(2)}, u32[]{:S(2)}) %collective-permute-start.28) | collective-permute-done | bytes 65568 | tf_op jit(solution)/shard_map/ppermute | solution.py:282
  101.6 4.8 %collective-permute-start.27 = (bf16[2,128,128]{2,1,0:T(8,128)(2,1)S(1)}, bf16[2,128,128]{2,1,0:T(8,128)(2,1)S(1)}, u32[]{:S(2)}, u32[]{:S(2)}) collective-permute-start(bf16[2,128,128]{2,1,0:T(8,128)(2,1)S(1)} %get-tuple-element.43.refs_4_), channel_id=1, source_target_pairs={{0,0},{1,1},{2,8},{3,9},{4,16},{5,17},{6,24},{7,25},{8,2},{9,3},{1... | collective-permute-start | bytes 196616 | tf_op jit(solution)/shard_map/ppermute | solution.py:283
  106.5 0.5 collective-permute-start.29
  106.9 3.5 %final.1 = (f32[4,12,64,128]{3,2,1,0:T(8,128)}, s32[1,12]{1,0:T(1,128)S(1)}) custom-call(s32[4,2,12]{2,1,0:T(2,128)S(1)} %bitcast.31, s32[4]{0:T(128)S(1)} %copy-done.4, bf16[6,128,128]{2,1,0:T(8,128)(2,1)S(1)} %get-tuple-element.30.refs_0_, bf16[6,128,128]{2,1,0:T(8,128)(2,1)S(1)} %get-tuple-element.31.refs_1_, ...), custom_call_target="tpu_custom_call" | custom-call | tf_op jit(solution)/shard_map/final/pallas_call | solution.py:289
  110.5 1.9 %patch.2.refs_8_ = f32[4,12,64,128]{3,2,1,0:T(8,128)} custom-call(s32[1,12]{1,0:T(1,128)S(1)} %get-tuple-element.45.table_ref, bf16[6,128,128]{2,1,0:T(8,128)(2,1)S(1)} %get-tuple-element.30.refs_0_, bf16[6,128,128]{2,1,0:T(8,128)(2,1)S(1)} %get-tuple-element.31.refs_1_, ...), custom_call_target="tpu_custom_call", output_to_operand_aliasing={{}: (9, {})} | custom-call | tf_op jit(solution)/shard_map/patch/pallas_call | solution.py:303
  112.5 2.7 %collective-permute-done.29.refs_7_ = bf16[2,128,128]{2,1,0:T(8,128)(2,1)S(1)} collective-permute-done((bf16[2,128,128]{2,1,0:T(8,128)(2,1)S(1)}, bf16[2,128,128]{2,1,0:T(8,128)(2,1)S(1)}, u32[]{:S(2)}, u32[]{:S(2)}) %collective-permute-start.29) | collective-permute-done | bytes 65568 | tf_op jit(solution)/shard_map/ppermute | solution.py:283
  115.2 1.5 %patch.3 = f32[4,12,64,128]{3,2,1,0:T(8,128)} custom-call(s32[1,12]{1,0:T(1,128)S(1)} %get-tuple-element.45.table_ref, bf16[6,128,128]{2,1,0:T(8,128)(2,1)S(1)} %get-tuple-element.30.refs_0_, bf16[6,128,128]{2,1,0:T(8,128)(2,1)S(1)} %get-tuple-element.31.refs_1_, bf16[4,128,128]{2,1,0:T(8,128)(2,1)S(1)} %get-tuple-element.37.refs_2_, ...), custom_call_target="tpu_custom_call", output_to_operand_aliasing={{}: (9, {})} | custom-call | tf_op jit(solution)/shard_map/patch/pallas_call | solution.py:303
  (39 shorter events, 0.3 us)
Async XLA Ops:
  0.0 1.1 copy-start.2
  1.5 19.8 %collective-permute-start.11 = (bf16[6,256,128]{2,1,0:T(8,128)(2,1)S(1)}, bf16[6,256,128]{2,1,0:T(8,128)(2,1)S(1)}, u32[]{:S(2)}, u32[]{:S(2)}) collective-permute-start(bf16[6,256,128]{2,1,0:T(8,128)(2,1)S(1)} %get-tuple-element.32.refs_1_), channel_id=1, source_target_pairs={{0,2},{1,3},{2,0},{3,1},{4,6},{5,7},{6,4},{7,5},{8,10},{9,11},{10,... | collective-permute-start | bytes 1179656 | tf_op jit(solution)/shard_map/ppermute | solution.py:258
  1.6 21.2 %collective-permute-start.13 = (bf16[6,256,128]{2,1,0:T(8,128)(2,1)S(1)}, bf16[6,256,128]{2,1,0:T(8,128)(2,1)S(1)}, u32[]{:S(2)}, u32[]{:S(2)}) collective-permute-start(bf16[6,256,128]{2,1,0:T(8,128)(2,1)S(1)} %get-tuple-element.32.refs_1_), channel_id=1, source_target_pairs={{0,4},{1,5},{2,6},{3,7},{4,0},{5,1},{6,2},{7,3},{8,12},{9,13},{10,... | collective-permute-start | bytes 1179656 | tf_op jit(solution)/shard_map/ppermute | solution.py:258
  3.1 1.9 %copy-start = (bf16[4,2,47,4096]{3,1,2,0:T(2,128)(2,1)S(1)}, bf16[4,2,47,4096]{3,1,2,0:T(2,128)(2,1)}, u32[]{:S(2)}) copy-start(bf16[4,2,47,4096]{3,1,2,0:T(2,128)(2,1)} %param.5) | copy-start | bytes 9240580
  5.0 0.7 copy-start.3
  6.8 9.8 %collective-permute-start.17 = (bf16[4,256,128]{2,1,0:T(8,128)(2,1)S(1)}, bf16[4,256,128]{2,1,0:T(8,128)(2,1)S(1)}, u32[]{:S(2)}, u32[]{:S(2)}) collective-permute-start(bf16[4,256,128]{2,1,0:T(8,128)(2,1)S(1)} %get-tuple-element.34), channel_id=1, source_target_pairs={{0,8},{8,0},{16,24},{24,16},{1,9},{9,1},{17,25},{25,17},{2,10},{10... | collective-permute-start | bytes 786440 | tf_op jit(solution)/shard_map/ppermute | solution.py:239
  8.1 14.7 %collective-permute-start.15 = (bf16[6,256,128]{2,1,0:T(8,128)(2,1)S(1)}, bf16[6,256,128]{2,1,0:T(8,128)(2,1)S(1)}, u32[]{:S(2)}, u32[]{:S(2)}) collective-permute-start(bf16[6,256,128]{2,1,0:T(8,128)(2,1)S(1)} %get-tuple-element.32.refs_1_), channel_id=1, source_target_pairs={{0,6},{1,7},{2,4},{3,5},{4,2},{5,3},{6,0},{7,1},{8,14},{9,15},{10,... | collective-permute-start | bytes 1179656 | tf_op jit(solution)/shard_map/ppermute | solution.py:258
  9.3 8.9 %collective-permute-start.18 = (bf16[4,256,128]{2,1,0:T(8,128)(2,1)S(1)}, bf16[4,256,128]{2,1,0:T(8,128)(2,1)S(1)}, u32[]{:S(2)}, u32[]{:S(2)}) collective-permute-start(bf16[4,256,128]{2,1,0:T(8,128)(2,1)S(1)} %get-tuple-element.35), channel_id=1, source_target_pairs={{0,16},{8,24},{16,0},{24,8},{1,17},{9,25},{17,1},{25,9},{2,18},{10... | collective-permute-start | bytes 786440 | tf_op jit(solution)/shard_map/ppermute | solution.py:239
  16.5 15.6 %collective-permute-start.7 = (bf16[6,256,128]{2,1,0:T(8,128)(2,1)S(1)}, bf16[6,256,128]{2,1,0:T(8,128)(2,1)S(1)}, u32[]{:S(2)}, u32[]{:S(2)}) collective-permute-start(bf16[6,256,128]{2,1,0:T(8,128)(2,1)S(1)} %get-tuple-element.28), channel_id=1, source_target_pairs={{0,8},{8,0},{16,24},{24,16},{1,9},{9,1},{17,25},{25,17},{2,10},{10... | collective-permute-start | bytes 1179656 | tf_op jit(solution)/shard_map/ppermute | solution.py:239
  18.2 19.0 %collective-permute-start.8 = (bf16[6,256,128]{2,1,0:T(8,128)(2,1)S(1)}, bf16[6,256,128]{2,1,0:T(8,128)(2,1)S(1)}, u32[]{:S(2)}, u32[]{:S(2)}) collective-permute-start(bf16[6,256,128]{2,1,0:T(8,128)(2,1)S(1)} %get-tuple-element.29), channel_id=1, source_target_pairs={{0,16},{8,24},{16,0},{24,8},{1,17},{9,25},{17,1},{25,9},{2,18},{10... | collective-permute-start | bytes 1179656 | tf_op jit(solution)/shard_map/ppermute | solution.py:239
  21.3 37.3 %copy-start.4 = (s32[4]{0:T(128)S(1)}, s32[4]{0:T(128)}, u32[]{:S(2)}) copy-start(s32[4]{0:T(128)} %count_ref.1) | copy-start | bytes 52
  21.3 31.7 %collective-permute-start.1 = (bf16[6,256,128]{2,1,0:T(8,128)(2,1)S(1)}, bf16[6,256,128]{2,1,0:T(8,128)(2,1)S(1)}, u32[]{:S(2)}, u32[]{:S(2)}) collective-permute-start(bf16[6,256,128]{2,1,0:T(8,128)(2,1)S(1)} %get-tuple-element.26.refs_1_), channel_id=1, source_target_pairs={{0,2},{1,3},{2,0},{3,1},{4,6},{5,7},{6,4},{7,5},{8,10},{9,11},{10,... | collective-permute-start | bytes 1179656 | tf_op jit(solution)/shard_map/ppermute | solution.py:258
  22.8 30.2 %collective-permute-start.3 = (bf16[6,256,128]{2,1,0:T(8,128)(2,1)S(1)}, bf16[6,256,128]{2,1,0:T(8,128)(2,1)S(1)}, u32[]{:S(2)}, u32[]{:S(2)}) collective-permute-start(bf16[6,256,128]{2,1,0:T(8,128)(2,1)S(1)} %get-tuple-element.26.refs_1_), channel_id=1, source_target_pairs={{0,4},{1,5},{2,6},{3,7},{4,0},{5,1},{6,2},{7,3},{8,12},{9,13},{10,... | collective-permute-start | bytes 1179656 | tf_op jit(solution)/shard_map/ppermute | solution.py:258
  22.8 30.7 %collective-permute-start.5 = (bf16[6,256,128]{2,1,0:T(8,128)(2,1)S(1)}, bf16[6,256,128]{2,1,0:T(8,128)(2,1)S(1)}, u32[]{:S(2)}, u32[]{:S(2)}) collective-permute-start(bf16[6,256,128]{2,1,0:T(8,128)(2,1)S(1)} %get-tuple-element.26.refs_1_), channel_id=1, source_target_pairs={{0,6},{1,7},{2,4},{3,5},{4,2},{5,3},{6,0},{7,1},{8,14},{9,15},{10,... | collective-permute-start | bytes 1179656 | tf_op jit(solution)/shard_map/ppermute | solution.py:258
  32.1 21.5 %collective-permute-start.9 = (bf16[6,256,128]{2,1,0:T(8,128)(2,1)S(1)}, bf16[6,256,128]{2,1,0:T(8,128)(2,1)S(1)}, u32[]{:S(2)}, u32[]{:S(2)}) collective-permute-start(bf16[6,256,128]{2,1,0:T(8,128)(2,1)S(1)} %pick.5), channel_id=1, source_target_pairs={{0,24},{8,16},{16,8},{24,0},{1,25},{9,17},{17,9},{25,1},{2,26},{10... | collective-permute-start | bytes 1179656 | tf_op jit(solution)/shard_map/ppermute | solution.py:239
  37.2 17.1 %collective-permute-start = (bf16[6,256,128]{2,1,0:T(8,128)(2,1)S(1)}, bf16[6,256,128]{2,1,0:T(8,128)(2,1)S(1)}, u32[]{:S(2)}, u32[]{:S(2)}) collective-permute-start(bf16[6,256,128]{2,1,0:T(8,128)(2,1)S(1)} %get-tuple-element.26.refs_1_), channel_id=1, source_target_pairs={{0,1},{1,0},{2,3},{3,2},{4,5},{5,4},{6,7},{7,6},{8,9},{9,8},{10,11... | collective-permute-start | bytes 1179656 | tf_op jit(solution)/shard_map/ppermute | solution.py:258
  53.0 1.9 %collective-permute-start.2 = (bf16[6,256,128]{2,1,0:T(8,128)(2,1)S(1)}, bf16[6,256,128]{2,1,0:T(8,128)(2,1)S(1)}, u32[]{:S(2)}, u32[]{:S(2)}) collective-permute-start(bf16[6,256,128]{2,1,0:T(8,128)(2,1)S(1)} %collective-permute-done.1.refs_3_), channel_id=1, source_target_pairs={{0,1},{1,0},{2,3},{3,2},{4,5},{5,4},{6,7},{7,6},{8,9},{9,8},{10,11... | collective-permute-start | bytes 1179656 | tf_op jit(solution)/shard_map/ppermute | solution.py:258
  53.0 4.9 %collective-permute-start.4 = (bf16[6,256,128]{2,1,0:T(8,128)(2,1)S(1)}, bf16[6,256,128]{2,1,0:T(8,128)(2,1)S(1)}, u32[]{:S(2)}, u32[]{:S(2)}) collective-permute-start(bf16[6,256,128]{2,1,0:T(8,128)(2,1)S(1)} %collective-permute-done.3.refs_5_), channel_id=1, source_target_pairs={{0,1},{1,0},{2,3},{3,2},{4,5},{5,4},{6,7},{7,6},{8,9},{9,8},{10,11... | collective-permute-start | bytes 1179656 | tf_op jit(solution)/shard_map/ppermute | solution.py:258
  53.5 5.0 %collective-permute-start.6 = (bf16[6,256,128]{2,1,0:T(8,128)(2,1)S(1)}, bf16[6,256,128]{2,1,0:T(8,128)(2,1)S(1)}, u32[]{:S(2)}, u32[]{:S(2)}) collective-permute-start(bf16[6,256,128]{2,1,0:T(8,128)(2,1)S(1)} %collective-permute-done.5.refs_7_), channel_id=1, source_target_pairs={{0,1},{1,0},{2,3},{3,2},{4,5},{5,4},{6,7},{7,6},{8,9},{9,8},{10,11... | collective-permute-start | bytes 1179656 | tf_op jit(solution)/shard_map/ppermute | solution.py:258
  53.6 11.5 %collective-permute-start.10 = (bf16[6,256,128]{2,1,0:T(8,128)(2,1)S(1)}, bf16[6,256,128]{2,1,0:T(8,128)(2,1)S(1)}, u32[]{:S(2)}, u32[]{:S(2)}) collective-permute-start(bf16[6,256,128]{2,1,0:T(8,128)(2,1)S(1)} %get-tuple-element.32.refs_1_), channel_id=1, source_target_pairs={{0,1},{1,0},{2,3},{3,2},{4,5},{5,4},{6,7},{7,6},{8,9},{9,8},{10,11... | collective-permute-start | bytes 1179656 | tf_op jit(solution)/shard_map/ppermute | solution.py:258
  54.3 13.9 %collective-permute-start.12 = (bf16[6,256,128]{2,1,0:T(8,128)(2,1)S(1)}, bf16[6,256,128]{2,1,0:T(8,128)(2,1)S(1)}, u32[]{:S(2)}, u32[]{:S(2)}) collective-permute-start(bf16[6,256,128]{2,1,0:T(8,128)(2,1)S(1)} %collective-permute-done.11.refs_3_), channel_id=1, source_target_pairs={{0,1},{1,0},{2,3},{3,2},{4,5},{5,4},{6,7},{7,6},{8,9},{9,8},{10,11... | collective-permute-start | bytes 1179656 | tf_op jit(solution)/shard_map/ppermute | solution.py:258
  54.9 9.3 %collective-permute-start.19 = (bf16[4,256,128]{2,1,0:T(8,128)(2,1)S(1)}, bf16[4,256,128]{2,1,0:T(8,128)(2,1)S(1)}, u32[]{:S(2)}, u32[]{:S(2)}) collective-permute-start(bf16[4,256,128]{2,1,0:T(8,128)(2,1)S(1)} %get-tuple-element.36), channel_id=1, source_target_pairs={{0,24},{8,16},{16,8},{24,0},{1,25},{9,17},{17,9},{25,1},{2,26},{10... | collective-permute-start | bytes 786440 | tf_op jit(solution)/shard_map/ppermute | solution.py:239
  57.9 17.0 %collective-permute-start.14 = (bf16[6,256,128]{2,1,0:T(8,128)(2,1)S(1)}, bf16[6,256,128]{2,1,0:T(8,128)(2,1)S(1)}, u32[]{:S(2)}, u32[]{:S(2)}) collective-permute-start(bf16[6,256,128]{2,1,0:T(8,128)(2,1)S(1)} %collective-permute-done.13.refs_5_), channel_id=1, source_target_pairs={{0,1},{1,0},{2,3},{3,2},{4,5},{5,4},{6,7},{7,6},{8,9},{9,8},{10,11... | collective-permute-start | bytes 1179656 | tf_op jit(solution)/shard_map/ppermute | solution.py:258
  58.5 17.9 %collective-permute-start.16 = (bf16[6,256,128]{2,1,0:T(8,128)(2,1)S(1)}, bf16[6,256,128]{2,1,0:T(8,128)(2,1)S(1)}, u32[]{:S(2)}, u32[]{:S(2)}) collective-permute-start(bf16[6,256,128]{2,1,0:T(8,128)(2,1)S(1)} %collective-permute-done.15.refs_7_), channel_id=1, source_target_pairs={{0,1},{1,0},{2,3},{3,2},{4,5},{5,4},{6,7},{7,6},{8,9},{9,8},{10,11... | collective-permute-start | bytes 1179656 | tf_op jit(solution)/shard_map/ppermute | solution.py:258
  58.6 5.7 %copy-start.1 = (bf16[4,2,47,4096]{3,1,2,0:T(2,128)(2,1)S(1)}, bf16[4,2,47,4096]{3,1,2,0:T(2,128)(2,1)}, u32[]{:S(2)}) copy-start(bf16[4,2,47,4096]{3,1,2,0:T(2,128)(2,1)} %param.5) | copy-start | bytes 9240580
  64.2 14.8 %collective-permute-start.23 = (bf16[6,128,128]{2,1,0:T(8,128)(2,1)S(1)}, bf16[6,128,128]{2,1,0:T(8,128)(2,1)S(1)}, u32[]{:S(2)}, u32[]{:S(2)}) collective-permute-start(bf16[6,128,128]{2,1,0:T(8,128)(2,1)S(1)} %get-tuple-element.30.refs_0_), channel_id=1, source_target_pairs={{0,2},{1,3},{2,0},{3,1},{4,6},{5,7},{6,4},{7,5},{8,10},{9,11},{10,... | collective-permute-start | bytes 589832 | tf_op jit(solution)/shard_map/ppermute | solution.py:282
  65.2 14.7 %collective-permute-start.25 = (bf16[6,128,128]{2,1,0:T(8,128)(2,1)S(1)}, bf16[6,128,128]{2,1,0:T(8,128)(2,1)S(1)}, u32[]{:S(2)}, u32[]{:S(2)}) collective-permute-start(bf16[6,128,128]{2,1,0:T(8,128)(2,1)S(1)} %get-tuple-element.31.refs_1_), channel_id=1, source_target_pairs={{0,6},{1,7},{2,4},{3,5},{4,2},{5,3},{6,0},{7,1},{8,14},{9,15},{10,... | collective-permute-start | bytes 589832 | tf_op jit(solution)/shard_map/ppermute | solution.py:282
  68.3 10.7 %collective-permute-start.20 = (bf16[2,256,128]{2,1,0:T(8,128)(2,1)S(1)}, bf16[2,256,128]{2,1,0:T(8,128)(2,1)S(1)}, u32[]{:S(2)}, u32[]{:S(2)}) collective-permute-start(bf16[2,256,128]{2,1,0:T(8,128)(2,1)S(1)} %get-tuple-element.40), channel_id=1, source_target_pairs={{0,8},{8,0},{16,24},{24,16},{1,9},{9,1},{17,25},{25,17},{2,10},{10... | collective-permute-start | bytes 393224 | tf_op jit(solution)/shard_map/ppermute | solution.py:239
  74.9 11.0 %collective-permute-start.21 = (bf16[2,256,128]{2,1,0:T(8,128)(2,1)S(1)}, bf16[2,256,128]{2,1,0:T(8,128)(2,1)S(1)}, u32[]{:S(2)}, u32[]{:S(2)}) collective-permute-start(bf16[2,256,128]{2,1,0:T(8,128)(2,1)S(1)} %get-tuple-element.41), channel_id=1, source_target_pairs={{0,16},{8,24},{16,0},{24,8},{1,17},{9,25},{17,1},{25,9},{2,18},{10... | collective-permute-start | bytes 393224 | tf_op jit(solution)/shard_map/ppermute | solution.py:239
  76.4 12.4 %collective-permute-start.22 = (bf16[2,256,128]{2,1,0:T(8,128)(2,1)S(1)}, bf16[2,256,128]{2,1,0:T(8,128)(2,1)S(1)}, u32[]{:S(2)}, u32[]{:S(2)}) collective-permute-start(bf16[2,256,128]{2,1,0:T(8,128)(2,1)S(1)} %get-tuple-element.42), channel_id=1, source_target_pairs={{0,24},{8,16},{16,8},{24,0},{1,25},{9,17},{17,9},{25,1},{2,26},{10... | collective-permute-start | bytes 393224 | tf_op jit(solution)/shard_map/ppermute | solution.py:239
  79.0 10.9 %collective-permute-start.31 = (bf16[4,128,128]{2,1,0:T(8,128)(2,1)S(1)}, bf16[4,128,128]{2,1,0:T(8,128)(2,1)S(1)}, u32[]{:S(2)}, u32[]{:S(2)}) collective-permute-start(bf16[4,128,128]{2,1,0:T(8,128)(2,1)S(1)} %get-tuple-element.38.refs_3_), channel_id=1, source_target_pairs={{0,4},{1,5},{2,6},{3,7},{4,0},{5,1},{6,2},{7,3},{8,12},{9,13},{10,... | collective-permute-start | bytes 393224 | tf_op jit(solution)/shard_map/ppermute | solution.py:282
  79.1 27.4 %collective-permute-start.24 = (bf16[6,128,128]{2,1,0:T(8,128)(2,1)S(1)}, bf16[6,128,128]{2,1,0:T(8,128)(2,1)S(1)}, u32[]{:S(2)}, u32[]{:S(2)}) collective-permute-start(bf16[6,128,128]{2,1,0:T(8,128)(2,1)S(1)} %collective-permute-done.23), channel_id=1, source_target_pairs={{2,0},{3,1},{0,8},{1,9},{6,16},{7,17},{4,24},{5,25},{10,2},{11,3},... | collective-permute-start | bytes 589832 | tf_op jit(solution)/shard_map/ppermute | solution.py:283
  79.8 27.1 %collective-permute-start.26 = (bf16[6,128,128]{2,1,0:T(8,128)(2,1)S(1)}, bf16[6,128,128]{2,1,0:T(8,128)(2,1)S(1)}, u32[]{:S(2)}, u32[]{:S(2)}) collective-permute-start(bf16[6,128,128]{2,1,0:T(8,128)(2,1)S(1)} %collective-permute-done.25), channel_id=1, source_target_pairs={{6,1},{7,0},{4,9},{5,8},{2,17},{3,16},{0,25},{1,24},{14,3},{15,2},... | collective-permute-start | bytes 589832 | tf_op jit(solution)/shard_map/ppermute | solution.py:283
  85.9 24.6 %collective-permute-start.30 = (bf16[4,128,128]{2,1,0:T(8,128)(2,1)S(1)}, bf16[4,128,128]{2,1,0:T(8,128)(2,1)S(1)}, u32[]{:S(2)}, u32[]{:S(2)}) collective-permute-start(bf16[4,128,128]{2,1,0:T(8,128)(2,1)S(1)} %get-tuple-element.37.refs_2_), channel_id=1, source_target_pairs={{0,0},{1,1},{2,8},{3,9},{4,16},{5,17},{6,24},{7,25},{8,2},{9,3},{1... | collective-permute-start | bytes 393224 | tf_op jit(solution)/shard_map/ppermute | solution.py:283
  89.8 20.7 %collective-permute-start.32 = (bf16[4,128,128]{2,1,0:T(8,128)(2,1)S(1)}, bf16[4,128,128]{2,1,0:T(8,128)(2,1)S(1)}, u32[]{:S(2)}, u32[]{:S(2)}) collective-permute-start(bf16[4,128,128]{2,1,0:T(8,128)(2,1)S(1)} %collective-permute-done.31), channel_id=1, source_target_pairs={{4,1},{5,0},{6,9},{7,8},{0,17},{1,16},{2,25},{3,24},{12,3},{13,2},... | collective-permute-start | bytes 393224 | tf_op jit(solution)/shard_map/ppermute | solution.py:283
  95.9 5.7 %collective-permute-start.28 = (bf16[2,128,128]{2,1,0:T(8,128)(2,1)S(1)}, bf16[2,128,128]{2,1,0:T(8,128)(2,1)S(1)}, u32[]{:S(2)}, u32[]{:S(2)}) collective-permute-start(bf16[2,128,128]{2,1,0:T(8,128)(2,1)S(1)} %get-tuple-element.44.refs_5_), channel_id=1, source_target_pairs={{0,4},{1,5},{2,6},{3,7},{4,0},{5,1},{6,2},{7,3},{8,12},{9,13},{10,... | collective-permute-start | bytes 196616 | tf_op jit(solution)/shard_map/ppermute | solution.py:282
  101.6 10.8 %collective-permute-start.27 = (bf16[2,128,128]{2,1,0:T(8,128)(2,1)S(1)}, bf16[2,128,128]{2,1,0:T(8,128)(2,1)S(1)}, u32[]{:S(2)}, u32[]{:S(2)}) collective-permute-start(bf16[2,128,128]{2,1,0:T(8,128)(2,1)S(1)} %get-tuple-element.43.refs_4_), channel_id=1, source_target_pairs={{0,0},{1,1},{2,8},{3,9},{4,16},{5,17},{6,24},{7,25},{8,2},{9,3},{1... | collective-permute-start | bytes 196616 | tf_op jit(solution)/shard_map/ppermute | solution.py:283
  106.5 8.7 %collective-permute-start.29 = (bf16[2,128,128]{2,1,0:T(8,128)(2,1)S(1)}, bf16[2,128,128]{2,1,0:T(8,128)(2,1)S(1)}, u32[]{:S(2)}, u32[]{:S(2)}) collective-permute-start(bf16[2,128,128]{2,1,0:T(8,128)(2,1)S(1)} %collective-permute-done.28), channel_id=1, source_target_pairs={{4,1},{5,0},{6,9},{7,8},{0,17},{1,16},{2,25},{3,24},{12,3},{13,2},... | collective-permute-start | bytes 196616 | tf_op jit(solution)/shard_map/ppermute | solution.py:283

commit v7 on v6

--- a/solution.py
+++ b/solution.py
@@ -10,7 +10,7 @@
 
 TILE = 64
 LANES = 128
-SPLIT = (6, 4, 2)
+SPLIT = (7, 3, 2)
 HOPS = ((1, 3), (0, 2), (0, 2))
 VMEM = pl.BlockSpec(memory_space=pltpu.VMEM)
 SMEM = pl.BlockSpec(memory_space=pltpu.SMEM)
@@ -119,23 +119,13 @@
     return own + jnp.concatenate([held_their[p, t].astype(jnp.float32).T for p in range(ratio)], axis=0)
 
 
-def final_kernel(ratio, sizes, list_ref, count_ref, *refs):
-    slots = sum(sizes)
-    early = sizes[0]
-    owns = refs[: len(sizes) * ratio]
-    theirs = refs[len(sizes) * ratio : -3]
-    out_ref, table_ref, held_own, held_their = refs[-4:]
+def match_kernel(list_ref, count_ref, table_ref):
+    slots = table_ref.shape[1]
     my_row = lax.axis_index("row")
-    my_col = lax.axis_index("col")
-    core = lax.rem(my_col, ratio)
-    partner = my_col // ratio
-    collect(owns, held_own, sizes, ratio, core)
-    collect(theirs, held_their, sizes[:1], ratio, core)
+    partner = lax.axis_index("col") // (lax.axis_size("col") // lax.axis_size("row"))
     my_count = count_ref[my_row]
-    depth = out_ref.shape[0]
-
     for t in range(slots):
-        table_ref[0, t] = -1
+        table_ref[1, t] = -1
 
     def one(s, _):
         first = list_ref[my_row, 0, s]
@@ -144,27 +134,66 @@
         for t in range(slots):
             hit = (list_ref[partner, 0, t] == second) & (list_ref[partner, 1, t] == first)
             found = jnp.where(hit, t, found)
-        use = (s < my_count) & (found >= 0)
+        found = jnp.where(s < my_count, found, -1)
+        table_ref[0, s] = found
+
+        @pl.when(found >= 0)
+        def _():
+            table_ref[1, found] = s
+
+        return 0
+
+    lax.fori_loop(0, slots, one, 0)
+
+
+def begin_kernel(ratio, sizes, *refs):
+    owns = refs[:ratio]
+    out_ref, held_own, built, sem = refs[ratio:]
+    collect(owns, held_own, sizes[:1], ratio, lax.rem(lax.axis_index("col"), ratio))
+    copies = []
+    for s in range(sizes[0]):
+        built[s] = swap(summed(held_own, s, None, None, ratio)).reshape(built.shape[1:])
+        copies.append(pltpu.make_async_copy(built.at[s], out_ref.at[:, s], sem.at[s]))
+        copies[s].start()
+    for copy in copies:
+        copy.wait()
+
+
+def final_kernel(ratio, sizes, table_ref, *refs):
+    slots = sum(sizes)
+    early = sizes[0]
+    owns = refs[: len(sizes) * ratio]
+    theirs = refs[len(sizes) * ratio : -6]
+    _, out_ref, held_own, held_their, built, sem = refs[-6:]
+    core = lax.rem(lax.axis_index("col"), ratio)
+    collect(owns, held_own, sizes, ratio, core)
+    collect(theirs, held_their, sizes[:1], ratio, core)
+    needs, copies = [], []
+    for s in range(slots):
+        found = table_ref[0, s]
+        use = (found >= 0) & (found < early)
+        needs.append(use if s < early else None)
+        copies.append(pltpu.make_async_copy(built.at[s], out_ref.at[:, s], sem.at[s]))
 
         @pl.when(use)
-        def _():
-            table_ref[0, found] = s
-
-        use = use & (found < early)
-
-        @pl.when(use)
-        def _():
+        def _(s=s, found=found, use=use):
             x = summed(held_own, s, held_their, jnp.where(use, found, 0), ratio)
-            out_ref[:, s] = swap(x).reshape(depth, TILE, LANES)
-
-        @pl.when(jnp.logical_not(use))
-        def _():
-            x = summed(held_own, s, None, None, ratio)
-            out_ref[:, s] = swap(x).reshape(depth, TILE, LANES)
-
-        return 0
-
-    lax.fori_loop(0, slots, one, 0)
+            built[s] = swap(x).reshape(built.shape[1:])
+
+        if s >= early:
+
+            @pl.when(jnp.logical_not(use))
+            def _(s=s):
+                built[s] = swap(summed(held_own, s, None, None, ratio)).reshape(built.shape[1:])
+
+            copies[s].start()
+        else:
+            pl.when(use)(copies[s].start)
+    for need, copy in zip(needs, copies):
+        if need is None:
+            copy.wait()
+        else:
+            pl.when(need)(copy.wait)
 
 
 def patch_kernel(ratio, sizes, chunk, table_ref, *refs):
@@ -178,7 +207,7 @@
     depth = out_ref.shape[0]
     uses, copies = [], []
     for t in range(sizes[chunk]):
-        found = table_ref[0, early + t]
+        found = table_ref[1, early + t]
         uses.append(found >= 0)
         s = jnp.maximum(found, 0)
         copies.append(pltpu.make_async_copy(built.at[t], out_ref.at[:, s], sem.at[t]))
@@ -286,18 +315,42 @@
     out_shape = jax.ShapeDtypeStruct((occ_row, slots, square // LANES * occ_col, LANES), jnp.float32)
     block = (tall // ratio, wide)
     split = ratio
-    out, table = pl.pallas_call(
+    table = pl.pallas_call(
+        match_kernel,
+        out_shape=jax.ShapeDtypeStruct((2, slots), jnp.int32),
+        in_specs=[SMEM, SMEM],
+        out_specs=SMEM,
+        compiler_params=PARAMS,
+        name="match",
+    )(lists, tile_counts)
+    out = pl.pallas_call(
+        functools.partial(begin_kernel, ratio, sizes),
+        out_shape=out_shape,
+        in_specs=[VMEM] * ratio,
+        out_specs=HBM,
+        scratch_shapes=[
+            pltpu.VMEM((ratio, sizes[0]) + block, bf16),
+            pltpu.VMEM((sizes[0], occ_row, TILE, LANES), jnp.float32),
+            pltpu.SemaphoreType.DMA((sizes[0],)),
+        ],
+        compiler_params=PARAMS,
+        name="begin",
+    )(*owns[:ratio])
+    out = pl.pallas_call(
         functools.partial(final_kernel, ratio, sizes),
-        out_shape=[out_shape, jax.ShapeDtypeStruct((1, slots), jnp.int32)],
-        in_specs=[SMEM, SMEM] + [VMEM] * (len(owns) + split),
-        out_specs=[VMEM, SMEM],
+        out_shape=out_shape,
+        in_specs=[SMEM] + [VMEM] * (len(owns) + split) + [HBM],
+        out_specs=HBM,
         scratch_shapes=[
             pltpu.VMEM((ratio, slots) + block, bf16),
             pltpu.VMEM((ratio, sizes[0]) + block, bf16),
+            pltpu.VMEM((slots, occ_row, TILE, LANES), jnp.float32),
+            pltpu.SemaphoreType.DMA((slots,)),
         ],
+        input_output_aliases={1 + len(owns) + split: 0},
         compiler_params=PARAMS,
         name="final",
-    )(lists, tile_counts, *owns, *theirs[:split])
+    )(table, *owns, *theirs[:split], out)
     for chunk in range(1, len(sizes)):
         late = sizes[chunk]
         out = pl.pallas_call(

time: 117 us -> 126 us (1.077)
  waiting for transfers between devices: 21.7 us -> 44 us
  starting transfers between devices: 75.6 us -> 61 us
  Pallas kernels: 15.5 us -> 16.8 us
    ppermute x9, waiting for transfers between devices: 16.6 us -> 42.1 us  [on_device(): got.append(lax.ppermute(picked[shift], 'row', pairs))]
    ppermute x14, starting transfers between devices: 23.3 us -> 9.37 us  [on_device(): lax.ppermute(source, 'col', [(c, c ^ step) for c in range(cols)])]
    ppermute x6, starting transfers between devices: 21 us -> 27.3 us  [on_device(): lax.ppermute(block, ('row', 'col'), mirror_pairs(rows, cols, step, hop))]
    ppermute x4, starting transfers between devices: 7.1 us -> 2.56 us  [on_device(): block = lax.ppermute(block, 'col', [(c, c ^ hop) for c in range(cols)])]
    ppermute x9, starting transfers between devices: 24.1 us -> 21.8 us  [on_device(): got.append(lax.ppermute(picked[shift], 'row', pairs))]
    ppermute x4, waiting for transfers between devices: 1.83 us -> 0.01 us  [on_device(): block = lax.ppermute(block, 'col', [(c, c ^ hop) for c in range(cols)])]
    ppermute x6, waiting for transfers between devices: 2.71 us -> 1.26 us  [on_device(): lax.ppermute(block, ('row', 'col'), mirror_pairs(rows, cols, step, hop))]
    pallas_call x1 -> x3, Pallas kernels: 3.54 us -> 4.98 us  [the longest x1 2.16 us: on_device(): pl.pallas_call(functools.partial(final_kernel, ratio, sizes), out_shape=o...]
  transfers between devices with their start and end apart: 33 -> 33, of which waited for: 8 -> 8; matrix products, arithmetic and copies ran while one was open for 0% -> 0% of each run, Pallas kernels for 12% -> 11%
where the time goes in v7:
time: 126 us
  starting transfers between devices  61 us (48%)
  waiting for transfers between devices  44 us (35%)
  Pallas kernels  16.8 us (13%)
  local copies, waits for them, and re-layouts  3.7 us (3%)
    ppermute x9, waiting for transfers between devices, on_device(): got.append(lax.ppermute(picked[shift], 'row', pairs))  42.1 us
    ppermute x6, starting transfers between devices, on_device(): lax.ppermute(block, ('row', 'col'), mirror_pairs(rows, cols, step, hop))  27.3 us
    ppermute x9, starting transfers between devices, on_device(): got.append(lax.ppermute(picked[shift], 'row', pairs))  21.8 us
    ppermute x14, starting transfers between devices, on_device(): lax.ppermute(source, 'col', [(c, c ^ step) for c in range(cols)])  9.37 us
    pallas_call x3, Pallas kernels, on_device(): pl.pallas_call(functools.partial(cycle_kernel, rows, cols, ratio, base, b...  4.17 us
    pallas_call x4, Pallas kernels, on_device(): pl.pallas_call(functools.partial(pick_kernel, base, size, tuple(shifts)),...  4.02 us
    unnamed x12, local copies, waits for them, and re-layouts  3.7 us
    pallas_call x2, Pallas kernels, on_device(): pl.pallas_call(functools.partial(patch_kernel, ratio, sizes, chunk), out_...  3.21 us
  transfers between devices with their start and end apart: 33, of which 8 were waited for; matrix products, arithmetic and copies ran while one was open for 0% of the time, Pallas kernels for 11%

profile of v7, /device:TPU:3, one launch (start us, length us, event | category | flops | bytes accessed | tf_op | source)
XLA Modules:
  0.0 125.7 jit_solution(16237111456533295332)
XLA Ops:
  0.0 1.9 %copy-done = bf16[4,2,47,4096]{3,1,2,0:T(2,128)(2,1)S(1)} copy-done((bf16[4,2,47,4096]{3,1,2,0:T(2,128)(2,1)S(1)}, bf16[4,2,47,4096]{3,1,2,0:T(2,128)(2,1)}, u32[]{:S(2)}) %copy-start) | copy-done | bytes 3080216
  1.9 0.7 copy-done.3
  2.6 1.0 pick.6
  3.6 1.4 %collective-permute-start.17 = (bf16[3,256,128]{2,1,0:T(8,128)(2,1)S(1)}, bf16[3,256,128]{2,1,0:T(8,128)(2,1)S(1)}, u32[]{:S(2)}, u32[]{:S(2)}) collective-permute-start(bf16[3,256,128]{2,1,0:T(8,128)(2,1)S(1)} %get-tuple-element.32), channel_id=1, source_target_pairs={{0,8},{8,0},{16,24},{24,16},{1,9},{9,1},{17,25},{25,17},{2,10},{10... | collective-permute-start | bytes 589832 | tf_op jit(solution)/shard_map/ppermute | solution.py:268
  4.9 1.1 copy-done.2
  6.1 0.4 left.1
  6.5 0.3 collective-permute-start.11
  6.8 1.2 collective-permute-start.13
  8.0 1.2 collective-permute-start.15
  9.2 2.3 %collective-permute-start.18 = (bf16[3,256,128]{2,1,0:T(8,128)(2,1)S(1)}, bf16[3,256,128]{2,1,0:T(8,128)(2,1)S(1)}, u32[]{:S(2)}, u32[]{:S(2)}) collective-permute-start(bf16[3,256,128]{2,1,0:T(8,128)(2,1)S(1)} %get-tuple-element.33), channel_id=1, source_target_pairs={{0,16},{8,24},{16,0},{24,8},{1,17},{9,25},{17,1},{25,9},{2,18},{10... | collective-permute-start | bytes 589832 | tf_op jit(solution)/shard_map/ppermute | solution.py:268
  11.5 1.3 %pick.4 = (bf16[7,256,128]{2,1,0:T(8,128)(2,1)S(1)}, bf16[7,256,128]{2,1,0:T(8,128)(2,1)S(1)}, bf16[7,256,128]{2,1,0:T(8,128)(2,1)S(1)}) custom-call(s32[4,2,12]{2,1,0:T(2,128)S(1)} %bitcast.28, bf16[4,47,64,128]{3,2,1,0:T(8,128)(2,1)S(1)} %bitcast.23), custom_call_target="tpu_custom_call" | custom-call | tf_op jit(solution)/shard_map/pick/pallas_call | solution.py:256
  12.8 0.2 collective-permute-start.7
  13.0 8.0 %collective-permute-done.18.refs_11_ = bf16[3,256,128]{2,1,0:T(8,128)(2,1)S(1)} collective-permute-done((bf16[3,256,128]{2,1,0:T(8,128)(2,1)S(1)}, bf16[3,256,128]{2,1,0:T(8,128)(2,1)S(1)}, u32[]{:S(2)}, u32[]{:S(2)}) %collective-permute-start.18) | collective-permute-done | bytes 196640 | tf_op jit(solution)/shard_map/ppermute | solution.py:268
  21.0 0.3 collective-permute-start.1
  21.3 1.2 collective-permute-start.3
  22.6 0.3 collective-permute-done.15.refs_7_
  22.8 0.9 collective-permute-start.5
  23.7 0.9 pick.5
  24.6 5.9 %collective-permute-done.7.refs_10_ = bf16[7,256,128]{2,1,0:T(8,128)(2,1)S(1)} collective-permute-done((bf16[7,256,128]{2,1,0:T(8,128)(2,1)S(1)}, bf16[7,256,128]{2,1,0:T(8,128)(2,1)S(1)}, u32[]{:S(2)}, u32[]{:S(2)}) %collective-permute-start.7) | collective-permute-done | bytes 458784 | tf_op jit(solution)/shard_map/ppermute | solution.py:268
  30.5 22.8 %collective-permute-done.8.refs_11_ = bf16[7,256,128]{2,1,0:T(8,128)(2,1)S(1)} collective-permute-done((bf16[7,256,128]{2,1,0:T(8,128)(2,1)S(1)}, bf16[7,256,128]{2,1,0:T(8,128)(2,1)S(1)}, u32[]{:S(2)}, u32[]{:S(2)}) %collective-permute-start.8) | collective-permute-done | bytes 458784 | tf_op jit(solution)/shard_map/ppermute | solution.py:268
  53.3 2.0 %collective-permute-start = (bf16[7,256,128]{2,1,0:T(8,128)(2,1)S(1)}, bf16[7,256,128]{2,1,0:T(8,128)(2,1)S(1)}, u32[]{:S(2)}, u32[]{:S(2)}) collective-permute-start(bf16[7,256,128]{2,1,0:T(8,128)(2,1)S(1)} %get-tuple-element.24.refs_1_), channel_id=1, source_target_pairs={{0,1},{1,0},{2,3},{3,2},{4,5},{5,4},{6,7},{7,6},{8,9},{9,8},{10,11... | collective-permute-start | bytes 1376264 | tf_op jit(solution)/shard_map/ppermute | solution.py:287
  55.3 0.5 collective-permute-start.4
  55.9 0.4 collective-permute-start.10
  56.3 0.4 collective-permute-done.refs_2_
  56.7 2.5 %collective-permute-start.19 = (bf16[3,256,128]{2,1,0:T(8,128)(2,1)S(1)}, bf16[3,256,128]{2,1,0:T(8,128)(2,1)S(1)}, u32[]{:S(2)}, u32[]{:S(2)}) collective-permute-start(bf16[3,256,128]{2,1,0:T(8,128)(2,1)S(1)} %get-tuple-element.34), channel_id=1, source_target_pairs={{0,24},{8,16},{16,8},{24,0},{1,25},{9,17},{17,9},{25,1},{2,26},{10... | collective-permute-start | bytes 589832 | tf_op jit(solution)/shard_map/ppermute | solution.py:268
  59.2 0.7 collective-permute-start.12
  59.9 0.4 collective-permute-start.16
  60.4 1.9 %cycle.3 = (bf16[7,128,128]{2,1,0:T(8,128)(2,1)S(1)}, bf16[7,128,128]{2,1,0:T(8,128)(2,1)S(1)}) custom-call(s32[4]{0:T(128)S(1)} %copy-done.5, bf16[7,256,128]{2,1,0:T(8,128)(2,1)S(1)} %get-tuple-element.24.refs_1_, bf16[7,256,128]{2,1,0:T(8,128)(2,1)S(1)} %collective-permute-done.refs_2_, bf16[7,256,128]{2,1,0:T(8,128)(2,1)S(1)} %collective-permute-done.1.refs_3_, ...), custom_call_target="tpu_custom_call" | custom-call | tf_op jit(solution)/shard_map/cycle/pallas_call | solution.py:293
  62.3 2.4 %collective-permute-done.19.refs_12_ = bf16[3,256,128]{2,1,0:T(8,128)(2,1)S(1)} collective-permute-done((bf16[3,256,128]{2,1,0:T(8,128)(2,1)S(1)}, bf16[3,256,128]{2,1,0:T(8,128)(2,1)S(1)}, u32[]{:S(2)}, u32[]{:S(2)}) %collective-permute-start.19) | collective-permute-done | bytes 196640 | tf_op jit(solution)/shard_map/ppermute | solution.py:268
  64.9 2.2 %collective-permute-start.31 = (bf16[7,128,128]{2,1,0:T(8,128)(2,1)S(1)}, bf16[7,128,128]{2,1,0:T(8,128)(2,1)S(1)}, u32[]{:S(2)}, u32[]{:S(2)}) collective-permute-start(bf16[7,128,128]{2,1,0:T(8,128)(2,1)S(1)} %get-tuple-element.29.refs_1_), channel_id=1, source_target_pairs={{0,6},{1,7},{2,4},{3,5},{4,2},{5,3},{6,0},{7,1},{8,14},{9,15},{10,... | collective-permute-start | bytes 688136 | tf_op jit(solution)/shard_map/ppermute | solution.py:311
  67.1 0.9 pick.7
  68.0 10.7 %collective-permute-start.20 = (bf16[2,256,128]{2,1,0:T(8,128)(2,1)S(1)}, bf16[2,256,128]{2,1,0:T(8,128)(2,1)S(1)}, u32[]{:S(2)}, u32[]{:S(2)}) collective-permute-start(bf16[2,256,128]{2,1,0:T(8,128)(2,1)S(1)} %get-tuple-element.38), channel_id=1, source_target_pairs={{0,8},{8,0},{16,24},{24,16},{1,9},{9,1},{17,25},{25,17},{2,10},{10... | collective-permute-start | bytes 393224 | tf_op jit(solution)/shard_map/ppermute | solution.py:268
  78.7 0.3 collective-permute-start.30
  78.9 2.7 %collective-permute-start.21 = (bf16[2,256,128]{2,1,0:T(8,128)(2,1)S(1)}, bf16[2,256,128]{2,1,0:T(8,128)(2,1)S(1)}, u32[]{:S(2)}, u32[]{:S(2)}) collective-permute-start(bf16[2,256,128]{2,1,0:T(8,128)(2,1)S(1)} %get-tuple-element.39), channel_id=1, source_target_pairs={{0,16},{8,24},{16,0},{24,8},{1,17},{9,25},{17,1},{25,9},{2,18},{10... | collective-permute-start | bytes 393224 | tf_op jit(solution)/shard_map/ppermute | solution.py:268
  81.6 2.1 %collective-permute-start.22 = (bf16[2,256,128]{2,1,0:T(8,128)(2,1)S(1)}, bf16[2,256,128]{2,1,0:T(8,128)(2,1)S(1)}, u32[]{:S(2)}, u32[]{:S(2)}) collective-permute-start(bf16[2,256,128]{2,1,0:T(8,128)(2,1)S(1)} %get-tuple-element.40), channel_id=1, source_target_pairs={{0,24},{8,16},{16,8},{24,0},{1,25},{9,17},{17,9},{25,1},{2,26},{10... | collective-permute-start | bytes 393224 | tf_op jit(solution)/shard_map/ppermute | solution.py:268
  83.7 11.6 %collective-permute-start.32 = (bf16[7,128,128]{2,1,0:T(8,128)(2,1)S(1)}, bf16[7,128,128]{2,1,0:T(8,128)(2,1)S(1)}, u32[]{:S(2)}, u32[]{:S(2)}) collective-permute-start(bf16[7,128,128]{2,1,0:T(8,128)(2,1)S(1)} %collective-permute-done.31), channel_id=1, source_target_pairs={{6,1},{7,0},{4,9},{5,8},{2,17},{3,16},{0,25},{1,24},{14,3},{15,2},... | collective-permute-start | bytes 688136 | tf_op jit(solution)/shard_map/ppermute | solution.py:312
  95.2 1.2 cycle.4
  96.6 3.1 %collective-permute-done.21.refs_11_ = bf16[2,256,128]{2,1,0:T(8,128)(2,1)S(1)} collective-permute-done((bf16[2,256,128]{2,1,0:T(8,128)(2,1)S(1)}, bf16[2,256,128]{2,1,0:T(8,128)(2,1)S(1)}, u32[]{:S(2)}, u32[]{:S(2)}) %collective-permute-start.21) | collective-permute-done | bytes 131104 | tf_op jit(solution)/shard_map/ppermute | solution.py:268
  99.6 1.0 cycle.5
  100.7 7.2 %collective-permute-start.26 = (bf16[3,128,128]{2,1,0:T(8,128)(2,1)S(1)}, bf16[3,128,128]{2,1,0:T(8,128)(2,1)S(1)}, u32[]{:S(2)}, u32[]{:S(2)}) collective-permute-start(bf16[3,128,128]{2,1,0:T(8,128)(2,1)S(1)} %get-tuple-element.35.refs_2_), channel_id=1, source_target_pairs={{0,0},{1,1},{2,8},{3,9},{4,16},{5,17},{6,24},{7,25},{8,2},{9,3},{1... | collective-permute-start | bytes 294920 | tf_op jit(solution)/shard_map/ppermute | solution.py:312
  107.9 3.9 %collective-permute-start.28 = (bf16[3,128,128]{2,1,0:T(8,128)(2,1)S(1)}, bf16[3,128,128]{2,1,0:T(8,128)(2,1)S(1)}, u32[]{:S(2)}, u32[]{:S(2)}) collective-permute-start(bf16[3,128,128]{2,1,0:T(8,128)(2,1)S(1)} %collective-permute-done.27), channel_id=1, source_target_pairs={{4,1},{5,0},{6,9},{7,8},{0,17},{1,16},{2,25},{3,24},{12,3},{13,2},... | collective-permute-start | bytes 294920 | tf_op jit(solution)/shard_map/ppermute | solution.py:312
  111.8 4.3 %collective-permute-start.23 = (bf16[2,128,128]{2,1,0:T(8,128)(2,1)S(1)}, bf16[2,128,128]{2,1,0:T(8,128)(2,1)S(1)}, u32[]{:S(2)}, u32[]{:S(2)}) collective-permute-start(bf16[2,128,128]{2,1,0:T(8,128)(2,1)S(1)} %get-tuple-element.41.refs_4_), channel_id=1, source_target_pairs={{0,0},{1,1},{2,8},{3,9},{4,16},{5,17},{6,24},{7,25},{8,2},{9,3},{1... | collective-permute-start | bytes 196616 | tf_op jit(solution)/shard_map/ppermute | solution.py:312
  116.2 1.7 %match.1.table_ref = s32[2,12]{1,0:T(2,128)S(1)} custom-call(s32[4,2,12]{2,1,0:T(2,128)S(1)} %bitcast.31, s32[4]{0:T(128)S(1)} %copy-done.5), custom_call_target="tpu_custom_call" | custom-call | tf_op jit(solution)/shard_map/match/pallas_call | solution.py:318
  117.9 1.1 begin.1.refs_8_
  119.0 2.2 %final.1.refs_8_ = f32[4,12,64,128]{3,2,1,0:T(8,128)} custom-call(s32[2,12]{1,0:T(2,128)S(1)} %match.1.table_ref, bf16[7,128,128]{2,1,0:T(8,128)(2,1)S(1)} %get-tuple-element.28.refs_0_, bf16[7,128,128]{2,1,0:T(8,128)(2,1)S(1)} %get-tuple-element.29.refs_1_, bf16[3,128,128]{2,1,0:T(8,128)(2,1)S(1)} %get-tuple-element.35.refs_2_, ...), custom_call_target="tpu_custom_call", output_to_operand_aliasing={{}: (9, {})} | custom-call | tf_op jit(solution)/shard_map/final/pallas_call | solution.py:339
  121.2 1.2 collective-permute-done.28.refs_7_
  122.5 1.7 %patch.2.refs_8_ = f32[4,12,64,128]{3,2,1,0:T(8,128)} custom-call(s32[2,12]{1,0:T(2,128)S(1)} %match.1.table_ref, bf16[7,128,128]{2,1,0:T(8,128)(2,1)S(1)} %get-tuple-element.28.refs_0_, bf16[7,128,128]{2,1,0:T(8,128)(2,1)S(1)} %get-tuple-element.29.refs_1_, bf16[3,128,128]{2,1,0:T(8,128)(2,1)S(1)} %get-tuple-element.35.refs_2_, ...), custom_call_target="tpu_custom_call", output_to_operand_aliasing={{}: (9, {})} | custom-call | tf_op jit(solution)/shard_map/patch/pallas_call | solution.py:356
  124.2 1.5 %patch.3 = f32[4,12,64,128]{3,2,1,0:T(8,128)} custom-call(s32[2,12]{1,0:T(2,128)S(1)} %match.1.table_ref, bf16[7,128,128]{2,1,0:T(8,128)(2,1)S(1)} %get-tuple-element.28.refs_0_, bf16[7,128,128]{2,1,0:T(8,128)(2,1)S(1)} %get-tuple-element.29.refs_1_, bf16[3,128,128]{2,1,0:T(8,128)(2,1)S(1)} %get-tuple-element.35.refs_2_, ...), custom_call_target="tpu_custom_call", output_to_operand_aliasing={{}: (9, {})} | custom-call | tf_op jit(solution)/shard_map/patch/pallas_call | solution.py:356
  (43 shorter events, 0.8 us)
Async XLA Ops:
  0.0 1.9 %copy-start = (bf16[4,2,47,4096]{3,1,2,0:T(2,128)(2,1)S(1)}, bf16[4,2,47,4096]{3,1,2,0:T(2,128)(2,1)}, u32[]{:S(2)}) copy-start(bf16[4,2,47,4096]{3,1,2,0:T(2,128)(2,1)} %param.5) | copy-start | bytes 9240580
  1.9 0.7 copy-start.3
  2.6 8.9 %copy-start.1 = (bf16[4,2,47,4096]{3,1,2,0:T(2,128)(2,1)S(1)}, bf16[4,2,47,4096]{3,1,2,0:T(2,128)(2,1)}, u32[]{:S(2)}) copy-start(bf16[4,2,47,4096]{3,1,2,0:T(2,128)(2,1)} %param.5) | copy-start | bytes 9240580
  2.6 8.9 %copy-start.4 = (s32[4,12,2]{1,2,0:T(2,128)S(1)}, s32[4,12,2]{1,2,0:T(2,128)}, u32[]{:S(2)}) copy-start(s32[4,12,2]{1,2,0:T(2,128)} %param.6) | copy-start | bytes 1156
  3.6 9.2 %collective-permute-start.17 = (bf16[3,256,128]{2,1,0:T(8,128)(2,1)S(1)}, bf16[3,256,128]{2,1,0:T(8,128)(2,1)S(1)}, u32[]{:S(2)}, u32[]{:S(2)}) collective-permute-start(bf16[3,256,128]{2,1,0:T(8,128)(2,1)S(1)} %get-tuple-element.32), channel_id=1, source_target_pairs={{0,8},{8,0},{16,24},{24,16},{1,9},{9,1},{17,25},{25,17},{2,10},{10... | collective-permute-start | bytes 589832 | tf_op jit(solution)/shard_map/ppermute | solution.py:268
  4.9 1.1 copy-start.2
  6.5 14.5 %collective-permute-start.11 = (bf16[5,256,128]{2,1,0:T(8,128)(2,1)S(1)}, bf16[5,256,128]{2,1,0:T(8,128)(2,1)S(1)}, u32[]{:S(2)}, u32[]{:S(2)}) collective-permute-start(bf16[5,256,128]{2,1,0:T(8,128)(2,1)S(1)} %get-tuple-element.30.refs_1_), channel_id=1, source_target_pairs={{0,2},{1,3},{2,0},{3,1},{4,6},{5,7},{6,4},{7,5},{8,10},{9,11},{10,... | collective-permute-start | bytes 983048 | tf_op jit(solution)/shard_map/ppermute | solution.py:287
  6.8 14.5 %collective-permute-start.13 = (bf16[5,256,128]{2,1,0:T(8,128)(2,1)S(1)}, bf16[5,256,128]{2,1,0:T(8,128)(2,1)S(1)}, u32[]{:S(2)}, u32[]{:S(2)}) collective-permute-start(bf16[5,256,128]{2,1,0:T(8,128)(2,1)S(1)} %get-tuple-element.30.refs_1_), channel_id=1, source_target_pairs={{0,4},{1,5},{2,6},{3,7},{4,0},{5,1},{6,2},{7,3},{8,12},{9,13},{10,... | collective-permute-start | bytes 983048 | tf_op jit(solution)/shard_map/ppermute | solution.py:287
  8.0 14.8 %collective-permute-start.15 = (bf16[5,256,128]{2,1,0:T(8,128)(2,1)S(1)}, bf16[5,256,128]{2,1,0:T(8,128)(2,1)S(1)}, u32[]{:S(2)}, u32[]{:S(2)}) collective-permute-start(bf16[5,256,128]{2,1,0:T(8,128)(2,1)S(1)} %get-tuple-element.30.refs_1_), channel_id=1, source_target_pairs={{0,6},{1,7},{2,4},{3,5},{4,2},{5,3},{6,0},{7,1},{8,14},{9,15},{10,... | collective-permute-start | bytes 983048 | tf_op jit(solution)/shard_map/ppermute | solution.py:287
  9.2 11.8 %collective-permute-start.18 = (bf16[3,256,128]{2,1,0:T(8,128)(2,1)S(1)}, bf16[3,256,128]{2,1,0:T(8,128)(2,1)S(1)}, u32[]{:S(2)}, u32[]{:S(2)}) collective-permute-start(bf16[3,256,128]{2,1,0:T(8,128)(2,1)S(1)} %get-tuple-element.33), channel_id=1, source_target_pairs={{0,16},{8,24},{16,0},{24,8},{1,17},{9,25},{17,1},{25,9},{2,18},{10... | collective-permute-start | bytes 589832 | tf_op jit(solution)/shard_map/ppermute | solution.py:268
  12.8 17.7 %collective-permute-start.7 = (bf16[7,256,128]{2,1,0:T(8,128)(2,1)S(1)}, bf16[7,256,128]{2,1,0:T(8,128)(2,1)S(1)}, u32[]{:S(2)}, u32[]{:S(2)}) collective-permute-start(bf16[7,256,128]{2,1,0:T(8,128)(2,1)S(1)} %get-tuple-element.26), channel_id=1, source_target_pairs={{0,8},{8,0},{16,24},{24,16},{1,9},{9,1},{17,25},{25,17},{2,10},{10... | collective-permute-start | bytes 1376264 | tf_op jit(solution)/shard_map/ppermute | solution.py:268
  21.0 32.3 %collective-permute-start.8 = (bf16[7,256,128]{2,1,0:T(8,128)(2,1)S(1)}, bf16[7,256,128]{2,1,0:T(8,128)(2,1)S(1)}, u32[]{:S(2)}, u32[]{:S(2)}) collective-permute-start(bf16[7,256,128]{2,1,0:T(8,128)(2,1)S(1)} %get-tuple-element.27), channel_id=1, source_target_pairs={{0,16},{8,24},{16,0},{24,8},{1,17},{9,25},{17,1},{25,9},{2,18},{10... | collective-permute-start | bytes 1376264 | tf_op jit(solution)/shard_map/ppermute | solution.py:268
  21.0 39.4 %copy-start.5 = (s32[4]{0:T(128)S(1)}, s32[4]{0:T(128)}, u32[]{:S(2)}) copy-start(s32[4]{0:T(128)} %refs_0_.5) | copy-start | bytes 52
  21.0 34.3 %collective-permute-start.1 = (bf16[7,256,128]{2,1,0:T(8,128)(2,1)S(1)}, bf16[7,256,128]{2,1,0:T(8,128)(2,1)S(1)}, u32[]{:S(2)}, u32[]{:S(2)}) collective-permute-start(bf16[7,256,128]{2,1,0:T(8,128)(2,1)S(1)} %get-tuple-element.24.refs_1_), channel_id=1, source_target_pairs={{0,2},{1,3},{2,0},{3,1},{4,6},{5,7},{6,4},{7,5},{8,10},{9,11},{10,... | collective-permute-start | bytes 1376264 | tf_op jit(solution)/shard_map/ppermute | solution.py:287
  21.3 34.0 %collective-permute-start.3 = (bf16[7,256,128]{2,1,0:T(8,128)(2,1)S(1)}, bf16[7,256,128]{2,1,0:T(8,128)(2,1)S(1)}, u32[]{:S(2)}, u32[]{:S(2)}) collective-permute-start(bf16[7,256,128]{2,1,0:T(8,128)(2,1)S(1)} %get-tuple-element.24.refs_1_), channel_id=1, source_target_pairs={{0,4},{1,5},{2,6},{3,7},{4,0},{5,1},{6,2},{7,3},{8,12},{9,13},{10,... | collective-permute-start | bytes 1376264 | tf_op jit(solution)/shard_map/ppermute | solution.py:287
  22.8 33.0 %collective-permute-start.5 = (bf16[7,256,128]{2,1,0:T(8,128)(2,1)S(1)}, bf16[7,256,128]{2,1,0:T(8,128)(2,1)S(1)}, u32[]{:S(2)}, u32[]{:S(2)}) collective-permute-start(bf16[7,256,128]{2,1,0:T(8,128)(2,1)S(1)} %get-tuple-element.24.refs_1_), channel_id=1, source_target_pairs={{0,6},{1,7},{2,4},{3,5},{4,2},{5,3},{6,0},{7,1},{8,14},{9,15},{10,... | collective-permute-start | bytes 1376264 | tf_op jit(solution)/shard_map/ppermute | solution.py:287
  30.4 25.4 %collective-permute-start.9 = (bf16[7,256,128]{2,1,0:T(8,128)(2,1)S(1)}, bf16[7,256,128]{2,1,0:T(8,128)(2,1)S(1)}, u32[]{:S(2)}, u32[]{:S(2)}) collective-permute-start(bf16[7,256,128]{2,1,0:T(8,128)(2,1)S(1)} %pick.5), channel_id=1, source_target_pairs={{0,24},{8,16},{16,8},{24,0},{1,25},{9,17},{17,9},{25,1},{2,26},{10... | collective-permute-start | bytes 1376264 | tf_op jit(solution)/shard_map/ppermute | solution.py:268
  53.3 3.5 %collective-permute-start = (bf16[7,256,128]{2,1,0:T(8,128)(2,1)S(1)}, bf16[7,256,128]{2,1,0:T(8,128)(2,1)S(1)}, u32[]{:S(2)}, u32[]{:S(2)}) collective-permute-start(bf16[7,256,128]{2,1,0:T(8,128)(2,1)S(1)} %get-tuple-element.24.refs_1_), channel_id=1, source_target_pairs={{0,1},{1,0},{2,3},{3,2},{4,5},{5,4},{6,7},{7,6},{8,9},{9,8},{10,11... | collective-permute-start | bytes 1376264 | tf_op jit(solution)/shard_map/ppermute | solution.py:287
  55.3 3.9 %collective-permute-start.2 = (bf16[7,256,128]{2,1,0:T(8,128)(2,1)S(1)}, bf16[7,256,128]{2,1,0:T(8,128)(2,1)S(1)}, u32[]{:S(2)}, u32[]{:S(2)}) collective-permute-start(bf16[7,256,128]{2,1,0:T(8,128)(2,1)S(1)} %collective-permute-done.1.refs_3_), channel_id=1, source_target_pairs={{0,1},{1,0},{2,3},{3,2},{4,5},{5,4},{6,7},{7,6},{8,9},{9,8},{10,11... | collective-permute-start | bytes 1376264 | tf_op jit(solution)/shard_map/ppermute | solution.py:287
  55.3 4.6 %collective-permute-start.4 = (bf16[7,256,128]{2,1,0:T(8,128)(2,1)S(1)}, bf16[7,256,128]{2,1,0:T(8,128)(2,1)S(1)}, u32[]{:S(2)}, u32[]{:S(2)}) collective-permute-start(bf16[7,256,128]{2,1,0:T(8,128)(2,1)S(1)} %collective-permute-done.3.refs_5_), channel_id=1, source_target_pairs={{0,1},{1,0},{2,3},{3,2},{4,5},{5,4},{6,7},{7,6},{8,9},{9,8},{10,11... | collective-permute-start | bytes 1376264 | tf_op jit(solution)/shard_map/ppermute | solution.py:287
  55.8 4.1 %collective-permute-start.6 = (bf16[7,256,128]{2,1,0:T(8,128)(2,1)S(1)}, bf16[7,256,128]{2,1,0:T(8,128)(2,1)S(1)}, u32[]{:S(2)}, u32[]{:S(2)}) collective-permute-start(bf16[7,256,128]{2,1,0:T(8,128)(2,1)S(1)} %collective-permute-done.5.refs_7_), channel_id=1, source_target_pairs={{0,1},{1,0},{2,3},{3,2},{4,5},{5,4},{6,7},{7,6},{8,9},{9,8},{10,11... | collective-permute-start | bytes 1376264 | tf_op jit(solution)/shard_map/ppermute | solution.py:287
  55.9 9.0 %collective-permute-start.10 = (bf16[5,256,128]{2,1,0:T(8,128)(2,1)S(1)}, bf16[5,256,128]{2,1,0:T(8,128)(2,1)S(1)}, u32[]{:S(2)}, u32[]{:S(2)}) collective-permute-start(bf16[5,256,128]{2,1,0:T(8,128)(2,1)S(1)} %get-tuple-element.30.refs_1_), channel_id=1, source_target_pairs={{0,1},{1,0},{2,3},{3,2},{4,5},{5,4},{6,7},{7,6},{8,9},{9,8},{10,11... | collective-permute-start | bytes 983048 | tf_op jit(solution)/shard_map/ppermute | solution.py:287
  56.7 7.9 %collective-permute-start.19 = (bf16[3,256,128]{2,1,0:T(8,128)(2,1)S(1)}, bf16[3,256,128]{2,1,0:T(8,128)(2,1)S(1)}, u32[]{:S(2)}, u32[]{:S(2)}) collective-permute-start(bf16[3,256,128]{2,1,0:T(8,128)(2,1)S(1)} %get-tuple-element.34), channel_id=1, source_target_pairs={{0,24},{8,16},{16,8},{24,0},{1,25},{9,17},{17,9},{25,1},{2,26},{10... | collective-permute-start | bytes 589832 | tf_op jit(solution)/shard_map/ppermute | solution.py:268
  59.2 8.8 %collective-permute-start.12 = (bf16[5,256,128]{2,1,0:T(8,128)(2,1)S(1)}, bf16[5,256,128]{2,1,0:T(8,128)(2,1)S(1)}, u32[]{:S(2)}, u32[]{:S(2)}) collective-permute-start(bf16[5,256,128]{2,1,0:T(8,128)(2,1)S(1)} %collective-permute-done.11.refs_3_), channel_id=1, source_target_pairs={{0,1},{1,0},{2,3},{3,2},{4,5},{5,4},{6,7},{7,6},{8,9},{9,8},{10,11... | collective-permute-start | bytes 983048 | tf_op jit(solution)/shard_map/ppermute | solution.py:287
  59.9 19.1 %collective-permute-start.14 = (bf16[5,256,128]{2,1,0:T(8,128)(2,1)S(1)}, bf16[5,256,128]{2,1,0:T(8,128)(2,1)S(1)}, u32[]{:S(2)}, u32[]{:S(2)}) collective-permute-start(bf16[5,256,128]{2,1,0:T(8,128)(2,1)S(1)} %collective-permute-done.13.refs_5_), channel_id=1, source_target_pairs={{0,1},{1,0},{2,3},{3,2},{4,5},{5,4},{6,7},{7,6},{8,9},{9,8},{10,11... | collective-permute-start | bytes 983048 | tf_op jit(solution)/shard_map/ppermute | solution.py:287
  59.9 21.7 %collective-permute-start.16 = (bf16[5,256,128]{2,1,0:T(8,128)(2,1)S(1)}, bf16[5,256,128]{2,1,0:T(8,128)(2,1)S(1)}, u32[]{:S(2)}, u32[]{:S(2)}) collective-permute-start(bf16[5,256,128]{2,1,0:T(8,128)(2,1)S(1)} %collective-permute-done.15.refs_7_), channel_id=1, source_target_pairs={{0,1},{1,0},{2,3},{3,2},{4,5},{5,4},{6,7},{7,6},{8,9},{9,8},{10,11... | collective-permute-start | bytes 983048 | tf_op jit(solution)/shard_map/ppermute | solution.py:287
  64.7 14.0 %collective-permute-start.29 = (bf16[7,128,128]{2,1,0:T(8,128)(2,1)S(1)}, bf16[7,128,128]{2,1,0:T(8,128)(2,1)S(1)}, u32[]{:S(2)}, u32[]{:S(2)}) collective-permute-start(bf16[7,128,128]{2,1,0:T(8,128)(2,1)S(1)} %get-tuple-element.28.refs_0_), channel_id=1, source_target_pairs={{0,2},{1,3},{2,0},{3,1},{4,6},{5,7},{6,4},{7,5},{8,10},{9,11},{10,... | collective-permute-start | bytes 688136 | tf_op jit(solution)/shard_map/ppermute | solution.py:311
  64.9 18.8 %collective-permute-start.31 = (bf16[7,128,128]{2,1,0:T(8,128)(2,1)S(1)}, bf16[7,128,128]{2,1,0:T(8,128)(2,1)S(1)}, u32[]{:S(2)}, u32[]{:S(2)}) collective-permute-start(bf16[7,128,128]{2,1,0:T(8,128)(2,1)S(1)} %get-tuple-element.29.refs_1_), channel_id=1, source_target_pairs={{0,6},{1,7},{2,4},{3,5},{4,2},{5,3},{6,0},{7,1},{8,14},{9,15},{10,... | collective-permute-start | bytes 688136 | tf_op jit(solution)/shard_map/ppermute | solution.py:311
  68.0 28.5 %collective-permute-start.20 = (bf16[2,256,128]{2,1,0:T(8,128)(2,1)S(1)}, bf16[2,256,128]{2,1,0:T(8,128)(2,1)S(1)}, u32[]{:S(2)}, u32[]{:S(2)}) collective-permute-start(bf16[2,256,128]{2,1,0:T(8,128)(2,1)S(1)} %get-tuple-element.38), channel_id=1, source_target_pairs={{0,8},{8,0},{16,24},{24,16},{1,9},{9,1},{17,25},{25,17},{2,10},{10... | collective-permute-start | bytes 393224 | tf_op jit(solution)/shard_map/ppermute | solution.py:268
  78.7 37.4 %collective-permute-start.30 = (bf16[7,128,128]{2,1,0:T(8,128)(2,1)S(1)}, bf16[7,128,128]{2,1,0:T(8,128)(2,1)S(1)}, u32[]{:S(2)}, u32[]{:S(2)}) collective-permute-start(bf16[7,128,128]{2,1,0:T(8,128)(2,1)S(1)} %collective-permute-done.29), channel_id=1, source_target_pairs={{2,0},{3,1},{0,8},{1,9},{6,16},{7,17},{4,24},{5,25},{10,2},{11,3},... | collective-permute-start | bytes 688136 | tf_op jit(solution)/shard_map/ppermute | solution.py:312
  78.9 20.7 %collective-permute-start.21 = (bf16[2,256,128]{2,1,0:T(8,128)(2,1)S(1)}, bf16[2,256,128]{2,1,0:T(8,128)(2,1)S(1)}, u32[]{:S(2)}, u32[]{:S(2)}) collective-permute-start(bf16[2,256,128]{2,1,0:T(8,128)(2,1)S(1)} %get-tuple-element.39), channel_id=1, source_target_pairs={{0,16},{8,24},{16,0},{24,8},{1,17},{9,25},{17,1},{25,9},{2,18},{10... | collective-permute-start | bytes 393224 | tf_op jit(solution)/shard_map/ppermute | solution.py:268
  81.6 18.0 %collective-permute-start.22 = (bf16[2,256,128]{2,1,0:T(8,128)(2,1)S(1)}, bf16[2,256,128]{2,1,0:T(8,128)(2,1)S(1)}, u32[]{:S(2)}, u32[]{:S(2)}) collective-permute-start(bf16[2,256,128]{2,1,0:T(8,128)(2,1)S(1)} %get-tuple-element.40), channel_id=1, source_target_pairs={{0,24},{8,16},{16,8},{24,0},{1,25},{9,17},{17,9},{25,1},{2,26},{10... | collective-permute-start | bytes 393224 | tf_op jit(solution)/shard_map/ppermute | solution.py:268
  83.7 35.4 %collective-permute-start.32 = (bf16[7,128,128]{2,1,0:T(8,128)(2,1)S(1)}, bf16[7,128,128]{2,1,0:T(8,128)(2,1)S(1)}, u32[]{:S(2)}, u32[]{:S(2)}) collective-permute-start(bf16[7,128,128]{2,1,0:T(8,128)(2,1)S(1)} %collective-permute-done.31), channel_id=1, source_target_pairs={{6,1},{7,0},{4,9},{5,8},{2,17},{3,16},{0,25},{1,24},{14,3},{15,2},... | collective-permute-start | bytes 688136 | tf_op jit(solution)/shard_map/ppermute | solution.py:312
  96.5 11.4 %collective-permute-start.27 = (bf16[3,128,128]{2,1,0:T(8,128)(2,1)S(1)}, bf16[3,128,128]{2,1,0:T(8,128)(2,1)S(1)}, u32[]{:S(2)}, u32[]{:S(2)}) collective-permute-start(bf16[3,128,128]{2,1,0:T(8,128)(2,1)S(1)} %get-tuple-element.36.refs_3_), channel_id=1, source_target_pairs={{0,4},{1,5},{2,6},{3,7},{4,0},{5,1},{6,2},{7,3},{8,12},{9,13},{10,... | collective-permute-start | bytes 294920 | tf_op jit(solution)/shard_map/ppermute | solution.py:311
  100.7 11.1 %collective-permute-start.24 = (bf16[2,128,128]{2,1,0:T(8,128)(2,1)S(1)}, bf16[2,128,128]{2,1,0:T(8,128)(2,1)S(1)}, u32[]{:S(2)}, u32[]{:S(2)}) collective-permute-start(bf16[2,128,128]{2,1,0:T(8,128)(2,1)S(1)} %get-tuple-element.42.refs_5_), channel_id=1, source_target_pairs={{0,4},{1,5},{2,6},{3,7},{4,0},{5,1},{6,2},{7,3},{8,12},{9,13},{10,... | collective-permute-start | bytes 196616 | tf_op jit(solution)/shard_map/ppermute | solution.py:311
  100.7 20.5 %collective-permute-start.26 = (bf16[3,128,128]{2,1,0:T(8,128)(2,1)S(1)}, bf16[3,128,128]{2,1,0:T(8,128)(2,1)S(1)}, u32[]{:S(2)}, u32[]{:S(2)}) collective-permute-start(bf16[3,128,128]{2,1,0:T(8,128)(2,1)S(1)} %get-tuple-element.35.refs_2_), channel_id=1, source_target_pairs={{0,0},{1,1},{2,8},{3,9},{4,16},{5,17},{6,24},{7,25},{8,2},{9,3},{1... | collective-permute-start | bytes 294920 | tf_op jit(solution)/shard_map/ppermute | solution.py:312
  107.9 14.6 %collective-permute-start.28 = (bf16[3,128,128]{2,1,0:T(8,128)(2,1)S(1)}, bf16[3,128,128]{2,1,0:T(8,128)(2,1)S(1)}, u32[]{:S(2)}, u32[]{:S(2)}) collective-permute-start(bf16[3,128,128]{2,1,0:T(8,128)(2,1)S(1)} %collective-permute-done.27), channel_id=1, source_target_pairs={{4,1},{5,0},{6,9},{7,8},{0,17},{1,16},{2,25},{3,24},{12,3},{13,2},... | collective-permute-start | bytes 294920 | tf_op jit(solution)/shard_map/ppermute | solution.py:312
  111.8 12.4 %collective-permute-start.23 = (bf16[2,128,128]{2,1,0:T(8,128)(2,1)S(1)}, bf16[2,128,128]{2,1,0:T(8,128)(2,1)S(1)}, u32[]{:S(2)}, u32[]{:S(2)}) collective-permute-start(bf16[2,128,128]{2,1,0:T(8,128)(2,1)S(1)} %get-tuple-element.41.refs_4_), channel_id=1, source_target_pairs={{0,0},{1,1},{2,8},{3,9},{4,16},{5,17},{6,24},{7,25},{8,2},{9,3},{1... | collective-permute-start | bytes 196616 | tf_op jit(solution)/shard_map/ppermute | solution.py:312
  116.0 8.2 %collective-permute-start.25 = (bf16[2,128,128]{2,1,0:T(8,128)(2,1)S(1)}, bf16[2,128,128]{2,1,0:T(8,128)(2,1)S(1)}, u32[]{:S(2)}, u32[]{:S(2)}) collective-permute-start(bf16[2,128,128]{2,1,0:T(8,128)(2,1)S(1)} %collective-permute-done.24), channel_id=1, source_target_pairs={{4,1},{5,0},{6,9},{7,8},{0,17},{1,16},{2,25},{3,24},{12,3},{13,2},... | collective-permute-start | bytes 196616 | tf_op jit(solution)/shard_map/ppermute | solution.py:312
